TPU v7x, 256 devices: a whole 4x4x8 slice. The times are simulated.
256 devices in a mesh: row: 16 (over z, core), col: 16 (over y, x).
Axes of the slice: x: 4, y: 4, z: 8, core: 2. Of those that a mesh axis runs over, the one named last changes fastest.
Arguments:
- right_sides: float32 [4, 1024, 4096], P(None, 'row', 'col'), may hold values from -6 to 6
- low_left: bfloat16 [6, 4096, 128], P(None, 'col'), may hold values from -0.25 to 0.25
- low_right: bfloat16 [6, 4096, 128], P(None, 'col'), may hold values from -0.09375 to 0.09375
- up_left: bfloat16 [6, 4096, 128], P(None, 'col'), may hold values from -0.25 to 0.25
- up_right: bfloat16 [6, 4096, 128], P(None, 'col'), may hold values from -0.09375 to 0.09375
- low_ranks: int32 [6], replicated, may hold values from 1 to 4
- up_ranks: int32 [6], replicated, may hold values from 1 to 4
- inv_lower: bfloat16 [4, 4096, 4096], P(None, 'col', 'row'), may hold values from -0.09375 to 0.09375
- inv_upper: bfloat16 [4, 4096, 4096], P(None, 'col', 'row'), may hold values from -0.09375 to 0.09375
Outputs:
- solution: float32 [4, 1024, 4096], P(None, 'row', 'col')
Inputs may be any that keep to these rules, and one draw needn't show every extreme that they name: `low_ranks`: factor columns beyond 32 times this value are padding with arbitrary values and must be masked out. `up_ranks`: factor columns beyond 32 times this value are padding with arbitrary values and must be masked out.
All inputs are finite; a program needn't handle non-finite values.
Results may differ from a plain program's by a relative error of at most 0.03.
Values may be sent and summed in bfloat16 or wider, within the bound.
No kernel may reach another device: no remote copies, remote signals or barrier semaphores. Data moves between devices by JAX's collectives and lax.ppermute only.
A program may use at most 64 MiB of HBM per device.

v0:
```python
import jax
import jax.numpy as jnp
from jax import lax
from jax.experimental import pallas as pl
from jax.experimental.pallas import tpu as pltpu
from jax.sharding import PartitionSpec as P

RBLK = 32
BF16 = jnp.bfloat16
F32 = jnp.float32
SIDE = 4
Z_GROUPS = [[2 * z + core for z in range(8)] for core in range(2)]


def routes(to):
    index = lambda q, j, y, x: (SIDE * q + j) * SIDE * SIDE + SIDE * y + x
    span = range(SIDE)
    return [
        (index(q, j, y, x), index(*to(q, j, y, x)))
        for q in span for j in span for y in span for x in span
    ]


def permuted(value, to):
    return lax.ppermute(value, ("row", "col"), routes(to))


def gathered_y(value):
    return [value] + [
        permuted(value, lambda q, j, y, x: (q, j, (y + s) % SIDE, x)) for s in range(1, SIDE)
    ]


def gathered_x(value):
    return [value] + [
        permuted(value, lambda q, j, y, x: (q, j, y, (x + s) % SIDE)) for s in range(1, SIDE)
    ]


def scattered_q(values):
    return [values[0]] + [
        permuted(values[s], lambda q, j, y, x: ((q + s) % SIDE, j, y, x))
        for s in range(1, SIDE)
    ]


def scattered_x(values, sign=1):
    return [values[0]] + [
        permuted(values[s], lambda q, j, y, x: (q, j, y, (x + sign * s) % SIDE))
        for s in range(1, SIDE)
    ]


def from_every_z(value):
    return lax.all_to_all(value, "row", 0, 0, tiled=True, axis_index_groups=Z_GROUPS)


def own_tile():
    return lax.rem(lax.axis_index("col"), SIDE)


def wrapped(value):
    return lax.rem(value + 2 * SIDE, SIDE)


def swapped(value):
    return permuted(value, lambda q, j, y, x: (y, j, q, x))


def swap_core(value):
    return permuted(value, lambda q, j, y, x: (q, j ^ 1, y, x))


def swap_pair(value):
    return permuted(value, lambda q, j, y, x: (q, j ^ 2, y, x))


def dot(left, right):
    return jnp.dot(left, right, preferred_element_type=F32)


def dot_t(left, right):
    return lax.dot_general(
        left, right, (((1,), (1,)), ((), ())), preferred_element_type=F32
    )


def pair_of(i, j):
    high, low = max(i, j), min(i, j)
    return high * (high - 1) // 2 + low


def partners(tile):
    return [t for t in range(SIDE) if t != tile]


def kernel_call(body, out_shape, smem=(), flops=0, grid=None, in_specs=None, out_specs=None, scratch=()):
    def run(*args):
        specs = in_specs or [
            pl.BlockSpec(memory_space=pltpu.SMEM if at in smem else pltpu.VMEM)
            for at in range(len(args))
        ]
        outs = jax.tree.leaves(out_shape)
        moved = sum(a.size * a.dtype.itemsize for a in [*args, *outs])
        more = {} if grid is None else {"grid": grid, "out_specs": out_specs}
        return pl.pallas_call(
            body,
            out_shape=out_shape,
            in_specs=specs,
            scratch_shapes=list(scratch),
            compiler_params=pltpu.CompilerParams(vmem_limit_bytes=30 * 2**20),
            cost_estimate=pl.CostEstimate(
                flops=flops, bytes_accessed=moved, transcendentals=0
            ),
            **more,
        )(*args)

    return run


def pack_kernel(right_ref, low_ref, up_ref, *out_refs):
    n = right_ref.shape[1]
    rank_cols = low_ref.shape[2]
    share = rank_cols // lax.axis_size("row")
    row = lax.axis_index("row")
    at = lax.broadcasted_iota(jnp.int32, (share, rank_cols), 1)
    want = lax.broadcasted_iota(jnp.int32, (share, rank_cols), 0) + row * share
    pick = (at == want).astype(F32).astype(BF16)
    for s, out_ref in enumerate(out_refs):
        tile = wrapped(own_tile() + s)
        out_ref[:n] = right_ref[tile].astype(BF16)
        pieces = []
        for slot in range(SIDE - 1):
            pair, is_low = partner_pair(tile, slot)
            piece = jnp.where(is_low, dot_t(pick, low_ref[pair]), dot_t(pick, up_ref[pair]))
            pieces.append(piece)
        out_ref[n:] = jnp.concatenate(pieces, axis=0).astype(BF16)


def partner_pair(tile, slot):
    is_low = slot < tile
    partner = jnp.where(is_low, slot, slot + 1)
    high = jnp.where(is_low, tile, partner)
    low = jnp.where(is_low, partner, tile)
    return jnp.where(high == 1, 0, jnp.where(high == 2, 1, 3)) + low, is_low


def order_kernel(sign, *refs):
    out_ref = refs[-1]
    for s in range(SIDE):
        out_ref[wrapped(own_tile() - sign * s)] = refs[s][...].astype(out_ref.dtype)


def stack_kernel(*refs):
    rows = refs[0].shape[0]
    for s, ref in enumerate(refs[:-1]):
        refs[-1][s * rows : (s + 1) * rows] = ref[...]


def deal_kernel(lower_ref, upper_ref, *out_refs):
    for s in range(SIDE):
        tile = wrapped(own_tile() + s)
        out_refs[s][...] = lower_ref[tile]
        out_refs[SIDE + s][...] = upper_ref[tile]


def turn_kernel(low_ref, up_ref, *out_refs):
    rank_cols = low_ref.shape[2]
    one = lax.broadcasted_iota(jnp.int32, (rank_cols, rank_cols), 0)
    two = lax.broadcasted_iota(jnp.int32, (rank_cols, rank_cols), 1)
    eye = (one == two).astype(F32).astype(BF16)
    for s, out_ref in enumerate(out_refs):
        tile = wrapped(own_tile() + s)
        for slot in range(SIDE - 1):
            pair, is_low = partner_pair(tile, slot)
            factor = jnp.where(is_low, up_ref[pair], low_ref[pair])
            out_ref[slot * rank_cols : (slot + 1) * rank_cols] = dot_t(eye, factor).astype(BF16)


def products_kernel(n, padded, count, *refs):
    x_refs, inverse_refs = refs[:SIDE], refs[SIDE : SIDE + count]
    out_refs = refs[SIDE + count : -2]
    joined_ref, extra_ref = refs[-2:]
    lower, upper = inverse_refs[:SIDE], inverse_refs[SIDE:]
    rows = x_refs[0].shape[1]

    @pl.when(pl.program_id(0) == 0)
    def _():
        row = lax.axis_index("row")
        flip, q = lax.rem(row, SIDE), row // SIDE
        y = lax.axis_index("col") // SIDE
        for s in range(SIDE):
            t = wrapped(y - s - q)
            for at in range(SIDE):
                block = x_refs[s][at ^ flip]
                joined_ref[at, t, :rows] = block
                if rows > n:
                    extra_ref[at, t, : rows - n] = block[n:]

    width = joined_ref.shape[3]
    value = sum(
        dot_t(joined_ref[at].reshape(SIDE * padded, width), lower[at][...])
        for at in range(SIDE)
    )
    if rows > n:
        other = sum(
            dot_t(extra_ref[at].reshape(SIDE * (padded - n), width), upper[at][...])
            for at in range(SIDE)
        )
        share = (rows - n) // (SIDE - 1)
        slot = lax.broadcasted_iota(jnp.int32, (rows - n, value.shape[1]), 0) // share
    for t in range(SIDE):
        start = t * padded
        out_refs[t][:n] = value[start : start + n].astype(BF16)
        if rows > n:
            mine = value[start + n : start + rows]
            its = other[t * (padded - n) : t * (padded - n) + rows - n]
            out_refs[t][n:] = jnp.where(slot < own_tile(), mine, its).astype(BF16)


def products(n, gathered, *inverses):
    blocks, rows, width = gathered[0].shape
    total = inverses[0].shape[0]
    padded = rows + -rows % 16
    count = len(inverses)
    whole = pl.BlockSpec(gathered[0].shape, lambda a: (0, 0, 0))
    return kernel_call(
        lambda *refs: products_kernel(n, padded, count, *refs),
        [jax.ShapeDtypeStruct((rows, total), BF16)] * SIDE,
        flops=2 * SIDE * blocks * rows * width * total,
        grid=(total // 256,),
        in_specs=[whole] * SIDE
        + [pl.BlockSpec((256, width), lambda a: (a, 0)) for _ in inverses],
        out_specs=[pl.BlockSpec((rows, 256), lambda a: (0, a))] * SIDE,
        scratch=[
            pltpu.VMEM((blocks, SIDE, padded, width), BF16),
            pltpu.VMEM((blocks, SIDE, max(padded - n, 16), width), BF16),
        ],
    )(*gathered, *inverses)


def summed(refs):
    whole = refs[0][...].astype(F32)
    for ref in refs[1:]:
        whole = whole + ref[...].astype(F32)
    return whole


def total_kernel(n, *refs):
    dense_ref, extra_ref = refs[SIDE:]
    whole = summed(refs[:SIDE])
    dense_ref[...] = whole[:n]
    extra = whole[n:].astype(BF16)
    for at in range(extra_ref.shape[0]):
        extra_ref[at] = extra


def project(dense, turned, slot, rank_cols):
    width = turned[0].shape[1]
    return sum(
        dot_t(
            dense[:, at * width : (at + 1) * width],
            turned[at][slot * rank_cols : (slot + 1) * rank_cols],
        )
        for at in range(SIDE)
    )


def couple_kernel(dense_ref, mine_ref, other_ref, *refs):
    turned, (extra_ref, send_ref, later_ref) = refs[:SIDE], refs[SIDE:]
    slots = SIDE - 1
    rank_cols = turned[0].shape[0] // slots
    width = turned[0].shape[1]
    share = mine_ref.shape[1] // slots
    even = lax.rem(lax.axis_index("row"), 2) == 0
    tile = own_tile()
    for z in range(mine_ref.shape[0]):
        mine, other = mine_ref[z].astype(F32), other_ref[z].astype(F32)
        first = jnp.where(even, mine, other)
        second = jnp.where(even, other, mine)
        for slot in range(slots):
            at = slice(slot * share, (slot + 1) * share)
            start = slot * rank_cols + z * 2 * share
            extra_ref[start : start + 2 * share] = jnp.concatenate(
                [first[at], second[at]], axis=0
            ).astype(BF16)
    dense = dense_ref[...].astype(BF16)
    pieces = [project(dense, turned, slot, rank_cols) for slot in range(slots)]

    def coupling(left, right):
        left = pl.multiple_of(left * rank_cols, rank_cols)
        right = pl.multiple_of(right * rank_cols, rank_cols)
        return sum(
            dot_t(
                extra_ref[pl.ds(left, rank_cols), at * width : (at + 1) * width],
                turned[at][pl.ds(right, rank_cols), :],
            )
            for at in range(SIDE)
        )

    one = tile == 1
    pick = lambda a, b: jnp.where(one, a, b)
    pieces += [coupling(0, pick(1, 2)), coupling(pick(0, 1), 2)]
    send_ref[...] = jnp.concatenate(pieces, axis=0).astype(BF16)
    later_ref[:rank_cols] = coupling(pick(1, 2), 0).astype(BF16)
    later_ref[rank_cols:] = coupling(2, pick(0, 1)).astype(BF16)


def last_project_kernel(*refs):
    turned, (later_ref, dense_ref, send_ref) = refs[SIDE : 2 * SIDE], refs[2 * SIDE :]
    slots = SIDE - 1
    rank_cols = turned[0].shape[0] // slots
    whole = summed(refs[:SIDE])
    dense_ref[...] = whole
    dense = whole.astype(BF16)
    pieces = [project(dense, turned, slot, rank_cols) for slot in range(slots)]
    send = jnp.concatenate(pieces, axis=0).astype(BF16)
    n = send.shape[0]
    send_ref[:n] = send
    send_ref[n:] = later_ref[...]


def add_kernel(*refs):
    refs[-1][...] = summed(refs[:-1]).astype(BF16)


def finish_kernel(is_lower, *refs):
    dense_ref, extra_ref, ranks_ref = refs[SIDE : SIDE + 3]
    out_refs, sums_ref = refs[SIDE + 3 : -1], refs[-1]
    for s in range(SIDE):
        sums_ref[wrapped(own_tile() - s)] = refs[s][...]
    n = dense_ref.shape[0]
    rank_cols = extra_ref.shape[0] // (SIDE - 1)
    width = dense_ref.shape[1] // SIDE
    tile = lax.rem(lax.axis_index("col"), SIDE)
    columns = lax.broadcasted_iota(jnp.int32, (n, rank_cols), 1)
    at_coupling = (SIDE - 1) * n
    coupling = {}
    order = list(range(SIDE)) if is_lower else list(range(SIDE))[::-1]
    first, second, third, last = order
    for which, key in enumerate(((third, second, first), (last, second, first))):
        coupling[key] = (second, which)
    for which, key in enumerate(((last, third, first), (last, third, second))):
        coupling[key] = (third, which)
    if not is_lower:
        coupling = {
            (0, 2, 3): (2, 0), (1, 2, 3): (2, 1), (0, 1, 2): (1, 0), (0, 1, 3): (1, 1)
        }
    masked = {}
    for at, source in enumerate(order):
        for target in order[at + 1 :]:
            slot = partners(source).index(target)
            value = sums_ref[source, slot * n : (slot + 1) * n].astype(F32)
            for before in order[:at]:
                held, which = coupling[target, source, before]
                start = at_coupling + which * rank_cols
                value = value - dot(
                    masked[source, before], sums_ref[held, start : start + rank_cols]
                )
            keep = columns < RBLK * ranks_ref[pair_of(source, target)]
            masked[target, source] = jnp.where(keep, value, 0.0).astype(BF16)
    result = dense_ref[...]
    nothing = jnp.zeros((n, rank_cols), BF16)
    for slot in range(SIDE - 1):
        mine = nothing
        for target in range(SIDE):
            source = partners(target)[slot]
            if (target, source) in masked:
                mine = jnp.where(tile == target, masked[target, source], mine)
        result = result - dot(
            mine, extra_ref[slot * rank_cols : (slot + 1) * rank_cols]
        )
    result = result.astype(BF16)
    for at in range(SIDE):
        block = result[:, at * width : (at + 1) * width]
        if is_lower:
            out_refs[0][wrapped(tile - at)] = block
        else:
            out_refs[at][...] = block


def shards(
    right_sides, low_left, low_right, up_left, up_right, low_ranks, up_ranks, inv_lower, inv_upper
):
    n, width = right_sides.shape[1:]
    rank_cols = low_left.shape[2]
    slots = SIDE - 1
    share = rank_cols // lax.axis_size("row")
    total = SIDE * width
    shape = jax.ShapeDtypeStruct

    height = n + slots * share
    rows = kernel_call(pack_kernel, [shape((height, width), BF16)] * SIDE)(
        right_sides, low_left, up_left
    )
    tied = lax.optimization_barrier
    rows = scattered_x(rows)
    rows, inv_lower, inv_upper = tied((rows, inv_lower, inv_upper))
    dealt = kernel_call(deal_kernel, [shape((width, width), BF16)] * 2 * SIDE)(
        inv_lower, inv_upper
    )
    rows = kernel_call(
        lambda *refs: order_kernel(1, *refs), shape((SIDE, height, width), BF16)
    )(*rows)
    rows = swapped(rows)
    stack = kernel_call(stack_kernel, shape((total, width), BF16))
    lower = stack(*scattered_x(dealt[:SIDE]))
    far_lower = swap_pair(lower)
    upper_parts, lower = tied((dealt[SIDE:], lower))
    upper = stack(*scattered_x(upper_parts))
    near = (swap_core(lower), swap_core(upper))
    gathered = gathered_y(rows)
    far_lower, upper, near, gathered = tied((far_lower, upper, near, gathered))
    far_upper = swap_pair(upper)
    lower = [lower, near[0], far_lower, swap_core(far_lower)]
    low_right, up_right, gathered = tied((low_right, up_right, gathered))
    turned = scattered_x(
        kernel_call(turn_kernel, [shape((slots * rank_cols, width), BF16)] * SIDE)(
            low_right, up_right
        )
    )
    turned, far_upper = tied((turned, far_upper))
    upper = [upper, near[1], far_upper, swap_core(far_upper)]
    dense, extra = kernel_call(
        lambda *refs: total_kernel(n, *refs),
        (shape((n, total), F32), shape((8, slots * share, total), BF16)),
    )(*scattered_q(products(n, gathered, *lower, *upper)))
    mine = from_every_z(extra)
    packed = slots * n + 2 * rank_cols
    extra, send, later = kernel_call(
        couple_kernel,
        (
            shape((slots * rank_cols, total), BF16),
            shape((packed, rank_cols), BF16),
            shape((2 * rank_cols, rank_cols), BF16),
        ),
    )(dense, mine, swap_core(mine), *turned)

    def finished(is_lower, send, dense, ranks):
        sums = kernel_call(add_kernel, shape((packed, rank_cols), BF16))(*gathered_y(send))
        outs = [shape((SIDE, n, width), BF16)] if is_lower else [shape((n, width), BF16)] * SIDE
        return kernel_call(
            lambda *refs: finish_kernel(is_lower, *refs),
            outs,
            smem=(SIDE + 2,),
            scratch=[pltpu.VMEM((SIDE, packed, rank_cols), BF16)],
        )(*gathered_x(sums), dense, extra, ranks)

    [rows] = finished(True, send, dense, low_ranks)
    parts = products(n, gathered_y(swapped(rows)), *upper)
    dense, send = kernel_call(
        last_project_kernel,
        (shape((n, total), F32), shape((packed, rank_cols), BF16)),
    )(*scattered_q(parts), *turned, later)
    rows = finished(False, send, dense, up_ranks)
    return kernel_call(
        lambda *refs: order_kernel(-1, *refs), shape((SIDE, n, width), F32)
    )(*scattered_x(rows, -1))


def solution(mesh):
    in_specs = (
        P(None, "row", "col"),
        P(None, "col", None),
        P(None, "col", None),
        P(None, "col", None),
        P(None, "col", None),
        P(),
        P(),
        P(None, "col", "row"),
        P(None, "col", "row"),
    )
    out_specs = P(None, "row", "col")
    return jax.shard_map(shards, mesh=mesh, in_specs=in_specs, out_specs=out_specs, check_vma=False)
```

profile of v0, /device:TPU:2, one launch (start us, length us, event | category | flops | bytes accessed | tf_op | source)
XLA Modules:
  0.0 211.8 jit_solution(4506759761355278771)
XLA Ops:
  3.5 1.5 collective-permute-start
  5.1 2.8 %collective-permute-start.1 = (bf16[88,256]{1,0:T(8,128)(2,1)S(1)}, bf16[88,256]{1,0:T(8,128)(2,1)S(1)}, u32[]{:S(2)}, u32[]{:S(2)}) collective-permute-start(bf16[88,256]{1,0:T(8,128)(2,1)S(1)} %get-tuple-element.72), channel_id=1, source_target_pairs={{0,2},{1,3},{2,0},{3,1},{4,6},{5,7},{6,4},{7,5},{8,10},{9,11},{10,... | collective-permute-start | bytes 135176 | tf_op jit(solution)/shard_map/ppermute | solution.py:25
  8.3 2.3 %collective-permute-done.1.refs_2_ = bf16[88,256]{1,0:T(8,128)(2,1)S(1)} collective-permute-done((bf16[88,256]{1,0:T(8,128)(2,1)S(1)}, bf16[88,256]{1,0:T(8,128)(2,1)S(1)}, u32[]{:S(2)}, u32[]{:S(2)}) %collective-permute-start.1) | collective-permute-done | bytes 45088 | tf_op jit(solution)/shard_map/ppermute | solution.py:25
  12.1 2.5 %collective-permute-start.4 = (bf16[256,256]{1,0:T(8,128)(2,1)S(1)}, bf16[256,256]{1,0:T(8,128)(2,1)S(1)}, u32[]{:S(2)}, u32[]{:S(2)}) collective-permute-start(bf16[256,256]{1,0:T(8,128)(2,1)S(1)} %get-tuple-element.78), channel_id=1, source_target_pairs={{0,2},{1,3},{2,0},{3,1},{4,6},{5,7},{6,4},{7,5},{8,10},{9,11},{10,... | collective-permute-start | bytes 393224 | tf_op jit(solution)/shard_map/ppermute | solution.py:25
  14.7 2.1 collective-permute-start.5
  21.3 2.6 %collective-permute-start.8 = (bf16[256,256]{1,0:T(8,128)(2,1)S(1)}, bf16[256,256]{1,0:T(8,128)(2,1)S(1)}, u32[]{:S(2)}, u32[]{:S(2)}) collective-permute-start(bf16[256,256]{1,0:T(8,128)(2,1)S(1)} %get-tuple-element.86), channel_id=1, source_target_pairs={{0,2},{1,3},{2,0},{3,1},{4,6},{5,7},{6,4},{7,5},{8,10},{9,11},{10,... | collective-permute-start | bytes 393224 | tf_op jit(solution)/shard_map/ppermute | solution.py:25
  23.9 1.4 collective-permute-start.9
  26.2 2.0 collective-permute-start.6
  29.3 14.8 %collective-permute-start.15 = (bf16[4,88,256]{2,1,0:T(8,128)(2,1)S(1)}, bf16[4,88,256]{2,1,0:T(8,128)(2,1)S(1)}, u32[]{:S(2)}, u32[]{:S(2)}) collective-permute-start(bf16[4,88,256]{2,1,0:T(8,128)(2,1)S(1)} %collective-permute-done.12.refs_0_), channel_id=1, source_target_pairs={{0,12},{1,13},{2,14},{3,15},{4,0},{5,1},{6,2},{7,3},{8,4},{9,5},{1... | collective-permute-start | bytes 540680 | tf_op jit(solution)/shard_map/ppermute | solution.py:25
  44.4 4.6 %collective-permute-done.15.refs_3_ = bf16[4,88,256]{2,1,0:T(8,128)(2,1)S(1)} collective-permute-done((bf16[4,88,256]{2,1,0:T(8,128)(2,1)S(1)}, bf16[4,88,256]{2,1,0:T(8,128)(2,1)S(1)}, u32[]{:S(2)}, u32[]{:S(2)}) %collective-permute-start.15) | collective-permute-done | bytes 180256 | tf_op jit(solution)/shard_map/ppermute | solution.py:25
  49.0 3.3 %collective-permute-done.14.refs_2_ = bf16[4,88,256]{2,1,0:T(8,128)(2,1)S(1)} collective-permute-done((bf16[4,88,256]{2,1,0:T(8,128)(2,1)S(1)}, bf16[4,88,256]{2,1,0:T(8,128)(2,1)S(1)}, u32[]{:S(2)}, u32[]{:S(2)}) %collective-permute-start.14) | collective-permute-done | bytes 180256 | tf_op jit(solution)/shard_map/ppermute | solution.py:25
  52.3 3.9 %collective-permute-done.13.refs_1_ = bf16[4,88,256]{2,1,0:T(8,128)(2,1)S(1)} collective-permute-done((bf16[4,88,256]{2,1,0:T(8,128)(2,1)S(1)}, bf16[4,88,256]{2,1,0:T(8,128)(2,1)S(1)}, u32[]{:S(2)}, u32[]{:S(2)}) %collective-permute-start.13) | collective-permute-done | bytes 180256 | tf_op jit(solution)/shard_map/ppermute | solution.py:25
  56.2 2.5 %collective-permute-start.20 = (bf16[1024,256]{1,0:T(8,128)(2,1)S(1)}, bf16[1024,256]{1,0:T(8,128)(2,1)S(1)}, u32[]{:S(2)}, u32[]{:S(2)}) collective-permute-start(bf16[1024,256]{1,0:T(8,128)(2,1)S(1)} %shard_map.94.refs_8_.refs_4_), channel_id=1, source_target_pairs={{0,32},{1,33},{2,34},{3,35},{4,36},{5,37},{6,38},{7,39},{8,40},{9,... | collective-permute-start | bytes 1572872 | tf_op jit(solution)/shard_map/ppermute | solution.py:25
  59.6 5.9 %collective-permute-start.18 = (bf16[384,256]{1,0:T(8,128)(2,1)S(1)}, bf16[384,256]{1,0:T(8,128)(2,1)S(1)}, u32[]{:S(2)}, u32[]{:S(2)}) collective-permute-start(bf16[384,256]{1,0:T(8,128)(2,1)S(1)} %get-tuple-element.109), channel_id=1, source_target_pairs={{0,2},{1,3},{2,0},{3,1},{4,6},{5,7},{6,4},{7,5},{8,10},{9,11},{10,... | collective-permute-start | bytes 589832 | tf_op jit(solution)/shard_map/ppermute | solution.py:25
  65.6 3.7 %collective-permute-done.17.refs_1_.refs_5_ = bf16[384,256]{1,0:T(8,128)(2,1)S(1)} collective-permute-done((bf16[384,256]{1,0:T(8,128)(2,1)S(1)}, bf16[384,256]{1,0:T(8,128)(2,1)S(1)}, u32[]{:S(2)}, u32[]{:S(2)}) %collective-permute-start.17) | collective-permute-done | bytes 196640 | tf_op jit(solution)/shard_map/ppermute | solution.py:25
  69.3 1.9 collective-permute-done.18.refs_2_.refs_6_
  71.2 2.1 collective-permute-done.19.refs_3_.refs_7_
  73.4 1.9 collective-permute-done.21.refs_11_.refs_7_
  75.3 2.4 %shard_map.97 = (bf16[88,1024]{1,0:T(8,128)(2,1)S(1)}, bf16[88,1024]{1,0:T(8,128)(2,1)S(1)}, bf16[88,1024]{1,0:T(8,128)(2,1)S(1)}, bf16[88,1024]{1,0:T(8,128)(2,1)S(1)}) custom-call(bf16[4,88,256]{2,1,0:T(8,128)(2,1)S(1)} %collective-permute-done.12.refs_0_, bf16[4,88,256]{2,1,0:T(8,128)(2,1)S(1)} %collective-permute-done.13.refs_1_, ...), custom_call_target="tpu_custom_call" | custom-call | flops 738197504 | bytes 5636096 | tf_op jit(solution)/shard_map/pallas_call | solution.py:106
  77.7 3.5 %collective-permute-start.23 = (bf16[88,1024]{1,0:T(8,128)(2,1)S(1)}, bf16[88,1024]{1,0:T(8,128)(2,1)S(1)}, u32[]{:S(2)}, u32[]{:S(2)}) collective-permute-start(bf16[88,1024]{1,0:T(8,128)(2,1)S(1)} %get-tuple-element.114), channel_id=1, source_target_pairs={{0,128},{1,129},{2,130},{3,131},{4,132},{5,133},{6,134},{7,135},{8... | collective-permute-start | bytes 540680 | tf_op jit(solution)/shard_map/ppermute | solution.py:25
  81.2 4.0 %collective-permute-start.24 = (bf16[88,1024]{1,0:T(8,128)(2,1)S(1)}, bf16[88,1024]{1,0:T(8,128)(2,1)S(1)}, u32[]{:S(2)}, u32[]{:S(2)}) collective-permute-start(bf16[88,1024]{1,0:T(8,128)(2,1)S(1)} %get-tuple-element.115), channel_id=1, source_target_pairs={{0,192},{1,193},{2,194},{3,195},{4,196},{5,197},{6,198},{7,199},{8... | collective-permute-start | bytes 540680 | tf_op jit(solution)/shard_map/ppermute | solution.py:25
  85.2 9.6 %collective-permute-done.22.refs_1_ = bf16[88,1024]{1,0:T(8,128)(2,1)S(1)} collective-permute-done((bf16[88,1024]{1,0:T(8,128)(2,1)S(1)}, bf16[88,1024]{1,0:T(8,128)(2,1)S(1)}, u32[]{:S(2)}, u32[]{:S(2)}) %collective-permute-start.22) | collective-permute-done | bytes 180256 | tf_op jit(solution)/shard_map/ppermute | solution.py:25
  94.9 4.8 %collective-permute-done.24.refs_3_ = bf16[88,1024]{1,0:T(8,128)(2,1)S(1)} collective-permute-done((bf16[88,1024]{1,0:T(8,128)(2,1)S(1)}, bf16[88,1024]{1,0:T(8,128)(2,1)S(1)}, u32[]{:S(2)}, u32[]{:S(2)}) %collective-permute-start.24) | collective-permute-done | bytes 180256 | tf_op jit(solution)/shard_map/ppermute | solution.py:25
  99.8 19.0 %all_to_all.5.mine_ref = bf16[8,24,1024]{2,1,0:T(8,128)(2,1)S(1)} all-to-all(bf16[8,24,1024]{2,1,0:T(8,128)(2,1)S(1)} %get-tuple-element.117), channel_id=1, replica_groups={{0,32,64,96,128,160,192,224},{16,48,80,112,144,176,208,240},{1,33,65,97..., dimensions={0} | all-to-all | bytes 786432 | tf_op jit(solution)/shard_map/all_to_all | solution.py:55
  118.8 1.7 collective-permute-done.25.other_ref
  121.2 1.5 collective-permute-start.28
  123.7 3.6 %collective-permute-done.28.refs_3_ = bf16[448,128]{1,0:T(8,128)(2,1)S(1)} collective-permute-done((bf16[448,128]{1,0:T(8,128)(2,1)S(1)}, bf16[448,128]{1,0:T(8,128)(2,1)S(1)}, u32[]{:S(2)}, u32[]{:S(2)}) %collective-permute-start.28) | collective-permute-done | bytes 114720 | tf_op jit(solution)/shard_map/ppermute | solution.py:25
  127.3 3.0 %collective-permute-done.27.refs_2_ = bf16[448,128]{1,0:T(8,128)(2,1)S(1)} collective-permute-done((bf16[448,128]{1,0:T(8,128)(2,1)S(1)}, bf16[448,128]{1,0:T(8,128)(2,1)S(1)}, u32[]{:S(2)}, u32[]{:S(2)}) %collective-permute-start.27) | collective-permute-done | bytes 114720 | tf_op jit(solution)/shard_map/ppermute | solution.py:25
  131.5 2.1 %collective-permute-start.31 = (bf16[448,128]{1,0:T(8,128)(2,1)S(1)}, bf16[448,128]{1,0:T(8,128)(2,1)S(1)}, u32[]{:S(2)}, u32[]{:S(2)}) collective-permute-start(bf16[448,128]{1,0:T(8,128)(2,1)S(1)} %shard_map.100.refs_0_), channel_id=1, source_target_pairs={{0,3},{1,0},{2,1},{3,2},{4,7},{5,4},{6,5},{7,6},{8,11},{9,8},{10,9... | collective-permute-start | bytes 344072 | tf_op jit(solution)/shard_map/ppermute | solution.py:25
  134.6 2.5 %collective-permute-start.29 = (bf16[448,128]{1,0:T(8,128)(2,1)S(1)}, bf16[448,128]{1,0:T(8,128)(2,1)S(1)}, u32[]{:S(2)}, u32[]{:S(2)}) collective-permute-start(bf16[448,128]{1,0:T(8,128)(2,1)S(1)} %shard_map.100.refs_0_), channel_id=1, source_target_pairs={{0,1},{1,2},{2,3},{3,0},{4,5},{5,6},{6,7},{7,4},{8,9},{9,10},{10,1... | collective-permute-start | bytes 344072 | tf_op jit(solution)/shard_map/ppermute | solution.py:25
  137.1 2.9 %collective-permute-done.30.refs_2_ = bf16[448,128]{1,0:T(8,128)(2,1)S(1)} collective-permute-done((bf16[448,128]{1,0:T(8,128)(2,1)S(1)}, bf16[448,128]{1,0:T(8,128)(2,1)S(1)}, u32[]{:S(2)}, u32[]{:S(2)}) %collective-permute-start.30) | collective-permute-done | bytes 114720 | tf_op jit(solution)/shard_map/ppermute | solution.py:25
  142.7 12.6 %collective-permute-start.35 = (bf16[4,64,256]{2,1,0:T(8,128)(2,1)S(1)}, bf16[4,64,256]{2,1,0:T(8,128)(2,1)S(1)}, u32[]{:S(2)}, u32[]{:S(2)}) collective-permute-start(bf16[4,64,256]{2,1,0:T(8,128)(2,1)S(1)} %collective-permute-done.32.refs_0_), channel_id=1, source_target_pairs={{0,12},{1,13},{2,14},{3,15},{4,0},{5,1},{6,2},{7,3},{8,4},{9,5},{1... | collective-permute-start | bytes 393224 | tf_op jit(solution)/shard_map/ppermute | solution.py:25
  155.4 1.4 collective-permute-start.33
  156.8 2.4 %collective-permute-done.35.refs_3_ = bf16[4,64,256]{2,1,0:T(8,128)(2,1)S(1)} collective-permute-done((bf16[4,64,256]{2,1,0:T(8,128)(2,1)S(1)}, bf16[4,64,256]{2,1,0:T(8,128)(2,1)S(1)}, u32[]{:S(2)}, u32[]{:S(2)}) %collective-permute-start.35) | collective-permute-done | bytes 131104 | tf_op jit(solution)/shard_map/ppermute | solution.py:25
  159.2 2.7 %collective-permute-done.34.refs_2_ = bf16[4,64,256]{2,1,0:T(8,128)(2,1)S(1)} collective-permute-done((bf16[4,64,256]{2,1,0:T(8,128)(2,1)S(1)}, bf16[4,64,256]{2,1,0:T(8,128)(2,1)S(1)}, u32[]{:S(2)}, u32[]{:S(2)}) %collective-permute-start.34) | collective-permute-done | bytes 131104 | tf_op jit(solution)/shard_map/ppermute | solution.py:25
  163.0 1.5 shard_map.102
  165.0 5.5 %collective-permute-start.37 = (bf16[64,1024]{1,0:T(8,128)(2,1)S(1)}, bf16[64,1024]{1,0:T(8,128)(2,1)S(1)}, u32[]{:S(2)}, u32[]{:S(2)}) collective-permute-start(bf16[64,1024]{1,0:T(8,128)(2,1)S(1)} %get-tuple-element.126), channel_id=1, source_target_pairs={{0,128},{1,129},{2,130},{3,131},{4,132},{5,133},{6,134},{7,135},{8... | collective-permute-start | bytes 393224 | tf_op jit(solution)/shard_map/ppermute | solution.py:25
  170.5 2.7 %collective-permute-done.36.refs_1_ = bf16[64,1024]{1,0:T(8,128)(2,1)S(1)} collective-permute-done((bf16[64,1024]{1,0:T(8,128)(2,1)S(1)}, bf16[64,1024]{1,0:T(8,128)(2,1)S(1)}, u32[]{:S(2)}, u32[]{:S(2)}) %collective-permute-start.36) | collective-permute-done | bytes 131104 | tf_op jit(solution)/shard_map/ppermute | solution.py:25
  173.2 8.2 %collective-permute-done.37.refs_2_ = bf16[64,1024]{1,0:T(8,128)(2,1)S(1)} collective-permute-done((bf16[64,1024]{1,0:T(8,128)(2,1)S(1)}, bf16[64,1024]{1,0:T(8,128)(2,1)S(1)}, u32[]{:S(2)}, u32[]{:S(2)}) %collective-permute-start.37) | collective-permute-done | bytes 131104 | tf_op jit(solution)/shard_map/ppermute | solution.py:25
  182.4 1.9 collective-permute-start.39
  184.3 3.1 %collective-permute-done.41.refs_3_ = bf16[448,128]{1,0:T(8,128)(2,1)S(1)} collective-permute-done((bf16[448,128]{1,0:T(8,128)(2,1)S(1)}, bf16[448,128]{1,0:T(8,128)(2,1)S(1)}, u32[]{:S(2)}, u32[]{:S(2)}) %collective-permute-start.41) | collective-permute-done | bytes 114720 | tf_op jit(solution)/shard_map/ppermute | solution.py:25
  187.4 2.3 %collective-permute-done.40.refs_2_ = bf16[448,128]{1,0:T(8,128)(2,1)S(1)} collective-permute-done((bf16[448,128]{1,0:T(8,128)(2,1)S(1)}, bf16[448,128]{1,0:T(8,128)(2,1)S(1)}, u32[]{:S(2)}, u32[]{:S(2)}) %collective-permute-start.40) | collective-permute-done | bytes 114720 | tf_op jit(solution)/shard_map/ppermute | solution.py:25
  190.5 4.3 %collective-permute-start.44 = (bf16[448,128]{1,0:T(8,128)(2,1)S(1)}, bf16[448,128]{1,0:T(8,128)(2,1)S(1)}, u32[]{:S(2)}, u32[]{:S(2)}) collective-permute-start(bf16[448,128]{1,0:T(8,128)(2,1)S(1)} %shard_map.104.refs_0_), channel_id=1, source_target_pairs={{0,3},{1,0},{2,1},{3,2},{4,7},{5,4},{6,5},{7,6},{8,11},{9,8},{10,9... | collective-permute-start | bytes 344072 | tf_op jit(solution)/shard_map/ppermute | solution.py:25
  194.8 2.5 %collective-permute-start.43 = (bf16[448,128]{1,0:T(8,128)(2,1)S(1)}, bf16[448,128]{1,0:T(8,128)(2,1)S(1)}, u32[]{:S(2)}, u32[]{:S(2)}) collective-permute-start(bf16[448,128]{1,0:T(8,128)(2,1)S(1)} %shard_map.104.refs_0_), channel_id=1, source_target_pairs={{0,2},{1,3},{2,0},{3,1},{4,6},{5,7},{6,4},{7,5},{8,10},{9,11},{10,... | collective-permute-start | bytes 344072 | tf_op jit(solution)/shard_map/ppermute | solution.py:25
  197.3 1.9 collective-permute-done.44.refs_3_
  199.2 3.6 %collective-permute-done.43.refs_2_ = bf16[448,128]{1,0:T(8,128)(2,1)S(1)} collective-permute-done((bf16[448,128]{1,0:T(8,128)(2,1)S(1)}, bf16[448,128]{1,0:T(8,128)(2,1)S(1)}, u32[]{:S(2)}, u32[]{:S(2)}) %collective-permute-start.43) | collective-permute-done | bytes 114720 | tf_op jit(solution)/shard_map/ppermute | solution.py:25
  205.6 1.6 collective-permute-start.46
  208.6 2.4 %collective-permute-done.46.refs_2_ = bf16[64,256]{1,0:T(8,128)(2,1)S(1)} collective-permute-done((bf16[64,256]{1,0:T(8,128)(2,1)S(1)}, bf16[64,256]{1,0:T(8,128)(2,1)S(1)}, u32[]{:S(2)}, u32[]{:S(2)}) %collective-permute-start.46) | collective-permute-done | bytes 32800 | tf_op jit(solution)/shard_map/ppermute | solution.py:25
  (83 shorter events, 28.4 us)
Async XLA Ops:
  3.5 4.8 %collective-permute-start = (bf16[88,256]{1,0:T(8,128)(2,1)S(1)}, bf16[88,256]{1,0:T(8,128)(2,1)S(1)}, u32[]{:S(2)}, u32[]{:S(2)}) collective-permute-start(bf16[88,256]{1,0:T(8,128)(2,1)S(1)} %get-tuple-element.71), channel_id=1, source_target_pairs={{0,1},{1,2},{2,3},{3,0},{4,5},{5,6},{6,7},{7,4},{8,9},{9,10},{10,1... | collective-permute-start | bytes 135176 | tf_op jit(solution)/shard_map/ppermute | solution.py:25
  5.1 5.6 %collective-permute-start.1 = (bf16[88,256]{1,0:T(8,128)(2,1)S(1)}, bf16[88,256]{1,0:T(8,128)(2,1)S(1)}, u32[]{:S(2)}, u32[]{:S(2)}) collective-permute-start(bf16[88,256]{1,0:T(8,128)(2,1)S(1)} %get-tuple-element.72), channel_id=1, source_target_pairs={{0,2},{1,3},{2,0},{3,1},{4,6},{5,7},{6,4},{7,5},{8,10},{9,11},{10,... | collective-permute-start | bytes 135176 | tf_op jit(solution)/shard_map/ppermute | solution.py:25
  7.9 4.0 %collective-permute-start.2 = (bf16[88,256]{1,0:T(8,128)(2,1)S(1)}, bf16[88,256]{1,0:T(8,128)(2,1)S(1)}, u32[]{:S(2)}, u32[]{:S(2)}) collective-permute-start(bf16[88,256]{1,0:T(8,128)(2,1)S(1)} %get-tuple-element.73), channel_id=1, source_target_pairs={{0,3},{1,0},{2,1},{3,2},{4,7},{5,4},{6,5},{7,6},{8,11},{9,8},{10,9... | collective-permute-start | bytes 135176 | tf_op jit(solution)/shard_map/ppermute | solution.py:25
  12.0 5.8 %collective-permute-start.3 = (bf16[256,256]{1,0:T(8,128)(2,1)S(1)}, bf16[256,256]{1,0:T(8,128)(2,1)S(1)}, u32[]{:S(2)}, u32[]{:S(2)}) collective-permute-start(bf16[256,256]{1,0:T(8,128)(2,1)S(1)} %get-tuple-element.77), channel_id=1, source_target_pairs={{0,1},{1,2},{2,3},{3,0},{4,5},{5,6},{6,7},{7,4},{8,9},{9,10},{10,1... | collective-permute-start | bytes 393224 | tf_op jit(solution)/shard_map/ppermute | solution.py:25
  12.1 6.6 %collective-permute-start.4 = (bf16[256,256]{1,0:T(8,128)(2,1)S(1)}, bf16[256,256]{1,0:T(8,128)(2,1)S(1)}, u32[]{:S(2)}, u32[]{:S(2)}) collective-permute-start(bf16[256,256]{1,0:T(8,128)(2,1)S(1)} %get-tuple-element.78), channel_id=1, source_target_pairs={{0,2},{1,3},{2,0},{3,1},{4,6},{5,7},{6,4},{7,5},{8,10},{9,11},{10,... | collective-permute-start | bytes 393224 | tf_op jit(solution)/shard_map/ppermute | solution.py:25
  14.7 5.4 %collective-permute-start.5 = (bf16[256,256]{1,0:T(8,128)(2,1)S(1)}, bf16[256,256]{1,0:T(8,128)(2,1)S(1)}, u32[]{:S(2)}, u32[]{:S(2)}) collective-permute-start(bf16[256,256]{1,0:T(8,128)(2,1)S(1)} %get-tuple-element.79), channel_id=1, source_target_pairs={{0,3},{1,0},{2,1},{3,2},{4,7},{5,4},{6,5},{7,6},{8,11},{9,8},{10,9... | collective-permute-start | bytes 393224 | tf_op jit(solution)/shard_map/ppermute | solution.py:25
  20.1 8.1 %collective-permute-start.7 = (bf16[256,256]{1,0:T(8,128)(2,1)S(1)}, bf16[256,256]{1,0:T(8,128)(2,1)S(1)}, u32[]{:S(2)}, u32[]{:S(2)}) collective-permute-start(bf16[256,256]{1,0:T(8,128)(2,1)S(1)} %get-tuple-element.85), channel_id=1, source_target_pairs={{0,1},{1,2},{2,3},{3,0},{4,5},{5,6},{6,7},{7,4},{8,9},{9,10},{10,1... | collective-permute-start | bytes 393224 | tf_op jit(solution)/shard_map/ppermute | solution.py:25
  21.3 6.9 %collective-permute-start.8 = (bf16[256,256]{1,0:T(8,128)(2,1)S(1)}, bf16[256,256]{1,0:T(8,128)(2,1)S(1)}, u32[]{:S(2)}, u32[]{:S(2)}) collective-permute-start(bf16[256,256]{1,0:T(8,128)(2,1)S(1)} %get-tuple-element.86), channel_id=1, source_target_pairs={{0,2},{1,3},{2,0},{3,1},{4,6},{5,7},{6,4},{7,5},{8,10},{9,11},{10,... | collective-permute-start | bytes 393224 | tf_op jit(solution)/shard_map/ppermute | solution.py:25
  23.9 5.2 %collective-permute-start.9 = (bf16[256,256]{1,0:T(8,128)(2,1)S(1)}, bf16[256,256]{1,0:T(8,128)(2,1)S(1)}, u32[]{:S(2)}, u32[]{:S(2)}) collective-permute-start(bf16[256,256]{1,0:T(8,128)(2,1)S(1)} %get-tuple-element.87), channel_id=1, source_target_pairs={{0,3},{1,0},{2,1},{3,2},{4,7},{5,4},{6,5},{7,6},{8,11},{9,8},{10,9... | collective-permute-start | bytes 393224 | tf_op jit(solution)/shard_map/ppermute | solution.py:25
  25.3 3.9 %collective-permute-start.12 = (bf16[4,88,256]{2,1,0:T(8,128)(2,1)S(1)}, bf16[4,88,256]{2,1,0:T(8,128)(2,1)S(1)}, u32[]{:S(2)}, u32[]{:S(2)}) collective-permute-start(bf16[4,88,256]{2,1,0:T(8,128)(2,1)S(1)} %shard_map.95), channel_id=1, source_target_pairs={{0,0},{1,1},{2,2},{3,3},{4,64},{5,65},{6,66},{7,67},{8,128},{9,129... | collective-permute-start | bytes 540680 | tf_op jit(solution)/shard_map/ppermute | solution.py:25
  26.2 30.0 %collective-permute-start.6 = (bf16[1024,256]{1,0:T(8,128)(2,1)S(1)}, bf16[1024,256]{1,0:T(8,128)(2,1)S(1)}, u32[]{:S(2)}, u32[]{:S(2)}) collective-permute-start(bf16[1024,256]{1,0:T(8,128)(2,1)S(1)} %shard_map.93.refs_4_), channel_id=1, source_target_pairs={{0,32},{1,33},{2,34},{3,35},{4,36},{5,37},{6,38},{7,39},{8,40},{9,... | collective-permute-start | bytes 1572872 | tf_op jit(solution)/shard_map/ppermute | solution.py:25
  28.2 28.0 %collective-permute-start.10 = (bf16[1024,256]{1,0:T(8,128)(2,1)S(1)}, bf16[1024,256]{1,0:T(8,128)(2,1)S(1)}, u32[]{:S(2)}, u32[]{:S(2)}) collective-permute-start(bf16[1024,256]{1,0:T(8,128)(2,1)S(1)} %shard_map.93.refs_4_), channel_id=1, source_target_pairs={{0,16},{1,17},{2,18},{3,19},{4,20},{5,21},{6,22},{7,23},{8,24},{9,... | collective-permute-start | bytes 1572872 | tf_op jit(solution)/shard_map/ppermute | solution.py:25
  29.2 27.0 %collective-permute-start.11 = (bf16[1024,256]{1,0:T(8,128)(2,1)S(1)}, bf16[1024,256]{1,0:T(8,128)(2,1)S(1)}, u32[]{:S(2)}, u32[]{:S(2)}) collective-permute-start(bf16[1024,256]{1,0:T(8,128)(2,1)S(1)} %shard_map.94.refs_8_.refs_4_), channel_id=1, source_target_pairs={{0,16},{1,17},{2,18},{3,19},{4,20},{5,21},{6,22},{7,23},{8,24},{9,... | collective-permute-start | bytes 1572872 | tf_op jit(solution)/shard_map/ppermute | solution.py:25
  29.3 19.7 %collective-permute-start.15 = (bf16[4,88,256]{2,1,0:T(8,128)(2,1)S(1)}, bf16[4,88,256]{2,1,0:T(8,128)(2,1)S(1)}, u32[]{:S(2)}, u32[]{:S(2)}) collective-permute-start(bf16[4,88,256]{2,1,0:T(8,128)(2,1)S(1)} %collective-permute-done.12.refs_0_), channel_id=1, source_target_pairs={{0,12},{1,13},{2,14},{3,15},{4,0},{5,1},{6,2},{7,3},{8,4},{9,5},{1... | collective-permute-start | bytes 540680 | tf_op jit(solution)/shard_map/ppermute | solution.py:25
  44.1 8.2 %collective-permute-start.14 = (bf16[4,88,256]{2,1,0:T(8,128)(2,1)S(1)}, bf16[4,88,256]{2,1,0:T(8,128)(2,1)S(1)}, u32[]{:S(2)}, u32[]{:S(2)}) collective-permute-start(bf16[4,88,256]{2,1,0:T(8,128)(2,1)S(1)} %collective-permute-done.12.refs_0_), channel_id=1, source_target_pairs={{0,8},{1,9},{2,10},{3,11},{4,12},{5,13},{6,14},{7,15},{8,0},{9,1},... | collective-permute-start | bytes 540680 | tf_op jit(solution)/shard_map/ppermute | solution.py:25
  49.0 7.1 %collective-permute-start.13 = (bf16[4,88,256]{2,1,0:T(8,128)(2,1)S(1)}, bf16[4,88,256]{2,1,0:T(8,128)(2,1)S(1)}, u32[]{:S(2)}, u32[]{:S(2)}) collective-permute-start(bf16[4,88,256]{2,1,0:T(8,128)(2,1)S(1)} %collective-permute-done.12.refs_0_), channel_id=1, source_target_pairs={{0,4},{1,5},{2,6},{3,7},{4,8},{5,9},{6,10},{7,11},{8,12},{9,13},{1... | collective-permute-start | bytes 540680 | tf_op jit(solution)/shard_map/ppermute | solution.py:25
  56.2 17.2 %collective-permute-start.20 = (bf16[1024,256]{1,0:T(8,128)(2,1)S(1)}, bf16[1024,256]{1,0:T(8,128)(2,1)S(1)}, u32[]{:S(2)}, u32[]{:S(2)}) collective-permute-start(bf16[1024,256]{1,0:T(8,128)(2,1)S(1)} %shard_map.94.refs_8_.refs_4_), channel_id=1, source_target_pairs={{0,32},{1,33},{2,34},{3,35},{4,36},{5,37},{6,38},{7,39},{8,40},{9,... | collective-permute-start | bytes 1572872 | tf_op jit(solution)/shard_map/ppermute | solution.py:25
  59.1 10.2 %collective-permute-start.17 = (bf16[384,256]{1,0:T(8,128)(2,1)S(1)}, bf16[384,256]{1,0:T(8,128)(2,1)S(1)}, u32[]{:S(2)}, u32[]{:S(2)}) collective-permute-start(bf16[384,256]{1,0:T(8,128)(2,1)S(1)} %get-tuple-element.108), channel_id=1, source_target_pairs={{0,1},{1,2},{2,3},{3,0},{4,5},{5,6},{6,7},{7,4},{8,9},{9,10},{10,1... | collective-permute-start | bytes 589832 | tf_op jit(solution)/shard_map/ppermute | solution.py:25
  59.6 11.6 %collective-permute-start.18 = (bf16[384,256]{1,0:T(8,128)(2,1)S(1)}, bf16[384,256]{1,0:T(8,128)(2,1)S(1)}, u32[]{:S(2)}, u32[]{:S(2)}) collective-permute-start(bf16[384,256]{1,0:T(8,128)(2,1)S(1)} %get-tuple-element.109), channel_id=1, source_target_pairs={{0,2},{1,3},{2,0},{3,1},{4,6},{5,7},{6,4},{7,5},{8,10},{9,11},{10,... | collective-permute-start | bytes 589832 | tf_op jit(solution)/shard_map/ppermute | solution.py:25
  65.6 7.8 %collective-permute-start.19 = (bf16[384,256]{1,0:T(8,128)(2,1)S(1)}, bf16[384,256]{1,0:T(8,128)(2,1)S(1)}, u32[]{:S(2)}, u32[]{:S(2)}) collective-permute-start(bf16[384,256]{1,0:T(8,128)(2,1)S(1)} %get-tuple-element.110), channel_id=1, source_target_pairs={{0,3},{1,0},{2,1},{3,2},{4,7},{5,4},{6,5},{7,6},{8,11},{9,8},{10,9... | collective-permute-start | bytes 589832 | tf_op jit(solution)/shard_map/ppermute | solution.py:25
  65.6 7.8 %collective-permute-start.16 = (bf16[1024,256]{1,0:T(8,128)(2,1)S(1)}, bf16[1024,256]{1,0:T(8,128)(2,1)S(1)}, u32[]{:S(2)}, u32[]{:S(2)}) collective-permute-start(bf16[1024,256]{1,0:T(8,128)(2,1)S(1)} %collective-permute-done.6.refs_6_), channel_id=1, source_target_pairs={{0,16},{1,17},{2,18},{3,19},{4,20},{5,21},{6,22},{7,23},{8,24},{9,... | collective-permute-start | bytes 1572872 | tf_op jit(solution)/shard_map/ppermute | solution.py:25
  73.3 1.9 collective-permute-start.21
  77.6 17.2 %collective-permute-start.22 = (bf16[88,1024]{1,0:T(8,128)(2,1)S(1)}, bf16[88,1024]{1,0:T(8,128)(2,1)S(1)}, u32[]{:S(2)}, u32[]{:S(2)}) collective-permute-start(bf16[88,1024]{1,0:T(8,128)(2,1)S(1)} %get-tuple-element.113), channel_id=1, source_target_pairs={{0,64},{1,65},{2,66},{3,67},{4,68},{5,69},{6,70},{7,71},{8,72},{9,... | collective-permute-start | bytes 540680 | tf_op jit(solution)/shard_map/ppermute | solution.py:25
  77.7 17.1 %collective-permute-start.23 = (bf16[88,1024]{1,0:T(8,128)(2,1)S(1)}, bf16[88,1024]{1,0:T(8,128)(2,1)S(1)}, u32[]{:S(2)}, u32[]{:S(2)}) collective-permute-start(bf16[88,1024]{1,0:T(8,128)(2,1)S(1)} %get-tuple-element.114), channel_id=1, source_target_pairs={{0,128},{1,129},{2,130},{3,131},{4,132},{5,133},{6,134},{7,135},{8... | collective-permute-start | bytes 540680 | tf_op jit(solution)/shard_map/ppermute | solution.py:25
  81.2 18.5 %collective-permute-start.24 = (bf16[88,1024]{1,0:T(8,128)(2,1)S(1)}, bf16[88,1024]{1,0:T(8,128)(2,1)S(1)}, u32[]{:S(2)}, u32[]{:S(2)}) collective-permute-start(bf16[88,1024]{1,0:T(8,128)(2,1)S(1)} %get-tuple-element.115), channel_id=1, source_target_pairs={{0,192},{1,193},{2,194},{3,195},{4,196},{5,197},{6,198},{7,199},{8... | collective-permute-start | bytes 540680 | tf_op jit(solution)/shard_map/ppermute | solution.py:25
  118.7 1.7 collective-permute-start.25
  121.2 6.1 %collective-permute-start.28 = (bf16[448,128]{1,0:T(8,128)(2,1)S(1)}, bf16[448,128]{1,0:T(8,128)(2,1)S(1)}, u32[]{:S(2)}, u32[]{:S(2)}) collective-permute-start(bf16[448,128]{1,0:T(8,128)(2,1)S(1)} %get-tuple-element.122.refs_0_), channel_id=1, source_target_pairs={{0,12},{1,13},{2,14},{3,15},{4,0},{5,1},{6,2},{7,3},{8,4},{9,5},{1... | collective-permute-start | bytes 344072 | tf_op jit(solution)/shard_map/ppermute | solution.py:25
  122.7 7.5 %collective-permute-start.27 = (bf16[448,128]{1,0:T(8,128)(2,1)S(1)}, bf16[448,128]{1,0:T(8,128)(2,1)S(1)}, u32[]{:S(2)}, u32[]{:S(2)}) collective-permute-start(bf16[448,128]{1,0:T(8,128)(2,1)S(1)} %get-tuple-element.122.refs_0_), channel_id=1, source_target_pairs={{0,8},{1,9},{2,10},{3,11},{4,12},{5,13},{6,14},{7,15},{8,0},{9,1},... | collective-permute-start | bytes 344072 | tf_op jit(solution)/shard_map/ppermute | solution.py:25
  123.1 8.3 %collective-permute-start.26 = (bf16[448,128]{1,0:T(8,128)(2,1)S(1)}, bf16[448,128]{1,0:T(8,128)(2,1)S(1)}, u32[]{:S(2)}, u32[]{:S(2)}) collective-permute-start(bf16[448,128]{1,0:T(8,128)(2,1)S(1)} %get-tuple-element.122.refs_0_), channel_id=1, source_target_pairs={{0,4},{1,5},{2,6},{3,7},{4,8},{5,9},{6,10},{7,11},{8,12},{9,13},{1... | collective-permute-start | bytes 344072 | tf_op jit(solution)/shard_map/ppermute | solution.py:25
  131.5 5.7 %collective-permute-start.31 = (bf16[448,128]{1,0:T(8,128)(2,1)S(1)}, bf16[448,128]{1,0:T(8,128)(2,1)S(1)}, u32[]{:S(2)}, u32[]{:S(2)}) collective-permute-start(bf16[448,128]{1,0:T(8,128)(2,1)S(1)} %shard_map.100.refs_0_), channel_id=1, source_target_pairs={{0,3},{1,0},{2,1},{3,2},{4,7},{5,4},{6,5},{7,6},{8,11},{9,8},{10,9... | collective-permute-start | bytes 344072 | tf_op jit(solution)/shard_map/ppermute | solution.py:25
  133.6 6.5 %collective-permute-start.30 = (bf16[448,128]{1,0:T(8,128)(2,1)S(1)}, bf16[448,128]{1,0:T(8,128)(2,1)S(1)}, u32[]{:S(2)}, u32[]{:S(2)}) collective-permute-start(bf16[448,128]{1,0:T(8,128)(2,1)S(1)} %shard_map.100.refs_0_), channel_id=1, source_target_pairs={{0,2},{1,3},{2,0},{3,1},{4,6},{5,7},{6,4},{7,5},{8,10},{9,11},{10,... | collective-permute-start | bytes 344072 | tf_op jit(solution)/shard_map/ppermute | solution.py:25
  134.6 6.4 %collective-permute-start.29 = (bf16[448,128]{1,0:T(8,128)(2,1)S(1)}, bf16[448,128]{1,0:T(8,128)(2,1)S(1)}, u32[]{:S(2)}, u32[]{:S(2)}) collective-permute-start(bf16[448,128]{1,0:T(8,128)(2,1)S(1)} %shard_map.100.refs_0_), channel_id=1, source_target_pairs={{0,1},{1,2},{2,3},{3,0},{4,5},{5,6},{6,7},{7,4},{8,9},{9,10},{10,1... | collective-permute-start | bytes 344072 | tf_op jit(solution)/shard_map/ppermute | solution.py:25
  142.0 0.7 collective-permute-start.32
  142.7 16.5 %collective-permute-start.35 = (bf16[4,64,256]{2,1,0:T(8,128)(2,1)S(1)}, bf16[4,64,256]{2,1,0:T(8,128)(2,1)S(1)}, u32[]{:S(2)}, u32[]{:S(2)}) collective-permute-start(bf16[4,64,256]{2,1,0:T(8,128)(2,1)S(1)} %collective-permute-done.32.refs_0_), channel_id=1, source_target_pairs={{0,12},{1,13},{2,14},{3,15},{4,0},{5,1},{6,2},{7,3},{8,4},{9,5},{1... | collective-permute-start | bytes 393224 | tf_op jit(solution)/shard_map/ppermute | solution.py:25
  155.3 6.6 %collective-permute-start.34 = (bf16[4,64,256]{2,1,0:T(8,128)(2,1)S(1)}, bf16[4,64,256]{2,1,0:T(8,128)(2,1)S(1)}, u32[]{:S(2)}, u32[]{:S(2)}) collective-permute-start(bf16[4,64,256]{2,1,0:T(8,128)(2,1)S(1)} %collective-permute-done.32.refs_0_), channel_id=1, source_target_pairs={{0,8},{1,9},{2,10},{3,11},{4,12},{5,13},{6,14},{7,15},{8,0},{9,1},... | collective-permute-start | bytes 393224 | tf_op jit(solution)/shard_map/ppermute | solution.py:25
  155.4 7.6 %collective-permute-start.33 = (bf16[4,64,256]{2,1,0:T(8,128)(2,1)S(1)}, bf16[4,64,256]{2,1,0:T(8,128)(2,1)S(1)}, u32[]{:S(2)}, u32[]{:S(2)}) collective-permute-start(bf16[4,64,256]{2,1,0:T(8,128)(2,1)S(1)} %collective-permute-done.32.refs_0_), channel_id=1, source_target_pairs={{0,4},{1,5},{2,6},{3,7},{4,8},{5,9},{6,10},{7,11},{8,12},{9,13},{1... | collective-permute-start | bytes 393224 | tf_op jit(solution)/shard_map/ppermute | solution.py:25
  164.5 8.7 %collective-permute-start.36 = (bf16[64,1024]{1,0:T(8,128)(2,1)S(1)}, bf16[64,1024]{1,0:T(8,128)(2,1)S(1)}, u32[]{:S(2)}, u32[]{:S(2)}) collective-permute-start(bf16[64,1024]{1,0:T(8,128)(2,1)S(1)} %get-tuple-element.125), channel_id=1, source_target_pairs={{0,64},{1,65},{2,66},{3,67},{4,68},{5,69},{6,70},{7,71},{8,72},{9,... | collective-permute-start | bytes 393224 | tf_op jit(solution)/shard_map/ppermute | solution.py:25
  165.0 16.4 %collective-permute-start.37 = (bf16[64,1024]{1,0:T(8,128)(2,1)S(1)}, bf16[64,1024]{1,0:T(8,128)(2,1)S(1)}, u32[]{:S(2)}, u32[]{:S(2)}) collective-permute-start(bf16[64,1024]{1,0:T(8,128)(2,1)S(1)} %get-tuple-element.126), channel_id=1, source_target_pairs={{0,128},{1,129},{2,130},{3,131},{4,132},{5,133},{6,134},{7,135},{8... | collective-permute-start | bytes 393224 | tf_op jit(solution)/shard_map/ppermute | solution.py:25
  170.5 11.3 %collective-permute-start.38 = (bf16[64,1024]{1,0:T(8,128)(2,1)S(1)}, bf16[64,1024]{1,0:T(8,128)(2,1)S(1)}, u32[]{:S(2)}, u32[]{:S(2)}) collective-permute-start(bf16[64,1024]{1,0:T(8,128)(2,1)S(1)} %get-tuple-element.127), channel_id=1, source_target_pairs={{0,192},{1,193},{2,194},{3,195},{4,196},{5,197},{6,198},{7,199},{8... | collective-permute-start | bytes 393224 | tf_op jit(solution)/shard_map/ppermute | solution.py:25
  182.2 5.2 %collective-permute-start.41 = (bf16[448,128]{1,0:T(8,128)(2,1)S(1)}, bf16[448,128]{1,0:T(8,128)(2,1)S(1)}, u32[]{:S(2)}, u32[]{:S(2)}) collective-permute-start(bf16[448,128]{1,0:T(8,128)(2,1)S(1)} %get-tuple-element.129.refs_0_), channel_id=1, source_target_pairs={{0,12},{1,13},{2,14},{3,15},{4,0},{5,1},{6,2},{7,3},{8,4},{9,5},{1... | collective-permute-start | bytes 344072 | tf_op jit(solution)/shard_map/ppermute | solution.py:25
  182.3 7.4 %collective-permute-start.40 = (bf16[448,128]{1,0:T(8,128)(2,1)S(1)}, bf16[448,128]{1,0:T(8,128)(2,1)S(1)}, u32[]{:S(2)}, u32[]{:S(2)}) collective-permute-start(bf16[448,128]{1,0:T(8,128)(2,1)S(1)} %get-tuple-element.129.refs_0_), channel_id=1, source_target_pairs={{0,8},{1,9},{2,10},{3,11},{4,12},{5,13},{6,14},{7,15},{8,0},{9,1},... | collective-permute-start | bytes 344072 | tf_op jit(solution)/shard_map/ppermute | solution.py:25
  182.4 8.0 %collective-permute-start.39 = (bf16[448,128]{1,0:T(8,128)(2,1)S(1)}, bf16[448,128]{1,0:T(8,128)(2,1)S(1)}, u32[]{:S(2)}, u32[]{:S(2)}) collective-permute-start(bf16[448,128]{1,0:T(8,128)(2,1)S(1)} %get-tuple-element.129.refs_0_), channel_id=1, source_target_pairs={{0,4},{1,5},{2,6},{3,7},{4,8},{5,9},{6,10},{7,11},{8,12},{9,13},{1... | collective-permute-start | bytes 344072 | tf_op jit(solution)/shard_map/ppermute | solution.py:25
  190.5 8.7 %collective-permute-start.44 = (bf16[448,128]{1,0:T(8,128)(2,1)S(1)}, bf16[448,128]{1,0:T(8,128)(2,1)S(1)}, u32[]{:S(2)}, u32[]{:S(2)}) collective-permute-start(bf16[448,128]{1,0:T(8,128)(2,1)S(1)} %shard_map.104.refs_0_), channel_id=1, source_target_pairs={{0,3},{1,0},{2,1},{3,2},{4,7},{5,4},{6,5},{7,6},{8,11},{9,8},{10,9... | collective-permute-start | bytes 344072 | tf_op jit(solution)/shard_map/ppermute | solution.py:25
  194.8 8.0 %collective-permute-start.43 = (bf16[448,128]{1,0:T(8,128)(2,1)S(1)}, bf16[448,128]{1,0:T(8,128)(2,1)S(1)}, u32[]{:S(2)}, u32[]{:S(2)}) collective-permute-start(bf16[448,128]{1,0:T(8,128)(2,1)S(1)} %shard_map.104.refs_0_), channel_id=1, source_target_pairs={{0,2},{1,3},{2,0},{3,1},{4,6},{5,7},{6,4},{7,5},{8,10},{9,11},{10,... | collective-permute-start | bytes 344072 | tf_op jit(solution)/shard_map/ppermute | solution.py:25
  197.3 6.3 %collective-permute-start.42 = (bf16[448,128]{1,0:T(8,128)(2,1)S(1)}, bf16[448,128]{1,0:T(8,128)(2,1)S(1)}, u32[]{:S(2)}, u32[]{:S(2)}) collective-permute-start(bf16[448,128]{1,0:T(8,128)(2,1)S(1)} %shard_map.104.refs_0_), channel_id=1, source_target_pairs={{0,1},{1,2},{2,3},{3,0},{4,5},{5,6},{6,7},{7,4},{8,9},{9,10},{10,1... | collective-permute-start | bytes 344072 | tf_op jit(solution)/shard_map/ppermute | solution.py:25
  204.6 4.0 %collective-permute-start.45 = (bf16[64,256]{1,0:T(8,128)(2,1)S(1)}, bf16[64,256]{1,0:T(8,128)(2,1)S(1)}, u32[]{:S(2)}, u32[]{:S(2)}) collective-permute-start(bf16[64,256]{1,0:T(8,128)(2,1)S(1)} %get-tuple-element.132), channel_id=1, source_target_pairs={{0,3},{1,0},{2,1},{3,2},{4,7},{5,4},{6,5},{7,6},{8,11},{9,8},{10,9... | collective-permute-start | bytes 98312 | tf_op jit(solution)/shard_map/ppermute | solution.py:25
  205.6 5.4 %collective-permute-start.46 = (bf16[64,256]{1,0:T(8,128)(2,1)S(1)}, bf16[64,256]{1,0:T(8,128)(2,1)S(1)}, u32[]{:S(2)}, u32[]{:S(2)}) collective-permute-start(bf16[64,256]{1,0:T(8,128)(2,1)S(1)} %get-tuple-element.133), channel_id=1, source_target_pairs={{0,2},{1,3},{2,0},{3,1},{4,6},{5,7},{6,4},{7,5},{8,10},{9,11},{10,... | collective-permute-start | bytes 98312 | tf_op jit(solution)/shard_map/ppermute | solution.py:25
  207.2 3.9 %collective-permute-start.47 = (bf16[64,256]{1,0:T(8,128)(2,1)S(1)}, bf16[64,256]{1,0:T(8,128)(2,1)S(1)}, u32[]{:S(2)}, u32[]{:S(2)}) collective-permute-start(bf16[64,256]{1,0:T(8,128)(2,1)S(1)} %get-tuple-element.134), channel_id=1, source_target_pairs={{0,1},{1,2},{2,3},{3,0},{4,5},{5,6},{6,7},{7,4},{8,9},{9,10},{10,1... | collective-permute-start | bytes 98312 | tf_op jit(solution)/shard_map/ppermute | solution.py:25
  (9 other events, 116.3 us)
where the time goes:
time: 213 us; the launch traced here: 212 us
  waiting for transfers between devices  90.6 us (43%)
  starting transfers between devices  89.8 us (42%)
  blocking collectives  19 us (9%)
  Pallas kernels  9.1 us (4%)
  local copies, waits for them, and re-layouts  3.06 us (1%)
    ppermute x48, waiting for transfers between devices, permuted(): return lax.ppermute(value, ('row', 'col'), routes(to))  90.6 us
    ppermute x48, starting transfers between devices, permuted(): return lax.ppermute(value, ('row', 'col'), routes(to))  89.8 us
    all_to_all x1, blocking collectives, from_every_z(): lax.all_to_all(value, 'row', 0, 0, tiled=True, axis_index_groups=Z_GROUPS)  19 us
    pallas_call x16, Pallas kernels, run(): pl.pallas_call(body, out_shape=out_shape, in_specs=specs, scratch_shapes=...  9.1 us
  transfers between devices with their start and end apart: 48, of which 36 were waited for; matrix products, arithmetic and copies ran while one was open for 0% of the time, Pallas kernels for 0%

commit v1 on v0

--- a/solution.py
+++ b/solution.py
@@ -152,16 +152,18 @@
 
 
 def stack_kernel(*refs):
-    rows = refs[0].shape[0]
+    half = refs[0].shape[0] // 2
     for s, ref in enumerate(refs[:-1]):
-        refs[-1][s * rows : (s + 1) * rows] = ref[...]
+        refs[-1][0, s * half : (s + 1) * half] = ref[:half]
+        refs[-1][1, s * half : (s + 1) * half] = ref[half:]
 
 
 def deal_kernel(lower_ref, upper_ref, *out_refs):
+    rows = lower_ref.shape[1]
     for s in range(SIDE):
         tile = wrapped(own_tile() + s)
-        out_refs[s][...] = lower_ref[tile]
-        out_refs[SIDE + s][...] = upper_ref[tile]
+        out_refs[s][:rows] = lower_ref[tile]
+        out_refs[s][rows:] = upper_ref[tile]
 
 
 def turn_kernel(low_ref, up_ref, *out_refs):
@@ -177,11 +179,12 @@
             out_ref[slot * rank_cols : (slot + 1) * rank_cols] = dot_t(eye, factor).astype(BF16)
 
 
-def products_kernel(n, padded, count, *refs):
-    x_refs, inverse_refs = refs[:SIDE], refs[SIDE : SIDE + count]
-    out_refs = refs[SIDE + count : -2]
+def products_kernel(n, padded, which, *refs):
+    x_refs, inverse_refs = refs[:SIDE], refs[SIDE : 2 * SIDE]
+    out_refs = refs[2 * SIDE : -2]
     joined_ref, extra_ref = refs[-2:]
-    lower, upper = inverse_refs[:SIDE], inverse_refs[SIDE:]
+    lower = [ref.at[0] for ref in inverse_refs]
+    upper = [ref.at[len(which) - 1] for ref in inverse_refs]
     rows = x_refs[0].shape[1]
 
     @pl.when(pl.program_id(0) == 0)
@@ -218,19 +221,19 @@
             out_refs[t][n:] = jnp.where(slot < own_tile(), mine, its).astype(BF16)
 
 
-def products(n, gathered, *inverses):
+def products(n, gathered, which, inverses):
     blocks, rows, width = gathered[0].shape
-    total = inverses[0].shape[0]
+    total = inverses[0].shape[1]
     padded = rows + -rows % 16
-    count = len(inverses)
+    count = len(which)
     whole = pl.BlockSpec(gathered[0].shape, lambda a: (0, 0, 0))
     return kernel_call(
-        lambda *refs: products_kernel(n, padded, count, *refs),
+        lambda *refs: products_kernel(n, padded, which, *refs),
         [jax.ShapeDtypeStruct((rows, total), BF16)] * SIDE,
         flops=2 * SIDE * blocks * rows * width * total,
         grid=(total // 256,),
         in_specs=[whole] * SIDE
-        + [pl.BlockSpec((256, width), lambda a: (a, 0)) for _ in inverses],
+        + [pl.BlockSpec((count, 256, width), lambda a: (which[-1] // count, a, 0))] * SIDE,
         out_specs=[pl.BlockSpec((rows, 256), lambda a: (0, a))] * SIDE,
         scratch=[
             pltpu.VMEM((blocks, SIDE, padded, width), BF16),
@@ -395,36 +398,32 @@
     )
     tied = lax.optimization_barrier
     rows = scattered_x(rows)
-    rows, inv_lower, inv_upper = tied((rows, inv_lower, inv_upper))
-    dealt = kernel_call(deal_kernel, [shape((width, width), BF16)] * 2 * SIDE)(
-        inv_lower, inv_upper
-    )
     rows = kernel_call(
         lambda *refs: order_kernel(1, *refs), shape((SIDE, height, width), BF16)
     )(*rows)
-    rows = swapped(rows)
-    stack = kernel_call(stack_kernel, shape((total, width), BF16))
-    lower = stack(*scattered_x(dealt[:SIDE]))
-    far_lower = swap_pair(lower)
-    upper_parts, lower = tied((dealt[SIDE:], lower))
-    upper = stack(*scattered_x(upper_parts))
-    near = (swap_core(lower), swap_core(upper))
-    gathered = gathered_y(rows)
-    far_lower, upper, near, gathered = tied((far_lower, upper, near, gathered))
-    far_upper = swap_pair(upper)
-    lower = [lower, near[0], far_lower, swap_core(far_lower)]
-    low_right, up_right, gathered = tied((low_right, up_right, gathered))
+    rows, inv_lower, inv_upper = tied((rows, inv_lower, inv_upper))
+    parts = scattered_x(
+        kernel_call(deal_kernel, [shape((2 * width, width), BF16)] * SIDE)(
+            inv_lower, inv_upper
+        )
+    )
+    parts, rows = tied((parts, swapped(rows)))
+    inverse = kernel_call(stack_kernel, shape((2, total, width), BF16))(*parts)
+    far = swap_pair(inverse)
+    near, gathered = tied((swap_core(inverse), gathered_y(rows)))
+    gathered, low_right, up_right = tied((gathered, low_right, up_right))
     turned = scattered_x(
         kernel_call(turn_kernel, [shape((slots * rank_cols, width), BF16)] * SIDE)(
             low_right, up_right
         )
     )
-    turned, far_upper = tied((turned, far_upper))
-    upper = [upper, near[1], far_upper, swap_core(far_upper)]
+    turned, far = tied((turned, far))
+    inverses = [inverse, near, far, swap_core(far)]
+    received = scattered_q(products(n, gathered, (0, 1), inverses))
     dense, extra = kernel_call(
         lambda *refs: total_kernel(n, *refs),
         (shape((n, total), F32), shape((8, slots * share, total), BF16)),
-    )(*scattered_q(products(n, gathered, *lower, *upper)))
+    )(*received)
     mine = from_every_z(extra)
     packed = slots * n + 2 * rank_cols
     extra, send, later = kernel_call(
@@ -447,7 +446,7 @@
         )(*gathered_x(sums), dense, extra, ranks)
 
     [rows] = finished(True, send, dense, low_ranks)
-    parts = products(n, gathered_y(swapped(rows)), *upper)
+    parts = products(n, gathered_y(swapped(rows)), (1,), inverses)
     dense, send = kernel_call(
         last_project_kernel,
         (shape((n, total), F32), shape((packed, rank_cols), BF16)),

time: 213 us -> 203 us (0.953)
  starting transfers between devices: 89.8 us -> 78.2 us
    ppermute x48 -> x42, starting transfers between devices: 89.8 us -> 78.2 us  [permuted(): return lax.ppermute(value, ('row', 'col'), routes(to))]
    ppermute x48 -> x42, waiting for transfers between devices: 90.6 us -> 92.2 us  [permuted(): return lax.ppermute(value, ('row', 'col'), routes(to))]
    pallas_call x16 -> x15, Pallas kernels: 9.1 us -> 9.52 us  [run(): pl.pallas_call(body, out_shape=out_shape, in_specs=specs, scratch_shapes=...]
  transfers between devices with their start and end apart: 48 -> 42, of which waited for: 36 -> 33; matrix products, arithmetic and copies ran while one was open for 0% -> 0% of each run, Pallas kernels for 0% -> 0%
where the time goes in v1:
time: 203 us
  waiting for transfers between devices  92.2 us (45%)
  starting transfers between devices  78.2 us (39%)
  blocking collectives  19.5 us (10%)
  Pallas kernels  9.52 us (5%)
  local copies, waits for them, and re-layouts  3.05 us (2%)
    ppermute x42, waiting for transfers between devices, permuted(): return lax.ppermute(value, ('row', 'col'), routes(to))  92.2 us
    ppermute x42, starting transfers between devices, permuted(): return lax.ppermute(value, ('row', 'col'), routes(to))  78.2 us
    all_to_all x1, blocking collectives, from_every_z(): lax.all_to_all(value, 'row', 0, 0, tiled=True, axis_index_groups=Z_GROUPS)  19.5 us
    pallas_call x15, Pallas kernels, run(): pl.pallas_call(body, out_shape=out_shape, in_specs=specs, scratch_shapes=...  9.52 us
  transfers between devices with their start and end apart: 42, of which 33 were waited for; matrix products, arithmetic and copies ran while one was open for 0% of the time, Pallas kernels for 0%

profile of v1, /device:TPU:2, one launch (start us, length us, event | category | flops | bytes accessed | tf_op | source)
XLA Modules:
  0.0 202.8 jit_solution(8256957609688023283)
XLA Ops:
  3.5 1.5 collective-permute-start
  5.1 2.8 %collective-permute-start.1 = (bf16[88,256]{1,0:T(8,128)(2,1)S(1)}, bf16[88,256]{1,0:T(8,128)(2,1)S(1)}, u32[]{:S(2)}, u32[]{:S(2)}) collective-permute-start(bf16[88,256]{1,0:T(8,128)(2,1)S(1)} %get-tuple-element.62), channel_id=1, source_target_pairs={{0,2},{1,3},{2,0},{3,1},{4,6},{5,7},{6,4},{7,5},{8,10},{9,11},{10,... | collective-permute-start | bytes 135176 | tf_op jit(solution)/shard_map/ppermute | solution.py:25
  8.3 2.3 %collective-permute-done.1.refs_2_ = bf16[88,256]{1,0:T(8,128)(2,1)S(1)} collective-permute-done((bf16[88,256]{1,0:T(8,128)(2,1)S(1)}, bf16[88,256]{1,0:T(8,128)(2,1)S(1)}, u32[]{:S(2)}, u32[]{:S(2)}) %collective-permute-start.1) | collective-permute-done | bytes 45088 | tf_op jit(solution)/shard_map/ppermute | solution.py:25
  12.2 2.5 %collective-permute-start.4 = (bf16[512,256]{1,0:T(8,128)(2,1)S(1)}, bf16[512,256]{1,0:T(8,128)(2,1)S(1)}, u32[]{:S(2)}, u32[]{:S(2)}) collective-permute-start(bf16[512,256]{1,0:T(8,128)(2,1)S(1)} %get-tuple-element.68), channel_id=1, source_target_pairs={{0,2},{1,3},{2,0},{3,1},{4,6},{5,7},{6,4},{7,5},{8,10},{9,11},{10,... | collective-permute-start | bytes 786440 | tf_op jit(solution)/shard_map/ppermute | solution.py:25
  14.7 2.1 %collective-permute-start.5 = (bf16[512,256]{1,0:T(8,128)(2,1)S(1)}, bf16[512,256]{1,0:T(8,128)(2,1)S(1)}, u32[]{:S(2)}, u32[]{:S(2)}) collective-permute-start(bf16[512,256]{1,0:T(8,128)(2,1)S(1)} %get-tuple-element.69), channel_id=1, source_target_pairs={{0,3},{1,0},{2,1},{3,2},{4,7},{5,4},{6,5},{7,6},{8,11},{9,8},{10,9... | collective-permute-start | bytes 786440 | tf_op jit(solution)/shard_map/ppermute | solution.py:25
  17.5 3.3 %collective-permute-done.3.refs_1_ = bf16[512,256]{1,0:T(8,128)(2,1)S(1)} collective-permute-done((bf16[512,256]{1,0:T(8,128)(2,1)S(1)}, bf16[512,256]{1,0:T(8,128)(2,1)S(1)}, u32[]{:S(2)}, u32[]{:S(2)}) %collective-permute-start.3) | collective-permute-done | bytes 262176 | tf_op jit(solution)/shard_map/ppermute | solution.py:25
  20.7 2.0 %collective-permute-done.4.refs_2_ = bf16[512,256]{1,0:T(8,128)(2,1)S(1)} collective-permute-done((bf16[512,256]{1,0:T(8,128)(2,1)S(1)}, bf16[512,256]{1,0:T(8,128)(2,1)S(1)}, u32[]{:S(2)}, u32[]{:S(2)}) %collective-permute-start.4) | collective-permute-done | bytes 262176 | tf_op jit(solution)/shard_map/ppermute | solution.py:25
  22.8 2.7 %collective-permute-done.5.refs_3_ = bf16[512,256]{1,0:T(8,128)(2,1)S(1)} collective-permute-done((bf16[512,256]{1,0:T(8,128)(2,1)S(1)}, bf16[512,256]{1,0:T(8,128)(2,1)S(1)}, u32[]{:S(2)}, u32[]{:S(2)}) %collective-permute-start.5) | collective-permute-done | bytes 262176 | tf_op jit(solution)/shard_map/ppermute | solution.py:25
  25.7 2.0 collective-permute-start.14
  27.7 11.5 %collective-permute-start.10 = (bf16[4,88,256]{2,1,0:T(8,128)(2,1)S(1)}, bf16[4,88,256]{2,1,0:T(8,128)(2,1)S(1)}, u32[]{:S(2)}, u32[]{:S(2)}) collective-permute-start(bf16[4,88,256]{2,1,0:T(8,128)(2,1)S(1)} %collective-permute-done.6.refs_0_), channel_id=1, source_target_pairs={{0,12},{1,13},{2,14},{3,15},{4,0},{5,1},{6,2},{7,3},{8,4},{9,5},{1... | collective-permute-start | bytes 540680 | tf_op jit(solution)/shard_map/ppermute | solution.py:25
  40.1 7.1 %collective-permute-done.10.refs_3_ = bf16[4,88,256]{2,1,0:T(8,128)(2,1)S(1)} collective-permute-done((bf16[4,88,256]{2,1,0:T(8,128)(2,1)S(1)}, bf16[4,88,256]{2,1,0:T(8,128)(2,1)S(1)}, u32[]{:S(2)}, u32[]{:S(2)}) %collective-permute-start.10) | collective-permute-done | bytes 180256 | tf_op jit(solution)/shard_map/ppermute | solution.py:25
  48.2 2.5 %collective-permute-done.8.refs_1_ = bf16[4,88,256]{2,1,0:T(8,128)(2,1)S(1)} collective-permute-done((bf16[4,88,256]{2,1,0:T(8,128)(2,1)S(1)}, bf16[4,88,256]{2,1,0:T(8,128)(2,1)S(1)}, u32[]{:S(2)}, u32[]{:S(2)}) %collective-permute-start.8) | collective-permute-done | bytes 180256 | tf_op jit(solution)/shard_map/ppermute | solution.py:25
  51.4 2.1 %collective-permute-start.12 = (bf16[384,256]{1,0:T(8,128)(2,1)S(1)}, bf16[384,256]{1,0:T(8,128)(2,1)S(1)}, u32[]{:S(2)}, u32[]{:S(2)}) collective-permute-start(bf16[384,256]{1,0:T(8,128)(2,1)S(1)} %get-tuple-element.89), channel_id=1, source_target_pairs={{0,2},{1,3},{2,0},{3,1},{4,6},{5,7},{6,4},{7,5},{8,10},{9,11},{10,... | collective-permute-start | bytes 589832 | tf_op jit(solution)/shard_map/ppermute | solution.py:25
  54.5 4.5 %collective-permute-done.11.refs_1_.refs_5_ = bf16[384,256]{1,0:T(8,128)(2,1)S(1)} collective-permute-done((bf16[384,256]{1,0:T(8,128)(2,1)S(1)}, bf16[384,256]{1,0:T(8,128)(2,1)S(1)}, u32[]{:S(2)}, u32[]{:S(2)}) %collective-permute-start.11) | collective-permute-done | bytes 196640 | tf_op jit(solution)/shard_map/ppermute | solution.py:25
  58.9 1.8 collective-permute-done.12.refs_2_.refs_6_
  60.7 2.7 %collective-permute-done.13.refs_3_.refs_7_ = bf16[384,256]{1,0:T(8,128)(2,1)S(1)} collective-permute-done((bf16[384,256]{1,0:T(8,128)(2,1)S(1)}, bf16[384,256]{1,0:T(8,128)(2,1)S(1)}, u32[]{:S(2)}, u32[]{:S(2)}) %collective-permute-start.13) | collective-permute-done | bytes 196640 | tf_op jit(solution)/shard_map/ppermute | solution.py:25
  63.5 2.6 %collective-permute-done.15.refs_7_ = bf16[2,1024,256]{2,1,0:T(8,128)(2,1)S(1)} collective-permute-done((bf16[2,1024,256]{2,1,0:T(8,128)(2,1)S(1)}, bf16[2,1024,256]{2,1,0:T(8,128)(2,1)S(1)}, u32[]{:S(2)}, u32[]{:S(2)}) %collective-permute-start.15) | collective-permute-done | bytes 1048608 | tf_op jit(solution)/shard_map/ppermute | solution.py:25
  66.1 2.8 %shard_map.96 = (bf16[88,1024]{1,0:T(8,128)(2,1)S(1)}, bf16[88,1024]{1,0:T(8,128)(2,1)S(1)}, bf16[88,1024]{1,0:T(8,128)(2,1)S(1)}, bf16[88,1024]{1,0:T(8,128)(2,1)S(1)}) custom-call(bf16[4,88,256]{2,1,0:T(8,128)(2,1)S(1)} %collective-permute-done.6.refs_0_, bf16[4,88,256]{2,1,0:T(8,128)(2,1)S(1)} %collective-permute-done.8.refs_1_, ...), custom_call_target="tpu_custom_call" | custom-call | flops 738197504 | bytes 5636096 | tf_op jit(solution)/shard_map/pallas_call | solution.py:106
  69.9 4.8 %collective-permute-start.17 = (bf16[88,1024]{1,0:T(8,128)(2,1)S(1)}, bf16[88,1024]{1,0:T(8,128)(2,1)S(1)}, u32[]{:S(2)}, u32[]{:S(2)}) collective-permute-start(bf16[88,1024]{1,0:T(8,128)(2,1)S(1)} %get-tuple-element.94), channel_id=1, source_target_pairs={{0,128},{1,129},{2,130},{3,131},{4,132},{5,133},{6,134},{7,135},{8... | collective-permute-start | bytes 540680 | tf_op jit(solution)/shard_map/ppermute | solution.py:25
  74.7 2.6 %collective-permute-start.18 = (bf16[88,1024]{1,0:T(8,128)(2,1)S(1)}, bf16[88,1024]{1,0:T(8,128)(2,1)S(1)}, u32[]{:S(2)}, u32[]{:S(2)}) collective-permute-start(bf16[88,1024]{1,0:T(8,128)(2,1)S(1)} %get-tuple-element.95), channel_id=1, source_target_pairs={{0,192},{1,193},{2,194},{3,195},{4,196},{5,197},{6,198},{7,199},{8... | collective-permute-start | bytes 540680 | tf_op jit(solution)/shard_map/ppermute | solution.py:25
  78.2 6.9 %collective-permute-done.17.refs_2_ = bf16[88,1024]{1,0:T(8,128)(2,1)S(1)} collective-permute-done((bf16[88,1024]{1,0:T(8,128)(2,1)S(1)}, bf16[88,1024]{1,0:T(8,128)(2,1)S(1)}, u32[]{:S(2)}, u32[]{:S(2)}) %collective-permute-start.17) | collective-permute-done | bytes 180256 | tf_op jit(solution)/shard_map/ppermute | solution.py:25
  85.0 6.1 %collective-permute-done.18.refs_3_ = bf16[88,1024]{1,0:T(8,128)(2,1)S(1)} collective-permute-done((bf16[88,1024]{1,0:T(8,128)(2,1)S(1)}, bf16[88,1024]{1,0:T(8,128)(2,1)S(1)}, u32[]{:S(2)}, u32[]{:S(2)}) %collective-permute-start.18) | collective-permute-done | bytes 180256 | tf_op jit(solution)/shard_map/ppermute | solution.py:25
  91.2 19.5 %all_to_all.5.mine_ref = bf16[8,24,1024]{2,1,0:T(8,128)(2,1)S(1)} all-to-all(bf16[8,24,1024]{2,1,0:T(8,128)(2,1)S(1)} %get-tuple-element.97), channel_id=1, replica_groups={{0,32,64,96,128,160,192,224},{16,48,80,112,144,176,208,240},{1,33,65,97..., dimensions={0} | all-to-all | bytes 786432 | tf_op jit(solution)/shard_map/all_to_all | solution.py:55
  110.7 1.7 collective-permute-done.19.other_ref
  115.8 3.4 %collective-permute-done.22.refs_3_ = bf16[448,128]{1,0:T(8,128)(2,1)S(1)} collective-permute-done((bf16[448,128]{1,0:T(8,128)(2,1)S(1)}, bf16[448,128]{1,0:T(8,128)(2,1)S(1)}, u32[]{:S(2)}, u32[]{:S(2)}) %collective-permute-start.22) | collective-permute-done | bytes 114720 | tf_op jit(solution)/shard_map/ppermute | solution.py:25
  119.3 2.9 %collective-permute-done.21.refs_2_ = bf16[448,128]{1,0:T(8,128)(2,1)S(1)} collective-permute-done((bf16[448,128]{1,0:T(8,128)(2,1)S(1)}, bf16[448,128]{1,0:T(8,128)(2,1)S(1)}, u32[]{:S(2)}, u32[]{:S(2)}) %collective-permute-start.21) | collective-permute-done | bytes 114720 | tf_op jit(solution)/shard_map/ppermute | solution.py:25
  124.1 1.6 collective-permute-start.24
  125.7 2.5 %collective-permute-start.23 = (bf16[448,128]{1,0:T(8,128)(2,1)S(1)}, bf16[448,128]{1,0:T(8,128)(2,1)S(1)}, u32[]{:S(2)}, u32[]{:S(2)}) collective-permute-start(bf16[448,128]{1,0:T(8,128)(2,1)S(1)} %shard_map.99.refs_0_), channel_id=1, source_target_pairs={{0,1},{1,2},{2,3},{3,0},{4,5},{5,6},{6,7},{7,4},{8,9},{9,10},{10,1... | collective-permute-start | bytes 344072 | tf_op jit(solution)/shard_map/ppermute | solution.py:25
  128.2 2.7 %collective-permute-done.25.refs_3_ = bf16[448,128]{1,0:T(8,128)(2,1)S(1)} collective-permute-done((bf16[448,128]{1,0:T(8,128)(2,1)S(1)}, bf16[448,128]{1,0:T(8,128)(2,1)S(1)}, u32[]{:S(2)}, u32[]{:S(2)}) %collective-permute-start.25) | collective-permute-done | bytes 114720 | tf_op jit(solution)/shard_map/ppermute | solution.py:25
  130.9 1.8 collective-permute-done.23.refs_1_
  134.4 11.7 %collective-permute-start.29 = (bf16[4,64,256]{2,1,0:T(8,128)(2,1)S(1)}, bf16[4,64,256]{2,1,0:T(8,128)(2,1)S(1)}, u32[]{:S(2)}, u32[]{:S(2)}) collective-permute-start(bf16[4,64,256]{2,1,0:T(8,128)(2,1)S(1)} %collective-permute-done.26.refs_0_), channel_id=1, source_target_pairs={{0,12},{1,13},{2,14},{3,15},{4,0},{5,1},{6,2},{7,3},{8,4},{9,5},{1... | collective-permute-start | bytes 393224 | tf_op jit(solution)/shard_map/ppermute | solution.py:25
  146.1 2.1 %collective-permute-start.28 = (bf16[4,64,256]{2,1,0:T(8,128)(2,1)S(1)}, bf16[4,64,256]{2,1,0:T(8,128)(2,1)S(1)}, u32[]{:S(2)}, u32[]{:S(2)}) collective-permute-start(bf16[4,64,256]{2,1,0:T(8,128)(2,1)S(1)} %collective-permute-done.26.refs_0_), channel_id=1, source_target_pairs={{0,8},{1,9},{2,10},{3,11},{4,12},{5,13},{6,14},{7,15},{8,0},{9,1},... | collective-permute-start | bytes 393224 | tf_op jit(solution)/shard_map/ppermute | solution.py:25
  149.6 3.0 %collective-permute-done.28.refs_2_ = bf16[4,64,256]{2,1,0:T(8,128)(2,1)S(1)} collective-permute-done((bf16[4,64,256]{2,1,0:T(8,128)(2,1)S(1)}, bf16[4,64,256]{2,1,0:T(8,128)(2,1)S(1)}, u32[]{:S(2)}, u32[]{:S(2)}) %collective-permute-start.28) | collective-permute-done | bytes 131104 | tf_op jit(solution)/shard_map/ppermute | solution.py:25
  152.6 1.8 collective-permute-done.27.refs_1_
  154.4 1.5 shard_map.101
  155.9 2.4 %collective-permute-start.30 = (bf16[64,1024]{1,0:T(8,128)(2,1)S(1)}, bf16[64,1024]{1,0:T(8,128)(2,1)S(1)}, u32[]{:S(2)}, u32[]{:S(2)}) collective-permute-start(bf16[64,1024]{1,0:T(8,128)(2,1)S(1)} %get-tuple-element.105), channel_id=1, source_target_pairs={{0,64},{1,65},{2,66},{3,67},{4,68},{5,69},{6,70},{7,71},{8,72},{9,... | collective-permute-start | bytes 393224 | tf_op jit(solution)/shard_map/ppermute | solution.py:25
  158.3 3.8 %collective-permute-start.31 = (bf16[64,1024]{1,0:T(8,128)(2,1)S(1)}, bf16[64,1024]{1,0:T(8,128)(2,1)S(1)}, u32[]{:S(2)}, u32[]{:S(2)}) collective-permute-start(bf16[64,1024]{1,0:T(8,128)(2,1)S(1)} %get-tuple-element.106), channel_id=1, source_target_pairs={{0,128},{1,129},{2,130},{3,131},{4,132},{5,133},{6,134},{7,135},{8... | collective-permute-start | bytes 393224 | tf_op jit(solution)/shard_map/ppermute | solution.py:25
  162.3 2.2 %collective-permute-done.30.refs_1_ = bf16[64,1024]{1,0:T(8,128)(2,1)S(1)} collective-permute-done((bf16[64,1024]{1,0:T(8,128)(2,1)S(1)}, bf16[64,1024]{1,0:T(8,128)(2,1)S(1)}, u32[]{:S(2)}, u32[]{:S(2)}) %collective-permute-start.30) | collective-permute-done | bytes 131104 | tf_op jit(solution)/shard_map/ppermute | solution.py:25
  164.6 7.6 %collective-permute-done.31.refs_2_ = bf16[64,1024]{1,0:T(8,128)(2,1)S(1)} collective-permute-done((bf16[64,1024]{1,0:T(8,128)(2,1)S(1)}, bf16[64,1024]{1,0:T(8,128)(2,1)S(1)}, u32[]{:S(2)}, u32[]{:S(2)}) %collective-permute-start.31) | collective-permute-done | bytes 131104 | tf_op jit(solution)/shard_map/ppermute | solution.py:25
  173.9 1.8 collective-permute-start.33
  175.7 3.9 %collective-permute-done.35.refs_3_ = bf16[448,128]{1,0:T(8,128)(2,1)S(1)} collective-permute-done((bf16[448,128]{1,0:T(8,128)(2,1)S(1)}, bf16[448,128]{1,0:T(8,128)(2,1)S(1)}, u32[]{:S(2)}, u32[]{:S(2)}) %collective-permute-start.35) | collective-permute-done | bytes 114720 | tf_op jit(solution)/shard_map/ppermute | solution.py:25
  180.7 1.8 collective-permute-done.33.refs_1_
  182.5 3.8 %collective-permute-start.38 = (bf16[448,128]{1,0:T(8,128)(2,1)S(1)}, bf16[448,128]{1,0:T(8,128)(2,1)S(1)}, u32[]{:S(2)}, u32[]{:S(2)}) collective-permute-start(bf16[448,128]{1,0:T(8,128)(2,1)S(1)} %shard_map.103.refs_0_), channel_id=1, source_target_pairs={{0,3},{1,0},{2,1},{3,2},{4,7},{5,4},{6,5},{7,6},{8,11},{9,8},{10,9... | collective-permute-start | bytes 344072 | tf_op jit(solution)/shard_map/ppermute | solution.py:25
  187.9 2.0 collective-permute-done.38.refs_3_
  189.8 2.8 %collective-permute-done.37.refs_2_ = bf16[448,128]{1,0:T(8,128)(2,1)S(1)} collective-permute-done((bf16[448,128]{1,0:T(8,128)(2,1)S(1)}, bf16[448,128]{1,0:T(8,128)(2,1)S(1)}, u32[]{:S(2)}, u32[]{:S(2)}) %collective-permute-start.37) | collective-permute-done | bytes 114720 | tf_op jit(solution)/shard_map/ppermute | solution.py:25
  193.7 2.9 %collective-permute-start.39 = (bf16[64,256]{1,0:T(8,128)(2,1)S(1)}, bf16[64,256]{1,0:T(8,128)(2,1)S(1)}, u32[]{:S(2)}, u32[]{:S(2)}) collective-permute-start(bf16[64,256]{1,0:T(8,128)(2,1)S(1)} %get-tuple-element.112), channel_id=1, source_target_pairs={{0,3},{1,0},{2,1},{3,2},{4,7},{5,4},{6,5},{7,6},{8,11},{9,8},{10,9... | collective-permute-start | bytes 98312 | tf_op jit(solution)/shard_map/ppermute | solution.py:25
  196.6 2.5 %collective-permute-start.41 = (bf16[64,256]{1,0:T(8,128)(2,1)S(1)}, bf16[64,256]{1,0:T(8,128)(2,1)S(1)}, u32[]{:S(2)}, u32[]{:S(2)}) collective-permute-start(bf16[64,256]{1,0:T(8,128)(2,1)S(1)} %get-tuple-element.114), channel_id=1, source_target_pairs={{0,1},{1,2},{2,3},{3,0},{4,5},{5,6},{6,7},{7,4},{8,9},{9,10},{10,1... | collective-permute-start | bytes 98312 | tf_op jit(solution)/shard_map/ppermute | solution.py:25
  199.1 2.9 %collective-permute-done.40.refs_2_ = bf16[64,256]{1,0:T(8,128)(2,1)S(1)} collective-permute-done((bf16[64,256]{1,0:T(8,128)(2,1)S(1)}, bf16[64,256]{1,0:T(8,128)(2,1)S(1)}, u32[]{:S(2)}, u32[]{:S(2)}) %collective-permute-start.40) | collective-permute-done | bytes 32800 | tf_op jit(solution)/shard_map/ppermute | solution.py:25
  (70 shorter events, 26.6 us)
Async XLA Ops:
  0.0 12.0 %copy-start.1 = (bf16[4,256,256]{2,1,0:T(8,128)(2,1)S(1)}, bf16[4,256,256]{2,1,0:T(8,128)(2,1)}, u32[]{:S(2)}) copy-start(bf16[4,256,256]{2,1,0:T(8,128)(2,1)} %upper_ref) | copy-start | bytes 1572868
  0.0 12.0 %copy-start = (bf16[4,256,256]{2,1,0:T(8,128)(2,1)S(1)}, bf16[4,256,256]{2,1,0:T(8,128)(2,1)}, u32[]{:S(2)}) copy-start(bf16[4,256,256]{2,1,0:T(8,128)(2,1)} %lower_ref) | copy-start | bytes 1572868
  3.5 4.8 %collective-permute-start = (bf16[88,256]{1,0:T(8,128)(2,1)S(1)}, bf16[88,256]{1,0:T(8,128)(2,1)S(1)}, u32[]{:S(2)}, u32[]{:S(2)}) collective-permute-start(bf16[88,256]{1,0:T(8,128)(2,1)S(1)} %get-tuple-element.61), channel_id=1, source_target_pairs={{0,1},{1,2},{2,3},{3,0},{4,5},{5,6},{6,7},{7,4},{8,9},{9,10},{10,1... | collective-permute-start | bytes 135176 | tf_op jit(solution)/shard_map/ppermute | solution.py:25
  5.1 5.6 %collective-permute-start.1 = (bf16[88,256]{1,0:T(8,128)(2,1)S(1)}, bf16[88,256]{1,0:T(8,128)(2,1)S(1)}, u32[]{:S(2)}, u32[]{:S(2)}) collective-permute-start(bf16[88,256]{1,0:T(8,128)(2,1)S(1)} %get-tuple-element.62), channel_id=1, source_target_pairs={{0,2},{1,3},{2,0},{3,1},{4,6},{5,7},{6,4},{7,5},{8,10},{9,11},{10,... | collective-permute-start | bytes 135176 | tf_op jit(solution)/shard_map/ppermute | solution.py:25
  7.9 4.0 %collective-permute-start.2 = (bf16[88,256]{1,0:T(8,128)(2,1)S(1)}, bf16[88,256]{1,0:T(8,128)(2,1)S(1)}, u32[]{:S(2)}, u32[]{:S(2)}) collective-permute-start(bf16[88,256]{1,0:T(8,128)(2,1)S(1)} %get-tuple-element.63), channel_id=1, source_target_pairs={{0,3},{1,0},{2,1},{3,2},{4,7},{5,4},{6,5},{7,6},{8,11},{9,8},{10,9... | collective-permute-start | bytes 135176 | tf_op jit(solution)/shard_map/ppermute | solution.py:25
  12.1 8.6 %collective-permute-start.3 = (bf16[512,256]{1,0:T(8,128)(2,1)S(1)}, bf16[512,256]{1,0:T(8,128)(2,1)S(1)}, u32[]{:S(2)}, u32[]{:S(2)}) collective-permute-start(bf16[512,256]{1,0:T(8,128)(2,1)S(1)} %get-tuple-element.67), channel_id=1, source_target_pairs={{0,1},{1,2},{2,3},{3,0},{4,5},{5,6},{6,7},{7,4},{8,9},{9,10},{10,1... | collective-permute-start | bytes 786440 | tf_op jit(solution)/shard_map/ppermute | solution.py:25
  12.2 10.6 %collective-permute-start.4 = (bf16[512,256]{1,0:T(8,128)(2,1)S(1)}, bf16[512,256]{1,0:T(8,128)(2,1)S(1)}, u32[]{:S(2)}, u32[]{:S(2)}) collective-permute-start(bf16[512,256]{1,0:T(8,128)(2,1)S(1)} %get-tuple-element.68), channel_id=1, source_target_pairs={{0,2},{1,3},{2,0},{3,1},{4,6},{5,7},{6,4},{7,5},{8,10},{9,11},{10,... | collective-permute-start | bytes 786440 | tf_op jit(solution)/shard_map/ppermute | solution.py:25
  14.7 10.8 %collective-permute-start.5 = (bf16[512,256]{1,0:T(8,128)(2,1)S(1)}, bf16[512,256]{1,0:T(8,128)(2,1)S(1)}, u32[]{:S(2)}, u32[]{:S(2)}) collective-permute-start(bf16[512,256]{1,0:T(8,128)(2,1)S(1)} %get-tuple-element.69), channel_id=1, source_target_pairs={{0,3},{1,0},{2,1},{3,2},{4,7},{5,4},{6,5},{7,6},{8,11},{9,8},{10,9... | collective-permute-start | bytes 786440 | tf_op jit(solution)/shard_map/ppermute | solution.py:25
  16.8 0.7 collective-permute-start.6
  25.5 25.1 %copy-start.2 = (bf16[6,256,128]{2,1,0:T(8,128)(2,1)S(1)}, bf16[6,256,128]{2,1,0:T(8,128)(2,1)}, u32[]{:S(2)}) copy-start(bf16[6,256,128]{2,1,0:T(8,128)(2,1)} %low_ref.2) | copy-start | bytes 1179652
  25.5 25.1 %copy-start.3 = (bf16[6,256,128]{2,1,0:T(8,128)(2,1)S(1)}, bf16[6,256,128]{2,1,0:T(8,128)(2,1)}, u32[]{:S(2)}) copy-start(bf16[6,256,128]{2,1,0:T(8,128)(2,1)} %up_ref.2) | copy-start | bytes 1179652
  25.6 25.0 %collective-permute-start.7 = (bf16[2,1024,256]{2,1,0:T(8,128)(2,1)S(1)}, bf16[2,1024,256]{2,1,0:T(8,128)(2,1)S(1)}, u32[]{:S(2)}, u32[]{:S(2)}) collective-permute-start(bf16[2,1024,256]{2,1,0:T(8,128)(2,1)S(1)} %shard_map.94.refs_4_), channel_id=1, source_target_pairs={{0,16},{1,17},{2,18},{3,19},{4,20},{5,21},{6,22},{7,23},{8,24},{9,... | collective-permute-start | bytes 3145736 | tf_op jit(solution)/shard_map/ppermute | solution.py:25
  25.7 28.8 %collective-permute-start.14 = (bf16[2,1024,256]{2,1,0:T(8,128)(2,1)S(1)}, bf16[2,1024,256]{2,1,0:T(8,128)(2,1)S(1)}, u32[]{:S(2)}, u32[]{:S(2)}) collective-permute-start(bf16[2,1024,256]{2,1,0:T(8,128)(2,1)S(1)} %shard_map.94.refs_4_), channel_id=1, source_target_pairs={{0,32},{1,33},{2,34},{3,35},{4,36},{5,37},{6,38},{7,39},{8,40},{9,... | collective-permute-start | bytes 3145736 | tf_op jit(solution)/shard_map/ppermute | solution.py:25
  27.7 19.5 %collective-permute-start.10 = (bf16[4,88,256]{2,1,0:T(8,128)(2,1)S(1)}, bf16[4,88,256]{2,1,0:T(8,128)(2,1)S(1)}, u32[]{:S(2)}, u32[]{:S(2)}) collective-permute-start(bf16[4,88,256]{2,1,0:T(8,128)(2,1)S(1)} %collective-permute-done.6.refs_0_), channel_id=1, source_target_pairs={{0,12},{1,13},{2,14},{3,15},{4,0},{5,1},{6,2},{7,3},{8,4},{9,5},{1... | collective-permute-start | bytes 540680 | tf_op jit(solution)/shard_map/ppermute | solution.py:25
  39.2 8.9 %collective-permute-start.9 = (bf16[4,88,256]{2,1,0:T(8,128)(2,1)S(1)}, bf16[4,88,256]{2,1,0:T(8,128)(2,1)S(1)}, u32[]{:S(2)}, u32[]{:S(2)}) collective-permute-start(bf16[4,88,256]{2,1,0:T(8,128)(2,1)S(1)} %collective-permute-done.6.refs_0_), channel_id=1, source_target_pairs={{0,8},{1,9},{2,10},{3,11},{4,12},{5,13},{6,14},{7,15},{8,0},{9,1},... | collective-permute-start | bytes 540680 | tf_op jit(solution)/shard_map/ppermute | solution.py:25
  39.2 11.4 %collective-permute-start.8 = (bf16[4,88,256]{2,1,0:T(8,128)(2,1)S(1)}, bf16[4,88,256]{2,1,0:T(8,128)(2,1)S(1)}, u32[]{:S(2)}, u32[]{:S(2)}) collective-permute-start(bf16[4,88,256]{2,1,0:T(8,128)(2,1)S(1)} %collective-permute-done.6.refs_0_), channel_id=1, source_target_pairs={{0,4},{1,5},{2,6},{3,7},{4,8},{5,9},{6,10},{7,11},{8,12},{9,13},{1... | collective-permute-start | bytes 540680 | tf_op jit(solution)/shard_map/ppermute | solution.py:25
  51.0 7.9 %collective-permute-start.11 = (bf16[384,256]{1,0:T(8,128)(2,1)S(1)}, bf16[384,256]{1,0:T(8,128)(2,1)S(1)}, u32[]{:S(2)}, u32[]{:S(2)}) collective-permute-start(bf16[384,256]{1,0:T(8,128)(2,1)S(1)} %get-tuple-element.88), channel_id=1, source_target_pairs={{0,1},{1,2},{2,3},{3,0},{4,5},{5,6},{6,7},{7,4},{8,9},{9,10},{10,1... | collective-permute-start | bytes 589832 | tf_op jit(solution)/shard_map/ppermute | solution.py:25
  51.4 9.4 %collective-permute-start.12 = (bf16[384,256]{1,0:T(8,128)(2,1)S(1)}, bf16[384,256]{1,0:T(8,128)(2,1)S(1)}, u32[]{:S(2)}, u32[]{:S(2)}) collective-permute-start(bf16[384,256]{1,0:T(8,128)(2,1)S(1)} %get-tuple-element.89), channel_id=1, source_target_pairs={{0,2},{1,3},{2,0},{3,1},{4,6},{5,7},{6,4},{7,5},{8,10},{9,11},{10,... | collective-permute-start | bytes 589832 | tf_op jit(solution)/shard_map/ppermute | solution.py:25
  53.5 10.0 %collective-permute-start.13 = (bf16[384,256]{1,0:T(8,128)(2,1)S(1)}, bf16[384,256]{1,0:T(8,128)(2,1)S(1)}, u32[]{:S(2)}, u32[]{:S(2)}) collective-permute-start(bf16[384,256]{1,0:T(8,128)(2,1)S(1)} %get-tuple-element.90), channel_id=1, source_target_pairs={{0,3},{1,0},{2,1},{3,2},{4,7},{5,4},{6,5},{7,6},{8,11},{9,8},{10,9... | collective-permute-start | bytes 589832 | tf_op jit(solution)/shard_map/ppermute | solution.py:25
  63.5 2.7 %collective-permute-start.15 = (bf16[2,1024,256]{2,1,0:T(8,128)(2,1)S(1)}, bf16[2,1024,256]{2,1,0:T(8,128)(2,1)S(1)}, u32[]{:S(2)}, u32[]{:S(2)}) collective-permute-start(bf16[2,1024,256]{2,1,0:T(8,128)(2,1)S(1)} %collective-permute-done.14.refs_6_), channel_id=1, source_target_pairs={{0,16},{1,17},{2,18},{3,19},{4,20},{5,21},{6,22},{7,23},{8,24},{9,... | collective-permute-start | bytes 3145736 | tf_op jit(solution)/shard_map/ppermute | solution.py:25
  68.9 9.3 %collective-permute-start.16 = (bf16[88,1024]{1,0:T(8,128)(2,1)S(1)}, bf16[88,1024]{1,0:T(8,128)(2,1)S(1)}, u32[]{:S(2)}, u32[]{:S(2)}) collective-permute-start(bf16[88,1024]{1,0:T(8,128)(2,1)S(1)} %get-tuple-element.93), channel_id=1, source_target_pairs={{0,64},{1,65},{2,66},{3,67},{4,68},{5,69},{6,70},{7,71},{8,72},{9,... | collective-permute-start | bytes 540680 | tf_op jit(solution)/shard_map/ppermute | solution.py:25
  69.9 15.2 %collective-permute-start.17 = (bf16[88,1024]{1,0:T(8,128)(2,1)S(1)}, bf16[88,1024]{1,0:T(8,128)(2,1)S(1)}, u32[]{:S(2)}, u32[]{:S(2)}) collective-permute-start(bf16[88,1024]{1,0:T(8,128)(2,1)S(1)} %get-tuple-element.94), channel_id=1, source_target_pairs={{0,128},{1,129},{2,130},{3,131},{4,132},{5,133},{6,134},{7,135},{8... | collective-permute-start | bytes 540680 | tf_op jit(solution)/shard_map/ppermute | solution.py:25
  74.7 16.4 %collective-permute-start.18 = (bf16[88,1024]{1,0:T(8,128)(2,1)S(1)}, bf16[88,1024]{1,0:T(8,128)(2,1)S(1)}, u32[]{:S(2)}, u32[]{:S(2)}) collective-permute-start(bf16[88,1024]{1,0:T(8,128)(2,1)S(1)} %get-tuple-element.95), channel_id=1, source_target_pairs={{0,192},{1,193},{2,194},{3,195},{4,196},{5,197},{6,198},{7,199},{8... | collective-permute-start | bytes 540680 | tf_op jit(solution)/shard_map/ppermute | solution.py:25
  110.7 1.7 collective-permute-start.19
  113.2 6.1 %collective-permute-start.22 = (bf16[448,128]{1,0:T(8,128)(2,1)S(1)}, bf16[448,128]{1,0:T(8,128)(2,1)S(1)}, u32[]{:S(2)}, u32[]{:S(2)}) collective-permute-start(bf16[448,128]{1,0:T(8,128)(2,1)S(1)} %get-tuple-element.102.refs_0_), channel_id=1, source_target_pairs={{0,12},{1,13},{2,14},{3,15},{4,0},{5,1},{6,2},{7,3},{8,4},{9,5},{1... | collective-permute-start | bytes 344072 | tf_op jit(solution)/shard_map/ppermute | solution.py:25
  114.6 7.5 %collective-permute-start.21 = (bf16[448,128]{1,0:T(8,128)(2,1)S(1)}, bf16[448,128]{1,0:T(8,128)(2,1)S(1)}, u32[]{:S(2)}, u32[]{:S(2)}) collective-permute-start(bf16[448,128]{1,0:T(8,128)(2,1)S(1)} %get-tuple-element.102.refs_0_), channel_id=1, source_target_pairs={{0,8},{1,9},{2,10},{3,11},{4,12},{5,13},{6,14},{7,15},{8,0},{9,1},... | collective-permute-start | bytes 344072 | tf_op jit(solution)/shard_map/ppermute | solution.py:25
  115.8 7.7 %collective-permute-start.20 = (bf16[448,128]{1,0:T(8,128)(2,1)S(1)}, bf16[448,128]{1,0:T(8,128)(2,1)S(1)}, u32[]{:S(2)}, u32[]{:S(2)}) collective-permute-start(bf16[448,128]{1,0:T(8,128)(2,1)S(1)} %get-tuple-element.102.refs_0_), channel_id=1, source_target_pairs={{0,4},{1,5},{2,6},{3,7},{4,8},{5,9},{6,10},{7,11},{8,12},{9,13},{1... | collective-permute-start | bytes 344072 | tf_op jit(solution)/shard_map/ppermute | solution.py:25
  123.6 9.2 %copy-start.7 = (s32[6]{0:T(128)S(1)}, s32[6]{0:T(128)}, u32[]{:S(2)}) copy-start(s32[6]{0:T(128)} %refs_6_.2) | copy-start | bytes 76
  123.6 7.4 %collective-permute-start.25 = (bf16[448,128]{1,0:T(8,128)(2,1)S(1)}, bf16[448,128]{1,0:T(8,128)(2,1)S(1)}, u32[]{:S(2)}, u32[]{:S(2)}) collective-permute-start(bf16[448,128]{1,0:T(8,128)(2,1)S(1)} %shard_map.99.refs_0_), channel_id=1, source_target_pairs={{0,3},{1,0},{2,1},{3,2},{4,7},{5,4},{6,5},{7,6},{8,11},{9,8},{10,9... | collective-permute-start | bytes 344072 | tf_op jit(solution)/shard_map/ppermute | solution.py:25
  124.1 6.9 %collective-permute-start.24 = (bf16[448,128]{1,0:T(8,128)(2,1)S(1)}, bf16[448,128]{1,0:T(8,128)(2,1)S(1)}, u32[]{:S(2)}, u32[]{:S(2)}) collective-permute-start(bf16[448,128]{1,0:T(8,128)(2,1)S(1)} %shard_map.99.refs_0_), channel_id=1, source_target_pairs={{0,2},{1,3},{2,0},{3,1},{4,6},{5,7},{6,4},{7,5},{8,10},{9,11},{10,... | collective-permute-start | bytes 344072 | tf_op jit(solution)/shard_map/ppermute | solution.py:25
  125.7 7.0 %collective-permute-start.23 = (bf16[448,128]{1,0:T(8,128)(2,1)S(1)}, bf16[448,128]{1,0:T(8,128)(2,1)S(1)}, u32[]{:S(2)}, u32[]{:S(2)}) collective-permute-start(bf16[448,128]{1,0:T(8,128)(2,1)S(1)} %shard_map.99.refs_0_), channel_id=1, source_target_pairs={{0,1},{1,2},{2,3},{3,0},{4,5},{5,6},{6,7},{7,4},{8,9},{9,10},{10,1... | collective-permute-start | bytes 344072 | tf_op jit(solution)/shard_map/ppermute | solution.py:25
  133.7 0.7 collective-permute-start.26
  134.4 15.2 %collective-permute-start.29 = (bf16[4,64,256]{2,1,0:T(8,128)(2,1)S(1)}, bf16[4,64,256]{2,1,0:T(8,128)(2,1)S(1)}, u32[]{:S(2)}, u32[]{:S(2)}) collective-permute-start(bf16[4,64,256]{2,1,0:T(8,128)(2,1)S(1)} %collective-permute-done.26.refs_0_), channel_id=1, source_target_pairs={{0,12},{1,13},{2,14},{3,15},{4,0},{5,1},{6,2},{7,3},{8,4},{9,5},{1... | collective-permute-start | bytes 393224 | tf_op jit(solution)/shard_map/ppermute | solution.py:25
  146.1 6.5 %collective-permute-start.28 = (bf16[4,64,256]{2,1,0:T(8,128)(2,1)S(1)}, bf16[4,64,256]{2,1,0:T(8,128)(2,1)S(1)}, u32[]{:S(2)}, u32[]{:S(2)}) collective-permute-start(bf16[4,64,256]{2,1,0:T(8,128)(2,1)S(1)} %collective-permute-done.26.refs_0_), channel_id=1, source_target_pairs={{0,8},{1,9},{2,10},{3,11},{4,12},{5,13},{6,14},{7,15},{8,0},{9,1},... | collective-permute-start | bytes 393224 | tf_op jit(solution)/shard_map/ppermute | solution.py:25
  148.2 6.2 %collective-permute-start.27 = (bf16[4,64,256]{2,1,0:T(8,128)(2,1)S(1)}, bf16[4,64,256]{2,1,0:T(8,128)(2,1)S(1)}, u32[]{:S(2)}, u32[]{:S(2)}) collective-permute-start(bf16[4,64,256]{2,1,0:T(8,128)(2,1)S(1)} %collective-permute-done.26.refs_0_), channel_id=1, source_target_pairs={{0,4},{1,5},{2,6},{3,7},{4,8},{5,9},{6,10},{7,11},{8,12},{9,13},{1... | collective-permute-start | bytes 393224 | tf_op jit(solution)/shard_map/ppermute | solution.py:25
  155.9 8.7 %collective-permute-start.30 = (bf16[64,1024]{1,0:T(8,128)(2,1)S(1)}, bf16[64,1024]{1,0:T(8,128)(2,1)S(1)}, u32[]{:S(2)}, u32[]{:S(2)}) collective-permute-start(bf16[64,1024]{1,0:T(8,128)(2,1)S(1)} %get-tuple-element.105), channel_id=1, source_target_pairs={{0,64},{1,65},{2,66},{3,67},{4,68},{5,69},{6,70},{7,71},{8,72},{9,... | collective-permute-start | bytes 393224 | tf_op jit(solution)/shard_map/ppermute | solution.py:25
  158.3 13.9 %collective-permute-start.31 = (bf16[64,1024]{1,0:T(8,128)(2,1)S(1)}, bf16[64,1024]{1,0:T(8,128)(2,1)S(1)}, u32[]{:S(2)}, u32[]{:S(2)}) collective-permute-start(bf16[64,1024]{1,0:T(8,128)(2,1)S(1)} %get-tuple-element.106), channel_id=1, source_target_pairs={{0,128},{1,129},{2,130},{3,131},{4,132},{5,133},{6,134},{7,135},{8... | collective-permute-start | bytes 393224 | tf_op jit(solution)/shard_map/ppermute | solution.py:25
  162.1 10.9 %collective-permute-start.32 = (bf16[64,1024]{1,0:T(8,128)(2,1)S(1)}, bf16[64,1024]{1,0:T(8,128)(2,1)S(1)}, u32[]{:S(2)}, u32[]{:S(2)}) collective-permute-start(bf16[64,1024]{1,0:T(8,128)(2,1)S(1)} %get-tuple-element.107), channel_id=1, source_target_pairs={{0,192},{1,193},{2,194},{3,195},{4,196},{5,197},{6,198},{7,199},{8... | collective-permute-start | bytes 393224 | tf_op jit(solution)/shard_map/ppermute | solution.py:25
  173.4 6.3 %collective-permute-start.35 = (bf16[448,128]{1,0:T(8,128)(2,1)S(1)}, bf16[448,128]{1,0:T(8,128)(2,1)S(1)}, u32[]{:S(2)}, u32[]{:S(2)}) collective-permute-start(bf16[448,128]{1,0:T(8,128)(2,1)S(1)} %get-tuple-element.109.refs_0_), channel_id=1, source_target_pairs={{0,12},{1,13},{2,14},{3,15},{4,0},{5,1},{6,2},{7,3},{8,4},{9,5},{1... | collective-permute-start | bytes 344072 | tf_op jit(solution)/shard_map/ppermute | solution.py:25
  173.8 6.9 %collective-permute-start.34 = (bf16[448,128]{1,0:T(8,128)(2,1)S(1)}, bf16[448,128]{1,0:T(8,128)(2,1)S(1)}, u32[]{:S(2)}, u32[]{:S(2)}) collective-permute-start(bf16[448,128]{1,0:T(8,128)(2,1)S(1)} %get-tuple-element.109.refs_0_), channel_id=1, source_target_pairs={{0,8},{1,9},{2,10},{3,11},{4,12},{5,13},{6,14},{7,15},{8,0},{9,1},... | collective-permute-start | bytes 344072 | tf_op jit(solution)/shard_map/ppermute | solution.py:25
  173.9 8.5 %collective-permute-start.33 = (bf16[448,128]{1,0:T(8,128)(2,1)S(1)}, bf16[448,128]{1,0:T(8,128)(2,1)S(1)}, u32[]{:S(2)}, u32[]{:S(2)}) collective-permute-start(bf16[448,128]{1,0:T(8,128)(2,1)S(1)} %get-tuple-element.109.refs_0_), channel_id=1, source_target_pairs={{0,4},{1,5},{2,6},{3,7},{4,8},{5,9},{6,10},{7,11},{8,12},{9,13},{1... | collective-permute-start | bytes 344072 | tf_op jit(solution)/shard_map/ppermute | solution.py:25
  182.5 10.1 %copy-start.8 = (s32[6]{0:T(128)S(1)}, s32[6]{0:T(128)}, u32[]{:S(2)}) copy-start(s32[6]{0:T(128)} %refs_6_.3) | copy-start | bytes 76
  182.5 7.3 %collective-permute-start.38 = (bf16[448,128]{1,0:T(8,128)(2,1)S(1)}, bf16[448,128]{1,0:T(8,128)(2,1)S(1)}, u32[]{:S(2)}, u32[]{:S(2)}) collective-permute-start(bf16[448,128]{1,0:T(8,128)(2,1)S(1)} %shard_map.103.refs_0_), channel_id=1, source_target_pairs={{0,3},{1,0},{2,1},{3,2},{4,7},{5,4},{6,5},{7,6},{8,11},{9,8},{10,9... | collective-permute-start | bytes 344072 | tf_op jit(solution)/shard_map/ppermute | solution.py:25
  186.3 6.3 %collective-permute-start.37 = (bf16[448,128]{1,0:T(8,128)(2,1)S(1)}, bf16[448,128]{1,0:T(8,128)(2,1)S(1)}, u32[]{:S(2)}, u32[]{:S(2)}) collective-permute-start(bf16[448,128]{1,0:T(8,128)(2,1)S(1)} %shard_map.103.refs_0_), channel_id=1, source_target_pairs={{0,2},{1,3},{2,0},{3,1},{4,6},{5,7},{6,4},{7,5},{8,10},{9,11},{10,... | collective-permute-start | bytes 344072 | tf_op jit(solution)/shard_map/ppermute | solution.py:25
  186.4 6.2 %collective-permute-start.36 = (bf16[448,128]{1,0:T(8,128)(2,1)S(1)}, bf16[448,128]{1,0:T(8,128)(2,1)S(1)}, u32[]{:S(2)}, u32[]{:S(2)}) collective-permute-start(bf16[448,128]{1,0:T(8,128)(2,1)S(1)} %shard_map.103.refs_0_), channel_id=1, source_target_pairs={{0,1},{1,2},{2,3},{3,0},{4,5},{5,6},{6,7},{7,4},{8,9},{9,10},{10,1... | collective-permute-start | bytes 344072 | tf_op jit(solution)/shard_map/ppermute | solution.py:25
  193.7 5.4 %collective-permute-start.39 = (bf16[64,256]{1,0:T(8,128)(2,1)S(1)}, bf16[64,256]{1,0:T(8,128)(2,1)S(1)}, u32[]{:S(2)}, u32[]{:S(2)}) collective-permute-start(bf16[64,256]{1,0:T(8,128)(2,1)S(1)} %get-tuple-element.112), channel_id=1, source_target_pairs={{0,3},{1,0},{2,1},{3,2},{4,7},{5,4},{6,5},{7,6},{8,11},{9,8},{10,9... | collective-permute-start | bytes 98312 | tf_op jit(solution)/shard_map/ppermute | solution.py:25
  196.6 5.4 %collective-permute-start.40 = (bf16[64,256]{1,0:T(8,128)(2,1)S(1)}, bf16[64,256]{1,0:T(8,128)(2,1)S(1)}, u32[]{:S(2)}, u32[]{:S(2)}) collective-permute-start(bf16[64,256]{1,0:T(8,128)(2,1)S(1)} %get-tuple-element.113), channel_id=1, source_target_pairs={{0,2},{1,3},{2,0},{3,1},{4,6},{5,7},{6,4},{7,5},{8,10},{9,11},{10,... | collective-permute-start | bytes 98312 | tf_op jit(solution)/shard_map/ppermute | solution.py:25
  196.6 5.4 %collective-permute-start.41 = (bf16[64,256]{1,0:T(8,128)(2,1)S(1)}, bf16[64,256]{1,0:T(8,128)(2,1)S(1)}, u32[]{:S(2)}, u32[]{:S(2)}) collective-permute-start(bf16[64,256]{1,0:T(8,128)(2,1)S(1)} %get-tuple-element.114), channel_id=1, source_target_pairs={{0,1},{1,2},{2,3},{3,0},{4,5},{5,6},{6,7},{7,4},{8,9},{9,10},{10,1... | collective-permute-start | bytes 98312 | tf_op jit(solution)/shard_map/ppermute | solution.py:25
  (3 other events, 3.0 us)

commit v2 on v1

--- a/solution.py
+++ b/solution.py
@@ -118,8 +118,9 @@
     return run
 
 
-def pack_kernel(right_ref, low_ref, up_ref, *out_refs):
+def pack_kernel(right_ref, low_ref, up_ref, lower_ref, upper_ref, *out_refs):
     n = right_ref.shape[1]
+    half = lower_ref.shape[1]
     rank_cols = low_ref.shape[2]
     share = rank_cols // lax.axis_size("row")
     row = lax.axis_index("row")
@@ -128,13 +129,16 @@
     pick = (at == want).astype(F32).astype(BF16)
     for s, out_ref in enumerate(out_refs):
         tile = wrapped(own_tile() + s)
-        out_ref[:n] = right_ref[tile].astype(BF16)
+        out_ref[:half] = lower_ref[tile]
+        out_ref[half : 2 * half] = upper_ref[tile]
+        out_ref[2 * half : 2 * half + n] = right_ref[tile].astype(BF16)
         pieces = []
         for slot in range(SIDE - 1):
             pair, is_low = partner_pair(tile, slot)
-            piece = jnp.where(is_low, dot_t(pick, low_ref[pair]), dot_t(pick, up_ref[pair]))
-            pieces.append(piece)
-        out_ref[n:] = jnp.concatenate(pieces, axis=0).astype(BF16)
+            pieces.append(
+                dot_t(pick, jnp.where(is_low, low_ref[pair], up_ref[pair]))
+            )
+        out_ref[2 * half + n :] = jnp.concatenate(pieces, axis=0).astype(BF16)
 
 
 def partner_pair(tile, slot):
@@ -145,25 +149,17 @@
     return jnp.where(high == 1, 0, jnp.where(high == 2, 1, 3)) + low, is_low
 
 
-def order_kernel(sign, *refs):
+def order_kernel(sign, start, *refs):
     out_ref = refs[-1]
     for s in range(SIDE):
-        out_ref[wrapped(own_tile() - sign * s)] = refs[s][...].astype(out_ref.dtype)
+        out_ref[wrapped(own_tile() - sign * s)] = refs[s][start:].astype(out_ref.dtype)
 
 
 def stack_kernel(*refs):
-    half = refs[0].shape[0] // 2
+    half = refs[-1].shape[1] // SIDE
     for s, ref in enumerate(refs[:-1]):
         refs[-1][0, s * half : (s + 1) * half] = ref[:half]
-        refs[-1][1, s * half : (s + 1) * half] = ref[half:]
-
-
-def deal_kernel(lower_ref, upper_ref, *out_refs):
-    rows = lower_ref.shape[1]
-    for s in range(SIDE):
-        tile = wrapped(own_tile() + s)
-        out_refs[s][:rows] = lower_ref[tile]
-        out_refs[s][rows:] = upper_ref[tile]
+        refs[-1][1, s * half : (s + 1) * half] = ref[half : 2 * half]
 
 
 def turn_kernel(low_ref, up_ref, *out_refs):
@@ -181,7 +177,7 @@
 
 def products_kernel(n, padded, which, *refs):
     x_refs, inverse_refs = refs[:SIDE], refs[SIDE : 2 * SIDE]
-    out_refs = refs[2 * SIDE : -2]
+    out_refs, more_refs = refs[2 * SIDE : 3 * SIDE], refs[3 * SIDE : -2]
     joined_ref, extra_ref = refs[-2:]
     lower = [ref.at[0] for ref in inverse_refs]
     upper = [ref.at[len(which) - 1] for ref in inverse_refs]
@@ -214,11 +210,11 @@
         slot = lax.broadcasted_iota(jnp.int32, (rows - n, value.shape[1]), 0) // share
     for t in range(SIDE):
         start = t * padded
-        out_refs[t][:n] = value[start : start + n].astype(BF16)
+        out_refs[t][...] = value[start : start + n].astype(BF16)
         if rows > n:
             mine = value[start + n : start + rows]
             its = other[t * (padded - n) : t * (padded - n) + rows - n]
-            out_refs[t][n:] = jnp.where(slot < own_tile(), mine, its).astype(BF16)
+            more_refs[t][...] = jnp.where(slot < own_tile(), mine, its).astype(BF16)
 
 
 def products(n, gathered, which, inverses):
@@ -227,14 +223,15 @@
     padded = rows + -rows % 16
     count = len(which)
     whole = pl.BlockSpec(gathered[0].shape, lambda a: (0, 0, 0))
+    heights = [n] * SIDE + [rows - n] * SIDE * (rows > n)
     return kernel_call(
         lambda *refs: products_kernel(n, padded, which, *refs),
-        [jax.ShapeDtypeStruct((rows, total), BF16)] * SIDE,
+        [jax.ShapeDtypeStruct((height, total), BF16) for height in heights],
         flops=2 * SIDE * blocks * rows * width * total,
         grid=(total // 256,),
         in_specs=[whole] * SIDE
         + [pl.BlockSpec((count, 256, width), lambda a: (which[-1] // count, a, 0))] * SIDE,
-        out_specs=[pl.BlockSpec((rows, 256), lambda a: (0, a))] * SIDE,
+        out_specs=[pl.BlockSpec((height, 256), lambda a: (0, a)) for height in heights],
         scratch=[
             pltpu.VMEM((blocks, SIDE, padded, width), BF16),
             pltpu.VMEM((blocks, SIDE, max(padded - n, 16), width), BF16),
@@ -249,13 +246,10 @@
     return whole
 
 
-def total_kernel(n, *refs):
-    dense_ref, extra_ref = refs[SIDE:]
-    whole = summed(refs[:SIDE])
-    dense_ref[...] = whole[:n]
-    extra = whole[n:].astype(BF16)
-    for at in range(extra_ref.shape[0]):
-        extra_ref[at] = extra
+def total_kernel(*refs):
+    extra = summed(refs[:SIDE]).astype(BF16)
+    for at in range(refs[-1].shape[0]):
+        refs[-1][at] = extra
 
 
 def project(dense, turned, slot, rank_cols):
@@ -269,10 +263,12 @@
     )
 
 
-def couple_kernel(dense_ref, mine_ref, other_ref, *refs):
-    turned, (extra_ref, send_ref, later_ref) = refs[:SIDE], refs[SIDE:]
+def couple_kernel(mine_ref, other_ref, *refs):
+    turned, parts = refs[:SIDE], refs[SIDE : 2 * SIDE]
+    dense_ref, extra_ref, send_ref, later_ref = refs[2 * SIDE :]
+    dense_ref[...] = summed(parts)
     slots = SIDE - 1
-    rank_cols = turned[0].shape[0] // slots
+    rank_cols = extra_ref.shape[0] // slots
     width = turned[0].shape[1]
     share = mine_ref.shape[1] // slots
     even = lax.rem(lax.axis_index("row"), 2) == 0
@@ -312,7 +308,7 @@
 def last_project_kernel(*refs):
     turned, (later_ref, dense_ref, send_ref) = refs[SIDE : 2 * SIDE], refs[2 * SIDE :]
     slots = SIDE - 1
-    rank_cols = turned[0].shape[0] // slots
+    rank_cols = later_ref.shape[0] // 2
     whole = summed(refs[:SIDE])
     dense_ref[...] = whole
     dense = whole.astype(BF16)
@@ -392,48 +388,46 @@
     total = SIDE * width
     shape = jax.ShapeDtypeStruct
 
-    height = n + slots * share
-    rows = kernel_call(pack_kernel, [shape((height, width), BF16)] * SIDE)(
-        right_sides, low_left, up_left
-    )
+    more = slots * share
+    height = n + more
+    packed = slots * n + 2 * rank_cols
     tied = lax.optimization_barrier
-    rows = scattered_x(rows)
+    parts = scattered_x(
+        kernel_call(pack_kernel, [shape((2 * width + height, width), BF16)] * SIDE)(
+            right_sides, low_left, up_left, inv_lower, inv_upper
+        )
+    )
     rows = kernel_call(
-        lambda *refs: order_kernel(1, *refs), shape((SIDE, height, width), BF16)
-    )(*rows)
-    rows, inv_lower, inv_upper = tied((rows, inv_lower, inv_upper))
-    parts = scattered_x(
-        kernel_call(deal_kernel, [shape((2 * width, width), BF16)] * SIDE)(
-            inv_lower, inv_upper
-        )
-    )
-    parts, rows = tied((parts, swapped(rows)))
+        lambda *refs: order_kernel(1, 2 * width, *refs),
+        shape((SIDE, height, width), BF16),
+    )(*parts)
     inverse = kernel_call(stack_kernel, shape((2, total, width), BF16))(*parts)
-    far = swap_pair(inverse)
-    near, gathered = tied((swap_core(inverse), gathered_y(rows)))
-    gathered, low_right, up_right = tied((gathered, low_right, up_right))
+    inverse, rows = tied((inverse, rows))
+    far, near = swap_pair(inverse), swap_core(inverse)
+    near, low_right, up_right = tied((near, low_right, up_right))
     turned = scattered_x(
         kernel_call(turn_kernel, [shape((slots * rank_cols, width), BF16)] * SIDE)(
             low_right, up_right
         )
     )
-    turned, far = tied((turned, far))
+    turned, rows = tied((turned, swapped(rows)))
     inverses = [inverse, near, far, swap_core(far)]
-    received = scattered_q(products(n, gathered, (0, 1), inverses))
-    dense, extra = kernel_call(
-        lambda *refs: total_kernel(n, *refs),
-        (shape((n, total), F32), shape((8, slots * share, total), BF16)),
-    )(*received)
-    mine = from_every_z(extra)
-    packed = slots * n + 2 * rank_cols
-    extra, send, later = kernel_call(
+    partial = products(n, gathered_y(rows), (0, 1), inverses)
+    dense, extra = tied((partial[:SIDE], scattered_q(partial[SIDE:])))
+    dense = scattered_q(dense)
+    mine = from_every_z(
+        kernel_call(total_kernel, shape((8, more, total), BF16))(*extra)
+    )
+    mine, dense = tied((mine, dense))
+    dense, extra, send, later = kernel_call(
         couple_kernel,
         (
+            shape((n, total), F32),
             shape((slots * rank_cols, total), BF16),
             shape((packed, rank_cols), BF16),
             shape((2 * rank_cols, rank_cols), BF16),
         ),
-    )(dense, mine, swap_core(mine), *turned)
+    )(mine, swap_core(mine), *turned, *dense)
 
     def finished(is_lower, send, dense, ranks):
         sums = kernel_call(add_kernel, shape((packed, rank_cols), BF16))(*gathered_y(send))
@@ -453,7 +447,7 @@
     )(*scattered_q(parts), *turned, later)
     rows = finished(False, send, dense, up_ranks)
     return kernel_call(
-        lambda *refs: order_kernel(-1, *refs), shape((SIDE, n, width), F32)
+        lambda *refs: order_kernel(-1, 0, *refs), shape((SIDE, n, width), F32)
     )(*scattered_x(rows, -1))
 
 

time: 203 us -> 239 us (1.18)
  waiting for transfers between devices: 92.2 us -> 118 us
  blocking collectives: 19.5 us -> 0 us
  local copies, waits for them, and re-layouts: 3.05 us -> 20.3 us
  starting transfers between devices: 78.2 us -> 90.7 us
    ppermute x42, waiting for transfers between devices: 92.2 us -> 118 us  [permuted(): return lax.ppermute(value, ('row', 'col'), routes(to))]
    all_to_all x1 -> x0, blocking collectives: 19.5 us -> none  [from_every_z(): lax.all_to_all(value, 'row', 0, 0, tiled=True, axis_index_groups=Z_GROUPS)]
    unnamed x18 -> x70, local copies, waits for them, and re-layouts: 3.05 us -> 20.3 us
    ppermute x42, starting transfers between devices: 78.2 us -> 85.9 us  [permuted(): return lax.ppermute(value, ('row', 'col'), routes(to))]
    all_to_all x0 -> x1, starting transfers between devices: none -> 4.85 us  [from_every_z(): lax.all_to_all(value, 'row', 0, 0, tiled=True, axis_index_groups=Z_GROUPS)]
    pallas_call x15 -> x14, Pallas kernels: 9.52 us -> 9.3 us  [run(): pl.pallas_call(body, out_shape=out_shape, in_specs=specs, scratch_shapes=...]
  transfers between devices with their start and end apart: 42 -> 43, of which waited for: 33 -> 33; matrix products, arithmetic and copies ran while one was open for 0% -> 0% of each run, Pallas kernels for 0% -> 0%
where the time goes in v2:
time: 239 us; the launch traced here: 238 us
  waiting for transfers between devices  118 us (49%)
  starting transfers between devices  90.7 us (38%)
  local copies, waits for them, and re-layouts  20.3 us (8%)
  Pallas kernels  9.3 us (4%)
    ppermute x42, waiting for transfers between devices, permuted(): return lax.ppermute(value, ('row', 'col'), routes(to))  118 us
    ppermute x42, starting transfers between devices, permuted(): return lax.ppermute(value, ('row', 'col'), routes(to))  85.9 us
    unnamed x70, local copies, waits for them, and re-layouts  20.3 us
    pallas_call x14, Pallas kernels, run(): pl.pallas_call(body, out_shape=out_shape, in_specs=specs, scratch_shapes=...  9.3 us
    all_to_all x1, starting transfers between devices, from_every_z(): lax.all_to_all(value, 'row', 0, 0, tiled=True, axis_index_groups=Z_GROUPS)  4.85 us
  transfers between devices with their start and end apart: 43, of which 33 were waited for; matrix products, arithmetic and copies ran while one was open for 0% of the time, Pallas kernels for 0%

profile of v2, /device:TPU:2, one launch (start us, length us, event | category | flops | bytes accessed | tf_op | source)
XLA Modules:
  0.0 238.2 jit_solution(16745264509288103885)
XLA Ops:
  5.4 1.5 collective-permute-start
  6.9 2.8 %collective-permute-start.1 = (bf16[600,256]{1,0:T(8,128)(2,1)S(1)}, bf16[600,256]{1,0:T(8,128)(2,1)S(1)}, u32[]{:S(2)}, u32[]{:S(2)}) collective-permute-start(bf16[600,256]{1,0:T(8,128)(2,1)S(1)} %get-tuple-element.60), channel_id=1, source_target_pairs={{0,2},{1,3},{2,0},{3,1},{4,6},{5,7},{6,4},{7,5},{8,10},{9,11},{10,... | collective-permute-start | bytes 921608 | tf_op jit(solution)/shard_map/ppermute | solution.py:25
  10.2 5.7 %collective-permute-done.refs_1_ = bf16[600,256]{1,0:T(8,128)(2,1)S(1)} collective-permute-done((bf16[600,256]{1,0:T(8,128)(2,1)S(1)}, bf16[600,256]{1,0:T(8,128)(2,1)S(1)}, u32[]{:S(2)}, u32[]{:S(2)}) %collective-permute-start) | collective-permute-done | bytes 307232 | tf_op jit(solution)/shard_map/ppermute | solution.py:25
  15.9 2.8 %collective-permute-done.1.refs_2_ = bf16[600,256]{1,0:T(8,128)(2,1)S(1)} collective-permute-done((bf16[600,256]{1,0:T(8,128)(2,1)S(1)}, bf16[600,256]{1,0:T(8,128)(2,1)S(1)}, u32[]{:S(2)}, u32[]{:S(2)}) %collective-permute-start.1) | collective-permute-done | bytes 307232 | tf_op jit(solution)/shard_map/ppermute | solution.py:25
  18.6 4.3 %collective-permute-done.2.refs_3_ = bf16[600,256]{1,0:T(8,128)(2,1)S(1)} collective-permute-done((bf16[600,256]{1,0:T(8,128)(2,1)S(1)}, bf16[600,256]{1,0:T(8,128)(2,1)S(1)}, u32[]{:S(2)}, u32[]{:S(2)}) %collective-permute-start.2) | collective-permute-done | bytes 307232 | tf_op jit(solution)/shard_map/ppermute | solution.py:25
  23.1 2.1 collective-permute-start.11
  25.2 22.6 %collective-permute-done.11.refs_6_ = bf16[2,1024,256]{2,1,0:T(8,128)(2,1)S(1)} collective-permute-done((bf16[2,1024,256]{2,1,0:T(8,128)(2,1)S(1)}, bf16[2,1024,256]{2,1,0:T(8,128)(2,1)S(1)}, u32[]{:S(2)}, u32[]{:S(2)}) %collective-permute-start.11) | collective-permute-done | bytes 1048608 | tf_op jit(solution)/shard_map/ppermute | solution.py:25
  49.6 1.8 collective-permute-start.5
  51.4 2.6 %collective-permute-start.6 = (bf16[384,256]{1,0:T(8,128)(2,1)S(1)}, bf16[384,256]{1,0:T(8,128)(2,1)S(1)}, u32[]{:S(2)}, u32[]{:S(2)}) collective-permute-start(bf16[384,256]{1,0:T(8,128)(2,1)S(1)} %get-tuple-element.68), channel_id=1, source_target_pairs={{0,3},{1,0},{2,1},{3,2},{4,7},{5,4},{6,5},{7,6},{8,11},{9,8},{10,9... | collective-permute-start | bytes 589832 | tf_op jit(solution)/shard_map/ppermute | solution.py:25
  54.7 1.9 collective-permute-done.4.refs_1_.refs_5_
  57.3 1.6 collective-permute-done.5.refs_2_.refs_6_
  59.6 2.8 %collective-permute-done.6.refs_3_.refs_7_ = bf16[384,256]{1,0:T(8,128)(2,1)S(1)} collective-permute-done((bf16[384,256]{1,0:T(8,128)(2,1)S(1)}, bf16[384,256]{1,0:T(8,128)(2,1)S(1)}, u32[]{:S(2)}, u32[]{:S(2)}) %collective-permute-start.6) | collective-permute-done | bytes 196640 | tf_op jit(solution)/shard_map/ppermute | solution.py:25
  63.0 15.1 %collective-permute-start.10 = (bf16[4,88,256]{2,1,0:T(8,128)(2,1)S(1)}, bf16[4,88,256]{2,1,0:T(8,128)(2,1)S(1)}, u32[]{:S(2)}, u32[]{:S(2)}) collective-permute-start(bf16[4,88,256]{2,1,0:T(8,128)(2,1)S(1)} %collective-permute-done.7.refs_0_), channel_id=1, source_target_pairs={{0,12},{1,13},{2,14},{3,15},{4,0},{5,1},{6,2},{7,3},{8,4},{9,5},{1... | collective-permute-start | bytes 540680 | tf_op jit(solution)/shard_map/ppermute | solution.py:25
  79.0 6.5 %collective-permute-done.10.refs_3_ = bf16[4,88,256]{2,1,0:T(8,128)(2,1)S(1)} collective-permute-done((bf16[4,88,256]{2,1,0:T(8,128)(2,1)S(1)}, bf16[4,88,256]{2,1,0:T(8,128)(2,1)S(1)}, u32[]{:S(2)}, u32[]{:S(2)}) %collective-permute-start.10) | collective-permute-done | bytes 180256 | tf_op jit(solution)/shard_map/ppermute | solution.py:25
  85.5 1.6 collective-permute-done.9.refs_2_
  87.1 1.8 collective-permute-done.8.refs_1_
  88.9 2.8 %shard_map.95 = (bf16[64,1024]{1,0:T(8,128)(2,1)S(1)}, bf16[64,1024]{1,0:T(8,128)(2,1)S(1)}, bf16[64,1024]{1,0:T(8,128)(2,1)S(1)}, bf16[64,1024]{1,0:T(8,128)(2,...) custom-call(bf16[4,88,256]{2,1,0:T(8,128)(2,1)S(1)} %collective-perm, ...), custom_call_target="tpu_custom_call" | custom-call | flops 738197504 | bytes 5636096 | tf_op jit(solution)/shard_map/pallas_call | solution.py:106
  94.5 6.8 %collective-permute-start.14 = (bf16[24,1024]{1,0:T(8,128)(2,1)S(1)}, bf16[24,1024]{1,0:T(8,128)(2,1)S(1)}, u32[]{:S(2)}, u32[]{:S(2)}) collective-permute-start(bf16[24,1024]{1,0:T(8,128)(2,1)S(1)} %get-tuple-element.78), channel_id=1, source_target_pairs={{0,128},{1,129},{2,130},{3,131},{4,132},{5,133},{6,134},{7,135},{8... | collective-permute-start | bytes 147464 | tf_op jit(solution)/shard_map/ppermute | solution.py:25
  101.3 2.7 %collective-permute-start.15 = (bf16[24,1024]{1,0:T(8,128)(2,1)S(1)}, bf16[24,1024]{1,0:T(8,128)(2,1)S(1)}, u32[]{:S(2)}, u32[]{:S(2)}) collective-permute-start(bf16[24,1024]{1,0:T(8,128)(2,1)S(1)} %get-tuple-element.79), channel_id=1, source_target_pairs={{0,192},{1,193},{2,194},{3,195},{4,196},{5,197},{6,198},{7,199},{8... | collective-permute-start | bytes 147464 | tf_op jit(solution)/shard_map/ppermute | solution.py:25
  104.8 2.3 collective-permute-done.15.refs_3_
  107.9 4.8 %all-to-all-start = ((bf16[8,24,1024]{2,1,0:T(8,128)(2,1)}), bf16[8,24,1024]{2,1,0:T(8,128)(2,1)S(1)}, u32[]{:S(2)}, u32[]{:S(2)}) async-start(bf16[8,24,1024]{2,1,0:T(8,128)(2,1)} %copy-done.2), calls=%async_computation | async-start | bytes 786432 | tf_op jit(solution)/shard_map/all_to_all | solution.py:55
  112.7 2.9 %collective-permute-start.16 = (bf16[64,1024]{1,0:T(8,128)(2,1)}, bf16[64,1024]{1,0:T(8,128)(2,1)S(1)}, u32[]{:S(2)}, u32[]{:S(2)}) collective-permute-start(bf16[64,1024]{1,0:T(8,128)(2,1)} %copy-done.34), channel_id=1, source_target_pairs={{0,64},{1,65},{2,66},{3,67},{4,68},{5,69},{6,70},{7,71},{8,72},{9,... | collective-permute-start | bytes 393224 | tf_op jit(solution)/shard_map/ppermute | solution.py:25
  115.7 3.6 %collective-permute-start.17 = (bf16[64,1024]{1,0:T(8,128)(2,1)}, bf16[64,1024]{1,0:T(8,128)(2,1)S(1)}, u32[]{:S(2)}, u32[]{:S(2)}) collective-permute-start(bf16[64,1024]{1,0:T(8,128)(2,1)} %copy-done.33), channel_id=1, source_target_pairs={{0,128},{1,129},{2,130},{3,131},{4,132},{5,133},{6,134},{7,135},{8... | collective-permute-start | bytes 393224 | tf_op jit(solution)/shard_map/ppermute | solution.py:25
  119.2 3.6 %collective-permute-start.18 = (bf16[64,1024]{1,0:T(8,128)(2,1)}, bf16[64,1024]{1,0:T(8,128)(2,1)S(1)}, u32[]{:S(2)}, u32[]{:S(2)}) collective-permute-start(bf16[64,1024]{1,0:T(8,128)(2,1)} %copy-done.32), channel_id=1, source_target_pairs={{0,192},{1,193},{2,194},{3,195},{4,196},{5,197},{6,198},{7,199},{8... | collective-permute-start | bytes 393224 | tf_op jit(solution)/shard_map/ppermute | solution.py:25
  122.8 9.8 %collective-permute-done.16.refs_5_ = bf16[64,1024]{1,0:T(8,128)(2,1)S(1)} collective-permute-done((bf16[64,1024]{1,0:T(8,128)(2,1)}, bf16[64,1024]{1,0:T(8,128)(2,1)S(1)}, u32[]{:S(2)}, u32[]{:S(2)}) %collective-permute-start.16) | collective-permute-done | bytes 131104 | tf_op jit(solution)/shard_map/ppermute | solution.py:25
  133.3 2.2 collective-permute-done.17.refs_6_
  136.7 1.7 collective-permute-done.19.other_ref
  148.7 4.0 %collective-permute-done.22.refs_3_ = bf16[448,128]{1,0:T(8,128)(2,1)S(1)} collective-permute-done((bf16[448,128]{1,0:T(8,128)(2,1)S(1)}, bf16[448,128]{1,0:T(8,128)(2,1)S(1)}, u32[]{:S(2)}, u32[]{:S(2)}) %collective-permute-start.22) | collective-permute-done | bytes 114720 | tf_op jit(solution)/shard_map/ppermute | solution.py:25
  153.9 2.0 collective-permute-done.20.refs_1_
  158.5 5.1 %collective-permute-done.25.refs_3_ = bf16[448,128]{1,0:T(8,128)(2,1)S(1)} collective-permute-done((bf16[448,128]{1,0:T(8,128)(2,1)S(1)}, bf16[448,128]{1,0:T(8,128)(2,1)S(1)}, u32[]{:S(2)}, u32[]{:S(2)}) %collective-permute-start.25) | collective-permute-done | bytes 114720 | tf_op jit(solution)/shard_map/ppermute | solution.py:25
  163.6 1.8 collective-permute-done.23.refs_1_
  167.2 12.9 %collective-permute-start.29 = (bf16[4,64,256]{2,1,0:T(8,128)(2,1)S(1)}, bf16[4,64,256]{2,1,0:T(8,128)(2,1)S(1)}, u32[]{:S(2)}, u32[]{:S(2)}) collective-permute-start(bf16[4,64,256]{2,1,0:T(8,128)(2,1)S(1)} %collective-permute-done.26.refs_0_), channel_id=1, source_target_pairs={{0,12},{1,13},{2,14},{3,15},{4,0},{5,1},{6,2},{7,3},{8,4},{9,5},{1... | collective-permute-start | bytes 393224 | tf_op jit(solution)/shard_map/ppermute | solution.py:25
  180.1 1.6 collective-permute-start.28
  181.8 2.2 collective-permute-done.29.refs_3_
  184.0 2.6 %collective-permute-done.28.refs_2_ = bf16[4,64,256]{2,1,0:T(8,128)(2,1)S(1)} collective-permute-done((bf16[4,64,256]{2,1,0:T(8,128)(2,1)S(1)}, bf16[4,64,256]{2,1,0:T(8,128)(2,1)S(1)}, u32[]{:S(2)}, u32[]{:S(2)}) %collective-permute-start.28) | collective-permute-done | bytes 131104 | tf_op jit(solution)/shard_map/ppermute | solution.py:25
  189.5 2.4 %collective-permute-start.30 = (bf16[64,1024]{1,0:T(8,128)(2,1)S(1)}, bf16[64,1024]{1,0:T(8,128)(2,1)S(1)}, u32[]{:S(2)}, u32[]{:S(2)}) collective-permute-start(bf16[64,1024]{1,0:T(8,128)(2,1)S(1)} %get-tuple-element.101), channel_id=1, source_target_pairs={{0,64},{1,65},{2,66},{3,67},{4,68},{5,69},{6,70},{7,71},{8,72},{9,... | collective-permute-start | bytes 393224 | tf_op jit(solution)/shard_map/ppermute | solution.py:25
  192.0 3.6 %collective-permute-start.31 = (bf16[64,1024]{1,0:T(8,128)(2,1)S(1)}, bf16[64,1024]{1,0:T(8,128)(2,1)S(1)}, u32[]{:S(2)}, u32[]{:S(2)}) collective-permute-start(bf16[64,1024]{1,0:T(8,128)(2,1)S(1)} %get-tuple-element.102), channel_id=1, source_target_pairs={{0,128},{1,129},{2,130},{3,131},{4,132},{5,133},{6,134},{7,135},{8... | collective-permute-start | bytes 393224 | tf_op jit(solution)/shard_map/ppermute | solution.py:25
  195.6 2.7 %collective-permute-done.30.refs_1_ = bf16[64,1024]{1,0:T(8,128)(2,1)S(1)} collective-permute-done((bf16[64,1024]{1,0:T(8,128)(2,1)S(1)}, bf16[64,1024]{1,0:T(8,128)(2,1)S(1)}, u32[]{:S(2)}, u32[]{:S(2)}) %collective-permute-start.30) | collective-permute-done | bytes 131104 | tf_op jit(solution)/shard_map/ppermute | solution.py:25
  198.4 7.6 %collective-permute-done.31.refs_2_ = bf16[64,1024]{1,0:T(8,128)(2,1)S(1)} collective-permute-done((bf16[64,1024]{1,0:T(8,128)(2,1)S(1)}, bf16[64,1024]{1,0:T(8,128)(2,1)S(1)}, u32[]{:S(2)}, u32[]{:S(2)}) %collective-permute-start.31) | collective-permute-done | bytes 131104 | tf_op jit(solution)/shard_map/ppermute | solution.py:25
  205.9 3.3 %collective-permute-done.32.refs_3_ = bf16[64,1024]{1,0:T(8,128)(2,1)S(1)} collective-permute-done((bf16[64,1024]{1,0:T(8,128)(2,1)S(1)}, bf16[64,1024]{1,0:T(8,128)(2,1)S(1)}, u32[]{:S(2)}, u32[]{:S(2)}) %collective-permute-start.32) | collective-permute-done | bytes 131104 | tf_op jit(solution)/shard_map/ppermute | solution.py:25
  212.0 4.0 %collective-permute-done.35.refs_3_ = bf16[448,128]{1,0:T(8,128)(2,1)S(1)} collective-permute-done((bf16[448,128]{1,0:T(8,128)(2,1)S(1)}, bf16[448,128]{1,0:T(8,128)(2,1)S(1)}, u32[]{:S(2)}, u32[]{:S(2)}) %collective-permute-start.35) | collective-permute-done | bytes 114720 | tf_op jit(solution)/shard_map/ppermute | solution.py:25
  217.4 1.7 collective-permute-done.33.refs_1_
  221.1 2.5 %collective-permute-start.36 = (bf16[448,128]{1,0:T(8,128)(2,1)S(1)}, bf16[448,128]{1,0:T(8,128)(2,1)S(1)}, u32[]{:S(2)}, u32[]{:S(2)}) collective-permute-start(bf16[448,128]{1,0:T(8,128)(2,1)S(1)} %shard_map.102.refs_0_), channel_id=1, source_target_pairs={{0,1},{1,2},{2,3},{3,0},{4,5},{5,6},{6,7},{7,4},{8,9},{9,10},{10,1... | collective-permute-start | bytes 344072 | tf_op jit(solution)/shard_map/ppermute | solution.py:25
  224.7 2.1 collective-permute-done.37.refs_2_
  226.7 1.7 collective-permute-done.36.refs_1_
  229.5 2.5 %collective-permute-start.39 = (bf16[64,256]{1,0:T(8,128)(2,1)S(1)}, bf16[64,256]{1,0:T(8,128)(2,1)S(1)}, u32[]{:S(2)}, u32[]{:S(2)}) collective-permute-start(bf16[64,256]{1,0:T(8,128)(2,1)S(1)} %get-tuple-element.108), channel_id=1, source_target_pairs={{0,3},{1,0},{2,1},{3,2},{4,7},{5,4},{6,5},{7,6},{8,11},{9,8},{10,9... | collective-permute-start | bytes 98312 | tf_op jit(solution)/shard_map/ppermute | solution.py:25
  232.5 1.6 collective-permute-start.41
  234.1 3.4 %collective-permute-done.40.refs_2_ = bf16[64,256]{1,0:T(8,128)(2,1)S(1)} collective-permute-done((bf16[64,256]{1,0:T(8,128)(2,1)S(1)}, bf16[64,256]{1,0:T(8,128)(2,1)S(1)}, u32[]{:S(2)}, u32[]{:S(2)}) %collective-permute-start.40) | collective-permute-done | bytes 32800 | tf_op jit(solution)/shard_map/ppermute | solution.py:25
  (122 shorter events, 45.9 us)
Async XLA Ops:
  5.4 10.5 %collective-permute-start = (bf16[600,256]{1,0:T(8,128)(2,1)S(1)}, bf16[600,256]{1,0:T(8,128)(2,1)S(1)}, u32[]{:S(2)}, u32[]{:S(2)}) collective-permute-start(bf16[600,256]{1,0:T(8,128)(2,1)S(1)} %get-tuple-element.59), channel_id=1, source_target_pairs={{0,1},{1,2},{2,3},{3,0},{4,5},{5,6},{6,7},{7,4},{8,9},{9,10},{10,1... | collective-permute-start | bytes 921608 | tf_op jit(solution)/shard_map/ppermute | solution.py:25
  6.9 11.7 %collective-permute-start.1 = (bf16[600,256]{1,0:T(8,128)(2,1)S(1)}, bf16[600,256]{1,0:T(8,128)(2,1)S(1)}, u32[]{:S(2)}, u32[]{:S(2)}) collective-permute-start(bf16[600,256]{1,0:T(8,128)(2,1)S(1)} %get-tuple-element.60), channel_id=1, source_target_pairs={{0,2},{1,3},{2,0},{3,1},{4,6},{5,7},{6,4},{7,5},{8,10},{9,11},{10,... | collective-permute-start | bytes 921608 | tf_op jit(solution)/shard_map/ppermute | solution.py:25
  9.8 13.2 %collective-permute-start.2 = (bf16[600,256]{1,0:T(8,128)(2,1)S(1)}, bf16[600,256]{1,0:T(8,128)(2,1)S(1)}, u32[]{:S(2)}, u32[]{:S(2)}) collective-permute-start(bf16[600,256]{1,0:T(8,128)(2,1)S(1)} %get-tuple-element.61), channel_id=1, source_target_pairs={{0,3},{1,0},{2,1},{3,2},{4,7},{5,4},{6,5},{7,6},{8,11},{9,8},{10,9... | collective-permute-start | bytes 921608 | tf_op jit(solution)/shard_map/ppermute | solution.py:25
  23.1 24.7 %collective-permute-start.11 = (bf16[2,1024,256]{2,1,0:T(8,128)(2,1)S(1)}, bf16[2,1024,256]{2,1,0:T(8,128)(2,1)S(1)}, u32[]{:S(2)}, u32[]{:S(2)}) collective-permute-start(bf16[2,1024,256]{2,1,0:T(8,128)(2,1)S(1)} %shard_map.92.refs_4_), channel_id=1, source_target_pairs={{0,32},{1,33},{2,34},{3,35},{4,36},{5,37},{6,38},{7,39},{8,40},{9,... | collective-permute-start | bytes 3145736 | tf_op jit(solution)/shard_map/ppermute | solution.py:25
  25.2 22.6 %collective-permute-start.3 = (bf16[2,1024,256]{2,1,0:T(8,128)(2,1)S(1)}, bf16[2,1024,256]{2,1,0:T(8,128)(2,1)S(1)}, u32[]{:S(2)}, u32[]{:S(2)}) collective-permute-start(bf16[2,1024,256]{2,1,0:T(8,128)(2,1)S(1)} %shard_map.92.refs_4_), channel_id=1, source_target_pairs={{0,16},{1,17},{2,18},{3,19},{4,20},{5,21},{6,22},{7,23},{8,24},{9,... | collective-permute-start | bytes 3145736 | tf_op jit(solution)/shard_map/ppermute | solution.py:25
  47.8 41.1 %collective-permute-start.12 = (bf16[2,1024,256]{2,1,0:T(8,128)(2,1)S(1)}, bf16[2,1024,256]{2,1,0:T(8,128)(2,1)S(1)}, u32[]{:S(2)}, u32[]{:S(2)}) collective-permute-start(bf16[2,1024,256]{2,1,0:T(8,128)(2,1)S(1)} %collective-permute-done.11.refs_6_), channel_id=1, source_target_pairs={{0,16},{1,17},{2,18},{3,19},{4,20},{5,21},{6,22},{7,23},{8,24},{9,... | collective-permute-start | bytes 3145736 | tf_op jit(solution)/shard_map/ppermute | solution.py:25
  48.9 7.7 %collective-permute-start.4 = (bf16[384,256]{1,0:T(8,128)(2,1)S(1)}, bf16[384,256]{1,0:T(8,128)(2,1)S(1)}, u32[]{:S(2)}, u32[]{:S(2)}) collective-permute-start(bf16[384,256]{1,0:T(8,128)(2,1)S(1)} %get-tuple-element.66), channel_id=1, source_target_pairs={{0,1},{1,2},{2,3},{3,0},{4,5},{5,6},{6,7},{7,4},{8,9},{9,10},{10,1... | collective-permute-start | bytes 589832 | tf_op jit(solution)/shard_map/ppermute | solution.py:25
  49.6 9.3 %collective-permute-start.5 = (bf16[384,256]{1,0:T(8,128)(2,1)S(1)}, bf16[384,256]{1,0:T(8,128)(2,1)S(1)}, u32[]{:S(2)}, u32[]{:S(2)}) collective-permute-start(bf16[384,256]{1,0:T(8,128)(2,1)S(1)} %get-tuple-element.67), channel_id=1, source_target_pairs={{0,2},{1,3},{2,0},{3,1},{4,6},{5,7},{6,4},{7,5},{8,10},{9,11},{10,... | collective-permute-start | bytes 589832 | tf_op jit(solution)/shard_map/ppermute | solution.py:25
  51.4 10.9 %collective-permute-start.6 = (bf16[384,256]{1,0:T(8,128)(2,1)S(1)}, bf16[384,256]{1,0:T(8,128)(2,1)S(1)}, u32[]{:S(2)}, u32[]{:S(2)}) collective-permute-start(bf16[384,256]{1,0:T(8,128)(2,1)S(1)} %get-tuple-element.68), channel_id=1, source_target_pairs={{0,3},{1,0},{2,1},{3,2},{4,7},{5,4},{6,5},{7,6},{8,11},{9,8},{10,9... | collective-permute-start | bytes 589832 | tf_op jit(solution)/shard_map/ppermute | solution.py:25
  54.1 0.7 collective-permute-start.7
  63.0 22.5 %collective-permute-start.10 = (bf16[4,88,256]{2,1,0:T(8,128)(2,1)S(1)}, bf16[4,88,256]{2,1,0:T(8,128)(2,1)S(1)}, u32[]{:S(2)}, u32[]{:S(2)}) collective-permute-start(bf16[4,88,256]{2,1,0:T(8,128)(2,1)S(1)} %collective-permute-done.7.refs_0_), channel_id=1, source_target_pairs={{0,12},{1,13},{2,14},{3,15},{4,0},{5,1},{6,2},{7,3},{8,4},{9,5},{1... | collective-permute-start | bytes 540680 | tf_op jit(solution)/shard_map/ppermute | solution.py:25
  78.1 9.0 %collective-permute-start.9 = (bf16[4,88,256]{2,1,0:T(8,128)(2,1)S(1)}, bf16[4,88,256]{2,1,0:T(8,128)(2,1)S(1)}, u32[]{:S(2)}, u32[]{:S(2)}) collective-permute-start(bf16[4,88,256]{2,1,0:T(8,128)(2,1)S(1)} %collective-permute-done.7.refs_0_), channel_id=1, source_target_pairs={{0,8},{1,9},{2,10},{3,11},{4,12},{5,13},{6,14},{7,15},{8,0},{9,1},... | collective-permute-start | bytes 540680 | tf_op jit(solution)/shard_map/ppermute | solution.py:25
  78.1 10.8 %collective-permute-start.8 = (bf16[4,88,256]{2,1,0:T(8,128)(2,1)S(1)}, bf16[4,88,256]{2,1,0:T(8,128)(2,1)S(1)}, u32[]{:S(2)}, u32[]{:S(2)}) collective-permute-start(bf16[4,88,256]{2,1,0:T(8,128)(2,1)S(1)} %collective-permute-done.7.refs_0_), channel_id=1, source_target_pairs={{0,4},{1,5},{2,6},{3,7},{4,8},{5,9},{6,10},{7,11},{8,12},{9,13},{1... | collective-permute-start | bytes 540680 | tf_op jit(solution)/shard_map/ppermute | solution.py:25
  94.4 9.7 %collective-permute-start.13 = (bf16[24,1024]{1,0:T(8,128)(2,1)S(1)}, bf16[24,1024]{1,0:T(8,128)(2,1)S(1)}, u32[]{:S(2)}, u32[]{:S(2)}) collective-permute-start(bf16[24,1024]{1,0:T(8,128)(2,1)S(1)} %get-tuple-element.77), channel_id=1, source_target_pairs={{0,64},{1,65},{2,66},{3,67},{4,68},{5,69},{6,70},{7,71},{8,72},{9,... | collective-permute-start | bytes 147464 | tf_op jit(solution)/shard_map/ppermute | solution.py:25
  94.5 10.3 %collective-permute-start.14 = (bf16[24,1024]{1,0:T(8,128)(2,1)S(1)}, bf16[24,1024]{1,0:T(8,128)(2,1)S(1)}, u32[]{:S(2)}, u32[]{:S(2)}) collective-permute-start(bf16[24,1024]{1,0:T(8,128)(2,1)S(1)} %get-tuple-element.78), channel_id=1, source_target_pairs={{0,128},{1,129},{2,130},{3,131},{4,132},{5,133},{6,134},{7,135},{8... | collective-permute-start | bytes 147464 | tf_op jit(solution)/shard_map/ppermute | solution.py:25
  101.3 5.8 %collective-permute-start.15 = (bf16[24,1024]{1,0:T(8,128)(2,1)S(1)}, bf16[24,1024]{1,0:T(8,128)(2,1)S(1)}, u32[]{:S(2)}, u32[]{:S(2)}) collective-permute-start(bf16[24,1024]{1,0:T(8,128)(2,1)S(1)} %get-tuple-element.79), channel_id=1, source_target_pairs={{0,192},{1,193},{2,194},{3,195},{4,196},{5,197},{6,198},{7,199},{8... | collective-permute-start | bytes 147464 | tf_op jit(solution)/shard_map/ppermute | solution.py:25
  107.9 28.9 %all-to-all-start = ((bf16[8,24,1024]{2,1,0:T(8,128)(2,1)}), bf16[8,24,1024]{2,1,0:T(8,128)(2,1)S(1)}, u32[]{:S(2)}, u32[]{:S(2)}) async-start(bf16[8,24,1024]{2,1,0:T(8,128)(2,1)} %copy-done.2), calls=%async_computation | async-start | bytes 786432 | tf_op jit(solution)/shard_map/all_to_all | solution.py:55
  112.7 19.9 %collective-permute-start.16 = (bf16[64,1024]{1,0:T(8,128)(2,1)}, bf16[64,1024]{1,0:T(8,128)(2,1)S(1)}, u32[]{:S(2)}, u32[]{:S(2)}) collective-permute-start(bf16[64,1024]{1,0:T(8,128)(2,1)} %copy-done.34), channel_id=1, source_target_pairs={{0,64},{1,65},{2,66},{3,67},{4,68},{5,69},{6,70},{7,71},{8,72},{9,... | collective-permute-start | bytes 393224 | tf_op jit(solution)/shard_map/ppermute | solution.py:25
  115.7 19.8 %collective-permute-start.17 = (bf16[64,1024]{1,0:T(8,128)(2,1)}, bf16[64,1024]{1,0:T(8,128)(2,1)S(1)}, u32[]{:S(2)}, u32[]{:S(2)}) collective-permute-start(bf16[64,1024]{1,0:T(8,128)(2,1)} %copy-done.33), channel_id=1, source_target_pairs={{0,128},{1,129},{2,130},{3,131},{4,132},{5,133},{6,134},{7,135},{8... | collective-permute-start | bytes 393224 | tf_op jit(solution)/shard_map/ppermute | solution.py:25
  119.2 16.9 %collective-permute-start.18 = (bf16[64,1024]{1,0:T(8,128)(2,1)}, bf16[64,1024]{1,0:T(8,128)(2,1)S(1)}, u32[]{:S(2)}, u32[]{:S(2)}) collective-permute-start(bf16[64,1024]{1,0:T(8,128)(2,1)} %copy-done.32), channel_id=1, source_target_pairs={{0,192},{1,193},{2,194},{3,195},{4,196},{5,197},{6,198},{7,199},{8... | collective-permute-start | bytes 393224 | tf_op jit(solution)/shard_map/ppermute | solution.py:25
  136.7 1.7 collective-permute-start.19
  146.5 41.4 %copy-start.1 = (bf16[2,1024,256]{2,1,0:T(8,128)(2,1)S(1)}, bf16[2,1024,256]{2,1,0:T(8,128)(2,1)}, u32[]{:S(2)}) copy-start(bf16[2,1024,256]{2,1,0:T(8,128)(2,1)} %copy-done) | copy-start | bytes 3145732
  146.6 6.1 %collective-permute-start.22 = (bf16[448,128]{1,0:T(8,128)(2,1)S(1)}, bf16[448,128]{1,0:T(8,128)(2,1)S(1)}, u32[]{:S(2)}, u32[]{:S(2)}) collective-permute-start(bf16[448,128]{1,0:T(8,128)(2,1)S(1)} %get-tuple-element.97.refs_0_), channel_id=1, source_target_pairs={{0,12},{1,13},{2,14},{3,15},{4,0},{5,1},{6,2},{7,3},{8,4},{9,5},{1... | collective-permute-start | bytes 344072 | tf_op jit(solution)/shard_map/ppermute | solution.py:25
  147.0 7.0 %collective-permute-start.21 = (bf16[448,128]{1,0:T(8,128)(2,1)S(1)}, bf16[448,128]{1,0:T(8,128)(2,1)S(1)}, u32[]{:S(2)}, u32[]{:S(2)}) collective-permute-start(bf16[448,128]{1,0:T(8,128)(2,1)S(1)} %get-tuple-element.97.refs_0_), channel_id=1, source_target_pairs={{0,8},{1,9},{2,10},{3,11},{4,12},{5,13},{6,14},{7,15},{8,0},{9,1},... | collective-permute-start | bytes 344072 | tf_op jit(solution)/shard_map/ppermute | solution.py:25
  147.9 8.0 %collective-permute-start.20 = (bf16[448,128]{1,0:T(8,128)(2,1)S(1)}, bf16[448,128]{1,0:T(8,128)(2,1)S(1)}, u32[]{:S(2)}, u32[]{:S(2)}) collective-permute-start(bf16[448,128]{1,0:T(8,128)(2,1)S(1)} %get-tuple-element.97.refs_0_), channel_id=1, source_target_pairs={{0,4},{1,5},{2,6},{3,7},{4,8},{5,9},{6,10},{7,11},{8,12},{9,13},{1... | collective-permute-start | bytes 344072 | tf_op jit(solution)/shard_map/ppermute | solution.py:25
  155.9 7.6 %collective-permute-start.25 = (bf16[448,128]{1,0:T(8,128)(2,1)S(1)}, bf16[448,128]{1,0:T(8,128)(2,1)S(1)}, u32[]{:S(2)}, u32[]{:S(2)}) collective-permute-start(bf16[448,128]{1,0:T(8,128)(2,1)S(1)} %shard_map.98.refs_0_), channel_id=1, source_target_pairs={{0,3},{1,0},{2,1},{3,2},{4,7},{5,4},{6,5},{7,6},{8,11},{9,8},{10,9... | collective-permute-start | bytes 344072 | tf_op jit(solution)/shard_map/ppermute | solution.py:25
  156.3 7.3 %collective-permute-start.24 = (bf16[448,128]{1,0:T(8,128)(2,1)S(1)}, bf16[448,128]{1,0:T(8,128)(2,1)S(1)}, u32[]{:S(2)}, u32[]{:S(2)}) collective-permute-start(bf16[448,128]{1,0:T(8,128)(2,1)S(1)} %shard_map.98.refs_0_), channel_id=1, source_target_pairs={{0,2},{1,3},{2,0},{3,1},{4,6},{5,7},{6,4},{7,5},{8,10},{9,11},{10,... | collective-permute-start | bytes 344072 | tf_op jit(solution)/shard_map/ppermute | solution.py:25
  157.2 8.1 %collective-permute-start.23 = (bf16[448,128]{1,0:T(8,128)(2,1)S(1)}, bf16[448,128]{1,0:T(8,128)(2,1)S(1)}, u32[]{:S(2)}, u32[]{:S(2)}) collective-permute-start(bf16[448,128]{1,0:T(8,128)(2,1)S(1)} %shard_map.98.refs_0_), channel_id=1, source_target_pairs={{0,1},{1,2},{2,3},{3,0},{4,5},{5,6},{6,7},{7,4},{8,9},{9,10},{10,1... | collective-permute-start | bytes 344072 | tf_op jit(solution)/shard_map/ppermute | solution.py:25
  166.4 42.9 %copy-start.5 = (bf16[384,256]{1,0:T(8,128)(2,1)S(1)}, bf16[384,256]{1,0:T(8,128)(2,1)}, u32[]{:S(2)}) copy-start(bf16[384,256]{1,0:T(8,128)(2,1)} %copy-done.3) | copy-start | bytes 589828
  166.4 42.9 %copy-start.8 = (bf16[384,256]{1,0:T(8,128)(2,1)S(1)}, bf16[384,256]{1,0:T(8,128)(2,1)}, u32[]{:S(2)}) copy-start(bf16[384,256]{1,0:T(8,128)(2,1)} %copy-done.6) | copy-start | bytes 589828
  166.4 42.9 %copy-start.11 = (bf16[384,256]{1,0:T(8,128)(2,1)S(1)}, bf16[384,256]{1,0:T(8,128)(2,1)}, u32[]{:S(2)}) copy-start(bf16[384,256]{1,0:T(8,128)(2,1)} %copy-done.9) | copy-start | bytes 589828
  166.4 42.9 %copy-start.14 = (bf16[384,256]{1,0:T(8,128)(2,1)S(1)}, bf16[384,256]{1,0:T(8,128)(2,1)}, u32[]{:S(2)}) copy-start(bf16[384,256]{1,0:T(8,128)(2,1)} %copy-done.12) | copy-start | bytes 589828
  166.4 0.8 collective-permute-start.26
  167.2 16.8 %collective-permute-start.29 = (bf16[4,64,256]{2,1,0:T(8,128)(2,1)S(1)}, bf16[4,64,256]{2,1,0:T(8,128)(2,1)S(1)}, u32[]{:S(2)}, u32[]{:S(2)}) collective-permute-start(bf16[4,64,256]{2,1,0:T(8,128)(2,1)S(1)} %collective-permute-done.26.refs_0_), channel_id=1, source_target_pairs={{0,12},{1,13},{2,14},{3,15},{4,0},{5,1},{6,2},{7,3},{8,4},{9,5},{1... | collective-permute-start | bytes 393224 | tf_op jit(solution)/shard_map/ppermute | solution.py:25
  180.1 6.5 %collective-permute-start.28 = (bf16[4,64,256]{2,1,0:T(8,128)(2,1)S(1)}, bf16[4,64,256]{2,1,0:T(8,128)(2,1)S(1)}, u32[]{:S(2)}, u32[]{:S(2)}) collective-permute-start(bf16[4,64,256]{2,1,0:T(8,128)(2,1)S(1)} %collective-permute-done.26.refs_0_), channel_id=1, source_target_pairs={{0,8},{1,9},{2,10},{3,11},{4,12},{5,13},{6,14},{7,15},{8,0},{9,1},... | collective-permute-start | bytes 393224 | tf_op jit(solution)/shard_map/ppermute | solution.py:25
  181.7 6.3 %collective-permute-start.27 = (bf16[4,64,256]{2,1,0:T(8,128)(2,1)S(1)}, bf16[4,64,256]{2,1,0:T(8,128)(2,1)S(1)}, u32[]{:S(2)}, u32[]{:S(2)}) collective-permute-start(bf16[4,64,256]{2,1,0:T(8,128)(2,1)S(1)} %collective-permute-done.26.refs_0_), channel_id=1, source_target_pairs={{0,4},{1,5},{2,6},{3,7},{4,8},{5,9},{6,10},{7,11},{8,12},{9,13},{1... | collective-permute-start | bytes 393224 | tf_op jit(solution)/shard_map/ppermute | solution.py:25
  189.5 8.8 %collective-permute-start.30 = (bf16[64,1024]{1,0:T(8,128)(2,1)S(1)}, bf16[64,1024]{1,0:T(8,128)(2,1)S(1)}, u32[]{:S(2)}, u32[]{:S(2)}) collective-permute-start(bf16[64,1024]{1,0:T(8,128)(2,1)S(1)} %get-tuple-element.101), channel_id=1, source_target_pairs={{0,64},{1,65},{2,66},{3,67},{4,68},{5,69},{6,70},{7,71},{8,72},{9,... | collective-permute-start | bytes 393224 | tf_op jit(solution)/shard_map/ppermute | solution.py:25
  192.0 13.9 %collective-permute-start.31 = (bf16[64,1024]{1,0:T(8,128)(2,1)S(1)}, bf16[64,1024]{1,0:T(8,128)(2,1)S(1)}, u32[]{:S(2)}, u32[]{:S(2)}) collective-permute-start(bf16[64,1024]{1,0:T(8,128)(2,1)S(1)} %get-tuple-element.102), channel_id=1, source_target_pairs={{0,128},{1,129},{2,130},{3,131},{4,132},{5,133},{6,134},{7,135},{8... | collective-permute-start | bytes 393224 | tf_op jit(solution)/shard_map/ppermute | solution.py:25
  195.6 13.6 %collective-permute-start.32 = (bf16[64,1024]{1,0:T(8,128)(2,1)S(1)}, bf16[64,1024]{1,0:T(8,128)(2,1)S(1)}, u32[]{:S(2)}, u32[]{:S(2)}) collective-permute-start(bf16[64,1024]{1,0:T(8,128)(2,1)S(1)} %get-tuple-element.103), channel_id=1, source_target_pairs={{0,192},{1,193},{2,194},{3,195},{4,196},{5,197},{6,198},{7,199},{8... | collective-permute-start | bytes 393224 | tf_op jit(solution)/shard_map/ppermute | solution.py:25
  209.6 6.3 %collective-permute-start.35 = (bf16[448,128]{1,0:T(8,128)(2,1)S(1)}, bf16[448,128]{1,0:T(8,128)(2,1)S(1)}, u32[]{:S(2)}, u32[]{:S(2)}) collective-permute-start(bf16[448,128]{1,0:T(8,128)(2,1)S(1)} %get-tuple-element.105.refs_0_), channel_id=1, source_target_pairs={{0,12},{1,13},{2,14},{3,15},{4,0},{5,1},{6,2},{7,3},{8,4},{9,5},{1... | collective-permute-start | bytes 344072 | tf_op jit(solution)/shard_map/ppermute | solution.py:25
  210.4 7.0 %collective-permute-start.34 = (bf16[448,128]{1,0:T(8,128)(2,1)S(1)}, bf16[448,128]{1,0:T(8,128)(2,1)S(1)}, u32[]{:S(2)}, u32[]{:S(2)}) collective-permute-start(bf16[448,128]{1,0:T(8,128)(2,1)S(1)} %get-tuple-element.105.refs_0_), channel_id=1, source_target_pairs={{0,8},{1,9},{2,10},{3,11},{4,12},{5,13},{6,14},{7,15},{8,0},{9,1},... | collective-permute-start | bytes 344072 | tf_op jit(solution)/shard_map/ppermute | solution.py:25
  210.4 8.6 %collective-permute-start.33 = (bf16[448,128]{1,0:T(8,128)(2,1)S(1)}, bf16[448,128]{1,0:T(8,128)(2,1)S(1)}, u32[]{:S(2)}, u32[]{:S(2)}) collective-permute-start(bf16[448,128]{1,0:T(8,128)(2,1)S(1)} %get-tuple-element.105.refs_0_), channel_id=1, source_target_pairs={{0,4},{1,5},{2,6},{3,7},{4,8},{5,9},{6,10},{7,11},{8,12},{9,13},{1... | collective-permute-start | bytes 344072 | tf_op jit(solution)/shard_map/ppermute | solution.py:25
  219.1 5.6 %collective-permute-start.38 = (bf16[448,128]{1,0:T(8,128)(2,1)S(1)}, bf16[448,128]{1,0:T(8,128)(2,1)S(1)}, u32[]{:S(2)}, u32[]{:S(2)}) collective-permute-start(bf16[448,128]{1,0:T(8,128)(2,1)S(1)} %shard_map.102.refs_0_), channel_id=1, source_target_pairs={{0,3},{1,0},{2,1},{3,2},{4,7},{5,4},{6,5},{7,6},{8,11},{9,8},{10,9... | collective-permute-start | bytes 344072 | tf_op jit(solution)/shard_map/ppermute | solution.py:25
  220.1 6.7 %collective-permute-start.37 = (bf16[448,128]{1,0:T(8,128)(2,1)S(1)}, bf16[448,128]{1,0:T(8,128)(2,1)S(1)}, u32[]{:S(2)}, u32[]{:S(2)}) collective-permute-start(bf16[448,128]{1,0:T(8,128)(2,1)S(1)} %shard_map.102.refs_0_), channel_id=1, source_target_pairs={{0,2},{1,3},{2,0},{3,1},{4,6},{5,7},{6,4},{7,5},{8,10},{9,11},{10,... | collective-permute-start | bytes 344072 | tf_op jit(solution)/shard_map/ppermute | solution.py:25
  221.1 7.4 %collective-permute-start.36 = (bf16[448,128]{1,0:T(8,128)(2,1)S(1)}, bf16[448,128]{1,0:T(8,128)(2,1)S(1)}, u32[]{:S(2)}, u32[]{:S(2)}) collective-permute-start(bf16[448,128]{1,0:T(8,128)(2,1)S(1)} %shard_map.102.refs_0_), channel_id=1, source_target_pairs={{0,1},{1,2},{2,3},{3,0},{4,5},{5,6},{6,7},{7,4},{8,9},{9,10},{10,1... | collective-permute-start | bytes 344072 | tf_op jit(solution)/shard_map/ppermute | solution.py:25
  229.5 4.6 %collective-permute-start.39 = (bf16[64,256]{1,0:T(8,128)(2,1)S(1)}, bf16[64,256]{1,0:T(8,128)(2,1)S(1)}, u32[]{:S(2)}, u32[]{:S(2)}) collective-permute-start(bf16[64,256]{1,0:T(8,128)(2,1)S(1)} %get-tuple-element.108), channel_id=1, source_target_pairs={{0,3},{1,0},{2,1},{3,2},{4,7},{5,4},{6,5},{7,6},{8,11},{9,8},{10,9... | collective-permute-start | bytes 98312 | tf_op jit(solution)/shard_map/ppermute | solution.py:25
  232.0 5.4 %collective-permute-start.40 = (bf16[64,256]{1,0:T(8,128)(2,1)S(1)}, bf16[64,256]{1,0:T(8,128)(2,1)S(1)}, u32[]{:S(2)}, u32[]{:S(2)}) collective-permute-start(bf16[64,256]{1,0:T(8,128)(2,1)S(1)} %get-tuple-element.109), channel_id=1, source_target_pairs={{0,2},{1,3},{2,0},{3,1},{4,6},{5,7},{6,4},{7,5},{8,10},{9,11},{10,... | collective-permute-start | bytes 98312 | tf_op jit(solution)/shard_map/ppermute | solution.py:25
  232.5 4.9 %collective-permute-start.41 = (bf16[64,256]{1,0:T(8,128)(2,1)S(1)}, bf16[64,256]{1,0:T(8,128)(2,1)S(1)}, u32[]{:S(2)}, u32[]{:S(2)}) collective-permute-start(bf16[64,256]{1,0:T(8,128)(2,1)S(1)} %get-tuple-element.110), channel_id=1, source_target_pairs={{0,1},{1,2},{2,3},{3,0},{4,5},{5,6},{6,7},{7,4},{8,9},{9,10},{10,1... | collective-permute-start | bytes 98312 | tf_op jit(solution)/shard_map/ppermute | solution.py:25
  (30 other events, 101.6 us)

commit v3 on v1

--- a/solution.py
+++ b/solution.py
@@ -108,7 +108,7 @@
             out_shape=out_shape,
             in_specs=specs,
             scratch_shapes=list(scratch),
-            compiler_params=pltpu.CompilerParams(vmem_limit_bytes=30 * 2**20),
+            compiler_params=pltpu.CompilerParams(vmem_limit_bytes=14 * 2**20),
             cost_estimate=pl.CostEstimate(
                 flops=flops, bytes_accessed=moved, transcendentals=0
             ),
@@ -118,8 +118,9 @@
     return run
 
 
-def pack_kernel(right_ref, low_ref, up_ref, *out_refs):
+def pack_kernel(right_ref, low_ref, up_ref, lower_ref, upper_ref, *out_refs):
     n = right_ref.shape[1]
+    half = lower_ref.shape[1]
     rank_cols = low_ref.shape[2]
     share = rank_cols // lax.axis_size("row")
     row = lax.axis_index("row")
@@ -128,13 +129,16 @@
     pick = (at == want).astype(F32).astype(BF16)
     for s, out_ref in enumerate(out_refs):
         tile = wrapped(own_tile() + s)
-        out_ref[:n] = right_ref[tile].astype(BF16)
+        out_ref[:half] = lower_ref[tile]
+        out_ref[half : 2 * half] = upper_ref[tile]
+        out_ref[2 * half : 2 * half + n] = right_ref[tile].astype(BF16)
         pieces = []
         for slot in range(SIDE - 1):
             pair, is_low = partner_pair(tile, slot)
-            piece = jnp.where(is_low, dot_t(pick, low_ref[pair]), dot_t(pick, up_ref[pair]))
-            pieces.append(piece)
-        out_ref[n:] = jnp.concatenate(pieces, axis=0).astype(BF16)
+            pieces.append(
+                dot_t(pick, jnp.where(is_low, low_ref[pair], up_ref[pair]))
+            )
+        out_ref[2 * half + n :] = jnp.concatenate(pieces, axis=0).astype(BF16)
 
 
 def partner_pair(tile, slot):
@@ -145,25 +149,17 @@
     return jnp.where(high == 1, 0, jnp.where(high == 2, 1, 3)) + low, is_low
 
 
-def order_kernel(sign, *refs):
+def order_kernel(sign, start, *refs):
     out_ref = refs[-1]
     for s in range(SIDE):
-        out_ref[wrapped(own_tile() - sign * s)] = refs[s][...].astype(out_ref.dtype)
+        out_ref[wrapped(own_tile() - sign * s)] = refs[s][start:].astype(out_ref.dtype)
 
 
 def stack_kernel(*refs):
-    half = refs[0].shape[0] // 2
+    half = refs[-1].shape[1] // SIDE
     for s, ref in enumerate(refs[:-1]):
         refs[-1][0, s * half : (s + 1) * half] = ref[:half]
-        refs[-1][1, s * half : (s + 1) * half] = ref[half:]
-
-
-def deal_kernel(lower_ref, upper_ref, *out_refs):
-    rows = lower_ref.shape[1]
-    for s in range(SIDE):
-        tile = wrapped(own_tile() + s)
-        out_refs[s][:rows] = lower_ref[tile]
-        out_refs[s][rows:] = upper_ref[tile]
+        refs[-1][1, s * half : (s + 1) * half] = ref[half : 2 * half]
 
 
 def turn_kernel(low_ref, up_ref, *out_refs):
@@ -393,33 +389,29 @@
     shape = jax.ShapeDtypeStruct
 
     height = n + slots * share
-    rows = kernel_call(pack_kernel, [shape((height, width), BF16)] * SIDE)(
-        right_sides, low_left, up_left
-    )
     tied = lax.optimization_barrier
-    rows = scattered_x(rows)
+    parts = scattered_x(
+        kernel_call(pack_kernel, [shape((2 * width + height, width), BF16)] * SIDE)(
+            right_sides, low_left, up_left, inv_lower, inv_upper
+        )
+    )
     rows = kernel_call(
-        lambda *refs: order_kernel(1, *refs), shape((SIDE, height, width), BF16)
-    )(*rows)
-    rows, inv_lower, inv_upper = tied((rows, inv_lower, inv_upper))
-    parts = scattered_x(
-        kernel_call(deal_kernel, [shape((2 * width, width), BF16)] * SIDE)(
-            inv_lower, inv_upper
-        )
-    )
-    parts, rows = tied((parts, swapped(rows)))
+        lambda *refs: order_kernel(1, 2 * width, *refs),
+        shape((SIDE, height, width), BF16),
+    )(*parts)
     inverse = kernel_call(stack_kernel, shape((2, total, width), BF16))(*parts)
-    far = swap_pair(inverse)
-    near, gathered = tied((swap_core(inverse), gathered_y(rows)))
-    gathered, low_right, up_right = tied((gathered, low_right, up_right))
+    inverse, rows = tied((inverse, rows))
+    far, near = swap_pair(inverse), swap_core(inverse)
+    near, gathered = tied((near, gathered_y(swapped(rows))))
+    gathered, far, low_right, up_right = tied((gathered, far, low_right, up_right))
     turned = scattered_x(
         kernel_call(turn_kernel, [shape((slots * rank_cols, width), BF16)] * SIDE)(
             low_right, up_right
         )
     )
-    turned, far = tied((turned, far))
     inverses = [inverse, near, far, swap_core(far)]
     received = scattered_q(products(n, gathered, (0, 1), inverses))
+    received, turned = tied((received, turned))
     dense, extra = kernel_call(
         lambda *refs: total_kernel(n, *refs),
         (shape((n, total), F32), shape((8, slots * share, total), BF16)),
@@ -453,7 +445,7 @@
     )(*scattered_q(parts), *turned, later)
     rows = finished(False, send, dense, up_ranks)
     return kernel_call(
-        lambda *refs: order_kernel(-1, *refs), shape((SIDE, n, width), F32)
+        lambda *refs: order_kernel(-1, 0, *refs), shape((SIDE, n, width), F32)
     )(*scattered_x(rows, -1))
 
 

time: 203 us -> 214 us (1.054)
  starting transfers between devices: 78.2 us -> 99.4 us
  waiting for transfers between devices: 92.2 us -> 79.6 us
    ppermute x42 -> x39, starting transfers between devices: 78.2 us -> 99.4 us  [permuted(): return lax.ppermute(value, ('row', 'col'), routes(to))]
    ppermute x42 -> x39, waiting for transfers between devices: 92.2 us -> 79.6 us  [permuted(): return lax.ppermute(value, ('row', 'col'), routes(to))]
    pallas_call x15 -> x14, Pallas kernels: 9.52 us -> 9.3 us  [run(): pl.pallas_call(body, out_shape=out_shape, in_specs=specs, scratch_shapes=...]
  transfers between devices with their start and end apart: 42 -> 39, of which waited for: 33 -> 27; matrix products, arithmetic and copies ran while one was open for 0% -> 0% of each run, Pallas kernels for 0% -> 1%
where the time goes in v3:
time: 214 us; the launch traced here: 213 us
  starting transfers between devices  99.4 us (46%)
  waiting for transfers between devices  79.6 us (37%)
  blocking collectives  19.6 us (9%)
  Pallas kernels  9.3 us (4%)
  local copies, waits for them, and re-layouts  5.05 us (2%)
    ppermute x39, starting transfers between devices, permuted(): return lax.ppermute(value, ('row', 'col'), routes(to))  99.4 us
    ppermute x39, waiting for transfers between devices, permuted(): return lax.ppermute(value, ('row', 'col'), routes(to))  79.6 us
    all_to_all x1, blocking collectives, from_every_z(): lax.all_to_all(value, 'row', 0, 0, tiled=True, axis_index_groups=Z_GROUPS)  19.6 us
    pallas_call x14, Pallas kernels, run(): pl.pallas_call(body, out_shape=out_shape, in_specs=specs, scratch_shapes=...  9.3 us
    unnamed x18, local copies, waits for them, and re-layouts  5.05 us
  transfers between devices with their start and end apart: 39, of which 27 were waited for; matrix products, arithmetic and copies ran while one was open for 0% of the time, Pallas kernels for 1%

profile of v3, /device:TPU:2, one launch (start us, length us, event | category | flops | bytes accessed | tf_op | source)
XLA Modules:
  0.0 213.1 jit_solution(15810155228674324833)
XLA Ops:
  5.4 1.5 collective-permute-start
  6.9 2.8 %collective-permute-start.1 = (bf16[600,256]{1,0:T(8,128)(2,1)S(1)}, bf16[600,256]{1,0:T(8,128)(2,1)S(1)}, u32[]{:S(2)}, u32[]{:S(2)}) collective-permute-start(bf16[600,256]{1,0:T(8,128)(2,1)S(1)} %get-tuple-element.56), channel_id=1, source_target_pairs={{0,2},{1,3},{2,0},{3,1},{4,6},{5,7},{6,4},{7,5},{8,10},{9,11},{10,... | collective-permute-start | bytes 921608 | tf_op jit(solution)/shard_map/ppermute | solution.py:25
  10.2 5.7 %collective-permute-done.refs_1_ = bf16[600,256]{1,0:T(8,128)(2,1)S(1)} collective-permute-done((bf16[600,256]{1,0:T(8,128)(2,1)S(1)}, bf16[600,256]{1,0:T(8,128)(2,1)S(1)}, u32[]{:S(2)}, u32[]{:S(2)}) %collective-permute-start) | collective-permute-done | bytes 307232 | tf_op jit(solution)/shard_map/ppermute | solution.py:25
  15.9 2.8 %collective-permute-done.1.refs_2_ = bf16[600,256]{1,0:T(8,128)(2,1)S(1)} collective-permute-done((bf16[600,256]{1,0:T(8,128)(2,1)S(1)}, bf16[600,256]{1,0:T(8,128)(2,1)S(1)}, u32[]{:S(2)}, u32[]{:S(2)}) %collective-permute-start.1) | collective-permute-done | bytes 307232 | tf_op jit(solution)/shard_map/ppermute | solution.py:25
  18.6 4.3 %collective-permute-done.2.refs_3_ = bf16[600,256]{1,0:T(8,128)(2,1)S(1)} collective-permute-done((bf16[600,256]{1,0:T(8,128)(2,1)S(1)}, bf16[600,256]{1,0:T(8,128)(2,1)S(1)}, u32[]{:S(2)}, u32[]{:S(2)}) %collective-permute-start.2) | collective-permute-done | bytes 307232 | tf_op jit(solution)/shard_map/ppermute | solution.py:25
  23.2 2.1 collective-permute-start.8
  26.0 38.6 %collective-permute-start.7 = (bf16[4,88,256]{2,1,0:T(8,128)(2,1)S(1)}, bf16[4,88,256]{2,1,0:T(8,128)(2,1)S(1)}, u32[]{:S(2)}, u32[]{:S(2)}) collective-permute-start(bf16[4,88,256]{2,1,0:T(8,128)(2,1)S(1)} %collective-permute-done.4.refs_0_), channel_id=1, source_target_pairs={{0,12},{1,13},{2,14},{3,15},{4,0},{5,1},{6,2},{7,3},{8,4},{9,5},{1... | collective-permute-start | bytes 540680 | tf_op jit(solution)/shard_map/ppermute | solution.py:25
  65.4 6.6 %collective-permute-done.7.refs_3_ = bf16[4,88,256]{2,1,0:T(8,128)(2,1)S(1)} collective-permute-done((bf16[4,88,256]{2,1,0:T(8,128)(2,1)S(1)}, bf16[4,88,256]{2,1,0:T(8,128)(2,1)S(1)}, u32[]{:S(2)}, u32[]{:S(2)}) %collective-permute-start.7) | collective-permute-done | bytes 180256 | tf_op jit(solution)/shard_map/ppermute | solution.py:25
  72.0 1.5 collective-permute-done.6.refs_2_
  73.6 1.9 collective-permute-done.5.refs_1_
  75.9 1.4 collective-permute-start.13
  77.3 1.5 collective-permute-start.14
  78.8 1.7 collective-permute-start.15
  80.4 2.8 %shard_map.94 = (bf16[88,1024]{1,0:T(8,128)(2,1)S(1)}, bf16[88,1024]{1,0:T(8,128)(2,1)S(1)}, bf16[88,1024]{1,0:T(8,128)(2,1)S(1)}, bf16[88,1024]{1,0:T(8,128)(2,1)S(1)}) custom-call(bf16[4,88,256]{2,1,0:T(8,128)(2,1)S(1)} %collective-permute-done.4.refs_0_, bf16[4,88,256]{2,1,0:T(8,128)(2,1)S(1)} %collective-permute-done.5.refs_1_, ...), custom_call_target="tpu_custom_call" | custom-call | flops 738197504 | bytes 5636096 | tf_op jit(solution)/shard_map/pallas_call | solution.py:106
  83.3 2.4 %collective-permute-start.11 = (bf16[88,1024]{1,0:T(8,128)(2,1)S(1)}, bf16[88,1024]{1,0:T(8,128)(2,1)S(1)}, u32[]{:S(2)}, u32[]{:S(2)}) collective-permute-start(bf16[88,1024]{1,0:T(8,128)(2,1)S(1)} %get-tuple-element.72), channel_id=1, source_target_pairs={{0,128},{1,129},{2,130},{3,131},{4,132},{5,133},{6,134},{7,135},{8... | collective-permute-start | bytes 540680 | tf_op jit(solution)/shard_map/ppermute | solution.py:25
  85.7 2.8 %collective-permute-start.12 = (bf16[88,1024]{1,0:T(8,128)(2,1)S(1)}, bf16[88,1024]{1,0:T(8,128)(2,1)S(1)}, u32[]{:S(2)}, u32[]{:S(2)}) collective-permute-start(bf16[88,1024]{1,0:T(8,128)(2,1)S(1)} %get-tuple-element.73), channel_id=1, source_target_pairs={{0,192},{1,193},{2,194},{3,195},{4,196},{5,197},{6,198},{7,199},{8... | collective-permute-start | bytes 540680 | tf_op jit(solution)/shard_map/ppermute | solution.py:25
  88.5 1.2 collective-permute-done.15.refs_3_.refs_7_
  89.7 10.8 %collective-permute-done.10.refs_1_ = bf16[88,1024]{1,0:T(8,128)(2,1)S(1)} collective-permute-done((bf16[88,1024]{1,0:T(8,128)(2,1)S(1)}, bf16[88,1024]{1,0:T(8,128)(2,1)S(1)}, u32[]{:S(2)}, u32[]{:S(2)}) %collective-permute-start.10) | collective-permute-done | bytes 180256 | tf_op jit(solution)/shard_map/ppermute | solution.py:25
  100.5 2.4 %collective-permute-done.12.refs_3_ = bf16[88,1024]{1,0:T(8,128)(2,1)S(1)} collective-permute-done((bf16[88,1024]{1,0:T(8,128)(2,1)S(1)}, bf16[88,1024]{1,0:T(8,128)(2,1)S(1)}, u32[]{:S(2)}, u32[]{:S(2)}) %collective-permute-start.12) | collective-permute-done | bytes 180256 | tf_op jit(solution)/shard_map/ppermute | solution.py:25
  103.0 19.6 %all_to_all.5.mine_ref = bf16[8,24,1024]{2,1,0:T(8,128)(2,1)S(1)} all-to-all(bf16[8,24,1024]{2,1,0:T(8,128)(2,1)S(1)} %get-tuple-element.85), channel_id=1, replica_groups={{0,32,64,96,128,160,192,224},{16,48,80,112,144,176,208,240},{1,33,65,97..., dimensions={0} | all-to-all | bytes 786432 | tf_op jit(solution)/shard_map/all_to_all | solution.py:55
  122.5 1.7 collective-permute-done.16.other_ref
  126.0 2.0 collective-permute-start.18
  128.6 2.4 %collective-permute-done.19.refs_3_ = bf16[448,128]{1,0:T(8,128)(2,1)S(1)} collective-permute-done((bf16[448,128]{1,0:T(8,128)(2,1)S(1)}, bf16[448,128]{1,0:T(8,128)(2,1)S(1)}, u32[]{:S(2)}, u32[]{:S(2)}) %collective-permute-start.19) | collective-permute-done | bytes 114720 | tf_op jit(solution)/shard_map/ppermute | solution.py:25
  131.1 2.4 %collective-permute-done.18.refs_2_ = bf16[448,128]{1,0:T(8,128)(2,1)S(1)} collective-permute-done((bf16[448,128]{1,0:T(8,128)(2,1)S(1)}, bf16[448,128]{1,0:T(8,128)(2,1)S(1)}, u32[]{:S(2)}, u32[]{:S(2)}) %collective-permute-start.18) | collective-permute-done | bytes 114720 | tf_op jit(solution)/shard_map/ppermute | solution.py:25
  133.4 1.4 collective-permute-done.17.refs_1_
  134.9 1.6 collective-permute-start.22
  136.9 1.5 collective-permute-start.20
  138.3 1.5 collective-permute-done.22.refs_3_
  139.8 3.1 %collective-permute-done.21.refs_2_ = bf16[448,128]{1,0:T(8,128)(2,1)S(1)} collective-permute-done((bf16[448,128]{1,0:T(8,128)(2,1)S(1)}, bf16[448,128]{1,0:T(8,128)(2,1)S(1)}, u32[]{:S(2)}, u32[]{:S(2)}) %collective-permute-start.21) | collective-permute-done | bytes 114720 | tf_op jit(solution)/shard_map/ppermute | solution.py:25
  145.4 12.3 %collective-permute-start.26 = (bf16[4,64,256]{2,1,0:T(8,128)(2,1)S(1)}, bf16[4,64,256]{2,1,0:T(8,128)(2,1)S(1)}, u32[]{:S(2)}, u32[]{:S(2)}) collective-permute-start(bf16[4,64,256]{2,1,0:T(8,128)(2,1)S(1)} %collective-permute-done.23.refs_0_), channel_id=1, source_target_pairs={{0,12},{1,13},{2,14},{3,15},{4,0},{5,1},{6,2},{7,3},{8,4},{9,5},{1... | collective-permute-start | bytes 393224 | tf_op jit(solution)/shard_map/ppermute | solution.py:25
  157.8 2.3 %collective-permute-start.25 = (bf16[4,64,256]{2,1,0:T(8,128)(2,1)S(1)}, bf16[4,64,256]{2,1,0:T(8,128)(2,1)S(1)}, u32[]{:S(2)}, u32[]{:S(2)}) collective-permute-start(bf16[4,64,256]{2,1,0:T(8,128)(2,1)S(1)} %collective-permute-done.23.refs_0_), channel_id=1, source_target_pairs={{0,8},{1,9},{2,10},{3,11},{4,12},{5,13},{6,14},{7,15},{8,0},{9,1},... | collective-permute-start | bytes 393224 | tf_op jit(solution)/shard_map/ppermute | solution.py:25
  160.1 1.4 collective-permute-start.24
  161.5 2.7 %collective-permute-done.25.refs_2_ = bf16[4,64,256]{2,1,0:T(8,128)(2,1)S(1)} collective-permute-done((bf16[4,64,256]{2,1,0:T(8,128)(2,1)S(1)}, bf16[4,64,256]{2,1,0:T(8,128)(2,1)S(1)}, u32[]{:S(2)}, u32[]{:S(2)}) %collective-permute-start.25) | collective-permute-done | bytes 131104 | tf_op jit(solution)/shard_map/ppermute | solution.py:25
  164.3 2.0 collective-permute-done.24.refs_1_
  166.3 1.5 shard_map.100
  167.8 2.1 collective-permute-start.27
  169.9 3.8 %collective-permute-start.28 = (bf16[64,1024]{1,0:T(8,128)(2,1)S(1)}, bf16[64,1024]{1,0:T(8,128)(2,1)S(1)}, u32[]{:S(2)}, u32[]{:S(2)}) collective-permute-start(bf16[64,1024]{1,0:T(8,128)(2,1)S(1)} %get-tuple-element.94), channel_id=1, source_target_pairs={{0,128},{1,129},{2,130},{3,131},{4,132},{5,133},{6,134},{7,135},{8... | collective-permute-start | bytes 393224 | tf_op jit(solution)/shard_map/ppermute | solution.py:25
  173.8 2.7 %collective-permute-done.27.refs_1_ = bf16[64,1024]{1,0:T(8,128)(2,1)S(1)} collective-permute-done((bf16[64,1024]{1,0:T(8,128)(2,1)S(1)}, bf16[64,1024]{1,0:T(8,128)(2,1)S(1)}, u32[]{:S(2)}, u32[]{:S(2)}) %collective-permute-start.27) | collective-permute-done | bytes 131104 | tf_op jit(solution)/shard_map/ppermute | solution.py:25
  176.5 7.6 %collective-permute-done.28.refs_2_ = bf16[64,1024]{1,0:T(8,128)(2,1)S(1)} collective-permute-done((bf16[64,1024]{1,0:T(8,128)(2,1)S(1)}, bf16[64,1024]{1,0:T(8,128)(2,1)S(1)}, u32[]{:S(2)}, u32[]{:S(2)}) %collective-permute-start.28) | collective-permute-done | bytes 131104 | tf_op jit(solution)/shard_map/ppermute | solution.py:25
  186.7 4.0 %collective-permute-done.32.refs_3_ = bf16[448,128]{1,0:T(8,128)(2,1)S(1)} collective-permute-done((bf16[448,128]{1,0:T(8,128)(2,1)S(1)}, bf16[448,128]{1,0:T(8,128)(2,1)S(1)}, u32[]{:S(2)}, u32[]{:S(2)}) %collective-permute-start.32) | collective-permute-done | bytes 114720 | tf_op jit(solution)/shard_map/ppermute | solution.py:25
  190.7 1.3 collective-permute-done.31.refs_2_
  192.0 1.5 collective-permute-done.30.refs_1_
  193.6 2.4 %collective-permute-start.35 = (bf16[448,128]{1,0:T(8,128)(2,1)S(1)}, bf16[448,128]{1,0:T(8,128)(2,1)S(1)}, u32[]{:S(2)}, u32[]{:S(2)}) collective-permute-start(bf16[448,128]{1,0:T(8,128)(2,1)S(1)} %shard_map.102.refs_0_), channel_id=1, source_target_pairs={{0,3},{1,0},{2,1},{3,2},{4,7},{5,4},{6,5},{7,6},{8,11},{9,8},{10,9... | collective-permute-start | bytes 344072 | tf_op jit(solution)/shard_map/ppermute | solution.py:25
  196.8 2.4 %collective-permute-start.33 = (bf16[448,128]{1,0:T(8,128)(2,1)S(1)}, bf16[448,128]{1,0:T(8,128)(2,1)S(1)}, u32[]{:S(2)}, u32[]{:S(2)}) collective-permute-start(bf16[448,128]{1,0:T(8,128)(2,1)S(1)} %shard_map.102.refs_0_), channel_id=1, source_target_pairs={{0,1},{1,2},{2,3},{3,0},{4,5},{5,6},{6,7},{7,4},{8,9},{9,10},{10,1... | collective-permute-start | bytes 344072 | tf_op jit(solution)/shard_map/ppermute | solution.py:25
  199.2 3.1 %collective-permute-done.34.refs_2_ = bf16[448,128]{1,0:T(8,128)(2,1)S(1)} collective-permute-done((bf16[448,128]{1,0:T(8,128)(2,1)S(1)}, bf16[448,128]{1,0:T(8,128)(2,1)S(1)}, u32[]{:S(2)}, u32[]{:S(2)}) %collective-permute-start.34) | collective-permute-done | bytes 114720 | tf_op jit(solution)/shard_map/ppermute | solution.py:25
  203.9 3.0 %collective-permute-start.36 = (bf16[64,256]{1,0:T(8,128)(2,1)S(1)}, bf16[64,256]{1,0:T(8,128)(2,1)S(1)}, u32[]{:S(2)}, u32[]{:S(2)}) collective-permute-start(bf16[64,256]{1,0:T(8,128)(2,1)S(1)} %get-tuple-element.100), channel_id=1, source_target_pairs={{0,3},{1,0},{2,1},{3,2},{4,7},{5,4},{6,5},{7,6},{8,11},{9,8},{10,9... | collective-permute-start | bytes 98312 | tf_op jit(solution)/shard_map/ppermute | solution.py:25
  207.0 2.1 %collective-permute-start.38 = (bf16[64,256]{1,0:T(8,128)(2,1)S(1)}, bf16[64,256]{1,0:T(8,128)(2,1)S(1)}, u32[]{:S(2)}, u32[]{:S(2)}) collective-permute-start(bf16[64,256]{1,0:T(8,128)(2,1)S(1)} %get-tuple-element.102), channel_id=1, source_target_pairs={{0,1},{1,2},{2,3},{3,0},{4,5},{5,6},{6,7},{7,4},{8,9},{9,10},{10,1... | collective-permute-start | bytes 98312 | tf_op jit(solution)/shard_map/ppermute | solution.py:25
  209.1 3.3 %collective-permute-done.37.refs_2_ = bf16[64,256]{1,0:T(8,128)(2,1)S(1)} collective-permute-done((bf16[64,256]{1,0:T(8,128)(2,1)S(1)}, bf16[64,256]{1,0:T(8,128)(2,1)S(1)}, u32[]{:S(2)}, u32[]{:S(2)}) %collective-permute-start.37) | collective-permute-done | bytes 32800 | tf_op jit(solution)/shard_map/ppermute | solution.py:25
  (63 shorter events, 19.2 us)
Async XLA Ops:
  0.0 1.0 copy-start
  1.0 1.0 copy-start.1
  2.1 1.0 copy-start.2
  3.1 1.0 copy-start.3
  4.1 0.9 copy-start.6
  5.4 10.5 %collective-permute-start = (bf16[600,256]{1,0:T(8,128)(2,1)S(1)}, bf16[600,256]{1,0:T(8,128)(2,1)S(1)}, u32[]{:S(2)}, u32[]{:S(2)}) collective-permute-start(bf16[600,256]{1,0:T(8,128)(2,1)S(1)} %get-tuple-element.55), channel_id=1, source_target_pairs={{0,1},{1,2},{2,3},{3,0},{4,5},{5,6},{6,7},{7,4},{8,9},{9,10},{10,1... | collective-permute-start | bytes 921608 | tf_op jit(solution)/shard_map/ppermute | solution.py:25
  6.9 11.7 %collective-permute-start.1 = (bf16[600,256]{1,0:T(8,128)(2,1)S(1)}, bf16[600,256]{1,0:T(8,128)(2,1)S(1)}, u32[]{:S(2)}, u32[]{:S(2)}) collective-permute-start(bf16[600,256]{1,0:T(8,128)(2,1)S(1)} %get-tuple-element.56), channel_id=1, source_target_pairs={{0,2},{1,3},{2,0},{3,1},{4,6},{5,7},{6,4},{7,5},{8,10},{9,11},{10,... | collective-permute-start | bytes 921608 | tf_op jit(solution)/shard_map/ppermute | solution.py:25
  9.8 13.2 %collective-permute-start.2 = (bf16[600,256]{1,0:T(8,128)(2,1)S(1)}, bf16[600,256]{1,0:T(8,128)(2,1)S(1)}, u32[]{:S(2)}, u32[]{:S(2)}) collective-permute-start(bf16[600,256]{1,0:T(8,128)(2,1)S(1)} %get-tuple-element.57), channel_id=1, source_target_pairs={{0,3},{1,0},{2,1},{3,2},{4,7},{5,4},{6,5},{7,6},{8,11},{9,8},{10,9... | collective-permute-start | bytes 921608 | tf_op jit(solution)/shard_map/ppermute | solution.py:25
  23.0 52.5 %copy-start.4 = (bf16[6,256,128]{2,1,0:T(8,128)(2,1)S(1)}, bf16[6,256,128]{2,1,0:T(8,128)(2,1)}, u32[]{:S(2)}) copy-start(bf16[6,256,128]{2,1,0:T(8,128)(2,1)} %low_ref.2) | copy-start | bytes 1179652
  23.0 52.5 %copy-start.5 = (bf16[6,256,128]{2,1,0:T(8,128)(2,1)S(1)}, bf16[6,256,128]{2,1,0:T(8,128)(2,1)}, u32[]{:S(2)}) copy-start(bf16[6,256,128]{2,1,0:T(8,128)(2,1)} %up_ref.2) | copy-start | bytes 1179652
  23.1 52.4 %collective-permute-start.3 = (bf16[2,1024,256]{2,1,0:T(8,128)(2,1)S(1)}, bf16[2,1024,256]{2,1,0:T(8,128)(2,1)S(1)}, u32[]{:S(2)}, u32[]{:S(2)}) collective-permute-start(bf16[2,1024,256]{2,1,0:T(8,128)(2,1)S(1)} %shard_map.92.refs_4_), channel_id=1, source_target_pairs={{0,16},{1,17},{2,18},{3,19},{4,20},{5,21},{6,22},{7,23},{8,24},{9,... | collective-permute-start | bytes 3145736 | tf_op jit(solution)/shard_map/ppermute | solution.py:25
  23.2 52.3 %collective-permute-start.8 = (bf16[2,1024,256]{2,1,0:T(8,128)(2,1)S(1)}, bf16[2,1024,256]{2,1,0:T(8,128)(2,1)S(1)}, u32[]{:S(2)}, u32[]{:S(2)}) collective-permute-start(bf16[2,1024,256]{2,1,0:T(8,128)(2,1)S(1)} %shard_map.92.refs_4_), channel_id=1, source_target_pairs={{0,32},{1,33},{2,34},{3,35},{4,36},{5,37},{6,38},{7,39},{8,40},{9,... | collective-permute-start | bytes 3145736 | tf_op jit(solution)/shard_map/ppermute | solution.py:25
  25.3 0.7 collective-permute-start.4
  26.0 46.1 %collective-permute-start.7 = (bf16[4,88,256]{2,1,0:T(8,128)(2,1)S(1)}, bf16[4,88,256]{2,1,0:T(8,128)(2,1)S(1)}, u32[]{:S(2)}, u32[]{:S(2)}) collective-permute-start(bf16[4,88,256]{2,1,0:T(8,128)(2,1)S(1)} %collective-permute-done.4.refs_0_), channel_id=1, source_target_pairs={{0,12},{1,13},{2,14},{3,15},{4,0},{5,1},{6,2},{7,3},{8,4},{9,5},{1... | collective-permute-start | bytes 540680 | tf_op jit(solution)/shard_map/ppermute | solution.py:25
  64.6 9.0 %collective-permute-start.6 = (bf16[4,88,256]{2,1,0:T(8,128)(2,1)S(1)}, bf16[4,88,256]{2,1,0:T(8,128)(2,1)S(1)}, u32[]{:S(2)}, u32[]{:S(2)}) collective-permute-start(bf16[4,88,256]{2,1,0:T(8,128)(2,1)S(1)} %collective-permute-done.4.refs_0_), channel_id=1, source_target_pairs={{0,8},{1,9},{2,10},{3,11},{4,12},{5,13},{6,14},{7,15},{8,0},{9,1},... | collective-permute-start | bytes 540680 | tf_op jit(solution)/shard_map/ppermute | solution.py:25
  64.6 10.9 %collective-permute-start.5 = (bf16[4,88,256]{2,1,0:T(8,128)(2,1)S(1)}, bf16[4,88,256]{2,1,0:T(8,128)(2,1)S(1)}, u32[]{:S(2)}, u32[]{:S(2)}) collective-permute-start(bf16[4,88,256]{2,1,0:T(8,128)(2,1)S(1)} %collective-permute-done.4.refs_0_), channel_id=1, source_target_pairs={{0,4},{1,5},{2,6},{3,7},{4,8},{5,9},{6,10},{7,11},{8,12},{9,13},{1... | collective-permute-start | bytes 540680 | tf_op jit(solution)/shard_map/ppermute | solution.py:25
  75.5 4.9 %collective-permute-start.9 = (bf16[2,1024,256]{2,1,0:T(8,128)(2,1)S(1)}, bf16[2,1024,256]{2,1,0:T(8,128)(2,1)S(1)}, u32[]{:S(2)}, u32[]{:S(2)}) collective-permute-start(bf16[2,1024,256]{2,1,0:T(8,128)(2,1)S(1)} %collective-permute-done.8.refs_6_), channel_id=1, source_target_pairs={{0,16},{1,17},{2,18},{3,19},{4,20},{5,21},{6,22},{7,23},{8,24},{9,... | collective-permute-start | bytes 3145736 | tf_op jit(solution)/shard_map/ppermute | solution.py:25
  75.9 9.7 %collective-permute-start.13 = (bf16[384,256]{1,0:T(8,128)(2,1)S(1)}, bf16[384,256]{1,0:T(8,128)(2,1)S(1)}, u32[]{:S(2)}, u32[]{:S(2)}) collective-permute-start(bf16[384,256]{1,0:T(8,128)(2,1)S(1)} %get-tuple-element.77), channel_id=1, source_target_pairs={{0,1},{1,2},{2,3},{3,0},{4,5},{5,6},{6,7},{7,4},{8,9},{9,10},{10,1... | collective-permute-start | bytes 589832 | tf_op jit(solution)/shard_map/ppermute | solution.py:25
  77.3 11.2 %collective-permute-start.14 = (bf16[384,256]{1,0:T(8,128)(2,1)S(1)}, bf16[384,256]{1,0:T(8,128)(2,1)S(1)}, u32[]{:S(2)}, u32[]{:S(2)}) collective-permute-start(bf16[384,256]{1,0:T(8,128)(2,1)S(1)} %get-tuple-element.78), channel_id=1, source_target_pairs={{0,2},{1,3},{2,0},{3,1},{4,6},{5,7},{6,4},{7,5},{8,10},{9,11},{10,... | collective-permute-start | bytes 589832 | tf_op jit(solution)/shard_map/ppermute | solution.py:25
  78.8 10.9 %collective-permute-start.15 = (bf16[384,256]{1,0:T(8,128)(2,1)S(1)}, bf16[384,256]{1,0:T(8,128)(2,1)S(1)}, u32[]{:S(2)}, u32[]{:S(2)}) collective-permute-start(bf16[384,256]{1,0:T(8,128)(2,1)S(1)} %get-tuple-element.79), channel_id=1, source_target_pairs={{0,3},{1,0},{2,1},{3,2},{4,7},{5,4},{6,5},{7,6},{8,11},{9,8},{10,9... | collective-permute-start | bytes 589832 | tf_op jit(solution)/shard_map/ppermute | solution.py:25
  83.2 17.3 %collective-permute-start.10 = (bf16[88,1024]{1,0:T(8,128)(2,1)S(1)}, bf16[88,1024]{1,0:T(8,128)(2,1)S(1)}, u32[]{:S(2)}, u32[]{:S(2)}) collective-permute-start(bf16[88,1024]{1,0:T(8,128)(2,1)S(1)} %get-tuple-element.71), channel_id=1, source_target_pairs={{0,64},{1,65},{2,66},{3,67},{4,68},{5,69},{6,70},{7,71},{8,72},{9,... | collective-permute-start | bytes 540680 | tf_op jit(solution)/shard_map/ppermute | solution.py:25
  83.3 17.2 %collective-permute-start.11 = (bf16[88,1024]{1,0:T(8,128)(2,1)S(1)}, bf16[88,1024]{1,0:T(8,128)(2,1)S(1)}, u32[]{:S(2)}, u32[]{:S(2)}) collective-permute-start(bf16[88,1024]{1,0:T(8,128)(2,1)S(1)} %get-tuple-element.72), channel_id=1, source_target_pairs={{0,128},{1,129},{2,130},{3,131},{4,132},{5,133},{6,134},{7,135},{8... | collective-permute-start | bytes 540680 | tf_op jit(solution)/shard_map/ppermute | solution.py:25
  85.7 17.2 %collective-permute-start.12 = (bf16[88,1024]{1,0:T(8,128)(2,1)S(1)}, bf16[88,1024]{1,0:T(8,128)(2,1)S(1)}, u32[]{:S(2)}, u32[]{:S(2)}) collective-permute-start(bf16[88,1024]{1,0:T(8,128)(2,1)S(1)} %get-tuple-element.73), channel_id=1, source_target_pairs={{0,192},{1,193},{2,194},{3,195},{4,196},{5,197},{6,198},{7,199},{8... | collective-permute-start | bytes 540680 | tf_op jit(solution)/shard_map/ppermute | solution.py:25
  122.5 1.7 collective-permute-start.16
  125.0 6.1 %collective-permute-start.19 = (bf16[448,128]{1,0:T(8,128)(2,1)S(1)}, bf16[448,128]{1,0:T(8,128)(2,1)S(1)}, u32[]{:S(2)}, u32[]{:S(2)}) collective-permute-start(bf16[448,128]{1,0:T(8,128)(2,1)S(1)} %get-tuple-element.90.refs_0_), channel_id=1, source_target_pairs={{0,12},{1,13},{2,14},{3,15},{4,0},{5,1},{6,2},{7,3},{8,4},{9,5},{1... | collective-permute-start | bytes 344072 | tf_op jit(solution)/shard_map/ppermute | solution.py:25
  126.0 7.4 %collective-permute-start.18 = (bf16[448,128]{1,0:T(8,128)(2,1)S(1)}, bf16[448,128]{1,0:T(8,128)(2,1)S(1)}, u32[]{:S(2)}, u32[]{:S(2)}) collective-permute-start(bf16[448,128]{1,0:T(8,128)(2,1)S(1)} %get-tuple-element.90.refs_0_), channel_id=1, source_target_pairs={{0,8},{1,9},{2,10},{3,11},{4,12},{5,13},{6,14},{7,15},{8,0},{9,1},... | collective-permute-start | bytes 344072 | tf_op jit(solution)/shard_map/ppermute | solution.py:25
  128.0 6.9 %collective-permute-start.17 = (bf16[448,128]{1,0:T(8,128)(2,1)S(1)}, bf16[448,128]{1,0:T(8,128)(2,1)S(1)}, u32[]{:S(2)}, u32[]{:S(2)}) collective-permute-start(bf16[448,128]{1,0:T(8,128)(2,1)S(1)} %get-tuple-element.90.refs_0_), channel_id=1, source_target_pairs={{0,4},{1,5},{2,6},{3,7},{4,8},{5,9},{6,10},{7,11},{8,12},{9,13},{1... | collective-permute-start | bytes 344072 | tf_op jit(solution)/shard_map/ppermute | solution.py:25
  134.9 8.8 %copy-start.7 = (s32[6]{0:T(128)S(1)}, s32[6]{0:T(128)}, u32[]{:S(2)}) copy-start(s32[6]{0:T(128)} %refs_6_.2) | copy-start | bytes 76
  134.9 4.9 %collective-permute-start.22 = (bf16[448,128]{1,0:T(8,128)(2,1)S(1)}, bf16[448,128]{1,0:T(8,128)(2,1)S(1)}, u32[]{:S(2)}, u32[]{:S(2)}) collective-permute-start(bf16[448,128]{1,0:T(8,128)(2,1)S(1)} %shard_map.98.refs_0_), channel_id=1, source_target_pairs={{0,3},{1,0},{2,1},{3,2},{4,7},{5,4},{6,5},{7,6},{8,11},{9,8},{10,9... | collective-permute-start | bytes 344072 | tf_op jit(solution)/shard_map/ppermute | solution.py:25
  136.6 6.3 %collective-permute-start.21 = (bf16[448,128]{1,0:T(8,128)(2,1)S(1)}, bf16[448,128]{1,0:T(8,128)(2,1)S(1)}, u32[]{:S(2)}, u32[]{:S(2)}) collective-permute-start(bf16[448,128]{1,0:T(8,128)(2,1)S(1)} %shard_map.98.refs_0_), channel_id=1, source_target_pairs={{0,2},{1,3},{2,0},{3,1},{4,6},{5,7},{6,4},{7,5},{8,10},{9,11},{10,... | collective-permute-start | bytes 344072 | tf_op jit(solution)/shard_map/ppermute | solution.py:25
  136.9 6.9 %collective-permute-start.20 = (bf16[448,128]{1,0:T(8,128)(2,1)S(1)}, bf16[448,128]{1,0:T(8,128)(2,1)S(1)}, u32[]{:S(2)}, u32[]{:S(2)}) collective-permute-start(bf16[448,128]{1,0:T(8,128)(2,1)S(1)} %shard_map.98.refs_0_), channel_id=1, source_target_pairs={{0,1},{1,2},{2,3},{3,0},{4,5},{5,6},{6,7},{7,4},{8,9},{9,10},{10,1... | collective-permute-start | bytes 344072 | tf_op jit(solution)/shard_map/ppermute | solution.py:25
  144.8 0.7 collective-permute-start.23
  145.4 16.1 %collective-permute-start.26 = (bf16[4,64,256]{2,1,0:T(8,128)(2,1)S(1)}, bf16[4,64,256]{2,1,0:T(8,128)(2,1)S(1)}, u32[]{:S(2)}, u32[]{:S(2)}) collective-permute-start(bf16[4,64,256]{2,1,0:T(8,128)(2,1)S(1)} %collective-permute-done.23.refs_0_), channel_id=1, source_target_pairs={{0,12},{1,13},{2,14},{3,15},{4,0},{5,1},{6,2},{7,3},{8,4},{9,5},{1... | collective-permute-start | bytes 393224 | tf_op jit(solution)/shard_map/ppermute | solution.py:25
  157.8 6.5 %collective-permute-start.25 = (bf16[4,64,256]{2,1,0:T(8,128)(2,1)S(1)}, bf16[4,64,256]{2,1,0:T(8,128)(2,1)S(1)}, u32[]{:S(2)}, u32[]{:S(2)}) collective-permute-start(bf16[4,64,256]{2,1,0:T(8,128)(2,1)S(1)} %collective-permute-done.23.refs_0_), channel_id=1, source_target_pairs={{0,8},{1,9},{2,10},{3,11},{4,12},{5,13},{6,14},{7,15},{8,0},{9,1},... | collective-permute-start | bytes 393224 | tf_op jit(solution)/shard_map/ppermute | solution.py:25
  160.1 6.2 %collective-permute-start.24 = (bf16[4,64,256]{2,1,0:T(8,128)(2,1)S(1)}, bf16[4,64,256]{2,1,0:T(8,128)(2,1)S(1)}, u32[]{:S(2)}, u32[]{:S(2)}) collective-permute-start(bf16[4,64,256]{2,1,0:T(8,128)(2,1)S(1)} %collective-permute-done.23.refs_0_), channel_id=1, source_target_pairs={{0,4},{1,5},{2,6},{3,7},{4,8},{5,9},{6,10},{7,11},{8,12},{9,13},{1... | collective-permute-start | bytes 393224 | tf_op jit(solution)/shard_map/ppermute | solution.py:25
  167.8 8.7 %collective-permute-start.27 = (bf16[64,1024]{1,0:T(8,128)(2,1)S(1)}, bf16[64,1024]{1,0:T(8,128)(2,1)S(1)}, u32[]{:S(2)}, u32[]{:S(2)}) collective-permute-start(bf16[64,1024]{1,0:T(8,128)(2,1)S(1)} %get-tuple-element.93), channel_id=1, source_target_pairs={{0,64},{1,65},{2,66},{3,67},{4,68},{5,69},{6,70},{7,71},{8,72},{9,... | collective-permute-start | bytes 393224 | tf_op jit(solution)/shard_map/ppermute | solution.py:25
  169.9 14.2 %collective-permute-start.28 = (bf16[64,1024]{1,0:T(8,128)(2,1)S(1)}, bf16[64,1024]{1,0:T(8,128)(2,1)S(1)}, u32[]{:S(2)}, u32[]{:S(2)}) collective-permute-start(bf16[64,1024]{1,0:T(8,128)(2,1)S(1)} %get-tuple-element.94), channel_id=1, source_target_pairs={{0,128},{1,129},{2,130},{3,131},{4,132},{5,133},{6,134},{7,135},{8... | collective-permute-start | bytes 393224 | tf_op jit(solution)/shard_map/ppermute | solution.py:25
  173.8 10.4 %collective-permute-start.29 = (bf16[64,1024]{1,0:T(8,128)(2,1)S(1)}, bf16[64,1024]{1,0:T(8,128)(2,1)S(1)}, u32[]{:S(2)}, u32[]{:S(2)}) collective-permute-start(bf16[64,1024]{1,0:T(8,128)(2,1)S(1)} %get-tuple-element.95), channel_id=1, source_target_pairs={{0,192},{1,193},{2,194},{3,195},{4,196},{5,197},{6,198},{7,199},{8... | collective-permute-start | bytes 393224 | tf_op jit(solution)/shard_map/ppermute | solution.py:25
  184.6 6.1 %collective-permute-start.32 = (bf16[448,128]{1,0:T(8,128)(2,1)S(1)}, bf16[448,128]{1,0:T(8,128)(2,1)S(1)}, u32[]{:S(2)}, u32[]{:S(2)}) collective-permute-start(bf16[448,128]{1,0:T(8,128)(2,1)S(1)} %get-tuple-element.97.refs_0_), channel_id=1, source_target_pairs={{0,12},{1,13},{2,14},{3,15},{4,0},{5,1},{6,2},{7,3},{8,4},{9,5},{1... | collective-permute-start | bytes 344072 | tf_op jit(solution)/shard_map/ppermute | solution.py:25
  185.0 7.0 %collective-permute-start.31 = (bf16[448,128]{1,0:T(8,128)(2,1)S(1)}, bf16[448,128]{1,0:T(8,128)(2,1)S(1)}, u32[]{:S(2)}, u32[]{:S(2)}) collective-permute-start(bf16[448,128]{1,0:T(8,128)(2,1)S(1)} %get-tuple-element.97.refs_0_), channel_id=1, source_target_pairs={{0,8},{1,9},{2,10},{3,11},{4,12},{5,13},{6,14},{7,15},{8,0},{9,1},... | collective-permute-start | bytes 344072 | tf_op jit(solution)/shard_map/ppermute | solution.py:25
  185.5 8.0 %collective-permute-start.30 = (bf16[448,128]{1,0:T(8,128)(2,1)S(1)}, bf16[448,128]{1,0:T(8,128)(2,1)S(1)}, u32[]{:S(2)}, u32[]{:S(2)}) collective-permute-start(bf16[448,128]{1,0:T(8,128)(2,1)S(1)} %get-tuple-element.97.refs_0_), channel_id=1, source_target_pairs={{0,4},{1,5},{2,6},{3,7},{4,8},{5,9},{6,10},{7,11},{8,12},{9,13},{1... | collective-permute-start | bytes 344072 | tf_op jit(solution)/shard_map/ppermute | solution.py:25
  193.6 9.3 %copy-start.8 = (s32[6]{0:T(128)S(1)}, s32[6]{0:T(128)}, u32[]{:S(2)}) copy-start(s32[6]{0:T(128)} %refs_6_.3) | copy-start | bytes 76
  193.6 5.6 %collective-permute-start.35 = (bf16[448,128]{1,0:T(8,128)(2,1)S(1)}, bf16[448,128]{1,0:T(8,128)(2,1)S(1)}, u32[]{:S(2)}, u32[]{:S(2)}) collective-permute-start(bf16[448,128]{1,0:T(8,128)(2,1)S(1)} %shard_map.102.refs_0_), channel_id=1, source_target_pairs={{0,3},{1,0},{2,1},{3,2},{4,7},{5,4},{6,5},{7,6},{8,11},{9,8},{10,9... | collective-permute-start | bytes 344072 | tf_op jit(solution)/shard_map/ppermute | solution.py:25
  196.0 6.3 %collective-permute-start.34 = (bf16[448,128]{1,0:T(8,128)(2,1)S(1)}, bf16[448,128]{1,0:T(8,128)(2,1)S(1)}, u32[]{:S(2)}, u32[]{:S(2)}) collective-permute-start(bf16[448,128]{1,0:T(8,128)(2,1)S(1)} %shard_map.102.refs_0_), channel_id=1, source_target_pairs={{0,2},{1,3},{2,0},{3,1},{4,6},{5,7},{6,4},{7,5},{8,10},{9,11},{10,... | collective-permute-start | bytes 344072 | tf_op jit(solution)/shard_map/ppermute | solution.py:25
  196.8 6.1 %collective-permute-start.33 = (bf16[448,128]{1,0:T(8,128)(2,1)S(1)}, bf16[448,128]{1,0:T(8,128)(2,1)S(1)}, u32[]{:S(2)}, u32[]{:S(2)}) collective-permute-start(bf16[448,128]{1,0:T(8,128)(2,1)S(1)} %shard_map.102.refs_0_), channel_id=1, source_target_pairs={{0,1},{1,2},{2,3},{3,0},{4,5},{5,6},{6,7},{7,4},{8,9},{9,10},{10,1... | collective-permute-start | bytes 344072 | tf_op jit(solution)/shard_map/ppermute | solution.py:25
  203.9 5.2 %collective-permute-start.36 = (bf16[64,256]{1,0:T(8,128)(2,1)S(1)}, bf16[64,256]{1,0:T(8,128)(2,1)S(1)}, u32[]{:S(2)}, u32[]{:S(2)}) collective-permute-start(bf16[64,256]{1,0:T(8,128)(2,1)S(1)} %get-tuple-element.100), channel_id=1, source_target_pairs={{0,3},{1,0},{2,1},{3,2},{4,7},{5,4},{6,5},{7,6},{8,11},{9,8},{10,9... | collective-permute-start | bytes 98312 | tf_op jit(solution)/shard_map/ppermute | solution.py:25
  207.0 5.4 %collective-permute-start.37 = (bf16[64,256]{1,0:T(8,128)(2,1)S(1)}, bf16[64,256]{1,0:T(8,128)(2,1)S(1)}, u32[]{:S(2)}, u32[]{:S(2)}) collective-permute-start(bf16[64,256]{1,0:T(8,128)(2,1)S(1)} %get-tuple-element.101), channel_id=1, source_target_pairs={{0,2},{1,3},{2,0},{3,1},{4,6},{5,7},{6,4},{7,5},{8,10},{9,11},{10,... | collective-permute-start | bytes 98312 | tf_op jit(solution)/shard_map/ppermute | solution.py:25
  207.0 5.4 %collective-permute-start.38 = (bf16[64,256]{1,0:T(8,128)(2,1)S(1)}, bf16[64,256]{1,0:T(8,128)(2,1)S(1)}, u32[]{:S(2)}, u32[]{:S(2)}) collective-permute-start(bf16[64,256]{1,0:T(8,128)(2,1)S(1)} %get-tuple-element.102), channel_id=1, source_target_pairs={{0,1},{1,2},{2,3},{3,0},{4,5},{5,6},{6,7},{7,4},{8,9},{9,10},{10,1... | collective-permute-start | bytes 98312 | tf_op jit(solution)/shard_map/ppermute | solution.py:25

commit v4 on v0

--- a/solution.py
+++ b/solution.py
@@ -157,11 +157,9 @@
         refs[-1][s * rows : (s + 1) * rows] = ref[...]
 
 
-def deal_kernel(lower_ref, upper_ref, *out_refs):
+def deal_kernel(inverse_ref, *out_refs):
     for s in range(SIDE):
-        tile = wrapped(own_tile() + s)
-        out_refs[s][...] = lower_ref[tile]
-        out_refs[SIDE + s][...] = upper_ref[tile]
+        out_refs[s][...] = inverse_ref[wrapped(own_tile() + s)]
 
 
 def turn_kernel(low_ref, up_ref, *out_refs):
@@ -390,41 +388,43 @@
     shape = jax.ShapeDtypeStruct
 
     height = n + slots * share
-    rows = kernel_call(pack_kernel, [shape((height, width), BF16)] * SIDE)(
-        right_sides, low_left, up_left
-    )
     tied = lax.optimization_barrier
-    rows = scattered_x(rows)
-    rows, inv_lower, inv_upper = tied((rows, inv_lower, inv_upper))
-    dealt = kernel_call(deal_kernel, [shape((width, width), BF16)] * 2 * SIDE)(
-        inv_lower, inv_upper
-    )
+    deal = kernel_call(deal_kernel, [shape((width, width), BF16)] * SIDE)
+    stack = kernel_call(stack_kernel, shape((total, width), BF16))
+    parts = scattered_x(deal(inv_lower))
+    rows = scattered_x(
+        kernel_call(pack_kernel, [shape((height, width), BF16)] * SIDE)(
+            right_sides, low_left, up_left
+        )
+    )
+    parts, rows = tied((parts, rows))
     rows = kernel_call(
         lambda *refs: order_kernel(1, *refs), shape((SIDE, height, width), BF16)
     )(*rows)
-    rows = swapped(rows)
-    stack = kernel_call(stack_kernel, shape((total, width), BF16))
-    lower = stack(*scattered_x(dealt[:SIDE]))
+    lower = stack(*parts)
+    rows, lower, inv_upper = tied((rows, lower, inv_upper))
     far_lower = swap_pair(lower)
-    upper_parts, lower = tied((dealt[SIDE:], lower))
-    upper = stack(*scattered_x(upper_parts))
-    near = (swap_core(lower), swap_core(upper))
+    parts, rows = tied((scattered_x(deal(inv_upper)), swapped(rows)))
+    upper = stack(*parts)
+    far_upper = swap_pair(upper)
     gathered = gathered_y(rows)
-    far_lower, upper, near, gathered = tied((far_lower, upper, near, gathered))
-    far_upper = swap_pair(upper)
-    lower = [lower, near[0], far_lower, swap_core(far_lower)]
-    low_right, up_right, gathered = tied((low_right, up_right, gathered))
+    gathered, far_lower, lower, near_upper = tied(
+        (gathered, far_lower, lower, swap_core(upper))
+    )
+    lower = [lower, swap_core(lower), far_lower, swap_core(far_lower)]
+    gathered, low_right, up_right = tied((gathered, low_right, up_right))
     turned = scattered_x(
         kernel_call(turn_kernel, [shape((slots * rank_cols, width), BF16)] * SIDE)(
             low_right, up_right
         )
     )
-    turned, far_upper = tied((turned, far_upper))
-    upper = [upper, near[1], far_upper, swap_core(far_upper)]
+    turned, far_upper, lower = tied((turned, far_upper, lower))
+    upper = [upper, near_upper, far_upper, swap_core(far_upper)]
+    received = scattered_q(products(n, gathered, *lower, *upper))
     dense, extra = kernel_call(
         lambda *refs: total_kernel(n, *refs),
         (shape((n, total), F32), shape((8, slots * share, total), BF16)),
-    )(*scattered_q(products(n, gathered, *lower, *upper)))
+    )(*received)
     mine = from_every_z(extra)
     packed = slots * n + 2 * rank_cols
     extra, send, later = kernel_call(

time: 213 us -> 209 us (0.981)
  waiting for transfers between devices: 90.6 us -> 86.3 us
    ppermute x48, waiting for transfers between devices: 90.6 us -> 86.3 us  [permuted(): return lax.ppermute(value, ('row', 'col'), routes(to))]
    pallas_call x16 -> x17, Pallas kernels: 9.1 us -> 9.11 us  [run(): pl.pallas_call(body, out_shape=out_shape, in_specs=specs, scratch_shapes=...]
  transfers between devices with their start and end apart: 48 -> 48, of which waited for: 36 -> 33; matrix products, arithmetic and copies ran while one was open for 0% -> 0% of each run, Pallas kernels for 0% -> 0%
where the time goes in v4:
time: 209 us; the launch traced here: 208 us
  starting transfers between devices  91.4 us (44%)
  waiting for transfers between devices  86.3 us (41%)
  blocking collectives  17.9 us (9%)
  Pallas kernels  9.11 us (4%)
  local copies, waits for them, and re-layouts  3.19 us (2%)
    ppermute x48, starting transfers between devices, permuted(): return lax.ppermute(value, ('row', 'col'), routes(to))  91.4 us
    ppermute x48, waiting for transfers between devices, permuted(): return lax.ppermute(value, ('row', 'col'), routes(to))  86.3 us
    all_to_all x1, blocking collectives, from_every_z(): lax.all_to_all(value, 'row', 0, 0, tiled=True, axis_index_groups=Z_GROUPS)  17.9 us
    pallas_call x17, Pallas kernels, run(): pl.pallas_call(body, out_shape=out_shape, in_specs=specs, scratch_shapes=...  9.11 us
  transfers between devices with their start and end apart: 48, of which 33 were waited for; matrix products, arithmetic and copies ran while one was open for 0% of the time, Pallas kernels for 0%

profile of v4, /device:TPU:2, one launch (start us, length us, event | category | flops | bytes accessed | tf_op | source)
XLA Modules:
  0.0 208.2 jit_solution(14636126824530633728)
XLA Ops:
  2.7 2.8 %collective-permute-start.1 = (bf16[256,256]{1,0:T(8,128)(2,1)S(1)}, bf16[256,256]{1,0:T(8,128)(2,1)S(1)}, u32[]{:S(2)}, u32[]{:S(2)}) collective-permute-start(bf16[256,256]{1,0:T(8,128)(2,1)S(1)} %get-tuple-element.80), channel_id=1, source_target_pairs={{0,2},{1,3},{2,0},{3,1},{4,6},{5,7},{6,4},{7,5},{8,10},{9,11},{10,... | collective-permute-start | bytes 393224 | tf_op jit(solution)/shard_map/ppermute | solution.py:25
  8.4 1.6 collective-permute-start.3
  10.0 1.9 collective-permute-start.4
  12.5 2.6 %collective-permute-start.5 = (bf16[88,256]{1,0:T(8,128)(2,1)S(1)}, bf16[88,256]{1,0:T(8,128)(2,1)S(1)}, u32[]{:S(2)}, u32[]{:S(2)}) collective-permute-start(bf16[88,256]{1,0:T(8,128)(2,1)S(1)} %get-tuple-element.85), channel_id=1, source_target_pairs={{0,3},{1,0},{2,1},{3,2},{4,7},{5,4},{6,5},{7,6},{8,11},{9,8},{10,9... | collective-permute-start | bytes 135176 | tf_op jit(solution)/shard_map/ppermute | solution.py:25
  19.3 3.1 %collective-permute-start.7 = (bf16[256,256]{1,0:T(8,128)(2,1)S(1)}, bf16[256,256]{1,0:T(8,128)(2,1)S(1)}, u32[]{:S(2)}, u32[]{:S(2)}) collective-permute-start(bf16[256,256]{1,0:T(8,128)(2,1)S(1)} %get-tuple-element.97), channel_id=1, source_target_pairs={{0,2},{1,3},{2,0},{3,1},{4,6},{5,7},{6,4},{7,5},{8,10},{9,11},{10,... | collective-permute-start | bytes 393224 | tf_op jit(solution)/shard_map/ppermute | solution.py:25
  23.0 1.9 collective-permute-start.13
  25.8 1.6 collective-permute-done.8.refs_3_
  27.5 10.1 %collective-permute-start.12 = (bf16[4,88,256]{2,1,0:T(8,128)(2,1)S(1)}, bf16[4,88,256]{2,1,0:T(8,128)(2,1)S(1)}, u32[]{:S(2)}, u32[]{:S(2)}) collective-permute-start(bf16[4,88,256]{2,1,0:T(8,128)(2,1)S(1)} %collective-permute-done.9.refs_0_), channel_id=1, source_target_pairs={{0,12},{1,13},{2,14},{3,15},{4,0},{5,1},{6,2},{7,3},{8,4},{9,5},{1... | collective-permute-start | bytes 540680 | tf_op jit(solution)/shard_map/ppermute | solution.py:25
  37.7 1.8 collective-permute-start.18
  40.0 6.0 %collective-permute-done.12.refs_3_ = bf16[4,88,256]{2,1,0:T(8,128)(2,1)S(1)} collective-permute-done((bf16[4,88,256]{2,1,0:T(8,128)(2,1)S(1)}, bf16[4,88,256]{2,1,0:T(8,128)(2,1)S(1)}, u32[]{:S(2)}, u32[]{:S(2)}) %collective-permute-start.12) | collective-permute-done | bytes 180256 | tf_op jit(solution)/shard_map/ppermute | solution.py:25
  47.3 6.7 %collective-permute-done.10.refs_1_ = bf16[4,88,256]{2,1,0:T(8,128)(2,1)S(1)} collective-permute-done((bf16[4,88,256]{2,1,0:T(8,128)(2,1)S(1)}, bf16[4,88,256]{2,1,0:T(8,128)(2,1)S(1)}, u32[]{:S(2)}, u32[]{:S(2)}) %collective-permute-start.10) | collective-permute-done | bytes 180256 | tf_op jit(solution)/shard_map/ppermute | solution.py:25
  55.2 3.6 %collective-permute-start.16 = (bf16[384,256]{1,0:T(8,128)(2,1)S(1)}, bf16[384,256]{1,0:T(8,128)(2,1)S(1)}, u32[]{:S(2)}, u32[]{:S(2)}) collective-permute-start(bf16[384,256]{1,0:T(8,128)(2,1)S(1)} %get-tuple-element.118), channel_id=1, source_target_pairs={{0,2},{1,3},{2,0},{3,1},{4,6},{5,7},{6,4},{7,5},{8,10},{9,11},{10,... | collective-permute-start | bytes 589832 | tf_op jit(solution)/shard_map/ppermute | solution.py:25
  60.4 2.5 %collective-permute-done.15.refs_1_.refs_5_ = bf16[384,256]{1,0:T(8,128)(2,1)S(1)} collective-permute-done((bf16[384,256]{1,0:T(8,128)(2,1)S(1)}, bf16[384,256]{1,0:T(8,128)(2,1)S(1)}, u32[]{:S(2)}, u32[]{:S(2)}) %collective-permute-start.15) | collective-permute-done | bytes 196640 | tf_op jit(solution)/shard_map/ppermute | solution.py:25
  62.9 1.7 collective-permute-done.16.refs_2_.refs_6_
  64.7 3.3 %collective-permute-done.17.refs_3_.refs_7_ = bf16[384,256]{1,0:T(8,128)(2,1)S(1)} collective-permute-done((bf16[384,256]{1,0:T(8,128)(2,1)S(1)}, bf16[384,256]{1,0:T(8,128)(2,1)S(1)}, u32[]{:S(2)}, u32[]{:S(2)}) %collective-permute-start.17) | collective-permute-done | bytes 196640 | tf_op jit(solution)/shard_map/ppermute | solution.py:25
  68.0 1.9 collective-permute-done.21.refs_11_.refs_7_
  69.9 2.4 %shard_map.98 = (bf16[88,1024]{1,0:T(8,128)(2,1)S(1)}, bf16[88,1024]{1,0:T(8,128)(2,1)S(1)}, bf16[88,1024]{1,0:T(8,128)(2,1)S(1)}, bf16[88,1024]{1,0:T(8,128)(2,1)S(1)}) custom-call(bf16[4,88,256]{2,1,0:T(8,128)(2,1)S(1)} %collective-permute-done.9.refs_0_, bf16[4,88,256]{2,1,0:T(8,128)(2,1)S(1)} %collective-permute-done.10.refs_1_, ...), custom_call_target="tpu_custom_call" | custom-call | flops 738197504 | bytes 5636096 | tf_op jit(solution)/shard_map/pallas_call | solution.py:106
  72.3 3.4 %collective-permute-start.22 = (bf16[88,1024]{1,0:T(8,128)(2,1)S(1)}, bf16[88,1024]{1,0:T(8,128)(2,1)S(1)}, u32[]{:S(2)}, u32[]{:S(2)}) collective-permute-start(bf16[88,1024]{1,0:T(8,128)(2,1)S(1)} %get-tuple-element.129), channel_id=1, source_target_pairs={{0,64},{1,65},{2,66},{3,67},{4,68},{5,69},{6,70},{7,71},{8,72},{9,... | collective-permute-start | bytes 540680 | tf_op jit(solution)/shard_map/ppermute | solution.py:25
  75.7 2.4 %collective-permute-start.23 = (bf16[88,1024]{1,0:T(8,128)(2,1)S(1)}, bf16[88,1024]{1,0:T(8,128)(2,1)S(1)}, u32[]{:S(2)}, u32[]{:S(2)}) collective-permute-start(bf16[88,1024]{1,0:T(8,128)(2,1)S(1)} %get-tuple-element.130), channel_id=1, source_target_pairs={{0,128},{1,129},{2,130},{3,131},{4,132},{5,133},{6,134},{7,135},{8... | collective-permute-start | bytes 540680 | tf_op jit(solution)/shard_map/ppermute | solution.py:25
  78.0 4.0 %collective-permute-start.24 = (bf16[88,1024]{1,0:T(8,128)(2,1)S(1)}, bf16[88,1024]{1,0:T(8,128)(2,1)S(1)}, u32[]{:S(2)}, u32[]{:S(2)}) collective-permute-start(bf16[88,1024]{1,0:T(8,128)(2,1)S(1)} %get-tuple-element.131), channel_id=1, source_target_pairs={{0,192},{1,193},{2,194},{3,195},{4,196},{5,197},{6,198},{7,199},{8... | collective-permute-start | bytes 540680 | tf_op jit(solution)/shard_map/ppermute | solution.py:25
  82.1 2.1 %collective-permute-done.22.refs_1_ = bf16[88,1024]{1,0:T(8,128)(2,1)S(1)} collective-permute-done((bf16[88,1024]{1,0:T(8,128)(2,1)S(1)}, bf16[88,1024]{1,0:T(8,128)(2,1)S(1)}, u32[]{:S(2)}, u32[]{:S(2)}) %collective-permute-start.22) | collective-permute-done | bytes 180256 | tf_op jit(solution)/shard_map/ppermute | solution.py:25
  84.2 8.7 %collective-permute-done.23.refs_2_ = bf16[88,1024]{1,0:T(8,128)(2,1)S(1)} collective-permute-done((bf16[88,1024]{1,0:T(8,128)(2,1)S(1)}, bf16[88,1024]{1,0:T(8,128)(2,1)S(1)}, u32[]{:S(2)}, u32[]{:S(2)}) %collective-permute-start.23) | collective-permute-done | bytes 180256 | tf_op jit(solution)/shard_map/ppermute | solution.py:25
  92.9 3.6 %collective-permute-done.24.refs_3_ = bf16[88,1024]{1,0:T(8,128)(2,1)S(1)} collective-permute-done((bf16[88,1024]{1,0:T(8,128)(2,1)S(1)}, bf16[88,1024]{1,0:T(8,128)(2,1)S(1)}, u32[]{:S(2)}, u32[]{:S(2)}) %collective-permute-start.24) | collective-permute-done | bytes 180256 | tf_op jit(solution)/shard_map/ppermute | solution.py:25
  96.6 17.9 %all_to_all.5.mine_ref = bf16[8,24,1024]{2,1,0:T(8,128)(2,1)S(1)} all-to-all(bf16[8,24,1024]{2,1,0:T(8,128)(2,1)S(1)} %get-tuple-element.133), channel_id=1, replica_groups={{0,32,64,96,128,160,192,224},{16,48,80,112,144,176,208,240},{1,33,65,97..., dimensions={0} | all-to-all | bytes 786432 | tf_op jit(solution)/shard_map/all_to_all | solution.py:55
  114.5 1.7 collective-permute-done.25.other_ref
  117.0 1.6 collective-permute-start.28
  120.9 2.2 %collective-permute-done.28.refs_3_ = bf16[448,128]{1,0:T(8,128)(2,1)S(1)} collective-permute-done((bf16[448,128]{1,0:T(8,128)(2,1)S(1)}, bf16[448,128]{1,0:T(8,128)(2,1)S(1)}, u32[]{:S(2)}, u32[]{:S(2)}) %collective-permute-start.28) | collective-permute-done | bytes 114720 | tf_op jit(solution)/shard_map/ppermute | solution.py:25
  123.0 3.1 %collective-permute-done.27.refs_2_ = bf16[448,128]{1,0:T(8,128)(2,1)S(1)} collective-permute-done((bf16[448,128]{1,0:T(8,128)(2,1)S(1)}, bf16[448,128]{1,0:T(8,128)(2,1)S(1)}, u32[]{:S(2)}, u32[]{:S(2)}) %collective-permute-start.27) | collective-permute-done | bytes 114720 | tf_op jit(solution)/shard_map/ppermute | solution.py:25
  127.5 1.8 collective-permute-start.31
  130.9 2.5 %collective-permute-start.29 = (bf16[448,128]{1,0:T(8,128)(2,1)S(1)}, bf16[448,128]{1,0:T(8,128)(2,1)S(1)}, u32[]{:S(2)}, u32[]{:S(2)}) collective-permute-start(bf16[448,128]{1,0:T(8,128)(2,1)S(1)} %shard_map.101.refs_0_), channel_id=1, source_target_pairs={{0,1},{1,2},{2,3},{3,0},{4,5},{5,6},{6,7},{7,4},{8,9},{9,10},{10,1... | collective-permute-start | bytes 344072 | tf_op jit(solution)/shard_map/ppermute | solution.py:25
  133.4 3.0 %collective-permute-done.30.refs_2_ = bf16[448,128]{1,0:T(8,128)(2,1)S(1)} collective-permute-done((bf16[448,128]{1,0:T(8,128)(2,1)S(1)}, bf16[448,128]{1,0:T(8,128)(2,1)S(1)}, u32[]{:S(2)}, u32[]{:S(2)}) %collective-permute-start.30) | collective-permute-done | bytes 114720 | tf_op jit(solution)/shard_map/ppermute | solution.py:25
  139.1 11.5 %collective-permute-start.35 = (bf16[4,64,256]{2,1,0:T(8,128)(2,1)S(1)}, bf16[4,64,256]{2,1,0:T(8,128)(2,1)S(1)}, u32[]{:S(2)}, u32[]{:S(2)}) collective-permute-start(bf16[4,64,256]{2,1,0:T(8,128)(2,1)S(1)} %collective-permute-done.32.refs_0_), channel_id=1, source_target_pairs={{0,12},{1,13},{2,14},{3,15},{4,0},{5,1},{6,2},{7,3},{8,4},{9,5},{1... | collective-permute-start | bytes 393224 | tf_op jit(solution)/shard_map/ppermute | solution.py:25
  150.6 1.7 collective-permute-start.34
  154.2 3.8 %collective-permute-done.34.refs_2_ = bf16[4,64,256]{2,1,0:T(8,128)(2,1)S(1)} collective-permute-done((bf16[4,64,256]{2,1,0:T(8,128)(2,1)S(1)}, bf16[4,64,256]{2,1,0:T(8,128)(2,1)S(1)}, u32[]{:S(2)}, u32[]{:S(2)}) %collective-permute-start.34) | collective-permute-done | bytes 131104 | tf_op jit(solution)/shard_map/ppermute | solution.py:25
  160.8 1.8 collective-permute-start.36
  162.6 5.0 %collective-permute-start.37 = (bf16[64,1024]{1,0:T(8,128)(2,1)S(1)}, bf16[64,1024]{1,0:T(8,128)(2,1)S(1)}, u32[]{:S(2)}, u32[]{:S(2)}) collective-permute-start(bf16[64,1024]{1,0:T(8,128)(2,1)S(1)} %get-tuple-element.142), channel_id=1, source_target_pairs={{0,128},{1,129},{2,130},{3,131},{4,132},{5,133},{6,134},{7,135},{8... | collective-permute-start | bytes 393224 | tf_op jit(solution)/shard_map/ppermute | solution.py:25
  167.6 2.0 collective-permute-done.36.refs_1_
  169.6 9.2 %collective-permute-done.37.refs_2_ = bf16[64,1024]{1,0:T(8,128)(2,1)S(1)} collective-permute-done((bf16[64,1024]{1,0:T(8,128)(2,1)S(1)}, bf16[64,1024]{1,0:T(8,128)(2,1)S(1)}, u32[]{:S(2)}, u32[]{:S(2)}) %collective-permute-start.37) | collective-permute-done | bytes 131104 | tf_op jit(solution)/shard_map/ppermute | solution.py:25
  179.4 1.9 collective-permute-start.39
  181.3 4.0 %collective-permute-done.41.refs_3_ = bf16[448,128]{1,0:T(8,128)(2,1)S(1)} collective-permute-done((bf16[448,128]{1,0:T(8,128)(2,1)S(1)}, bf16[448,128]{1,0:T(8,128)(2,1)S(1)}, u32[]{:S(2)}, u32[]{:S(2)}) %collective-permute-start.41) | collective-permute-done | bytes 114720 | tf_op jit(solution)/shard_map/ppermute | solution.py:25
  186.4 2.0 collective-permute-done.39.refs_1_
  188.4 3.3 %collective-permute-start.44 = (bf16[448,128]{1,0:T(8,128)(2,1)S(1)}, bf16[448,128]{1,0:T(8,128)(2,1)S(1)}, u32[]{:S(2)}, u32[]{:S(2)}) collective-permute-start(bf16[448,128]{1,0:T(8,128)(2,1)S(1)} %shard_map.105.refs_0_), channel_id=1, source_target_pairs={{0,3},{1,0},{2,1},{3,2},{4,7},{5,4},{6,5},{7,6},{8,11},{9,8},{10,9... | collective-permute-start | bytes 344072 | tf_op jit(solution)/shard_map/ppermute | solution.py:25
  191.9 1.7 collective-permute-start.42
  193.6 1.7 collective-permute-done.44.refs_3_
  195.2 2.7 %collective-permute-done.43.refs_2_ = bf16[448,128]{1,0:T(8,128)(2,1)S(1)} collective-permute-done((bf16[448,128]{1,0:T(8,128)(2,1)S(1)}, bf16[448,128]{1,0:T(8,128)(2,1)S(1)}, u32[]{:S(2)}, u32[]{:S(2)}) %collective-permute-start.43) | collective-permute-done | bytes 114720 | tf_op jit(solution)/shard_map/ppermute | solution.py:25
  199.2 2.8 %collective-permute-start.45 = (bf16[64,256]{1,0:T(8,128)(2,1)S(1)}, bf16[64,256]{1,0:T(8,128)(2,1)S(1)}, u32[]{:S(2)}, u32[]{:S(2)}) collective-permute-start(bf16[64,256]{1,0:T(8,128)(2,1)S(1)} %get-tuple-element.148), channel_id=1, source_target_pairs={{0,3},{1,0},{2,1},{3,2},{4,7},{5,4},{6,5},{7,6},{8,11},{9,8},{10,9... | collective-permute-start | bytes 98312 | tf_op jit(solution)/shard_map/ppermute | solution.py:25
  202.2 2.1 %collective-permute-start.47 = (bf16[64,256]{1,0:T(8,128)(2,1)S(1)}, bf16[64,256]{1,0:T(8,128)(2,1)S(1)}, u32[]{:S(2)}, u32[]{:S(2)}) collective-permute-start(bf16[64,256]{1,0:T(8,128)(2,1)S(1)} %get-tuple-element.150), channel_id=1, source_target_pairs={{0,1},{1,2},{2,3},{3,0},{4,5},{5,6},{6,7},{7,4},{8,9},{9,10},{10,1... | collective-permute-start | bytes 98312 | tf_op jit(solution)/shard_map/ppermute | solution.py:25
  204.3 3.2 %collective-permute-done.46.refs_2_ = bf16[64,256]{1,0:T(8,128)(2,1)S(1)} collective-permute-done((bf16[64,256]{1,0:T(8,128)(2,1)S(1)}, bf16[64,256]{1,0:T(8,128)(2,1)S(1)}, u32[]{:S(2)}, u32[]{:S(2)}) %collective-permute-start.46) | collective-permute-done | bytes 32800 | tf_op jit(solution)/shard_map/ppermute | solution.py:25
  (84 shorter events, 33.8 us)
Async XLA Ops:
  1.1 15.7 %collective-permute-start = (bf16[256,256]{1,0:T(8,128)(2,1)S(1)}, bf16[256,256]{1,0:T(8,128)(2,1)S(1)}, u32[]{:S(2)}, u32[]{:S(2)}) collective-permute-start(bf16[256,256]{1,0:T(8,128)(2,1)S(1)} %get-tuple-element.79), channel_id=1, source_target_pairs={{0,1},{1,2},{2,3},{3,0},{4,5},{5,6},{6,7},{7,4},{8,9},{9,10},{10,1... | collective-permute-start | bytes 393224 | tf_op jit(solution)/shard_map/ppermute | solution.py:25
  2.7 14.2 %collective-permute-start.1 = (bf16[256,256]{1,0:T(8,128)(2,1)S(1)}, bf16[256,256]{1,0:T(8,128)(2,1)S(1)}, u32[]{:S(2)}, u32[]{:S(2)}) collective-permute-start(bf16[256,256]{1,0:T(8,128)(2,1)S(1)} %get-tuple-element.80), channel_id=1, source_target_pairs={{0,2},{1,3},{2,0},{3,1},{4,6},{5,7},{6,4},{7,5},{8,10},{9,11},{10,... | collective-permute-start | bytes 393224 | tf_op jit(solution)/shard_map/ppermute | solution.py:25
  5.5 11.3 %collective-permute-start.2 = (bf16[256,256]{1,0:T(8,128)(2,1)S(1)}, bf16[256,256]{1,0:T(8,128)(2,1)S(1)}, u32[]{:S(2)}, u32[]{:S(2)}) collective-permute-start(bf16[256,256]{1,0:T(8,128)(2,1)S(1)} %get-tuple-element.81), channel_id=1, source_target_pairs={{0,3},{1,0},{2,1},{3,2},{4,7},{5,4},{6,5},{7,6},{8,11},{9,8},{10,9... | collective-permute-start | bytes 393224 | tf_op jit(solution)/shard_map/ppermute | solution.py:25
  8.4 4.1 %collective-permute-start.3 = (bf16[88,256]{1,0:T(8,128)(2,1)S(1)}, bf16[88,256]{1,0:T(8,128)(2,1)S(1)}, u32[]{:S(2)}, u32[]{:S(2)}) collective-permute-start(bf16[88,256]{1,0:T(8,128)(2,1)S(1)} %get-tuple-element.83), channel_id=1, source_target_pairs={{0,1},{1,2},{2,3},{3,0},{4,5},{5,6},{6,7},{7,4},{8,9},{9,10},{10,1... | collective-permute-start | bytes 135176 | tf_op jit(solution)/shard_map/ppermute | solution.py:25
  10.0 5.6 %collective-permute-start.4 = (bf16[88,256]{1,0:T(8,128)(2,1)S(1)}, bf16[88,256]{1,0:T(8,128)(2,1)S(1)}, u32[]{:S(2)}, u32[]{:S(2)}) collective-permute-start(bf16[88,256]{1,0:T(8,128)(2,1)S(1)} %get-tuple-element.84), channel_id=1, source_target_pairs={{0,2},{1,3},{2,0},{3,1},{4,6},{5,7},{6,4},{7,5},{8,10},{9,11},{10,... | collective-permute-start | bytes 135176 | tf_op jit(solution)/shard_map/ppermute | solution.py:25
  12.5 4.4 %collective-permute-start.5 = (bf16[88,256]{1,0:T(8,128)(2,1)S(1)}, bf16[88,256]{1,0:T(8,128)(2,1)S(1)}, u32[]{:S(2)}, u32[]{:S(2)}) collective-permute-start(bf16[88,256]{1,0:T(8,128)(2,1)S(1)} %get-tuple-element.85), channel_id=1, source_target_pairs={{0,3},{1,0},{2,1},{3,2},{4,7},{5,4},{6,5},{7,6},{8,11},{9,8},{10,9... | collective-permute-start | bytes 135176 | tf_op jit(solution)/shard_map/ppermute | solution.py:25
  16.9 10.5 %collective-permute-start.9 = (bf16[4,88,256]{2,1,0:T(8,128)(2,1)S(1)}, bf16[4,88,256]{2,1,0:T(8,128)(2,1)S(1)}, u32[]{:S(2)}, u32[]{:S(2)}) collective-permute-start(bf16[4,88,256]{2,1,0:T(8,128)(2,1)S(1)} %shard_map.93), channel_id=1, source_target_pairs={{0,0},{1,1},{2,2},{3,3},{4,64},{5,65},{6,66},{7,67},{8,128},{9,129... | collective-permute-start | bytes 540680 | tf_op jit(solution)/shard_map/ppermute | solution.py:25
  17.9 7.0 %collective-permute-start.6 = (bf16[256,256]{1,0:T(8,128)(2,1)S(1)}, bf16[256,256]{1,0:T(8,128)(2,1)S(1)}, u32[]{:S(2)}, u32[]{:S(2)}) collective-permute-start(bf16[256,256]{1,0:T(8,128)(2,1)S(1)} %get-tuple-element.96), channel_id=1, source_target_pairs={{0,1},{1,2},{2,3},{3,0},{4,5},{5,6},{6,7},{7,4},{8,9},{9,10},{10,1... | collective-permute-start | bytes 393224 | tf_op jit(solution)/shard_map/ppermute | solution.py:25
  19.3 6.5 %collective-permute-start.7 = (bf16[256,256]{1,0:T(8,128)(2,1)S(1)}, bf16[256,256]{1,0:T(8,128)(2,1)S(1)}, u32[]{:S(2)}, u32[]{:S(2)}) collective-permute-start(bf16[256,256]{1,0:T(8,128)(2,1)S(1)} %get-tuple-element.97), channel_id=1, source_target_pairs={{0,2},{1,3},{2,0},{3,1},{4,6},{5,7},{6,4},{7,5},{8,10},{9,11},{10,... | collective-permute-start | bytes 393224 | tf_op jit(solution)/shard_map/ppermute | solution.py:25
  22.4 5.0 %collective-permute-start.8 = (bf16[256,256]{1,0:T(8,128)(2,1)S(1)}, bf16[256,256]{1,0:T(8,128)(2,1)S(1)}, u32[]{:S(2)}, u32[]{:S(2)}) collective-permute-start(bf16[256,256]{1,0:T(8,128)(2,1)S(1)} %get-tuple-element.98), channel_id=1, source_target_pairs={{0,3},{1,0},{2,1},{3,2},{4,7},{5,4},{6,5},{7,6},{8,11},{9,8},{10,9... | collective-permute-start | bytes 393224 | tf_op jit(solution)/shard_map/ppermute | solution.py:25
  23.0 31.0 %collective-permute-start.13 = (bf16[1024,256]{1,0:T(8,128)(2,1)S(1)}, bf16[1024,256]{1,0:T(8,128)(2,1)S(1)}, u32[]{:S(2)}, u32[]{:S(2)}) collective-permute-start(bf16[1024,256]{1,0:T(8,128)(2,1)S(1)} %shard_map.94.refs_4_), channel_id=1, source_target_pairs={{0,32},{1,33},{2,34},{3,35},{4,36},{5,37},{6,38},{7,39},{8,40},{9,... | collective-permute-start | bytes 1572872 | tf_op jit(solution)/shard_map/ppermute | solution.py:25
  27.4 26.6 %collective-permute-start.14 = (bf16[1024,256]{1,0:T(8,128)(2,1)S(1)}, bf16[1024,256]{1,0:T(8,128)(2,1)S(1)}, u32[]{:S(2)}, u32[]{:S(2)}) collective-permute-start(bf16[1024,256]{1,0:T(8,128)(2,1)S(1)} %shard_map.96.refs_8_.refs_4_), channel_id=1, source_target_pairs={{0,16},{1,17},{2,18},{3,19},{4,20},{5,21},{6,22},{7,23},{8,24},{9,... | collective-permute-start | bytes 1572872 | tf_op jit(solution)/shard_map/ppermute | solution.py:25
  27.5 18.4 %collective-permute-start.12 = (bf16[4,88,256]{2,1,0:T(8,128)(2,1)S(1)}, bf16[4,88,256]{2,1,0:T(8,128)(2,1)S(1)}, u32[]{:S(2)}, u32[]{:S(2)}) collective-permute-start(bf16[4,88,256]{2,1,0:T(8,128)(2,1)S(1)} %collective-permute-done.9.refs_0_), channel_id=1, source_target_pairs={{0,12},{1,13},{2,14},{3,15},{4,0},{5,1},{6,2},{7,3},{8,4},{9,5},{1... | collective-permute-start | bytes 540680 | tf_op jit(solution)/shard_map/ppermute | solution.py:25
  37.7 21.2 %collective-permute-start.18 = (bf16[1024,256]{1,0:T(8,128)(2,1)S(1)}, bf16[1024,256]{1,0:T(8,128)(2,1)S(1)}, u32[]{:S(2)}, u32[]{:S(2)}) collective-permute-start(bf16[1024,256]{1,0:T(8,128)(2,1)S(1)} %shard_map.96.refs_8_.refs_4_), channel_id=1, source_target_pairs={{0,32},{1,33},{2,34},{3,35},{4,36},{5,37},{6,38},{7,39},{8,40},{9,... | collective-permute-start | bytes 1572872 | tf_op jit(solution)/shard_map/ppermute | solution.py:25
  39.5 7.8 %collective-permute-start.11 = (bf16[4,88,256]{2,1,0:T(8,128)(2,1)S(1)}, bf16[4,88,256]{2,1,0:T(8,128)(2,1)S(1)}, u32[]{:S(2)}, u32[]{:S(2)}) collective-permute-start(bf16[4,88,256]{2,1,0:T(8,128)(2,1)S(1)} %collective-permute-done.9.refs_0_), channel_id=1, source_target_pairs={{0,8},{1,9},{2,10},{3,11},{4,12},{5,13},{6,14},{7,15},{8,0},{9,1},... | collective-permute-start | bytes 540680 | tf_op jit(solution)/shard_map/ppermute | solution.py:25
  46.0 8.0 %collective-permute-start.10 = (bf16[4,88,256]{2,1,0:T(8,128)(2,1)S(1)}, bf16[4,88,256]{2,1,0:T(8,128)(2,1)S(1)}, u32[]{:S(2)}, u32[]{:S(2)}) collective-permute-start(bf16[4,88,256]{2,1,0:T(8,128)(2,1)S(1)} %collective-permute-done.9.refs_0_), channel_id=1, source_target_pairs={{0,4},{1,5},{2,6},{3,7},{4,8},{5,9},{6,10},{7,11},{8,12},{9,13},{1... | collective-permute-start | bytes 540680 | tf_op jit(solution)/shard_map/ppermute | solution.py:25
  54.0 14.0 %collective-permute-start.19 = (bf16[1024,256]{1,0:T(8,128)(2,1)S(1)}, bf16[1024,256]{1,0:T(8,128)(2,1)S(1)}, u32[]{:S(2)}, u32[]{:S(2)}) collective-permute-start(bf16[1024,256]{1,0:T(8,128)(2,1)S(1)} %shard_map.94.refs_4_), channel_id=1, source_target_pairs={{0,16},{1,17},{2,18},{3,19},{4,20},{5,21},{6,22},{7,23},{8,24},{9,... | collective-permute-start | bytes 1572872 | tf_op jit(solution)/shard_map/ppermute | solution.py:25
  54.0 14.0 %collective-permute-start.20 = (bf16[1024,256]{1,0:T(8,128)(2,1)S(1)}, bf16[1024,256]{1,0:T(8,128)(2,1)S(1)}, u32[]{:S(2)}, u32[]{:S(2)}) collective-permute-start(bf16[1024,256]{1,0:T(8,128)(2,1)S(1)} %collective-permute-done.13.refs_6_), channel_id=1, source_target_pairs={{0,16},{1,17},{2,18},{3,19},{4,20},{5,21},{6,22},{7,23},{8,24},{9,... | collective-permute-start | bytes 1572872 | tf_op jit(solution)/shard_map/ppermute | solution.py:25
  54.9 8.0 %collective-permute-start.15 = (bf16[384,256]{1,0:T(8,128)(2,1)S(1)}, bf16[384,256]{1,0:T(8,128)(2,1)S(1)}, u32[]{:S(2)}, u32[]{:S(2)}) collective-permute-start(bf16[384,256]{1,0:T(8,128)(2,1)S(1)} %get-tuple-element.117), channel_id=1, source_target_pairs={{0,1},{1,2},{2,3},{3,0},{4,5},{5,6},{6,7},{7,4},{8,9},{9,10},{10,1... | collective-permute-start | bytes 589832 | tf_op jit(solution)/shard_map/ppermute | solution.py:25
  55.2 9.4 %collective-permute-start.16 = (bf16[384,256]{1,0:T(8,128)(2,1)S(1)}, bf16[384,256]{1,0:T(8,128)(2,1)S(1)}, u32[]{:S(2)}, u32[]{:S(2)}) collective-permute-start(bf16[384,256]{1,0:T(8,128)(2,1)S(1)} %get-tuple-element.118), channel_id=1, source_target_pairs={{0,2},{1,3},{2,0},{3,1},{4,6},{5,7},{6,4},{7,5},{8,10},{9,11},{10,... | collective-permute-start | bytes 589832 | tf_op jit(solution)/shard_map/ppermute | solution.py:25
  58.9 9.1 %collective-permute-start.17 = (bf16[384,256]{1,0:T(8,128)(2,1)S(1)}, bf16[384,256]{1,0:T(8,128)(2,1)S(1)}, u32[]{:S(2)}, u32[]{:S(2)}) collective-permute-start(bf16[384,256]{1,0:T(8,128)(2,1)S(1)} %get-tuple-element.119), channel_id=1, source_target_pairs={{0,3},{1,0},{2,1},{3,2},{4,7},{5,4},{6,5},{7,6},{8,11},{9,8},{10,9... | collective-permute-start | bytes 589832 | tf_op jit(solution)/shard_map/ppermute | solution.py:25
  68.0 1.9 collective-permute-start.21
  72.3 11.9 %collective-permute-start.22 = (bf16[88,1024]{1,0:T(8,128)(2,1)S(1)}, bf16[88,1024]{1,0:T(8,128)(2,1)S(1)}, u32[]{:S(2)}, u32[]{:S(2)}) collective-permute-start(bf16[88,1024]{1,0:T(8,128)(2,1)S(1)} %get-tuple-element.129), channel_id=1, source_target_pairs={{0,64},{1,65},{2,66},{3,67},{4,68},{5,69},{6,70},{7,71},{8,72},{9,... | collective-permute-start | bytes 540680 | tf_op jit(solution)/shard_map/ppermute | solution.py:25
  75.7 17.3 %collective-permute-start.23 = (bf16[88,1024]{1,0:T(8,128)(2,1)S(1)}, bf16[88,1024]{1,0:T(8,128)(2,1)S(1)}, u32[]{:S(2)}, u32[]{:S(2)}) collective-permute-start(bf16[88,1024]{1,0:T(8,128)(2,1)S(1)} %get-tuple-element.130), channel_id=1, source_target_pairs={{0,128},{1,129},{2,130},{3,131},{4,132},{5,133},{6,134},{7,135},{8... | collective-permute-start | bytes 540680 | tf_op jit(solution)/shard_map/ppermute | solution.py:25
  78.0 18.5 %collective-permute-start.24 = (bf16[88,1024]{1,0:T(8,128)(2,1)S(1)}, bf16[88,1024]{1,0:T(8,128)(2,1)S(1)}, u32[]{:S(2)}, u32[]{:S(2)}) collective-permute-start(bf16[88,1024]{1,0:T(8,128)(2,1)S(1)} %get-tuple-element.131), channel_id=1, source_target_pairs={{0,192},{1,193},{2,194},{3,195},{4,196},{5,197},{6,198},{7,199},{8... | collective-permute-start | bytes 540680 | tf_op jit(solution)/shard_map/ppermute | solution.py:25
  114.5 1.7 collective-permute-start.25
  117.0 6.1 %collective-permute-start.28 = (bf16[448,128]{1,0:T(8,128)(2,1)S(1)}, bf16[448,128]{1,0:T(8,128)(2,1)S(1)}, u32[]{:S(2)}, u32[]{:S(2)}) collective-permute-start(bf16[448,128]{1,0:T(8,128)(2,1)S(1)} %get-tuple-element.138.refs_0_), channel_id=1, source_target_pairs={{0,12},{1,13},{2,14},{3,15},{4,0},{5,1},{6,2},{7,3},{8,4},{9,5},{1... | collective-permute-start | bytes 344072 | tf_op jit(solution)/shard_map/ppermute | solution.py:25
  118.6 7.5 %collective-permute-start.27 = (bf16[448,128]{1,0:T(8,128)(2,1)S(1)}, bf16[448,128]{1,0:T(8,128)(2,1)S(1)}, u32[]{:S(2)}, u32[]{:S(2)}) collective-permute-start(bf16[448,128]{1,0:T(8,128)(2,1)S(1)} %get-tuple-element.138.refs_0_), channel_id=1, source_target_pairs={{0,8},{1,9},{2,10},{3,11},{4,12},{5,13},{6,14},{7,15},{8,0},{9,1},... | collective-permute-start | bytes 344072 | tf_op jit(solution)/shard_map/ppermute | solution.py:25
  119.8 7.7 %collective-permute-start.26 = (bf16[448,128]{1,0:T(8,128)(2,1)S(1)}, bf16[448,128]{1,0:T(8,128)(2,1)S(1)}, u32[]{:S(2)}, u32[]{:S(2)}) collective-permute-start(bf16[448,128]{1,0:T(8,128)(2,1)S(1)} %get-tuple-element.138.refs_0_), channel_id=1, source_target_pairs={{0,4},{1,5},{2,6},{3,7},{4,8},{5,9},{6,10},{7,11},{8,12},{9,13},{1... | collective-permute-start | bytes 344072 | tf_op jit(solution)/shard_map/ppermute | solution.py:25
  127.5 5.9 %collective-permute-start.31 = (bf16[448,128]{1,0:T(8,128)(2,1)S(1)}, bf16[448,128]{1,0:T(8,128)(2,1)S(1)}, u32[]{:S(2)}, u32[]{:S(2)}) collective-permute-start(bf16[448,128]{1,0:T(8,128)(2,1)S(1)} %shard_map.101.refs_0_), channel_id=1, source_target_pairs={{0,3},{1,0},{2,1},{3,2},{4,7},{5,4},{6,5},{7,6},{8,11},{9,8},{10,9... | collective-permute-start | bytes 344072 | tf_op jit(solution)/shard_map/ppermute | solution.py:25
  129.3 7.1 %collective-permute-start.30 = (bf16[448,128]{1,0:T(8,128)(2,1)S(1)}, bf16[448,128]{1,0:T(8,128)(2,1)S(1)}, u32[]{:S(2)}, u32[]{:S(2)}) collective-permute-start(bf16[448,128]{1,0:T(8,128)(2,1)S(1)} %shard_map.101.refs_0_), channel_id=1, source_target_pairs={{0,2},{1,3},{2,0},{3,1},{4,6},{5,7},{6,4},{7,5},{8,10},{9,11},{10,... | collective-permute-start | bytes 344072 | tf_op jit(solution)/shard_map/ppermute | solution.py:25
  130.9 6.4 %collective-permute-start.29 = (bf16[448,128]{1,0:T(8,128)(2,1)S(1)}, bf16[448,128]{1,0:T(8,128)(2,1)S(1)}, u32[]{:S(2)}, u32[]{:S(2)}) collective-permute-start(bf16[448,128]{1,0:T(8,128)(2,1)S(1)} %shard_map.101.refs_0_), channel_id=1, source_target_pairs={{0,1},{1,2},{2,3},{3,0},{4,5},{5,6},{6,7},{7,4},{8,9},{9,10},{10,1... | collective-permute-start | bytes 344072 | tf_op jit(solution)/shard_map/ppermute | solution.py:25
  138.4 0.7 collective-permute-start.32
  139.1 15.1 %collective-permute-start.35 = (bf16[4,64,256]{2,1,0:T(8,128)(2,1)S(1)}, bf16[4,64,256]{2,1,0:T(8,128)(2,1)S(1)}, u32[]{:S(2)}, u32[]{:S(2)}) collective-permute-start(bf16[4,64,256]{2,1,0:T(8,128)(2,1)S(1)} %collective-permute-done.32.refs_0_), channel_id=1, source_target_pairs={{0,12},{1,13},{2,14},{3,15},{4,0},{5,1},{6,2},{7,3},{8,4},{9,5},{1... | collective-permute-start | bytes 393224 | tf_op jit(solution)/shard_map/ppermute | solution.py:25
  150.6 7.4 %collective-permute-start.34 = (bf16[4,64,256]{2,1,0:T(8,128)(2,1)S(1)}, bf16[4,64,256]{2,1,0:T(8,128)(2,1)S(1)}, u32[]{:S(2)}, u32[]{:S(2)}) collective-permute-start(bf16[4,64,256]{2,1,0:T(8,128)(2,1)S(1)} %collective-permute-done.32.refs_0_), channel_id=1, source_target_pairs={{0,8},{1,9},{2,10},{3,11},{4,12},{5,13},{6,14},{7,15},{8,0},{9,1},... | collective-permute-start | bytes 393224 | tf_op jit(solution)/shard_map/ppermute | solution.py:25
  152.3 7.0 %collective-permute-start.33 = (bf16[4,64,256]{2,1,0:T(8,128)(2,1)S(1)}, bf16[4,64,256]{2,1,0:T(8,128)(2,1)S(1)}, u32[]{:S(2)}, u32[]{:S(2)}) collective-permute-start(bf16[4,64,256]{2,1,0:T(8,128)(2,1)S(1)} %collective-permute-done.32.refs_0_), channel_id=1, source_target_pairs={{0,4},{1,5},{2,6},{3,7},{4,8},{5,9},{6,10},{7,11},{8,12},{9,13},{1... | collective-permute-start | bytes 393224 | tf_op jit(solution)/shard_map/ppermute | solution.py:25
  160.8 8.8 %collective-permute-start.36 = (bf16[64,1024]{1,0:T(8,128)(2,1)S(1)}, bf16[64,1024]{1,0:T(8,128)(2,1)S(1)}, u32[]{:S(2)}, u32[]{:S(2)}) collective-permute-start(bf16[64,1024]{1,0:T(8,128)(2,1)S(1)} %get-tuple-element.141), channel_id=1, source_target_pairs={{0,64},{1,65},{2,66},{3,67},{4,68},{5,69},{6,70},{7,71},{8,72},{9,... | collective-permute-start | bytes 393224 | tf_op jit(solution)/shard_map/ppermute | solution.py:25
  162.6 16.2 %collective-permute-start.37 = (bf16[64,1024]{1,0:T(8,128)(2,1)S(1)}, bf16[64,1024]{1,0:T(8,128)(2,1)S(1)}, u32[]{:S(2)}, u32[]{:S(2)}) collective-permute-start(bf16[64,1024]{1,0:T(8,128)(2,1)S(1)} %get-tuple-element.142), channel_id=1, source_target_pairs={{0,128},{1,129},{2,130},{3,131},{4,132},{5,133},{6,134},{7,135},{8... | collective-permute-start | bytes 393224 | tf_op jit(solution)/shard_map/ppermute | solution.py:25
  167.6 11.2 %collective-permute-start.38 = (bf16[64,1024]{1,0:T(8,128)(2,1)S(1)}, bf16[64,1024]{1,0:T(8,128)(2,1)S(1)}, u32[]{:S(2)}, u32[]{:S(2)}) collective-permute-start(bf16[64,1024]{1,0:T(8,128)(2,1)S(1)} %get-tuple-element.143), channel_id=1, source_target_pairs={{0,192},{1,193},{2,194},{3,195},{4,196},{5,197},{6,198},{7,199},{8... | collective-permute-start | bytes 393224 | tf_op jit(solution)/shard_map/ppermute | solution.py:25
  179.2 6.1 %collective-permute-start.41 = (bf16[448,128]{1,0:T(8,128)(2,1)S(1)}, bf16[448,128]{1,0:T(8,128)(2,1)S(1)}, u32[]{:S(2)}, u32[]{:S(2)}) collective-permute-start(bf16[448,128]{1,0:T(8,128)(2,1)S(1)} %get-tuple-element.145.refs_0_), channel_id=1, source_target_pairs={{0,12},{1,13},{2,14},{3,15},{4,0},{5,1},{6,2},{7,3},{8,4},{9,5},{1... | collective-permute-start | bytes 344072 | tf_op jit(solution)/shard_map/ppermute | solution.py:25
  179.3 7.1 %collective-permute-start.40 = (bf16[448,128]{1,0:T(8,128)(2,1)S(1)}, bf16[448,128]{1,0:T(8,128)(2,1)S(1)}, u32[]{:S(2)}, u32[]{:S(2)}) collective-permute-start(bf16[448,128]{1,0:T(8,128)(2,1)S(1)} %get-tuple-element.145.refs_0_), channel_id=1, source_target_pairs={{0,8},{1,9},{2,10},{3,11},{4,12},{5,13},{6,14},{7,15},{8,0},{9,1},... | collective-permute-start | bytes 344072 | tf_op jit(solution)/shard_map/ppermute | solution.py:25
  179.4 9.0 %collective-permute-start.39 = (bf16[448,128]{1,0:T(8,128)(2,1)S(1)}, bf16[448,128]{1,0:T(8,128)(2,1)S(1)}, u32[]{:S(2)}, u32[]{:S(2)}) collective-permute-start(bf16[448,128]{1,0:T(8,128)(2,1)S(1)} %get-tuple-element.145.refs_0_), channel_id=1, source_target_pairs={{0,4},{1,5},{2,6},{3,7},{4,8},{5,9},{6,10},{7,11},{8,12},{9,13},{1... | collective-permute-start | bytes 344072 | tf_op jit(solution)/shard_map/ppermute | solution.py:25
  188.4 6.8 %collective-permute-start.44 = (bf16[448,128]{1,0:T(8,128)(2,1)S(1)}, bf16[448,128]{1,0:T(8,128)(2,1)S(1)}, u32[]{:S(2)}, u32[]{:S(2)}) collective-permute-start(bf16[448,128]{1,0:T(8,128)(2,1)S(1)} %shard_map.105.refs_0_), channel_id=1, source_target_pairs={{0,3},{1,0},{2,1},{3,2},{4,7},{5,4},{6,5},{7,6},{8,11},{9,8},{10,9... | collective-permute-start | bytes 344072 | tf_op jit(solution)/shard_map/ppermute | solution.py:25
  191.7 6.3 %collective-permute-start.43 = (bf16[448,128]{1,0:T(8,128)(2,1)S(1)}, bf16[448,128]{1,0:T(8,128)(2,1)S(1)}, u32[]{:S(2)}, u32[]{:S(2)}) collective-permute-start(bf16[448,128]{1,0:T(8,128)(2,1)S(1)} %shard_map.105.refs_0_), channel_id=1, source_target_pairs={{0,2},{1,3},{2,0},{3,1},{4,6},{5,7},{6,4},{7,5},{8,10},{9,11},{10,... | collective-permute-start | bytes 344072 | tf_op jit(solution)/shard_map/ppermute | solution.py:25
  191.9 6.2 %collective-permute-start.42 = (bf16[448,128]{1,0:T(8,128)(2,1)S(1)}, bf16[448,128]{1,0:T(8,128)(2,1)S(1)}, u32[]{:S(2)}, u32[]{:S(2)}) collective-permute-start(bf16[448,128]{1,0:T(8,128)(2,1)S(1)} %shard_map.105.refs_0_), channel_id=1, source_target_pairs={{0,1},{1,2},{2,3},{3,0},{4,5},{5,6},{6,7},{7,4},{8,9},{9,10},{10,1... | collective-permute-start | bytes 344072 | tf_op jit(solution)/shard_map/ppermute | solution.py:25
  199.2 5.1 %collective-permute-start.45 = (bf16[64,256]{1,0:T(8,128)(2,1)S(1)}, bf16[64,256]{1,0:T(8,128)(2,1)S(1)}, u32[]{:S(2)}, u32[]{:S(2)}) collective-permute-start(bf16[64,256]{1,0:T(8,128)(2,1)S(1)} %get-tuple-element.148), channel_id=1, source_target_pairs={{0,3},{1,0},{2,1},{3,2},{4,7},{5,4},{6,5},{7,6},{8,11},{9,8},{10,9... | collective-permute-start | bytes 98312 | tf_op jit(solution)/shard_map/ppermute | solution.py:25
  202.0 5.4 %collective-permute-start.46 = (bf16[64,256]{1,0:T(8,128)(2,1)S(1)}, bf16[64,256]{1,0:T(8,128)(2,1)S(1)}, u32[]{:S(2)}, u32[]{:S(2)}) collective-permute-start(bf16[64,256]{1,0:T(8,128)(2,1)S(1)} %get-tuple-element.149), channel_id=1, source_target_pairs={{0,2},{1,3},{2,0},{3,1},{4,6},{5,7},{6,4},{7,5},{8,10},{9,11},{10,... | collective-permute-start | bytes 98312 | tf_op jit(solution)/shard_map/ppermute | solution.py:25
  202.2 5.3 %collective-permute-start.47 = (bf16[64,256]{1,0:T(8,128)(2,1)S(1)}, bf16[64,256]{1,0:T(8,128)(2,1)S(1)}, u32[]{:S(2)}, u32[]{:S(2)}) collective-permute-start(bf16[64,256]{1,0:T(8,128)(2,1)S(1)} %get-tuple-element.150), channel_id=1, source_target_pairs={{0,1},{1,2},{2,3},{3,0},{4,5},{5,6},{6,7},{7,4},{8,9},{9,10},{10,1... | collective-permute-start | bytes 98312 | tf_op jit(solution)/shard_map/ppermute | solution.py:25
  (9 other events, 82.7 us)

commit v5 on v4

--- a/solution.py
+++ b/solution.py
@@ -408,9 +408,8 @@
     upper = stack(*parts)
     far_upper = swap_pair(upper)
     gathered = gathered_y(rows)
-    gathered, far_lower, lower, near_upper = tied(
-        (gathered, far_lower, lower, swap_core(upper))
-    )
+    gathered, far_lower, lower, upper = tied((gathered, far_lower, lower, upper))
+    near_upper = swap_core(upper)
     lower = [lower, swap_core(lower), far_lower, swap_core(far_lower)]
     gathered, low_right, up_right = tied((gathered, low_right, up_right))
     turned = scattered_x(
@@ -418,9 +417,9 @@
             low_right, up_right
         )
     )
-    turned, far_upper, lower = tied((turned, far_upper, lower))
     upper = [upper, near_upper, far_upper, swap_core(far_upper)]
     received = scattered_q(products(n, gathered, *lower, *upper))
+    received, turned = tied((received, turned))
     dense, extra = kernel_call(
         lambda *refs: total_kernel(n, *refs),
         (shape((n, total), F32), shape((8, slots * share, total), BF16)),

time: 209 us -> 200 us (0.957)
  waiting for transfers between devices: 86.3 us -> 72.1 us
  starting transfers between devices: 91.4 us -> 94.9 us
    ppermute x48, waiting for transfers between devices: 86.3 us -> 72.1 us  [permuted(): return lax.ppermute(value, ('row', 'col'), routes(to))]
    ppermute x48, starting transfers between devices: 91.4 us -> 94.9 us  [permuted(): return lax.ppermute(value, ('row', 'col'), routes(to))]
  transfers between devices with their start and end apart: 48 -> 48, of which waited for: 33 -> 28; matrix products, arithmetic and copies ran while one was open for 0% -> 0% of each run, Pallas kernels for 0% -> 2%
where the time goes in v5:
time: 200 us; the launch traced here: 199 us
  starting transfers between devices  94.9 us (47%)
  waiting for transfers between devices  72.1 us (36%)
  blocking collectives  19.8 us (10%)
  Pallas kernels  9.12 us (5%)
  local copies, waits for them, and re-layouts  3.19 us (2%)
    ppermute x48, starting transfers between devices, permuted(): return lax.ppermute(value, ('row', 'col'), routes(to))  94.9 us
    ppermute x48, waiting for transfers between devices, permuted(): return lax.ppermute(value, ('row', 'col'), routes(to))  72.1 us
    all_to_all x1, blocking collectives, from_every_z(): lax.all_to_all(value, 'row', 0, 0, tiled=True, axis_index_groups=Z_GROUPS)  19.8 us
    pallas_call x17, Pallas kernels, run(): pl.pallas_call(body, out_shape=out_shape, in_specs=specs, scratch_shapes=...  9.12 us
  transfers between devices with their start and end apart: 48, of which 28 were waited for; matrix products, arithmetic and copies ran while one was open for 0% of the time, Pallas kernels for 2%

profile of v5, /device:TPU:2, one launch (start us, length us, event | category | flops | bytes accessed | tf_op | source)
XLA Modules:
  0.0 199.3 jit_solution(13743785732961297694)
XLA Ops:
  1.1 1.6 collective-permute-start
  2.7 2.8 %collective-permute-start.1 = (bf16[256,256]{1,0:T(8,128)(2,1)S(1)}, bf16[256,256]{1,0:T(8,128)(2,1)S(1)}, u32[]{:S(2)}, u32[]{:S(2)}) collective-permute-start(bf16[256,256]{1,0:T(8,128)(2,1)S(1)} %get-tuple-element.79), channel_id=1, source_target_pairs={{0,2},{1,3},{2,0},{3,1},{4,6},{5,7},{6,4},{7,5},{8,10},{9,11},{10,... | collective-permute-start | bytes 393224 | tf_op jit(solution)/shard_map/ppermute | solution.py:25
  8.4 1.6 collective-permute-start.3
  10.0 1.9 collective-permute-start.4
  12.5 2.6 %collective-permute-start.5 = (bf16[88,256]{1,0:T(8,128)(2,1)S(1)}, bf16[88,256]{1,0:T(8,128)(2,1)S(1)}, u32[]{:S(2)}, u32[]{:S(2)}) collective-permute-start(bf16[88,256]{1,0:T(8,128)(2,1)S(1)} %get-tuple-element.84), channel_id=1, source_target_pairs={{0,3},{1,0},{2,1},{3,2},{4,7},{5,4},{6,5},{7,6},{8,11},{9,8},{10,9... | collective-permute-start | bytes 135176 | tf_op jit(solution)/shard_map/ppermute | solution.py:25
  19.3 3.1 %collective-permute-start.7 = (bf16[256,256]{1,0:T(8,128)(2,1)S(1)}, bf16[256,256]{1,0:T(8,128)(2,1)S(1)}, u32[]{:S(2)}, u32[]{:S(2)}) collective-permute-start(bf16[256,256]{1,0:T(8,128)(2,1)S(1)} %get-tuple-element.96), channel_id=1, source_target_pairs={{0,2},{1,3},{2,0},{3,1},{4,6},{5,7},{6,4},{7,5},{8,10},{9,11},{10,... | collective-permute-start | bytes 393224 | tf_op jit(solution)/shard_map/ppermute | solution.py:25
  23.0 1.9 collective-permute-start.13
  25.8 1.6 collective-permute-done.8.refs_3_
  27.4 2.0 %collective-permute-start.17 = (bf16[1024,256]{1,0:T(8,128)(2,1)S(1)}, bf16[1024,256]{1,0:T(8,128)(2,1)S(1)}, u32[]{:S(2)}, u32[]{:S(2)}) collective-permute-start(bf16[1024,256]{1,0:T(8,128)(2,1)S(1)} %shard_map.96.refs_8_.refs_4_), channel_id=1, source_target_pairs={{0,32},{1,33},{2,34},{3,35},{4,36},{5,37},{6,38},{7,39},{8,40},{9,... | collective-permute-start | bytes 1572872 | tf_op jit(solution)/shard_map/ppermute | solution.py:25
  29.4 9.9 %collective-permute-start.12 = (bf16[4,88,256]{2,1,0:T(8,128)(2,1)S(1)}, bf16[4,88,256]{2,1,0:T(8,128)(2,1)S(1)}, u32[]{:S(2)}, u32[]{:S(2)}) collective-permute-start(bf16[4,88,256]{2,1,0:T(8,128)(2,1)S(1)} %collective-permute-done.9.refs_0_), channel_id=1, source_target_pairs={{0,12},{1,13},{2,14},{3,15},{4,0},{5,1},{6,2},{7,3},{8,4},{9,5},{1... | collective-permute-start | bytes 540680 | tf_op jit(solution)/shard_map/ppermute | solution.py:25
  41.2 5.7 %collective-permute-done.12.refs_3_ = bf16[4,88,256]{2,1,0:T(8,128)(2,1)S(1)} collective-permute-done((bf16[4,88,256]{2,1,0:T(8,128)(2,1)S(1)}, bf16[4,88,256]{2,1,0:T(8,128)(2,1)S(1)}, u32[]{:S(2)}, u32[]{:S(2)}) %collective-permute-start.12) | collective-permute-done | bytes 180256 | tf_op jit(solution)/shard_map/ppermute | solution.py:25
  46.9 1.5 collective-permute-done.11.refs_2_
  48.4 1.9 collective-permute-done.10.refs_1_
  52.4 3.6 %collective-permute-start.23 = (bf16[384,256]{1,0:T(8,128)(2,1)S(1)}, bf16[384,256]{1,0:T(8,128)(2,1)S(1)}, u32[]{:S(2)}, u32[]{:S(2)}) collective-permute-start(bf16[384,256]{1,0:T(8,128)(2,1)S(1)} %get-tuple-element.124), channel_id=1, source_target_pairs={{0,2},{1,3},{2,0},{3,1},{4,6},{5,7},{6,4},{7,5},{8,10},{9,11},{10,... | collective-permute-start | bytes 589832 | tf_op jit(solution)/shard_map/ppermute | solution.py:25
  56.3 2.4 %shard_map.97 = (bf16[88,1024]{1,0:T(8,128)(2,1)S(1)}, bf16[88,1024]{1,0:T(8,128)(2,1)S(1)}, bf16[88,1024]{1,0:T(8,128)(2,1)S(1)}, bf16[88,1024]{1,0:T(8,128)(2,1)S(1)}) custom-call(bf16[4,88,256]{2,1,0:T(8,128)(2,1)S(1)} %collective-permute-done.9.refs_0_, bf16[4,88,256]{2,1,0:T(8,128)(2,1)S(1)} %collective-permute-done.10.refs_1_, ...), custom_call_target="tpu_custom_call" | custom-call | flops 738197504 | bytes 5636096 | tf_op jit(solution)/shard_map/pallas_call | solution.py:106
  58.7 2.6 %collective-permute-start.19 = (bf16[88,1024]{1,0:T(8,128)(2,1)S(1)}, bf16[88,1024]{1,0:T(8,128)(2,1)S(1)}, u32[]{:S(2)}, u32[]{:S(2)}) collective-permute-start(bf16[88,1024]{1,0:T(8,128)(2,1)S(1)} %get-tuple-element.117), channel_id=1, source_target_pairs={{0,64},{1,65},{2,66},{3,67},{4,68},{5,69},{6,70},{7,71},{8,72},{9,... | collective-permute-start | bytes 540680 | tf_op jit(solution)/shard_map/ppermute | solution.py:25
  61.3 2.0 collective-permute-start.20
  63.3 3.2 %collective-permute-start.21 = (bf16[88,1024]{1,0:T(8,128)(2,1)S(1)}, bf16[88,1024]{1,0:T(8,128)(2,1)S(1)}, u32[]{:S(2)}, u32[]{:S(2)}) collective-permute-start(bf16[88,1024]{1,0:T(8,128)(2,1)S(1)} %get-tuple-element.119), channel_id=1, source_target_pairs={{0,192},{1,193},{2,194},{3,195},{4,196},{5,197},{6,198},{7,199},{8... | collective-permute-start | bytes 540680 | tf_op jit(solution)/shard_map/ppermute | solution.py:25
  66.5 3.2 %collective-permute-done.19.refs_1_ = bf16[88,1024]{1,0:T(8,128)(2,1)S(1)} collective-permute-done((bf16[88,1024]{1,0:T(8,128)(2,1)S(1)}, bf16[88,1024]{1,0:T(8,128)(2,1)S(1)}, u32[]{:S(2)}, u32[]{:S(2)}) %collective-permute-start.19) | collective-permute-done | bytes 180256 | tf_op jit(solution)/shard_map/ppermute | solution.py:25
  69.7 5.1 %collective-permute-done.20.refs_2_ = bf16[88,1024]{1,0:T(8,128)(2,1)S(1)} collective-permute-done((bf16[88,1024]{1,0:T(8,128)(2,1)S(1)}, bf16[88,1024]{1,0:T(8,128)(2,1)S(1)}, u32[]{:S(2)}, u32[]{:S(2)}) %collective-permute-start.20) | collective-permute-done | bytes 180256 | tf_op jit(solution)/shard_map/ppermute | solution.py:25
  74.7 6.3 %collective-permute-done.21.refs_3_ = bf16[88,1024]{1,0:T(8,128)(2,1)S(1)} collective-permute-done((bf16[88,1024]{1,0:T(8,128)(2,1)S(1)}, bf16[88,1024]{1,0:T(8,128)(2,1)S(1)}, u32[]{:S(2)}, u32[]{:S(2)}) %collective-permute-start.21) | collective-permute-done | bytes 180256 | tf_op jit(solution)/shard_map/ppermute | solution.py:25
  81.1 19.8 %all_to_all.5.mine_ref = bf16[8,24,1024]{2,1,0:T(8,128)(2,1)S(1)} all-to-all(bf16[8,24,1024]{2,1,0:T(8,128)(2,1)S(1)} %get-tuple-element.131), channel_id=1, replica_groups={{0,32,64,96,128,160,192,224},{16,48,80,112,144,176,208,240},{1,33,65,97..., dimensions={0} | all-to-all | bytes 786432 | tf_op jit(solution)/shard_map/all_to_all | solution.py:55
  100.9 1.7 collective-permute-done.25.other_ref
  103.4 4.6 %collective-permute-start.28 = (bf16[448,128]{1,0:T(8,128)(2,1)S(1)}, bf16[448,128]{1,0:T(8,128)(2,1)S(1)}, u32[]{:S(2)}, u32[]{:S(2)}) collective-permute-start(bf16[448,128]{1,0:T(8,128)(2,1)S(1)} %get-tuple-element.136.refs_0_), channel_id=1, source_target_pairs={{0,12},{1,13},{2,14},{3,15},{4,0},{5,1},{6,2},{7,3},{8,4},{9,5},{1... | collective-permute-start | bytes 344072 | tf_op jit(solution)/shard_map/ppermute | solution.py:25
  109.0 4.2 %collective-permute-done.28.refs_3_ = bf16[448,128]{1,0:T(8,128)(2,1)S(1)} collective-permute-done((bf16[448,128]{1,0:T(8,128)(2,1)S(1)}, bf16[448,128]{1,0:T(8,128)(2,1)S(1)}, u32[]{:S(2)}, u32[]{:S(2)}) %collective-permute-start.28) | collective-permute-done | bytes 114720 | tf_op jit(solution)/shard_map/ppermute | solution.py:25
  113.2 2.4 %collective-permute-done.27.refs_2_ = bf16[448,128]{1,0:T(8,128)(2,1)S(1)} collective-permute-done((bf16[448,128]{1,0:T(8,128)(2,1)S(1)}, bf16[448,128]{1,0:T(8,128)(2,1)S(1)}, u32[]{:S(2)}, u32[]{:S(2)}) %collective-permute-start.27) | collective-permute-done | bytes 114720 | tf_op jit(solution)/shard_map/ppermute | solution.py:25
  116.7 3.0 %collective-permute-start.31 = (bf16[448,128]{1,0:T(8,128)(2,1)S(1)}, bf16[448,128]{1,0:T(8,128)(2,1)S(1)}, u32[]{:S(2)}, u32[]{:S(2)}) collective-permute-start(bf16[448,128]{1,0:T(8,128)(2,1)S(1)} %shard_map.101.refs_0_), channel_id=1, source_target_pairs={{0,3},{1,0},{2,1},{3,2},{4,7},{5,4},{6,5},{7,6},{8,11},{9,8},{10,9... | collective-permute-start | bytes 344072 | tf_op jit(solution)/shard_map/ppermute | solution.py:25
  119.8 1.5 collective-permute-start.29
  121.3 2.0 collective-permute-done.31.refs_3_
  123.2 2.8 %collective-permute-done.30.refs_2_ = bf16[448,128]{1,0:T(8,128)(2,1)S(1)} collective-permute-done((bf16[448,128]{1,0:T(8,128)(2,1)S(1)}, bf16[448,128]{1,0:T(8,128)(2,1)S(1)}, u32[]{:S(2)}, u32[]{:S(2)}) %collective-permute-start.30) | collective-permute-done | bytes 114720 | tf_op jit(solution)/shard_map/ppermute | solution.py:25
  127.7 11.3 %collective-permute-start.35 = (bf16[4,64,256]{2,1,0:T(8,128)(2,1)S(1)}, bf16[4,64,256]{2,1,0:T(8,128)(2,1)S(1)}, u32[]{:S(2)}, u32[]{:S(2)}) collective-permute-start(bf16[4,64,256]{2,1,0:T(8,128)(2,1)S(1)} %collective-permute-done.32.refs_0_), channel_id=1, source_target_pairs={{0,12},{1,13},{2,14},{3,15},{4,0},{5,1},{6,2},{7,3},{8,4},{9,5},{1... | collective-permute-start | bytes 393224 | tf_op jit(solution)/shard_map/ppermute | solution.py:25
  139.0 1.8 collective-permute-start.34
  142.7 3.8 %collective-permute-done.34.refs_2_ = bf16[4,64,256]{2,1,0:T(8,128)(2,1)S(1)} collective-permute-done((bf16[4,64,256]{2,1,0:T(8,128)(2,1)S(1)}, bf16[4,64,256]{2,1,0:T(8,128)(2,1)S(1)}, u32[]{:S(2)}, u32[]{:S(2)}) %collective-permute-start.34) | collective-permute-done | bytes 131104 | tf_op jit(solution)/shard_map/ppermute | solution.py:25
  147.6 1.5 shard_map.103
  149.2 1.5 collective-permute-start.36
  150.7 5.4 %collective-permute-start.37 = (bf16[64,1024]{1,0:T(8,128)(2,1)S(1)}, bf16[64,1024]{1,0:T(8,128)(2,1)S(1)}, u32[]{:S(2)}, u32[]{:S(2)}) collective-permute-start(bf16[64,1024]{1,0:T(8,128)(2,1)S(1)} %get-tuple-element.140), channel_id=1, source_target_pairs={{0,128},{1,129},{2,130},{3,131},{4,132},{5,133},{6,134},{7,135},{8... | collective-permute-start | bytes 393224 | tf_op jit(solution)/shard_map/ppermute | solution.py:25
  156.1 2.0 %collective-permute-done.36.refs_1_ = bf16[64,1024]{1,0:T(8,128)(2,1)S(1)} collective-permute-done((bf16[64,1024]{1,0:T(8,128)(2,1)S(1)}, bf16[64,1024]{1,0:T(8,128)(2,1)S(1)}, u32[]{:S(2)}, u32[]{:S(2)}) %collective-permute-start.36) | collective-permute-done | bytes 131104 | tf_op jit(solution)/shard_map/ppermute | solution.py:25
  158.1 8.2 %collective-permute-done.37.refs_2_ = bf16[64,1024]{1,0:T(8,128)(2,1)S(1)} collective-permute-done((bf16[64,1024]{1,0:T(8,128)(2,1)S(1)}, bf16[64,1024]{1,0:T(8,128)(2,1)S(1)}, u32[]{:S(2)}, u32[]{:S(2)}) %collective-permute-start.37) | collective-permute-done | bytes 131104 | tf_op jit(solution)/shard_map/ppermute | solution.py:25
  167.3 1.6 collective-permute-start.39
  168.9 4.0 %collective-permute-done.41.refs_3_ = bf16[448,128]{1,0:T(8,128)(2,1)S(1)} collective-permute-done((bf16[448,128]{1,0:T(8,128)(2,1)S(1)}, bf16[448,128]{1,0:T(8,128)(2,1)S(1)}, u32[]{:S(2)}, u32[]{:S(2)}) %collective-permute-start.41) | collective-permute-done | bytes 114720 | tf_op jit(solution)/shard_map/ppermute | solution.py:25
  172.9 1.6 collective-permute-done.40.refs_2_
  175.8 4.7 %collective-permute-start.44 = (bf16[448,128]{1,0:T(8,128)(2,1)S(1)}, bf16[448,128]{1,0:T(8,128)(2,1)S(1)}, u32[]{:S(2)}, u32[]{:S(2)}) collective-permute-start(bf16[448,128]{1,0:T(8,128)(2,1)S(1)} %shard_map.105.refs_0_), channel_id=1, source_target_pairs={{0,3},{1,0},{2,1},{3,2},{4,7},{5,4},{6,5},{7,6},{8,11},{9,8},{10,9... | collective-permute-start | bytes 344072 | tf_op jit(solution)/shard_map/ppermute | solution.py:25
  180.5 2.0 collective-permute-start.43
  182.4 2.5 %collective-permute-start.42 = (bf16[448,128]{1,0:T(8,128)(2,1)S(1)}, bf16[448,128]{1,0:T(8,128)(2,1)S(1)}, u32[]{:S(2)}, u32[]{:S(2)}) collective-permute-start(bf16[448,128]{1,0:T(8,128)(2,1)S(1)} %shard_map.105.refs_0_), channel_id=1, source_target_pairs={{0,1},{1,2},{2,3},{3,0},{4,5},{5,6},{6,7},{7,4},{8,9},{9,10},{10,1... | collective-permute-start | bytes 344072 | tf_op jit(solution)/shard_map/ppermute | solution.py:25
  185.0 3.1 %collective-permute-done.43.refs_2_ = bf16[448,128]{1,0:T(8,128)(2,1)S(1)} collective-permute-done((bf16[448,128]{1,0:T(8,128)(2,1)S(1)}, bf16[448,128]{1,0:T(8,128)(2,1)S(1)}, u32[]{:S(2)}, u32[]{:S(2)}) %collective-permute-start.43) | collective-permute-done | bytes 114720 | tf_op jit(solution)/shard_map/ppermute | solution.py:25
  190.1 3.0 %collective-permute-start.45 = (bf16[64,256]{1,0:T(8,128)(2,1)S(1)}, bf16[64,256]{1,0:T(8,128)(2,1)S(1)}, u32[]{:S(2)}, u32[]{:S(2)}) collective-permute-start(bf16[64,256]{1,0:T(8,128)(2,1)S(1)} %get-tuple-element.146), channel_id=1, source_target_pairs={{0,3},{1,0},{2,1},{3,2},{4,7},{5,4},{6,5},{7,6},{8,11},{9,8},{10,9... | collective-permute-start | bytes 98312 | tf_op jit(solution)/shard_map/ppermute | solution.py:25
  193.1 2.4 %collective-permute-start.47 = (bf16[64,256]{1,0:T(8,128)(2,1)S(1)}, bf16[64,256]{1,0:T(8,128)(2,1)S(1)}, u32[]{:S(2)}, u32[]{:S(2)}) collective-permute-start(bf16[64,256]{1,0:T(8,128)(2,1)S(1)} %get-tuple-element.148), channel_id=1, source_target_pairs={{0,1},{1,2},{2,3},{3,0},{4,5},{5,6},{6,7},{7,4},{8,9},{9,10},{10,1... | collective-permute-start | bytes 98312 | tf_op jit(solution)/shard_map/ppermute | solution.py:25
  195.5 3.1 %collective-permute-done.46.refs_2_ = bf16[64,256]{1,0:T(8,128)(2,1)S(1)} collective-permute-done((bf16[64,256]{1,0:T(8,128)(2,1)S(1)}, bf16[64,256]{1,0:T(8,128)(2,1)S(1)}, u32[]{:S(2)}, u32[]{:S(2)}) %collective-permute-start.46) | collective-permute-done | bytes 32800 | tf_op jit(solution)/shard_map/ppermute | solution.py:25
  (84 shorter events, 27.1 us)
Async XLA Ops:
  1.1 15.7 %collective-permute-start = (bf16[256,256]{1,0:T(8,128)(2,1)S(1)}, bf16[256,256]{1,0:T(8,128)(2,1)S(1)}, u32[]{:S(2)}, u32[]{:S(2)}) collective-permute-start(bf16[256,256]{1,0:T(8,128)(2,1)S(1)} %get-tuple-element.78), channel_id=1, source_target_pairs={{0,1},{1,2},{2,3},{3,0},{4,5},{5,6},{6,7},{7,4},{8,9},{9,10},{10,1... | collective-permute-start | bytes 393224 | tf_op jit(solution)/shard_map/ppermute | solution.py:25
  2.7 14.2 %collective-permute-start.1 = (bf16[256,256]{1,0:T(8,128)(2,1)S(1)}, bf16[256,256]{1,0:T(8,128)(2,1)S(1)}, u32[]{:S(2)}, u32[]{:S(2)}) collective-permute-start(bf16[256,256]{1,0:T(8,128)(2,1)S(1)} %get-tuple-element.79), channel_id=1, source_target_pairs={{0,2},{1,3},{2,0},{3,1},{4,6},{5,7},{6,4},{7,5},{8,10},{9,11},{10,... | collective-permute-start | bytes 393224 | tf_op jit(solution)/shard_map/ppermute | solution.py:25
  5.5 11.3 %collective-permute-start.2 = (bf16[256,256]{1,0:T(8,128)(2,1)S(1)}, bf16[256,256]{1,0:T(8,128)(2,1)S(1)}, u32[]{:S(2)}, u32[]{:S(2)}) collective-permute-start(bf16[256,256]{1,0:T(8,128)(2,1)S(1)} %get-tuple-element.80), channel_id=1, source_target_pairs={{0,3},{1,0},{2,1},{3,2},{4,7},{5,4},{6,5},{7,6},{8,11},{9,8},{10,9... | collective-permute-start | bytes 393224 | tf_op jit(solution)/shard_map/ppermute | solution.py:25
  8.4 4.1 %collective-permute-start.3 = (bf16[88,256]{1,0:T(8,128)(2,1)S(1)}, bf16[88,256]{1,0:T(8,128)(2,1)S(1)}, u32[]{:S(2)}, u32[]{:S(2)}) collective-permute-start(bf16[88,256]{1,0:T(8,128)(2,1)S(1)} %get-tuple-element.82), channel_id=1, source_target_pairs={{0,1},{1,2},{2,3},{3,0},{4,5},{5,6},{6,7},{7,4},{8,9},{9,10},{10,1... | collective-permute-start | bytes 135176 | tf_op jit(solution)/shard_map/ppermute | solution.py:25
  10.0 5.6 %collective-permute-start.4 = (bf16[88,256]{1,0:T(8,128)(2,1)S(1)}, bf16[88,256]{1,0:T(8,128)(2,1)S(1)}, u32[]{:S(2)}, u32[]{:S(2)}) collective-permute-start(bf16[88,256]{1,0:T(8,128)(2,1)S(1)} %get-tuple-element.83), channel_id=1, source_target_pairs={{0,2},{1,3},{2,0},{3,1},{4,6},{5,7},{6,4},{7,5},{8,10},{9,11},{10,... | collective-permute-start | bytes 135176 | tf_op jit(solution)/shard_map/ppermute | solution.py:25
  12.5 4.4 %collective-permute-start.5 = (bf16[88,256]{1,0:T(8,128)(2,1)S(1)}, bf16[88,256]{1,0:T(8,128)(2,1)S(1)}, u32[]{:S(2)}, u32[]{:S(2)}) collective-permute-start(bf16[88,256]{1,0:T(8,128)(2,1)S(1)} %get-tuple-element.84), channel_id=1, source_target_pairs={{0,3},{1,0},{2,1},{3,2},{4,7},{5,4},{6,5},{7,6},{8,11},{9,8},{10,9... | collective-permute-start | bytes 135176 | tf_op jit(solution)/shard_map/ppermute | solution.py:25
  16.9 10.5 %collective-permute-start.9 = (bf16[4,88,256]{2,1,0:T(8,128)(2,1)S(1)}, bf16[4,88,256]{2,1,0:T(8,128)(2,1)S(1)}, u32[]{:S(2)}, u32[]{:S(2)}) collective-permute-start(bf16[4,88,256]{2,1,0:T(8,128)(2,1)S(1)} %shard_map.93), channel_id=1, source_target_pairs={{0,0},{1,1},{2,2},{3,3},{4,64},{5,65},{6,66},{7,67},{8,128},{9,129... | collective-permute-start | bytes 540680 | tf_op jit(solution)/shard_map/ppermute | solution.py:25
  17.9 7.0 %collective-permute-start.6 = (bf16[256,256]{1,0:T(8,128)(2,1)S(1)}, bf16[256,256]{1,0:T(8,128)(2,1)S(1)}, u32[]{:S(2)}, u32[]{:S(2)}) collective-permute-start(bf16[256,256]{1,0:T(8,128)(2,1)S(1)} %get-tuple-element.95), channel_id=1, source_target_pairs={{0,1},{1,2},{2,3},{3,0},{4,5},{5,6},{6,7},{7,4},{8,9},{9,10},{10,1... | collective-permute-start | bytes 393224 | tf_op jit(solution)/shard_map/ppermute | solution.py:25
  19.3 6.5 %collective-permute-start.7 = (bf16[256,256]{1,0:T(8,128)(2,1)S(1)}, bf16[256,256]{1,0:T(8,128)(2,1)S(1)}, u32[]{:S(2)}, u32[]{:S(2)}) collective-permute-start(bf16[256,256]{1,0:T(8,128)(2,1)S(1)} %get-tuple-element.96), channel_id=1, source_target_pairs={{0,2},{1,3},{2,0},{3,1},{4,6},{5,7},{6,4},{7,5},{8,10},{9,11},{10,... | collective-permute-start | bytes 393224 | tf_op jit(solution)/shard_map/ppermute | solution.py:25
  22.4 5.0 %collective-permute-start.8 = (bf16[256,256]{1,0:T(8,128)(2,1)S(1)}, bf16[256,256]{1,0:T(8,128)(2,1)S(1)}, u32[]{:S(2)}, u32[]{:S(2)}) collective-permute-start(bf16[256,256]{1,0:T(8,128)(2,1)S(1)} %get-tuple-element.97), channel_id=1, source_target_pairs={{0,3},{1,0},{2,1},{3,2},{4,7},{5,4},{6,5},{7,6},{8,11},{9,8},{10,9... | collective-permute-start | bytes 393224 | tf_op jit(solution)/shard_map/ppermute | solution.py:25
  23.0 27.3 %collective-permute-start.13 = (bf16[1024,256]{1,0:T(8,128)(2,1)S(1)}, bf16[1024,256]{1,0:T(8,128)(2,1)S(1)}, u32[]{:S(2)}, u32[]{:S(2)}) collective-permute-start(bf16[1024,256]{1,0:T(8,128)(2,1)S(1)} %shard_map.94.refs_4_), channel_id=1, source_target_pairs={{0,32},{1,33},{2,34},{3,35},{4,36},{5,37},{6,38},{7,39},{8,40},{9,... | collective-permute-start | bytes 1572872 | tf_op jit(solution)/shard_map/ppermute | solution.py:25
  27.4 23.4 %collective-permute-start.17 = (bf16[1024,256]{1,0:T(8,128)(2,1)S(1)}, bf16[1024,256]{1,0:T(8,128)(2,1)S(1)}, u32[]{:S(2)}, u32[]{:S(2)}) collective-permute-start(bf16[1024,256]{1,0:T(8,128)(2,1)S(1)} %shard_map.96.refs_8_.refs_4_), channel_id=1, source_target_pairs={{0,32},{1,33},{2,34},{3,35},{4,36},{5,37},{6,38},{7,39},{8,40},{9,... | collective-permute-start | bytes 1572872 | tf_op jit(solution)/shard_map/ppermute | solution.py:25
  29.4 17.5 %collective-permute-start.12 = (bf16[4,88,256]{2,1,0:T(8,128)(2,1)S(1)}, bf16[4,88,256]{2,1,0:T(8,128)(2,1)S(1)}, u32[]{:S(2)}, u32[]{:S(2)}) collective-permute-start(bf16[4,88,256]{2,1,0:T(8,128)(2,1)S(1)} %collective-permute-done.9.refs_0_), channel_id=1, source_target_pairs={{0,12},{1,13},{2,14},{3,15},{4,0},{5,1},{6,2},{7,3},{8,4},{9,5},{1... | collective-permute-start | bytes 540680 | tf_op jit(solution)/shard_map/ppermute | solution.py:25
  39.4 9.0 %collective-permute-start.11 = (bf16[4,88,256]{2,1,0:T(8,128)(2,1)S(1)}, bf16[4,88,256]{2,1,0:T(8,128)(2,1)S(1)}, u32[]{:S(2)}, u32[]{:S(2)}) collective-permute-start(bf16[4,88,256]{2,1,0:T(8,128)(2,1)S(1)} %collective-permute-done.9.refs_0_), channel_id=1, source_target_pairs={{0,8},{1,9},{2,10},{3,11},{4,12},{5,13},{6,14},{7,15},{8,0},{9,1},... | collective-permute-start | bytes 540680 | tf_op jit(solution)/shard_map/ppermute | solution.py:25
  39.8 10.5 %collective-permute-start.10 = (bf16[4,88,256]{2,1,0:T(8,128)(2,1)S(1)}, bf16[4,88,256]{2,1,0:T(8,128)(2,1)S(1)}, u32[]{:S(2)}, u32[]{:S(2)}) collective-permute-start(bf16[4,88,256]{2,1,0:T(8,128)(2,1)S(1)} %collective-permute-done.9.refs_0_), channel_id=1, source_target_pairs={{0,4},{1,5},{2,6},{3,7},{4,8},{5,9},{6,10},{7,11},{8,12},{9,13},{1... | collective-permute-start | bytes 540680 | tf_op jit(solution)/shard_map/ppermute | solution.py:25
  50.3 2.1 %collective-permute-start.14 = (bf16[1024,256]{1,0:T(8,128)(2,1)S(1)}, bf16[1024,256]{1,0:T(8,128)(2,1)S(1)}, u32[]{:S(2)}, u32[]{:S(2)}) collective-permute-start(bf16[1024,256]{1,0:T(8,128)(2,1)S(1)} %shard_map.94.refs_4_), channel_id=1, source_target_pairs={{0,16},{1,17},{2,18},{3,19},{4,20},{5,21},{6,22},{7,23},{8,24},{9,... | collective-permute-start | bytes 1572872 | tf_op jit(solution)/shard_map/ppermute | solution.py:25
  50.3 5.7 %collective-permute-start.15 = (bf16[1024,256]{1,0:T(8,128)(2,1)S(1)}, bf16[1024,256]{1,0:T(8,128)(2,1)S(1)}, u32[]{:S(2)}, u32[]{:S(2)}) collective-permute-start(bf16[1024,256]{1,0:T(8,128)(2,1)S(1)} %collective-permute-done.13.refs_6_), channel_id=1, source_target_pairs={{0,16},{1,17},{2,18},{3,19},{4,20},{5,21},{6,22},{7,23},{8,24},{9,... | collective-permute-start | bytes 1572872 | tf_op jit(solution)/shard_map/ppermute | solution.py:25
  50.8 5.5 %collective-permute-start.16 = (bf16[1024,256]{1,0:T(8,128)(2,1)S(1)}, bf16[1024,256]{1,0:T(8,128)(2,1)S(1)}, u32[]{:S(2)}, u32[]{:S(2)}) collective-permute-start(bf16[1024,256]{1,0:T(8,128)(2,1)S(1)} %shard_map.96.refs_8_.refs_4_), channel_id=1, source_target_pairs={{0,16},{1,17},{2,18},{3,19},{4,20},{5,21},{6,22},{7,23},{8,24},{9,... | collective-permute-start | bytes 1572872 | tf_op jit(solution)/shard_map/ppermute | solution.py:25
  50.8 5.5 %collective-permute-start.18 = (bf16[1024,256]{1,0:T(8,128)(2,1)S(1)}, bf16[1024,256]{1,0:T(8,128)(2,1)S(1)}, u32[]{:S(2)}, u32[]{:S(2)}) collective-permute-start(bf16[1024,256]{1,0:T(8,128)(2,1)S(1)} %collective-permute-done.17.refs_10_.refs_6_), channel_id=1, source_target_pairs={{0,16},{1,17},{2,18},{3,19},{4,20},{5,21},{6,22},{7,23},{8,24},{9,... | collective-permute-start | bytes 1572872 | tf_op jit(solution)/shard_map/ppermute | solution.py:25
  51.7 11.5 %collective-permute-start.22 = (bf16[384,256]{1,0:T(8,128)(2,1)S(1)}, bf16[384,256]{1,0:T(8,128)(2,1)S(1)}, u32[]{:S(2)}, u32[]{:S(2)}) collective-permute-start(bf16[384,256]{1,0:T(8,128)(2,1)S(1)} %get-tuple-element.123), channel_id=1, source_target_pairs={{0,1},{1,2},{2,3},{3,0},{4,5},{5,6},{6,7},{7,4},{8,9},{9,10},{10,1... | collective-permute-start | bytes 589832 | tf_op jit(solution)/shard_map/ppermute | solution.py:25
  52.4 14.1 %collective-permute-start.23 = (bf16[384,256]{1,0:T(8,128)(2,1)S(1)}, bf16[384,256]{1,0:T(8,128)(2,1)S(1)}, u32[]{:S(2)}, u32[]{:S(2)}) collective-permute-start(bf16[384,256]{1,0:T(8,128)(2,1)S(1)} %get-tuple-element.124), channel_id=1, source_target_pairs={{0,2},{1,3},{2,0},{3,1},{4,6},{5,7},{6,4},{7,5},{8,10},{9,11},{10,... | collective-permute-start | bytes 589832 | tf_op jit(solution)/shard_map/ppermute | solution.py:25
  56.0 10.5 %collective-permute-start.24 = (bf16[384,256]{1,0:T(8,128)(2,1)S(1)}, bf16[384,256]{1,0:T(8,128)(2,1)S(1)}, u32[]{:S(2)}, u32[]{:S(2)}) collective-permute-start(bf16[384,256]{1,0:T(8,128)(2,1)S(1)} %get-tuple-element.125), channel_id=1, source_target_pairs={{0,3},{1,0},{2,1},{3,2},{4,7},{5,4},{6,5},{7,6},{8,11},{9,8},{10,9... | collective-permute-start | bytes 589832 | tf_op jit(solution)/shard_map/ppermute | solution.py:25
  58.7 10.9 %collective-permute-start.19 = (bf16[88,1024]{1,0:T(8,128)(2,1)S(1)}, bf16[88,1024]{1,0:T(8,128)(2,1)S(1)}, u32[]{:S(2)}, u32[]{:S(2)}) collective-permute-start(bf16[88,1024]{1,0:T(8,128)(2,1)S(1)} %get-tuple-element.117), channel_id=1, source_target_pairs={{0,64},{1,65},{2,66},{3,67},{4,68},{5,69},{6,70},{7,71},{8,72},{9,... | collective-permute-start | bytes 540680 | tf_op jit(solution)/shard_map/ppermute | solution.py:25
  61.3 13.4 %collective-permute-start.20 = (bf16[88,1024]{1,0:T(8,128)(2,1)S(1)}, bf16[88,1024]{1,0:T(8,128)(2,1)S(1)}, u32[]{:S(2)}, u32[]{:S(2)}) collective-permute-start(bf16[88,1024]{1,0:T(8,128)(2,1)S(1)} %get-tuple-element.118), channel_id=1, source_target_pairs={{0,128},{1,129},{2,130},{3,131},{4,132},{5,133},{6,134},{7,135},{8... | collective-permute-start | bytes 540680 | tf_op jit(solution)/shard_map/ppermute | solution.py:25
  63.3 17.7 %collective-permute-start.21 = (bf16[88,1024]{1,0:T(8,128)(2,1)S(1)}, bf16[88,1024]{1,0:T(8,128)(2,1)S(1)}, u32[]{:S(2)}, u32[]{:S(2)}) collective-permute-start(bf16[88,1024]{1,0:T(8,128)(2,1)S(1)} %get-tuple-element.119), channel_id=1, source_target_pairs={{0,192},{1,193},{2,194},{3,195},{4,196},{5,197},{6,198},{7,199},{8... | collective-permute-start | bytes 540680 | tf_op jit(solution)/shard_map/ppermute | solution.py:25
  100.9 1.7 collective-permute-start.25
  103.4 9.8 %collective-permute-start.28 = (bf16[448,128]{1,0:T(8,128)(2,1)S(1)}, bf16[448,128]{1,0:T(8,128)(2,1)S(1)}, u32[]{:S(2)}, u32[]{:S(2)}) collective-permute-start(bf16[448,128]{1,0:T(8,128)(2,1)S(1)} %get-tuple-element.136.refs_0_), channel_id=1, source_target_pairs={{0,12},{1,13},{2,14},{3,15},{4,0},{5,1},{6,2},{7,3},{8,4},{9,5},{1... | collective-permute-start | bytes 344072 | tf_op jit(solution)/shard_map/ppermute | solution.py:25
  108.0 7.5 %collective-permute-start.27 = (bf16[448,128]{1,0:T(8,128)(2,1)S(1)}, bf16[448,128]{1,0:T(8,128)(2,1)S(1)}, u32[]{:S(2)}, u32[]{:S(2)}) collective-permute-start(bf16[448,128]{1,0:T(8,128)(2,1)S(1)} %get-tuple-element.136.refs_0_), channel_id=1, source_target_pairs={{0,8},{1,9},{2,10},{3,11},{4,12},{5,13},{6,14},{7,15},{8,0},{9,1},... | collective-permute-start | bytes 344072 | tf_op jit(solution)/shard_map/ppermute | solution.py:25
  108.1 8.5 %collective-permute-start.26 = (bf16[448,128]{1,0:T(8,128)(2,1)S(1)}, bf16[448,128]{1,0:T(8,128)(2,1)S(1)}, u32[]{:S(2)}, u32[]{:S(2)}) collective-permute-start(bf16[448,128]{1,0:T(8,128)(2,1)S(1)} %get-tuple-element.136.refs_0_), channel_id=1, source_target_pairs={{0,4},{1,5},{2,6},{3,7},{4,8},{5,9},{6,10},{7,11},{8,12},{9,13},{1... | collective-permute-start | bytes 344072 | tf_op jit(solution)/shard_map/ppermute | solution.py:25
  116.7 6.6 %collective-permute-start.31 = (bf16[448,128]{1,0:T(8,128)(2,1)S(1)}, bf16[448,128]{1,0:T(8,128)(2,1)S(1)}, u32[]{:S(2)}, u32[]{:S(2)}) collective-permute-start(bf16[448,128]{1,0:T(8,128)(2,1)S(1)} %shard_map.101.refs_0_), channel_id=1, source_target_pairs={{0,3},{1,0},{2,1},{3,2},{4,7},{5,4},{6,5},{7,6},{8,11},{9,8},{10,9... | collective-permute-start | bytes 344072 | tf_op jit(solution)/shard_map/ppermute | solution.py:25
  119.7 6.3 %collective-permute-start.30 = (bf16[448,128]{1,0:T(8,128)(2,1)S(1)}, bf16[448,128]{1,0:T(8,128)(2,1)S(1)}, u32[]{:S(2)}, u32[]{:S(2)}) collective-permute-start(bf16[448,128]{1,0:T(8,128)(2,1)S(1)} %shard_map.101.refs_0_), channel_id=1, source_target_pairs={{0,2},{1,3},{2,0},{3,1},{4,6},{5,7},{6,4},{7,5},{8,10},{9,11},{10,... | collective-permute-start | bytes 344072 | tf_op jit(solution)/shard_map/ppermute | solution.py:25
  119.8 6.2 %collective-permute-start.29 = (bf16[448,128]{1,0:T(8,128)(2,1)S(1)}, bf16[448,128]{1,0:T(8,128)(2,1)S(1)}, u32[]{:S(2)}, u32[]{:S(2)}) collective-permute-start(bf16[448,128]{1,0:T(8,128)(2,1)S(1)} %shard_map.101.refs_0_), channel_id=1, source_target_pairs={{0,1},{1,2},{2,3},{3,0},{4,5},{5,6},{6,7},{7,4},{8,9},{9,10},{10,1... | collective-permute-start | bytes 344072 | tf_op jit(solution)/shard_map/ppermute | solution.py:25
  127.0 0.7 collective-permute-start.32
  127.7 15.0 %collective-permute-start.35 = (bf16[4,64,256]{2,1,0:T(8,128)(2,1)S(1)}, bf16[4,64,256]{2,1,0:T(8,128)(2,1)S(1)}, u32[]{:S(2)}, u32[]{:S(2)}) collective-permute-start(bf16[4,64,256]{2,1,0:T(8,128)(2,1)S(1)} %collective-permute-done.32.refs_0_), channel_id=1, source_target_pairs={{0,12},{1,13},{2,14},{3,15},{4,0},{5,1},{6,2},{7,3},{8,4},{9,5},{1... | collective-permute-start | bytes 393224 | tf_op jit(solution)/shard_map/ppermute | solution.py:25
  139.0 7.5 %collective-permute-start.34 = (bf16[4,64,256]{2,1,0:T(8,128)(2,1)S(1)}, bf16[4,64,256]{2,1,0:T(8,128)(2,1)S(1)}, u32[]{:S(2)}, u32[]{:S(2)}) collective-permute-start(bf16[4,64,256]{2,1,0:T(8,128)(2,1)S(1)} %collective-permute-done.32.refs_0_), channel_id=1, source_target_pairs={{0,8},{1,9},{2,10},{3,11},{4,12},{5,13},{6,14},{7,15},{8,0},{9,1},... | collective-permute-start | bytes 393224 | tf_op jit(solution)/shard_map/ppermute | solution.py:25
  140.8 6.9 %collective-permute-start.33 = (bf16[4,64,256]{2,1,0:T(8,128)(2,1)S(1)}, bf16[4,64,256]{2,1,0:T(8,128)(2,1)S(1)}, u32[]{:S(2)}, u32[]{:S(2)}) collective-permute-start(bf16[4,64,256]{2,1,0:T(8,128)(2,1)S(1)} %collective-permute-done.32.refs_0_), channel_id=1, source_target_pairs={{0,4},{1,5},{2,6},{3,7},{4,8},{5,9},{6,10},{7,11},{8,12},{9,13},{1... | collective-permute-start | bytes 393224 | tf_op jit(solution)/shard_map/ppermute | solution.py:25
  149.2 8.9 %collective-permute-start.36 = (bf16[64,1024]{1,0:T(8,128)(2,1)S(1)}, bf16[64,1024]{1,0:T(8,128)(2,1)S(1)}, u32[]{:S(2)}, u32[]{:S(2)}) collective-permute-start(bf16[64,1024]{1,0:T(8,128)(2,1)S(1)} %get-tuple-element.139), channel_id=1, source_target_pairs={{0,64},{1,65},{2,66},{3,67},{4,68},{5,69},{6,70},{7,71},{8,72},{9,... | collective-permute-start | bytes 393224 | tf_op jit(solution)/shard_map/ppermute | solution.py:25
  150.7 15.7 %collective-permute-start.37 = (bf16[64,1024]{1,0:T(8,128)(2,1)S(1)}, bf16[64,1024]{1,0:T(8,128)(2,1)S(1)}, u32[]{:S(2)}, u32[]{:S(2)}) collective-permute-start(bf16[64,1024]{1,0:T(8,128)(2,1)S(1)} %get-tuple-element.140), channel_id=1, source_target_pairs={{0,128},{1,129},{2,130},{3,131},{4,132},{5,133},{6,134},{7,135},{8... | collective-permute-start | bytes 393224 | tf_op jit(solution)/shard_map/ppermute | solution.py:25
  156.1 10.3 %collective-permute-start.38 = (bf16[64,1024]{1,0:T(8,128)(2,1)S(1)}, bf16[64,1024]{1,0:T(8,128)(2,1)S(1)}, u32[]{:S(2)}, u32[]{:S(2)}) collective-permute-start(bf16[64,1024]{1,0:T(8,128)(2,1)S(1)} %get-tuple-element.141), channel_id=1, source_target_pairs={{0,192},{1,193},{2,194},{3,195},{4,196},{5,197},{6,198},{7,199},{8... | collective-permute-start | bytes 393224 | tf_op jit(solution)/shard_map/ppermute | solution.py:25
  166.8 6.1 %collective-permute-start.41 = (bf16[448,128]{1,0:T(8,128)(2,1)S(1)}, bf16[448,128]{1,0:T(8,128)(2,1)S(1)}, u32[]{:S(2)}, u32[]{:S(2)}) collective-permute-start(bf16[448,128]{1,0:T(8,128)(2,1)S(1)} %get-tuple-element.143.refs_0_), channel_id=1, source_target_pairs={{0,12},{1,13},{2,14},{3,15},{4,0},{5,1},{6,2},{7,3},{8,4},{9,5},{1... | collective-permute-start | bytes 344072 | tf_op jit(solution)/shard_map/ppermute | solution.py:25
  167.3 7.2 %collective-permute-start.40 = (bf16[448,128]{1,0:T(8,128)(2,1)S(1)}, bf16[448,128]{1,0:T(8,128)(2,1)S(1)}, u32[]{:S(2)}, u32[]{:S(2)}) collective-permute-start(bf16[448,128]{1,0:T(8,128)(2,1)S(1)} %get-tuple-element.143.refs_0_), channel_id=1, source_target_pairs={{0,8},{1,9},{2,10},{3,11},{4,12},{5,13},{6,14},{7,15},{8,0},{9,1},... | collective-permute-start | bytes 344072 | tf_op jit(solution)/shard_map/ppermute | solution.py:25
  167.3 8.4 %collective-permute-start.39 = (bf16[448,128]{1,0:T(8,128)(2,1)S(1)}, bf16[448,128]{1,0:T(8,128)(2,1)S(1)}, u32[]{:S(2)}, u32[]{:S(2)}) collective-permute-start(bf16[448,128]{1,0:T(8,128)(2,1)S(1)} %get-tuple-element.143.refs_0_), channel_id=1, source_target_pairs={{0,4},{1,5},{2,6},{3,7},{4,8},{5,9},{6,10},{7,11},{8,12},{9,13},{1... | collective-permute-start | bytes 344072 | tf_op jit(solution)/shard_map/ppermute | solution.py:25
  175.8 9.2 %collective-permute-start.44 = (bf16[448,128]{1,0:T(8,128)(2,1)S(1)}, bf16[448,128]{1,0:T(8,128)(2,1)S(1)}, u32[]{:S(2)}, u32[]{:S(2)}) collective-permute-start(bf16[448,128]{1,0:T(8,128)(2,1)S(1)} %shard_map.105.refs_0_), channel_id=1, source_target_pairs={{0,3},{1,0},{2,1},{3,2},{4,7},{5,4},{6,5},{7,6},{8,11},{9,8},{10,9... | collective-permute-start | bytes 344072 | tf_op jit(solution)/shard_map/ppermute | solution.py:25
  180.5 7.6 %collective-permute-start.43 = (bf16[448,128]{1,0:T(8,128)(2,1)S(1)}, bf16[448,128]{1,0:T(8,128)(2,1)S(1)}, u32[]{:S(2)}, u32[]{:S(2)}) collective-permute-start(bf16[448,128]{1,0:T(8,128)(2,1)S(1)} %shard_map.105.refs_0_), channel_id=1, source_target_pairs={{0,2},{1,3},{2,0},{3,1},{4,6},{5,7},{6,4},{7,5},{8,10},{9,11},{10,... | collective-permute-start | bytes 344072 | tf_op jit(solution)/shard_map/ppermute | solution.py:25
  182.4 6.6 %collective-permute-start.42 = (bf16[448,128]{1,0:T(8,128)(2,1)S(1)}, bf16[448,128]{1,0:T(8,128)(2,1)S(1)}, u32[]{:S(2)}, u32[]{:S(2)}) collective-permute-start(bf16[448,128]{1,0:T(8,128)(2,1)S(1)} %shard_map.105.refs_0_), channel_id=1, source_target_pairs={{0,1},{1,2},{2,3},{3,0},{4,5},{5,6},{6,7},{7,4},{8,9},{9,10},{10,1... | collective-permute-start | bytes 344072 | tf_op jit(solution)/shard_map/ppermute | solution.py:25
  190.1 5.4 %collective-permute-start.45 = (bf16[64,256]{1,0:T(8,128)(2,1)S(1)}, bf16[64,256]{1,0:T(8,128)(2,1)S(1)}, u32[]{:S(2)}, u32[]{:S(2)}) collective-permute-start(bf16[64,256]{1,0:T(8,128)(2,1)S(1)} %get-tuple-element.146), channel_id=1, source_target_pairs={{0,3},{1,0},{2,1},{3,2},{4,7},{5,4},{6,5},{7,6},{8,11},{9,8},{10,9... | collective-permute-start | bytes 98312 | tf_op jit(solution)/shard_map/ppermute | solution.py:25
  193.1 5.4 %collective-permute-start.46 = (bf16[64,256]{1,0:T(8,128)(2,1)S(1)}, bf16[64,256]{1,0:T(8,128)(2,1)S(1)}, u32[]{:S(2)}, u32[]{:S(2)}) collective-permute-start(bf16[64,256]{1,0:T(8,128)(2,1)S(1)} %get-tuple-element.147), channel_id=1, source_target_pairs={{0,2},{1,3},{2,0},{3,1},{4,6},{5,7},{6,4},{7,5},{8,10},{9,11},{10,... | collective-permute-start | bytes 98312 | tf_op jit(solution)/shard_map/ppermute | solution.py:25
  193.1 5.4 %collective-permute-start.47 = (bf16[64,256]{1,0:T(8,128)(2,1)S(1)}, bf16[64,256]{1,0:T(8,128)(2,1)S(1)}, u32[]{:S(2)}, u32[]{:S(2)}) collective-permute-start(bf16[64,256]{1,0:T(8,128)(2,1)S(1)} %get-tuple-element.148), channel_id=1, source_target_pairs={{0,1},{1,2},{2,3},{3,0},{4,5},{5,6},{6,7},{7,4},{8,9},{9,10},{10,1... | collective-permute-start | bytes 98312 | tf_op jit(solution)/shard_map/ppermute | solution.py:25
  (9 other events, 79.4 us)

commit v6 on v5

--- a/solution.py
+++ b/solution.py
@@ -305,17 +305,14 @@
 
 
 def last_project_kernel(*refs):
-    turned, (later_ref, dense_ref, send_ref) = refs[SIDE : 2 * SIDE], refs[2 * SIDE :]
+    turned, (dense_ref, send_ref) = refs[SIDE : 2 * SIDE], refs[2 * SIDE :]
     slots = SIDE - 1
     rank_cols = turned[0].shape[0] // slots
     whole = summed(refs[:SIDE])
     dense_ref[...] = whole
     dense = whole.astype(BF16)
     pieces = [project(dense, turned, slot, rank_cols) for slot in range(slots)]
-    send = jnp.concatenate(pieces, axis=0).astype(BF16)
-    n = send.shape[0]
-    send_ref[:n] = send
-    send_ref[n:] = later_ref[...]
+    send_ref[...] = jnp.concatenate(pieces, axis=0).astype(BF16)
 
 
 def add_kernel(*refs):
@@ -323,10 +320,15 @@
 
 
 def finish_kernel(is_lower, *refs):
-    dense_ref, extra_ref, ranks_ref = refs[SIDE : SIDE + 3]
-    out_refs, sums_ref = refs[SIDE + 3 : -1], refs[-1]
+    count = SIDE if is_lower else 2 * SIDE
+    dense_ref, extra_ref, ranks_ref = refs[count : count + 3]
+    out_refs, sums_ref = refs[count + 3 : -1], refs[-1]
     for s in range(SIDE):
-        sums_ref[wrapped(own_tile() - s)] = refs[s][...]
+        tile = wrapped(own_tile() - s)
+        held = refs[s].shape[0]
+        sums_ref[tile, :held] = refs[s][...]
+        if not is_lower:
+            sums_ref[tile, held:] = refs[SIDE + s][...]
     n = dense_ref.shape[0]
     rank_cols = extra_ref.shape[0] // (SIDE - 1)
     width = dense_ref.shape[1] // SIDE
@@ -435,23 +437,31 @@
         ),
     )(dense, mine, swap_core(mine), *turned)
 
-    def finished(is_lower, send, dense, ranks):
-        sums = kernel_call(add_kernel, shape((packed, rank_cols), BF16))(*gathered_y(send))
+    def summed_everywhere(value):
+        add = kernel_call(add_kernel, shape(value.shape, BF16))
+        return gathered_x(add(*gathered_y(value)))
+
+    def finished(is_lower, sums, dense, ranks):
         outs = [shape((SIDE, n, width), BF16)] if is_lower else [shape((n, width), BF16)] * SIDE
         return kernel_call(
             lambda *refs: finish_kernel(is_lower, *refs),
             outs,
-            smem=(SIDE + 2,),
+            smem=(len(sums) + 2,),
             scratch=[pltpu.VMEM((SIDE, packed, rank_cols), BF16)],
-        )(*gathered_x(sums), dense, extra, ranks)
-
-    [rows] = finished(True, send, dense, low_ranks)
-    parts = products(n, gathered_y(swapped(rows)), *upper)
+        )(*sums, dense, extra, ranks)
+
+    [rows] = finished(True, summed_everywhere(send), dense, low_ranks)
+    rows, later = tied((swapped(rows), later))
+    gathered = gathered_y(rows)
+    add = kernel_call(add_kernel, shape(later.shape, BF16))
+    later = add(*gathered_y(later))
+    received = scattered_q(products(n, gathered, *upper))
+    received, later = tied((received, gathered_x(later)))
     dense, send = kernel_call(
         last_project_kernel,
-        (shape((n, total), F32), shape((packed, rank_cols), BF16)),
-    )(*scattered_q(parts), *turned, later)
-    rows = finished(False, send, dense, up_ranks)
+        (shape((n, total), F32), shape((slots * n, rank_cols), BF16)),
+    )(*received, *turned)
+    rows = finished(False, summed_everywhere(send) + list(later), dense, up_ranks)
     return kernel_call(
         lambda *refs: order_kernel(-1, *refs), shape((SIDE, n, width), F32)
     )(*scattered_x(rows, -1))

time: 200 us -> 213 us (1.065)
  the two profiles are of different devices: /device:TPU:2 before, /device:TPU:32 now
where the time goes in v6:
time: 213 us; the launch traced here: 209 us
  starting transfers between devices  95.5 us (45%)
  waiting for transfers between devices  76.8 us (36%)
  blocking collectives  23.8 us (11%)
  Pallas kernels  9.16 us (4%)
  local copies, waits for them, and re-layouts  3.19 us (1%)
    ppermute x54, starting transfers between devices, permuted(): return lax.ppermute(value, ('row', 'col'), routes(to))  95.5 us
    ppermute x54, waiting for transfers between devices, permuted(): return lax.ppermute(value, ('row', 'col'), routes(to))  76.8 us
    all_to_all x1, blocking collectives, from_every_z(): lax.all_to_all(value, 'row', 0, 0, tiled=True, axis_index_groups=Z_GROUPS)  23.8 us
    pallas_call x18, Pallas kernels, run(): pl.pallas_call(body, out_shape=out_shape, in_specs=specs, scratch_shapes=...  9.16 us
  transfers between devices with their start and end apart: 54, of which 36 were waited for; matrix products, arithmetic and copies ran while one was open for 0% of the time, Pallas kernels for 2%

profile of v6, /device:TPU:32, one launch (start us, length us, event | category | flops | bytes accessed | tf_op | source)
XLA Modules:
  0.0 208.9 jit_solution(18099544595189845213)
XLA Ops:
  1.1 1.6 collective-permute-start
  2.7 2.7 %collective-permute-start.1 = (bf16[256,256]{1,0:T(8,128)(2,1)S(1)}, bf16[256,256]{1,0:T(8,128)(2,1)S(1)}, u32[]{:S(2)}, u32[]{:S(2)}) collective-permute-start(bf16[256,256]{1,0:T(8,128)(2,1)S(1)} %get-tuple-element.89), channel_id=1, source_target_pairs={{0,2},{1,3},{2,0},{3,1},{4,6},{5,7},{6,4},{7,5},{8,10},{9,11},{10,... | collective-permute-start | bytes 393224 | tf_op jit(solution)/shard_map/ppermute | solution.py:25
  5.4 1.4 collective-permute-start.2
  10.8 3.8 %collective-permute-done.3.refs_1_ = bf16[88,256]{1,0:T(8,128)(2,1)S(1)} collective-permute-done((bf16[88,256]{1,0:T(8,128)(2,1)S(1)}, bf16[88,256]{1,0:T(8,128)(2,1)S(1)}, u32[]{:S(2)}, u32[]{:S(2)}) %collective-permute-start.3) | collective-permute-done | bytes 45088 | tf_op jit(solution)/shard_map/ppermute | solution.py:25
  15.4 3.2 %collective-permute-done.5.refs_3_ = bf16[88,256]{1,0:T(8,128)(2,1)S(1)} collective-permute-done((bf16[88,256]{1,0:T(8,128)(2,1)S(1)}, bf16[88,256]{1,0:T(8,128)(2,1)S(1)}, u32[]{:S(2)}, u32[]{:S(2)}) %collective-permute-start.5) | collective-permute-done | bytes 45088 | tf_op jit(solution)/shard_map/ppermute | solution.py:25
  19.8 2.7 %collective-permute-start.7 = (bf16[256,256]{1,0:T(8,128)(2,1)S(1)}, bf16[256,256]{1,0:T(8,128)(2,1)S(1)}, u32[]{:S(2)}, u32[]{:S(2)}) collective-permute-start(bf16[256,256]{1,0:T(8,128)(2,1)S(1)} %get-tuple-element.106), channel_id=1, source_target_pairs={{0,2},{1,3},{2,0},{3,1},{4,6},{5,7},{6,4},{7,5},{8,10},{9,11},{10,... | collective-permute-start | bytes 393224 | tf_op jit(solution)/shard_map/ppermute | solution.py:25
  23.6 3.8 %collective-permute-done.6.refs_1_ = bf16[256,256]{1,0:T(8,128)(2,1)S(1)} collective-permute-done((bf16[256,256]{1,0:T(8,128)(2,1)S(1)}, bf16[256,256]{1,0:T(8,128)(2,1)S(1)}, u32[]{:S(2)}, u32[]{:S(2)}) %collective-permute-start.6) | collective-permute-done | bytes 131104 | tf_op jit(solution)/shard_map/ppermute | solution.py:25
  28.5 10.6 %collective-permute-start.12 = (bf16[4,88,256]{2,1,0:T(8,128)(2,1)S(1)}, bf16[4,88,256]{2,1,0:T(8,128)(2,1)S(1)}, u32[]{:S(2)}, u32[]{:S(2)}) collective-permute-start(bf16[4,88,256]{2,1,0:T(8,128)(2,1)S(1)} %collective-permute-done.9.refs_0_), channel_id=1, source_target_pairs={{0,12},{1,13},{2,14},{3,15},{4,0},{5,1},{6,2},{7,3},{8,4},{9,5},{1... | collective-permute-start | bytes 540680 | tf_op jit(solution)/shard_map/ppermute | solution.py:25
  39.8 1.4 collective-permute-start.10
  41.2 5.7 %collective-permute-done.12.refs_3_ = bf16[4,88,256]{2,1,0:T(8,128)(2,1)S(1)} collective-permute-done((bf16[4,88,256]{2,1,0:T(8,128)(2,1)S(1)}, bf16[4,88,256]{2,1,0:T(8,128)(2,1)S(1)}, u32[]{:S(2)}, u32[]{:S(2)}) %collective-permute-start.12) | collective-permute-done | bytes 180256 | tf_op jit(solution)/shard_map/ppermute | solution.py:25
  46.9 1.2 collective-permute-done.11.refs_2_
  48.1 2.2 %collective-permute-done.10.refs_1_ = bf16[4,88,256]{2,1,0:T(8,128)(2,1)S(1)} collective-permute-done((bf16[4,88,256]{2,1,0:T(8,128)(2,1)S(1)}, bf16[4,88,256]{2,1,0:T(8,128)(2,1)S(1)}, u32[]{:S(2)}, u32[]{:S(2)}) %collective-permute-start.10) | collective-permute-done | bytes 180256 | tf_op jit(solution)/shard_map/ppermute | solution.py:25
  52.3 2.2 %collective-permute-start.23 = (bf16[384,256]{1,0:T(8,128)(2,1)S(1)}, bf16[384,256]{1,0:T(8,128)(2,1)S(1)}, u32[]{:S(2)}, u32[]{:S(2)}) collective-permute-start(bf16[384,256]{1,0:T(8,128)(2,1)S(1)} %get-tuple-element.134), channel_id=1, source_target_pairs={{0,2},{1,3},{2,0},{3,1},{4,6},{5,7},{6,4},{7,5},{8,10},{9,11},{10,... | collective-permute-start | bytes 589832 | tf_op jit(solution)/shard_map/ppermute | solution.py:25
  55.4 2.4 %shard_map.97 = (bf16[88,1024]{1,0:T(8,128)(2,1)S(1)}, bf16[88,1024]{1,0:T(8,128)(2,1)S(1)}, bf16[88,1024]{1,0:T(8,128)(2,1)S(1)}, bf16[88,1024]{1,0:T(8,128)(2,1)S(1)}) custom-call(bf16[4,88,256]{2,1,0:T(8,128)(2,1)S(1)} %collective-permute-done.9.refs_0_, bf16[4,88,256]{2,1,0:T(8,128)(2,1)S(1)} %collective-permute-done.10.refs_1_, ...), custom_call_target="tpu_custom_call" | custom-call | flops 738197504 | bytes 5636096 | tf_op jit(solution)/shard_map/pallas_call | solution.py:106
  57.8 2.0 collective-permute-start.19
  59.9 4.4 %collective-permute-start.20 = (bf16[88,1024]{1,0:T(8,128)(2,1)S(1)}, bf16[88,1024]{1,0:T(8,128)(2,1)S(1)}, u32[]{:S(2)}, u32[]{:S(2)}) collective-permute-start(bf16[88,1024]{1,0:T(8,128)(2,1)S(1)} %get-tuple-element.128), channel_id=1, source_target_pairs={{0,128},{1,129},{2,130},{3,131},{4,132},{5,133},{6,134},{7,135},{8... | collective-permute-start | bytes 540680 | tf_op jit(solution)/shard_map/ppermute | solution.py:25
  64.4 4.5 %collective-permute-start.21 = (bf16[88,1024]{1,0:T(8,128)(2,1)S(1)}, bf16[88,1024]{1,0:T(8,128)(2,1)S(1)}, u32[]{:S(2)}, u32[]{:S(2)}) collective-permute-start(bf16[88,1024]{1,0:T(8,128)(2,1)S(1)} %get-tuple-element.129), channel_id=1, source_target_pairs={{0,192},{1,193},{2,194},{3,195},{4,196},{5,197},{6,198},{7,199},{8... | collective-permute-start | bytes 540680 | tf_op jit(solution)/shard_map/ppermute | solution.py:25
  68.8 4.3 %collective-permute-done.19.refs_1_ = bf16[88,1024]{1,0:T(8,128)(2,1)S(1)} collective-permute-done((bf16[88,1024]{1,0:T(8,128)(2,1)S(1)}, bf16[88,1024]{1,0:T(8,128)(2,1)S(1)}, u32[]{:S(2)}, u32[]{:S(2)}) %collective-permute-start.19) | collective-permute-done | bytes 180256 | tf_op jit(solution)/shard_map/ppermute | solution.py:25
  73.5 3.1 %collective-permute-done.21.refs_3_ = bf16[88,1024]{1,0:T(8,128)(2,1)S(1)} collective-permute-done((bf16[88,1024]{1,0:T(8,128)(2,1)S(1)}, bf16[88,1024]{1,0:T(8,128)(2,1)S(1)}, u32[]{:S(2)}, u32[]{:S(2)}) %collective-permute-start.21) | collective-permute-done | bytes 180256 | tf_op jit(solution)/shard_map/ppermute | solution.py:25
  76.7 23.8 %all_to_all.5.mine_ref = bf16[8,24,1024]{2,1,0:T(8,128)(2,1)S(1)} all-to-all(bf16[8,24,1024]{2,1,0:T(8,128)(2,1)S(1)} %get-tuple-element.141), channel_id=1, replica_groups={{0,32,64,96,128,160,192,224},{16,48,80,112,144,176,208,240},{1,33,65,97..., dimensions={0} | all-to-all | bytes 786432 | tf_op jit(solution)/shard_map/all_to_all | solution.py:55
  100.5 1.7 collective-permute-done.25.other_ref
  103.0 6.3 %collective-permute-start.28 = (bf16[448,128]{1,0:T(8,128)(2,1)S(1)}, bf16[448,128]{1,0:T(8,128)(2,1)S(1)}, u32[]{:S(2)}, u32[]{:S(2)}) collective-permute-start(bf16[448,128]{1,0:T(8,128)(2,1)S(1)} %get-tuple-element.146.refs_0_), channel_id=1, source_target_pairs={{0,12},{1,13},{2,14},{3,15},{4,0},{5,1},{6,2},{7,3},{8,4},{9,5},{1... | collective-permute-start | bytes 344072 | tf_op jit(solution)/shard_map/ppermute | solution.py:25
  110.3 4.2 %collective-permute-done.28.refs_3_ = bf16[448,128]{1,0:T(8,128)(2,1)S(1)} collective-permute-done((bf16[448,128]{1,0:T(8,128)(2,1)S(1)}, bf16[448,128]{1,0:T(8,128)(2,1)S(1)}, u32[]{:S(2)}, u32[]{:S(2)}) %collective-permute-start.28) | collective-permute-done | bytes 114720 | tf_op jit(solution)/shard_map/ppermute | solution.py:25
  114.5 2.4 %collective-permute-done.27.refs_2_ = bf16[448,128]{1,0:T(8,128)(2,1)S(1)} collective-permute-done((bf16[448,128]{1,0:T(8,128)(2,1)S(1)}, bf16[448,128]{1,0:T(8,128)(2,1)S(1)}, u32[]{:S(2)}, u32[]{:S(2)}) %collective-permute-start.27) | collective-permute-done | bytes 114720 | tf_op jit(solution)/shard_map/ppermute | solution.py:25
  118.1 1.1 collective-permute-start.30
  120.2 3.9 %collective-permute-done.31.refs_3_ = bf16[448,128]{1,0:T(8,128)(2,1)S(1)} collective-permute-done((bf16[448,128]{1,0:T(8,128)(2,1)S(1)}, bf16[448,128]{1,0:T(8,128)(2,1)S(1)}, u32[]{:S(2)}, u32[]{:S(2)}) %collective-permute-start.31) | collective-permute-done | bytes 114720 | tf_op jit(solution)/shard_map/ppermute | solution.py:25
  125.0 1.9 collective-permute-done.29.refs_1_
  128.6 14.9 %collective-permute-start.41 = (bf16[256,128]{1,0:T(8,128)(2,1)S(1)}, bf16[256,128]{1,0:T(8,128)(2,1)S(1)}, u32[]{:S(2)}, u32[]{:S(2)}) collective-permute-start(bf16[256,128]{1,0:T(8,128)(2,1)S(1)} %get-tuple-element.154.refs_0_), channel_id=1, source_target_pairs={{0,12},{1,13},{2,14},{3,15},{4,0},{5,1},{6,2},{7,3},{8,4},{9,5},{1... | collective-permute-start | bytes 196616 | tf_op jit(solution)/shard_map/ppermute | solution.py:25
  143.5 9.5 %collective-permute-start.35 = (bf16[4,64,256]{2,1,0:T(8,128)(2,1)S(1)}, bf16[4,64,256]{2,1,0:T(8,128)(2,1)S(1)}, u32[]{:S(2)}, u32[]{:S(2)}) collective-permute-start(bf16[4,64,256]{2,1,0:T(8,128)(2,1)S(1)} %collective-permute-done.32.refs_0_), channel_id=1, source_target_pairs={{0,12},{1,13},{2,14},{3,15},{4,0},{5,1},{6,2},{7,3},{8,4},{9,5},{1... | collective-permute-start | bytes 393224 | tf_op jit(solution)/shard_map/ppermute | solution.py:25
  153.0 1.9 collective-permute-start.33
  155.0 4.1 %collective-permute-start.40 = (bf16[256,128]{1,0:T(8,128)(2,1)S(1)}, bf16[256,128]{1,0:T(8,128)(2,1)S(1)}, u32[]{:S(2)}, u32[]{:S(2)}) collective-permute-start(bf16[256,128]{1,0:T(8,128)(2,1)S(1)} %get-tuple-element.154.refs_0_), channel_id=1, source_target_pairs={{0,8},{1,9},{2,10},{3,11},{4,12},{5,13},{6,14},{7,15},{8,0},{9,1},... | collective-permute-start | bytes 196616 | tf_op jit(solution)/shard_map/ppermute | solution.py:25
  159.1 3.6 %collective-permute-done.40.refs_2_ = bf16[256,128]{1,0:T(8,128)(2,1)S(1)} collective-permute-done((bf16[256,128]{1,0:T(8,128)(2,1)S(1)}, bf16[256,128]{1,0:T(8,128)(2,1)S(1)}, u32[]{:S(2)}, u32[]{:S(2)}) %collective-permute-start.40) | collective-permute-done | bytes 65568 | tf_op jit(solution)/shard_map/ppermute | solution.py:25
  162.7 1.8 collective-permute-done.39.refs_1_
  164.6 2.3 %collective-permute-start.44 = (bf16[256,128]{1,0:T(8,128)(2,1)S(1)}, bf16[256,128]{1,0:T(8,128)(2,1)S(1)}, u32[]{:S(2)}, u32[]{:S(2)}) collective-permute-start(bf16[256,128]{1,0:T(8,128)(2,1)S(1)} %shard_map.104.refs_4_), channel_id=1, source_target_pairs={{0,3},{1,0},{2,1},{3,2},{4,7},{5,4},{6,5},{7,6},{8,11},{9,8},{10,9... | collective-permute-start | bytes 196616 | tf_op jit(solution)/shard_map/ppermute | solution.py:25
  167.0 1.6 shard_map.103
  168.9 3.9 %collective-permute-start.38 = (bf16[64,1024]{1,0:T(8,128)(2,1)S(1)}, bf16[64,1024]{1,0:T(8,128)(2,1)S(1)}, u32[]{:S(2)}, u32[]{:S(2)}) collective-permute-start(bf16[64,1024]{1,0:T(8,128)(2,1)S(1)} %get-tuple-element.153), channel_id=1, source_target_pairs={{0,192},{1,193},{2,194},{3,195},{4,196},{5,197},{6,198},{7,199},{8... | collective-permute-start | bytes 393224 | tf_op jit(solution)/shard_map/ppermute | solution.py:25
  173.7 5.0 %collective-permute-done.43.refs_6_ = bf16[256,128]{1,0:T(8,128)(2,1)S(1)} collective-permute-done((bf16[256,128]{1,0:T(8,128)(2,1)S(1)}, bf16[256,128]{1,0:T(8,128)(2,1)S(1)}, u32[]{:S(2)}, u32[]{:S(2)}) %collective-permute-start.43) | collective-permute-done | bytes 65568 | tf_op jit(solution)/shard_map/ppermute | solution.py:25
  179.0 3.0 %collective-permute-done.36.refs_1_ = bf16[64,1024]{1,0:T(8,128)(2,1)S(1)} collective-permute-done((bf16[64,1024]{1,0:T(8,128)(2,1)S(1)}, bf16[64,1024]{1,0:T(8,128)(2,1)S(1)}, u32[]{:S(2)}, u32[]{:S(2)}) %collective-permute-start.36) | collective-permute-done | bytes 131104 | tf_op jit(solution)/shard_map/ppermute | solution.py:25
  182.4 2.0 collective-permute-done.38.refs_3_
  185.7 1.2 collective-permute-start.45
  186.9 2.1 collective-permute-done.47.refs_3_
  189.0 2.4 %collective-permute-done.46.refs_2_ = bf16[192,128]{1,0:T(8,128)(2,1)S(1)} collective-permute-done((bf16[192,128]{1,0:T(8,128)(2,1)S(1)}, bf16[192,128]{1,0:T(8,128)(2,1)S(1)}, u32[]{:S(2)}, u32[]{:S(2)}) %collective-permute-start.46) | collective-permute-done | bytes 49184 | tf_op jit(solution)/shard_map/ppermute | solution.py:25
  192.1 1.9 collective-permute-start.48
  194.0 2.1 collective-permute-done.50.refs_3_
  196.1 1.6 collective-permute-done.49.refs_2_
  198.8 1.1 shard_map.107
  199.8 2.1 %collective-permute-start.51 = (bf16[64,256]{1,0:T(8,128)(2,1)S(1)}, bf16[64,256]{1,0:T(8,128)(2,1)S(1)}, u32[]{:S(2)}, u32[]{:S(2)}) collective-permute-start(bf16[64,256]{1,0:T(8,128)(2,1)S(1)} %get-tuple-element.166), channel_id=1, source_target_pairs={{0,3},{1,0},{2,1},{3,2},{4,7},{5,4},{6,5},{7,6},{8,11},{9,8},{10,9... | collective-permute-start | bytes 98312 | tf_op jit(solution)/shard_map/ppermute | solution.py:25
  203.8 3.5 %collective-permute-done.52.refs_2_ = bf16[64,256]{1,0:T(8,128)(2,1)S(1)} collective-permute-done((bf16[64,256]{1,0:T(8,128)(2,1)S(1)}, bf16[64,256]{1,0:T(8,128)(2,1)S(1)}, u32[]{:S(2)}, u32[]{:S(2)}) %collective-permute-start.52) | collective-permute-done | bytes 32800 | tf_op jit(solution)/shard_map/ppermute | solution.py:25
  (97 shorter events, 28.2 us)
Async XLA Ops:
  1.1 17.5 %collective-permute-start = (bf16[256,256]{1,0:T(8,128)(2,1)S(1)}, bf16[256,256]{1,0:T(8,128)(2,1)S(1)}, u32[]{:S(2)}, u32[]{:S(2)}) collective-permute-start(bf16[256,256]{1,0:T(8,128)(2,1)S(1)} %get-tuple-element.88), channel_id=1, source_target_pairs={{0,1},{1,2},{2,3},{3,0},{4,5},{5,6},{6,7},{7,4},{8,9},{9,10},{10,1... | collective-permute-start | bytes 393224 | tf_op jit(solution)/shard_map/ppermute | solution.py:25
  2.7 16.0 %collective-permute-start.1 = (bf16[256,256]{1,0:T(8,128)(2,1)S(1)}, bf16[256,256]{1,0:T(8,128)(2,1)S(1)}, u32[]{:S(2)}, u32[]{:S(2)}) collective-permute-start(bf16[256,256]{1,0:T(8,128)(2,1)S(1)} %get-tuple-element.89), channel_id=1, source_target_pairs={{0,2},{1,3},{2,0},{3,1},{4,6},{5,7},{6,4},{7,5},{8,10},{9,11},{10,... | collective-permute-start | bytes 393224 | tf_op jit(solution)/shard_map/ppermute | solution.py:25
  5.4 13.2 %collective-permute-start.2 = (bf16[256,256]{1,0:T(8,128)(2,1)S(1)}, bf16[256,256]{1,0:T(8,128)(2,1)S(1)}, u32[]{:S(2)}, u32[]{:S(2)}) collective-permute-start(bf16[256,256]{1,0:T(8,128)(2,1)S(1)} %get-tuple-element.90), channel_id=1, source_target_pairs={{0,3},{1,0},{2,1},{3,2},{4,7},{5,4},{6,5},{7,6},{8,11},{9,8},{10,9... | collective-permute-start | bytes 393224 | tf_op jit(solution)/shard_map/ppermute | solution.py:25
  9.3 5.3 %collective-permute-start.3 = (bf16[88,256]{1,0:T(8,128)(2,1)S(1)}, bf16[88,256]{1,0:T(8,128)(2,1)S(1)}, u32[]{:S(2)}, u32[]{:S(2)}) collective-permute-start(bf16[88,256]{1,0:T(8,128)(2,1)S(1)} %get-tuple-element.92), channel_id=1, source_target_pairs={{0,1},{1,2},{2,3},{3,0},{4,5},{5,6},{6,7},{7,4},{8,9},{9,10},{10,1... | collective-permute-start | bytes 135176 | tf_op jit(solution)/shard_map/ppermute | solution.py:25
  9.9 5.6 %collective-permute-start.4 = (bf16[88,256]{1,0:T(8,128)(2,1)S(1)}, bf16[88,256]{1,0:T(8,128)(2,1)S(1)}, u32[]{:S(2)}, u32[]{:S(2)}) collective-permute-start(bf16[88,256]{1,0:T(8,128)(2,1)S(1)} %get-tuple-element.93), channel_id=1, source_target_pairs={{0,2},{1,3},{2,0},{3,1},{4,6},{5,7},{6,4},{7,5},{8,10},{9,11},{10,... | collective-permute-start | bytes 135176 | tf_op jit(solution)/shard_map/ppermute | solution.py:25
  18.7 9.6 %collective-permute-start.9 = (bf16[4,88,256]{2,1,0:T(8,128)(2,1)S(1)}, bf16[4,88,256]{2,1,0:T(8,128)(2,1)S(1)}, u32[]{:S(2)}, u32[]{:S(2)}) collective-permute-start(bf16[4,88,256]{2,1,0:T(8,128)(2,1)S(1)} %shard_map.93), channel_id=1, source_target_pairs={{0,0},{1,1},{2,2},{3,3},{4,64},{5,65},{6,66},{7,67},{8,128},{9,129... | collective-permute-start | bytes 540680 | tf_op jit(solution)/shard_map/ppermute | solution.py:25
  19.7 7.7 %collective-permute-start.6 = (bf16[256,256]{1,0:T(8,128)(2,1)S(1)}, bf16[256,256]{1,0:T(8,128)(2,1)S(1)}, u32[]{:S(2)}, u32[]{:S(2)}) collective-permute-start(bf16[256,256]{1,0:T(8,128)(2,1)S(1)} %get-tuple-element.105), channel_id=1, source_target_pairs={{0,1},{1,2},{2,3},{3,0},{4,5},{5,6},{6,7},{7,4},{8,9},{9,10},{10,1... | collective-permute-start | bytes 393224 | tf_op jit(solution)/shard_map/ppermute | solution.py:25
  19.8 7.6 %collective-permute-start.7 = (bf16[256,256]{1,0:T(8,128)(2,1)S(1)}, bf16[256,256]{1,0:T(8,128)(2,1)S(1)}, u32[]{:S(2)}, u32[]{:S(2)}) collective-permute-start(bf16[256,256]{1,0:T(8,128)(2,1)S(1)} %get-tuple-element.106), channel_id=1, source_target_pairs={{0,2},{1,3},{2,0},{3,1},{4,6},{5,7},{6,4},{7,5},{8,10},{9,11},{10,... | collective-permute-start | bytes 393224 | tf_op jit(solution)/shard_map/ppermute | solution.py:25
  22.5 5.8 %collective-permute-start.8 = (bf16[256,256]{1,0:T(8,128)(2,1)S(1)}, bf16[256,256]{1,0:T(8,128)(2,1)S(1)}, u32[]{:S(2)}, u32[]{:S(2)}) collective-permute-start(bf16[256,256]{1,0:T(8,128)(2,1)S(1)} %get-tuple-element.107), channel_id=1, source_target_pairs={{0,3},{1,0},{2,1},{3,2},{4,7},{5,4},{6,5},{7,6},{8,11},{9,8},{10,9... | collective-permute-start | bytes 393224 | tf_op jit(solution)/shard_map/ppermute | solution.py:25
  23.1 27.3 %collective-permute-start.13 = (bf16[1024,256]{1,0:T(8,128)(2,1)S(1)}, bf16[1024,256]{1,0:T(8,128)(2,1)S(1)}, u32[]{:S(2)}, u32[]{:S(2)}) collective-permute-start(bf16[1024,256]{1,0:T(8,128)(2,1)S(1)} %shard_map.94.refs_4_), channel_id=1, source_target_pairs={{0,32},{1,33},{2,34},{3,35},{4,36},{5,37},{6,38},{7,39},{8,40},{9,... | collective-permute-start | bytes 1572872 | tf_op jit(solution)/shard_map/ppermute | solution.py:25
  28.4 22.5 %collective-permute-start.17 = (bf16[1024,256]{1,0:T(8,128)(2,1)S(1)}, bf16[1024,256]{1,0:T(8,128)(2,1)S(1)}, u32[]{:S(2)}, u32[]{:S(2)}) collective-permute-start(bf16[1024,256]{1,0:T(8,128)(2,1)S(1)} %shard_map.96.refs_8_.refs_4_), channel_id=1, source_target_pairs={{0,32},{1,33},{2,34},{3,35},{4,36},{5,37},{6,38},{7,39},{8,40},{9,... | collective-permute-start | bytes 1572872 | tf_op jit(solution)/shard_map/ppermute | solution.py:25
  28.5 18.4 %collective-permute-start.12 = (bf16[4,88,256]{2,1,0:T(8,128)(2,1)S(1)}, bf16[4,88,256]{2,1,0:T(8,128)(2,1)S(1)}, u32[]{:S(2)}, u32[]{:S(2)}) collective-permute-start(bf16[4,88,256]{2,1,0:T(8,128)(2,1)S(1)} %collective-permute-done.9.refs_0_), channel_id=1, source_target_pairs={{0,12},{1,13},{2,14},{3,15},{4,0},{5,1},{6,2},{7,3},{8,4},{9,5},{1... | collective-permute-start | bytes 540680 | tf_op jit(solution)/shard_map/ppermute | solution.py:25
  39.1 9.0 %collective-permute-start.11 = (bf16[4,88,256]{2,1,0:T(8,128)(2,1)S(1)}, bf16[4,88,256]{2,1,0:T(8,128)(2,1)S(1)}, u32[]{:S(2)}, u32[]{:S(2)}) collective-permute-start(bf16[4,88,256]{2,1,0:T(8,128)(2,1)S(1)} %collective-permute-done.9.refs_0_), channel_id=1, source_target_pairs={{0,8},{1,9},{2,10},{3,11},{4,12},{5,13},{6,14},{7,15},{8,0},{9,1},... | collective-permute-start | bytes 540680 | tf_op jit(solution)/shard_map/ppermute | solution.py:25
  39.8 10.6 %collective-permute-start.10 = (bf16[4,88,256]{2,1,0:T(8,128)(2,1)S(1)}, bf16[4,88,256]{2,1,0:T(8,128)(2,1)S(1)}, u32[]{:S(2)}, u32[]{:S(2)}) collective-permute-start(bf16[4,88,256]{2,1,0:T(8,128)(2,1)S(1)} %collective-permute-done.9.refs_0_), channel_id=1, source_target_pairs={{0,4},{1,5},{2,6},{3,7},{4,8},{5,9},{6,10},{7,11},{8,12},{9,13},{1... | collective-permute-start | bytes 540680 | tf_op jit(solution)/shard_map/ppermute | solution.py:25
  50.9 4.6 %collective-permute-start.16 = (bf16[1024,256]{1,0:T(8,128)(2,1)S(1)}, bf16[1024,256]{1,0:T(8,128)(2,1)S(1)}, u32[]{:S(2)}, u32[]{:S(2)}) collective-permute-start(bf16[1024,256]{1,0:T(8,128)(2,1)S(1)} %shard_map.96.refs_8_.refs_4_), channel_id=1, source_target_pairs={{0,16},{1,17},{2,18},{3,19},{4,20},{5,21},{6,22},{7,23},{8,24},{9,... | collective-permute-start | bytes 1572872 | tf_op jit(solution)/shard_map/ppermute | solution.py:25
  50.9 4.6 %collective-permute-start.18 = (bf16[1024,256]{1,0:T(8,128)(2,1)S(1)}, bf16[1024,256]{1,0:T(8,128)(2,1)S(1)}, u32[]{:S(2)}, u32[]{:S(2)}) collective-permute-start(bf16[1024,256]{1,0:T(8,128)(2,1)S(1)} %collective-permute-done.17.refs_10_.refs_6_), channel_id=1, source_target_pairs={{0,16},{1,17},{2,18},{3,19},{4,20},{5,21},{6,22},{7,23},{8,24},{9,... | collective-permute-start | bytes 1572872 | tf_op jit(solution)/shard_map/ppermute | solution.py:25
  52.0 12.3 %collective-permute-start.22 = (bf16[384,256]{1,0:T(8,128)(2,1)S(1)}, bf16[384,256]{1,0:T(8,128)(2,1)S(1)}, u32[]{:S(2)}, u32[]{:S(2)}) collective-permute-start(bf16[384,256]{1,0:T(8,128)(2,1)S(1)} %get-tuple-element.133), channel_id=1, source_target_pairs={{0,1},{1,2},{2,3},{3,0},{4,5},{5,6},{6,7},{7,4},{8,9},{9,10},{10,1... | collective-permute-start | bytes 589832 | tf_op jit(solution)/shard_map/ppermute | solution.py:25
  52.3 16.6 %collective-permute-start.23 = (bf16[384,256]{1,0:T(8,128)(2,1)S(1)}, bf16[384,256]{1,0:T(8,128)(2,1)S(1)}, u32[]{:S(2)}, u32[]{:S(2)}) collective-permute-start(bf16[384,256]{1,0:T(8,128)(2,1)S(1)} %get-tuple-element.134), channel_id=1, source_target_pairs={{0,2},{1,3},{2,0},{3,1},{4,6},{5,7},{6,4},{7,5},{8,10},{9,11},{10,... | collective-permute-start | bytes 589832 | tf_op jit(solution)/shard_map/ppermute | solution.py:25
  54.5 14.3 %collective-permute-start.24 = (bf16[384,256]{1,0:T(8,128)(2,1)S(1)}, bf16[384,256]{1,0:T(8,128)(2,1)S(1)}, u32[]{:S(2)}, u32[]{:S(2)}) collective-permute-start(bf16[384,256]{1,0:T(8,128)(2,1)S(1)} %get-tuple-element.135), channel_id=1, source_target_pairs={{0,3},{1,0},{2,1},{3,2},{4,7},{5,4},{6,5},{7,6},{8,11},{9,8},{10,9... | collective-permute-start | bytes 589832 | tf_op jit(solution)/shard_map/ppermute | solution.py:25
  57.8 15.4 %collective-permute-start.19 = (bf16[88,1024]{1,0:T(8,128)(2,1)S(1)}, bf16[88,1024]{1,0:T(8,128)(2,1)S(1)}, u32[]{:S(2)}, u32[]{:S(2)}) collective-permute-start(bf16[88,1024]{1,0:T(8,128)(2,1)S(1)} %get-tuple-element.127), channel_id=1, source_target_pairs={{0,64},{1,65},{2,66},{3,67},{4,68},{5,69},{6,70},{7,71},{8,72},{9,... | collective-permute-start | bytes 540680 | tf_op jit(solution)/shard_map/ppermute | solution.py:25
  59.9 13.6 %collective-permute-start.20 = (bf16[88,1024]{1,0:T(8,128)(2,1)S(1)}, bf16[88,1024]{1,0:T(8,128)(2,1)S(1)}, u32[]{:S(2)}, u32[]{:S(2)}) collective-permute-start(bf16[88,1024]{1,0:T(8,128)(2,1)S(1)} %get-tuple-element.128), channel_id=1, source_target_pairs={{0,128},{1,129},{2,130},{3,131},{4,132},{5,133},{6,134},{7,135},{8... | collective-permute-start | bytes 540680 | tf_op jit(solution)/shard_map/ppermute | solution.py:25
  64.4 12.3 %collective-permute-start.21 = (bf16[88,1024]{1,0:T(8,128)(2,1)S(1)}, bf16[88,1024]{1,0:T(8,128)(2,1)S(1)}, u32[]{:S(2)}, u32[]{:S(2)}) collective-permute-start(bf16[88,1024]{1,0:T(8,128)(2,1)S(1)} %get-tuple-element.129), channel_id=1, source_target_pairs={{0,192},{1,193},{2,194},{3,195},{4,196},{5,197},{6,198},{7,199},{8... | collective-permute-start | bytes 540680 | tf_op jit(solution)/shard_map/ppermute | solution.py:25
  103.0 11.5 %collective-permute-start.28 = (bf16[448,128]{1,0:T(8,128)(2,1)S(1)}, bf16[448,128]{1,0:T(8,128)(2,1)S(1)}, u32[]{:S(2)}, u32[]{:S(2)}) collective-permute-start(bf16[448,128]{1,0:T(8,128)(2,1)S(1)} %get-tuple-element.146.refs_0_), channel_id=1, source_target_pairs={{0,12},{1,13},{2,14},{3,15},{4,0},{5,1},{6,2},{7,3},{8,4},{9,5},{1... | collective-permute-start | bytes 344072 | tf_op jit(solution)/shard_map/ppermute | solution.py:25
  109.3 7.5 %collective-permute-start.27 = (bf16[448,128]{1,0:T(8,128)(2,1)S(1)}, bf16[448,128]{1,0:T(8,128)(2,1)S(1)}, u32[]{:S(2)}, u32[]{:S(2)}) collective-permute-start(bf16[448,128]{1,0:T(8,128)(2,1)S(1)} %get-tuple-element.146.refs_0_), channel_id=1, source_target_pairs={{0,8},{1,9},{2,10},{3,11},{4,12},{5,13},{6,14},{7,15},{8,0},{9,1},... | collective-permute-start | bytes 344072 | tf_op jit(solution)/shard_map/ppermute | solution.py:25
  109.3 8.6 %collective-permute-start.26 = (bf16[448,128]{1,0:T(8,128)(2,1)S(1)}, bf16[448,128]{1,0:T(8,128)(2,1)S(1)}, u32[]{:S(2)}, u32[]{:S(2)}) collective-permute-start(bf16[448,128]{1,0:T(8,128)(2,1)S(1)} %get-tuple-element.146.refs_0_), channel_id=1, source_target_pairs={{0,4},{1,5},{2,6},{3,7},{4,8},{5,9},{6,10},{7,11},{8,12},{9,13},{1... | collective-permute-start | bytes 344072 | tf_op jit(solution)/shard_map/ppermute | solution.py:25
  118.0 6.1 %collective-permute-start.31 = (bf16[448,128]{1,0:T(8,128)(2,1)S(1)}, bf16[448,128]{1,0:T(8,128)(2,1)S(1)}, u32[]{:S(2)}, u32[]{:S(2)}) collective-permute-start(bf16[448,128]{1,0:T(8,128)(2,1)S(1)} %shard_map.101.refs_0_), channel_id=1, source_target_pairs={{0,3},{1,0},{2,1},{3,2},{4,7},{5,4},{6,5},{7,6},{8,11},{9,8},{10,9... | collective-permute-start | bytes 344072 | tf_op jit(solution)/shard_map/ppermute | solution.py:25
  118.1 6.9 %collective-permute-start.30 = (bf16[448,128]{1,0:T(8,128)(2,1)S(1)}, bf16[448,128]{1,0:T(8,128)(2,1)S(1)}, u32[]{:S(2)}, u32[]{:S(2)}) collective-permute-start(bf16[448,128]{1,0:T(8,128)(2,1)S(1)} %shard_map.101.refs_0_), channel_id=1, source_target_pairs={{0,2},{1,3},{2,0},{3,1},{4,6},{5,7},{6,4},{7,5},{8,10},{9,11},{10,... | collective-permute-start | bytes 344072 | tf_op jit(solution)/shard_map/ppermute | solution.py:25
  119.2 7.7 %collective-permute-start.29 = (bf16[448,128]{1,0:T(8,128)(2,1)S(1)}, bf16[448,128]{1,0:T(8,128)(2,1)S(1)}, u32[]{:S(2)}, u32[]{:S(2)}) collective-permute-start(bf16[448,128]{1,0:T(8,128)(2,1)S(1)} %shard_map.101.refs_0_), channel_id=1, source_target_pairs={{0,1},{1,2},{2,3},{3,0},{4,5},{5,6},{6,7},{7,4},{8,9},{9,10},{10,1... | collective-permute-start | bytes 344072 | tf_op jit(solution)/shard_map/ppermute | solution.py:25
  128.6 30.5 %collective-permute-start.41 = (bf16[256,128]{1,0:T(8,128)(2,1)S(1)}, bf16[256,128]{1,0:T(8,128)(2,1)S(1)}, u32[]{:S(2)}, u32[]{:S(2)}) collective-permute-start(bf16[256,128]{1,0:T(8,128)(2,1)S(1)} %get-tuple-element.154.refs_0_), channel_id=1, source_target_pairs={{0,12},{1,13},{2,14},{3,15},{4,0},{5,1},{6,2},{7,3},{8,4},{9,5},{1... | collective-permute-start | bytes 196616 | tf_op jit(solution)/shard_map/ppermute | solution.py:25
  143.5 23.5 %collective-permute-start.35 = (bf16[4,64,256]{2,1,0:T(8,128)(2,1)S(1)}, bf16[4,64,256]{2,1,0:T(8,128)(2,1)S(1)}, u32[]{:S(2)}, u32[]{:S(2)}) collective-permute-start(bf16[4,64,256]{2,1,0:T(8,128)(2,1)S(1)} %collective-permute-done.32.refs_0_), channel_id=1, source_target_pairs={{0,12},{1,13},{2,14},{3,15},{4,0},{5,1},{6,2},{7,3},{8,4},{9,5},{1... | collective-permute-start | bytes 393224 | tf_op jit(solution)/shard_map/ppermute | solution.py:25
  152.9 14.0 %collective-permute-start.34 = (bf16[4,64,256]{2,1,0:T(8,128)(2,1)S(1)}, bf16[4,64,256]{2,1,0:T(8,128)(2,1)S(1)}, u32[]{:S(2)}, u32[]{:S(2)}) collective-permute-start(bf16[4,64,256]{2,1,0:T(8,128)(2,1)S(1)} %collective-permute-done.32.refs_0_), channel_id=1, source_target_pairs={{0,8},{1,9},{2,10},{3,11},{4,12},{5,13},{6,14},{7,15},{8,0},{9,1},... | collective-permute-start | bytes 393224 | tf_op jit(solution)/shard_map/ppermute | solution.py:25
  153.0 13.9 %collective-permute-start.33 = (bf16[4,64,256]{2,1,0:T(8,128)(2,1)S(1)}, bf16[4,64,256]{2,1,0:T(8,128)(2,1)S(1)}, u32[]{:S(2)}, u32[]{:S(2)}) collective-permute-start(bf16[4,64,256]{2,1,0:T(8,128)(2,1)S(1)} %collective-permute-done.32.refs_0_), channel_id=1, source_target_pairs={{0,4},{1,5},{2,6},{3,7},{4,8},{5,9},{6,10},{7,11},{8,12},{9,13},{1... | collective-permute-start | bytes 393224 | tf_op jit(solution)/shard_map/ppermute | solution.py:25
  155.0 7.8 %collective-permute-start.40 = (bf16[256,128]{1,0:T(8,128)(2,1)S(1)}, bf16[256,128]{1,0:T(8,128)(2,1)S(1)}, u32[]{:S(2)}, u32[]{:S(2)}) collective-permute-start(bf16[256,128]{1,0:T(8,128)(2,1)S(1)} %get-tuple-element.154.refs_0_), channel_id=1, source_target_pairs={{0,8},{1,9},{2,10},{3,11},{4,12},{5,13},{6,14},{7,15},{8,0},{9,1},... | collective-permute-start | bytes 196616 | tf_op jit(solution)/shard_map/ppermute | solution.py:25
  159.1 5.5 %collective-permute-start.39 = (bf16[256,128]{1,0:T(8,128)(2,1)S(1)}, bf16[256,128]{1,0:T(8,128)(2,1)S(1)}, u32[]{:S(2)}, u32[]{:S(2)}) collective-permute-start(bf16[256,128]{1,0:T(8,128)(2,1)S(1)} %get-tuple-element.154.refs_0_), channel_id=1, source_target_pairs={{0,4},{1,5},{2,6},{3,7},{4,8},{5,9},{6,10},{7,11},{8,12},{9,13},{1... | collective-permute-start | bytes 196616 | tf_op jit(solution)/shard_map/ppermute | solution.py:25
  164.6 8.2 %collective-permute-start.44 = (bf16[256,128]{1,0:T(8,128)(2,1)S(1)}, bf16[256,128]{1,0:T(8,128)(2,1)S(1)}, u32[]{:S(2)}, u32[]{:S(2)}) collective-permute-start(bf16[256,128]{1,0:T(8,128)(2,1)S(1)} %shard_map.104.refs_4_), channel_id=1, source_target_pairs={{0,3},{1,0},{2,1},{3,2},{4,7},{5,4},{6,5},{7,6},{8,11},{9,8},{10,9... | collective-permute-start | bytes 196616 | tf_op jit(solution)/shard_map/ppermute | solution.py:25
  168.6 13.4 %collective-permute-start.36 = (bf16[64,1024]{1,0:T(8,128)(2,1)S(1)}, bf16[64,1024]{1,0:T(8,128)(2,1)S(1)}, u32[]{:S(2)}, u32[]{:S(2)}) collective-permute-start(bf16[64,1024]{1,0:T(8,128)(2,1)S(1)} %get-tuple-element.151), channel_id=1, source_target_pairs={{0,64},{1,65},{2,66},{3,67},{4,68},{5,69},{6,70},{7,71},{8,72},{9,... | collective-permute-start | bytes 393224 | tf_op jit(solution)/shard_map/ppermute | solution.py:25
  168.6 13.8 %collective-permute-start.37 = (bf16[64,1024]{1,0:T(8,128)(2,1)S(1)}, bf16[64,1024]{1,0:T(8,128)(2,1)S(1)}, u32[]{:S(2)}, u32[]{:S(2)}) collective-permute-start(bf16[64,1024]{1,0:T(8,128)(2,1)S(1)} %get-tuple-element.152), channel_id=1, source_target_pairs={{0,128},{1,129},{2,130},{3,131},{4,132},{5,133},{6,134},{7,135},{8... | collective-permute-start | bytes 393224 | tf_op jit(solution)/shard_map/ppermute | solution.py:25
  168.9 15.6 %collective-permute-start.38 = (bf16[64,1024]{1,0:T(8,128)(2,1)S(1)}, bf16[64,1024]{1,0:T(8,128)(2,1)S(1)}, u32[]{:S(2)}, u32[]{:S(2)}) collective-permute-start(bf16[64,1024]{1,0:T(8,128)(2,1)S(1)} %get-tuple-element.153), channel_id=1, source_target_pairs={{0,192},{1,193},{2,194},{3,195},{4,196},{5,197},{6,198},{7,199},{8... | collective-permute-start | bytes 393224 | tf_op jit(solution)/shard_map/ppermute | solution.py:25
  172.8 5.9 %collective-permute-start.43 = (bf16[256,128]{1,0:T(8,128)(2,1)S(1)}, bf16[256,128]{1,0:T(8,128)(2,1)S(1)}, u32[]{:S(2)}, u32[]{:S(2)}) collective-permute-start(bf16[256,128]{1,0:T(8,128)(2,1)S(1)} %shard_map.104.refs_4_), channel_id=1, source_target_pairs={{0,2},{1,3},{2,0},{3,1},{4,6},{5,7},{6,4},{7,5},{8,10},{9,11},{10,... | collective-permute-start | bytes 196616 | tf_op jit(solution)/shard_map/ppermute | solution.py:25
  172.8 6.2 %collective-permute-start.42 = (bf16[256,128]{1,0:T(8,128)(2,1)S(1)}, bf16[256,128]{1,0:T(8,128)(2,1)S(1)}, u32[]{:S(2)}, u32[]{:S(2)}) collective-permute-start(bf16[256,128]{1,0:T(8,128)(2,1)S(1)} %shard_map.104.refs_4_), channel_id=1, source_target_pairs={{0,1},{1,2},{2,3},{3,0},{4,5},{5,6},{6,7},{7,4},{8,9},{9,10},{10,1... | collective-permute-start | bytes 196616 | tf_op jit(solution)/shard_map/ppermute | solution.py:25
  184.8 4.2 %collective-permute-start.47 = (bf16[192,128]{1,0:T(8,128)(2,1)S(1)}, bf16[192,128]{1,0:T(8,128)(2,1)S(1)}, u32[]{:S(2)}, u32[]{:S(2)}) collective-permute-start(bf16[192,128]{1,0:T(8,128)(2,1)S(1)} %get-tuple-element.159.refs_0_), channel_id=1, source_target_pairs={{0,12},{1,13},{2,14},{3,15},{4,0},{5,1},{6,2},{7,3},{8,4},{9,5},{1... | collective-permute-start | bytes 147464 | tf_op jit(solution)/shard_map/ppermute | solution.py:25
  185.7 5.6 %collective-permute-start.46 = (bf16[192,128]{1,0:T(8,128)(2,1)S(1)}, bf16[192,128]{1,0:T(8,128)(2,1)S(1)}, u32[]{:S(2)}, u32[]{:S(2)}) collective-permute-start(bf16[192,128]{1,0:T(8,128)(2,1)S(1)} %get-tuple-element.159.refs_0_), channel_id=1, source_target_pairs={{0,8},{1,9},{2,10},{3,11},{4,12},{5,13},{6,14},{7,15},{8,0},{9,1},... | collective-permute-start | bytes 147464 | tf_op jit(solution)/shard_map/ppermute | solution.py:25
  185.7 6.1 %collective-permute-start.45 = (bf16[192,128]{1,0:T(8,128)(2,1)S(1)}, bf16[192,128]{1,0:T(8,128)(2,1)S(1)}, u32[]{:S(2)}, u32[]{:S(2)}) collective-permute-start(bf16[192,128]{1,0:T(8,128)(2,1)S(1)} %get-tuple-element.159.refs_0_), channel_id=1, source_target_pairs={{0,4},{1,5},{2,6},{3,7},{4,8},{5,9},{6,10},{7,11},{8,12},{9,13},{1... | collective-permute-start | bytes 147464 | tf_op jit(solution)/shard_map/ppermute | solution.py:25
  191.9 4.2 %collective-permute-start.50 = (bf16[192,128]{1,0:T(8,128)(2,1)S(1)}, bf16[192,128]{1,0:T(8,128)(2,1)S(1)}, u32[]{:S(2)}, u32[]{:S(2)}) collective-permute-start(bf16[192,128]{1,0:T(8,128)(2,1)S(1)} %shard_map.106.refs_0_), channel_id=1, source_target_pairs={{0,3},{1,0},{2,1},{3,2},{4,7},{5,4},{6,5},{7,6},{8,11},{9,8},{10,9... | collective-permute-start | bytes 147464 | tf_op jit(solution)/shard_map/ppermute | solution.py:25
  192.1 5.6 %collective-permute-start.49 = (bf16[192,128]{1,0:T(8,128)(2,1)S(1)}, bf16[192,128]{1,0:T(8,128)(2,1)S(1)}, u32[]{:S(2)}, u32[]{:S(2)}) collective-permute-start(bf16[192,128]{1,0:T(8,128)(2,1)S(1)} %shard_map.106.refs_0_), channel_id=1, source_target_pairs={{0,2},{1,3},{2,0},{3,1},{4,6},{5,7},{6,4},{7,5},{8,10},{9,11},{10,... | collective-permute-start | bytes 147464 | tf_op jit(solution)/shard_map/ppermute | solution.py:25
  192.1 6.7 %collective-permute-start.48 = (bf16[192,128]{1,0:T(8,128)(2,1)S(1)}, bf16[192,128]{1,0:T(8,128)(2,1)S(1)}, u32[]{:S(2)}, u32[]{:S(2)}) collective-permute-start(bf16[192,128]{1,0:T(8,128)(2,1)S(1)} %shard_map.106.refs_0_), channel_id=1, source_target_pairs={{0,1},{1,2},{2,3},{3,0},{4,5},{5,6},{6,7},{7,4},{8,9},{9,10},{10,1... | collective-permute-start | bytes 147464 | tf_op jit(solution)/shard_map/ppermute | solution.py:25
  201.9 5.4 %collective-permute-start.52 = (bf16[64,256]{1,0:T(8,128)(2,1)S(1)}, bf16[64,256]{1,0:T(8,128)(2,1)S(1)}, u32[]{:S(2)}, u32[]{:S(2)}) collective-permute-start(bf16[64,256]{1,0:T(8,128)(2,1)S(1)} %get-tuple-element.167), channel_id=1, source_target_pairs={{0,2},{1,3},{2,0},{3,1},{4,6},{5,7},{6,4},{7,5},{8,10},{9,11},{10,... | collective-permute-start | bytes 98312 | tf_op jit(solution)/shard_map/ppermute | solution.py:25
  202.8 5.1 %collective-permute-start.53 = (bf16[64,256]{1,0:T(8,128)(2,1)S(1)}, bf16[64,256]{1,0:T(8,128)(2,1)S(1)}, u32[]{:S(2)}, u32[]{:S(2)}) collective-permute-start(bf16[64,256]{1,0:T(8,128)(2,1)S(1)} %get-tuple-element.168), channel_id=1, source_target_pairs={{0,1},{1,2},{2,3},{3,0},{4,5},{5,6},{6,7},{7,4},{8,9},{9,10},{10,1... | collective-permute-start | bytes 98312 | tf_op jit(solution)/shard_map/ppermute | solution.py:25
  (15 other events, 88.7 us)

commit v7 on v5

--- a/solution.py
+++ b/solution.py
@@ -391,18 +391,17 @@
     tied = lax.optimization_barrier
     deal = kernel_call(deal_kernel, [shape((width, width), BF16)] * SIDE)
     stack = kernel_call(stack_kernel, shape((total, width), BF16))
+    rows = kernel_call(pack_kernel, [shape((height, width), BF16)] * SIDE)(
+        right_sides, low_left, up_left
+    )
+    rows, inv_lower = tied((rows, inv_lower))
+    rows = scattered_x(rows)
     parts = scattered_x(deal(inv_lower))
-    rows = scattered_x(
-        kernel_call(pack_kernel, [shape((height, width), BF16)] * SIDE)(
-            right_sides, low_left, up_left
-        )
-    )
-    parts, rows = tied((parts, rows))
     rows = kernel_call(
         lambda *refs: order_kernel(1, *refs), shape((SIDE, height, width), BF16)
     )(*rows)
+    rows, inv_upper = tied((rows, inv_upper))
     lower = stack(*parts)
-    rows, lower, inv_upper = tied((rows, lower, inv_upper))
     far_lower = swap_pair(lower)
     parts, rows = tied((scattered_x(deal(inv_upper)), swapped(rows)))
     upper = stack(*parts)

time: 200 us -> 197 us (0.985)
  starting transfers between devices: 94.9 us -> 89.9 us
  waiting for transfers between devices: 72.1 us -> 75 us
    ppermute x48, starting transfers between devices: 94.9 us -> 89.9 us  [permuted(): return lax.ppermute(value, ('row', 'col'), routes(to))]
    ppermute x48, waiting for transfers between devices: 72.1 us -> 75 us  [permuted(): return lax.ppermute(value, ('row', 'col'), routes(to))]
  transfers between devices with their start and end apart: 48 -> 48, of which waited for: 28 -> 29; matrix products, arithmetic and copies ran while one was open for 0% -> 0% of each run, Pallas kernels for 2% -> 2%
where the time goes in v7:
time: 197 us
  starting transfers between devices  89.9 us (46%)
  waiting for transfers between devices  75 us (38%)
  blocking collectives  19.6 us (10%)
  Pallas kernels  9.19 us (5%)
  local copies, waits for them, and re-layouts  3.03 us (2%)
    ppermute x48, starting transfers between devices, permuted(): return lax.ppermute(value, ('row', 'col'), routes(to))  89.9 us
    ppermute x48, waiting for transfers between devices, permuted(): return lax.ppermute(value, ('row', 'col'), routes(to))  75 us
    all_to_all x1, blocking collectives, from_every_z(): lax.all_to_all(value, 'row', 0, 0, tiled=True, axis_index_groups=Z_GROUPS)  19.6 us
    pallas_call x17, Pallas kernels, run(): pl.pallas_call(body, out_shape=out_shape, in_specs=specs, scratch_shapes=...  9.19 us
  transfers between devices with their start and end apart: 48, of which 29 were waited for; matrix products, arithmetic and copies ran while one was open for 0% of the time, Pallas kernels for 2%

profile of v7, /device:TPU:2, one launch (start us, length us, event | category | flops | bytes accessed | tf_op | source)
XLA Modules:
  0.0 197.0 jit_solution(9637027882231815807)
XLA Ops:
  3.6 1.6 collective-permute-start.10
  5.1 2.8 %collective-permute-start.11 = (bf16[256,256]{1,0:T(8,128)(2,1)S(1)}, bf16[256,256]{1,0:T(8,128)(2,1)S(1)}, u32[]{:S(2)}, u32[]{:S(2)}) collective-permute-start(bf16[256,256]{1,0:T(8,128)(2,1)S(1)} %get-tuple-element.91), channel_id=1, source_target_pairs={{0,2},{1,3},{2,0},{3,1},{4,6},{5,7},{6,4},{7,5},{8,10},{9,11},{10,... | collective-permute-start | bytes 393224 | tf_op jit(solution)/shard_map/ppermute | solution.py:25
  8.0 2.5 %collective-permute-start.1 = (bf16[88,256]{1,0:T(8,128)(2,1)S(1)}, bf16[88,256]{1,0:T(8,128)(2,1)S(1)}, u32[]{:S(2)}, u32[]{:S(2)}) collective-permute-start(bf16[88,256]{1,0:T(8,128)(2,1)S(1)} %get-tuple-element.79), channel_id=1, source_target_pairs={{0,2},{1,3},{2,0},{3,1},{4,6},{5,7},{6,4},{7,5},{8,10},{9,11},{10,... | collective-permute-start | bytes 135176 | tf_op jit(solution)/shard_map/ppermute | solution.py:25
  11.3 1.9 collective-permute-done.refs_1_
  15.2 2.3 %collective-permute-start.12 = (bf16[256,256]{1,0:T(8,128)(2,1)S(1)}, bf16[256,256]{1,0:T(8,128)(2,1)S(1)}, u32[]{:S(2)}, u32[]{:S(2)}) collective-permute-start(bf16[256,256]{1,0:T(8,128)(2,1)S(1)} %get-tuple-element.92), channel_id=1, source_target_pairs={{0,3},{1,0},{2,1},{3,2},{4,7},{5,4},{6,5},{7,6},{8,11},{9,8},{10,9... | collective-permute-start | bytes 393224 | tf_op jit(solution)/shard_map/ppermute | solution.py:25
  17.7 3.3 %collective-permute-start.4 = (bf16[256,256]{1,0:T(8,128)(2,1)S(1)}, bf16[256,256]{1,0:T(8,128)(2,1)S(1)}, u32[]{:S(2)}, u32[]{:S(2)}) collective-permute-start(bf16[256,256]{1,0:T(8,128)(2,1)S(1)} %get-tuple-element.84), channel_id=1, source_target_pairs={{0,2},{1,3},{2,0},{3,1},{4,6},{5,7},{6,4},{7,5},{8,10},{9,11},{10,... | collective-permute-start | bytes 393224 | tf_op jit(solution)/shard_map/ppermute | solution.py:25
  21.0 2.1 %collective-permute-start.13 = (bf16[1024,256]{1,0:T(8,128)(2,1)S(1)}, bf16[1024,256]{1,0:T(8,128)(2,1)S(1)}, u32[]{:S(2)}, u32[]{:S(2)}) collective-permute-start(bf16[1024,256]{1,0:T(8,128)(2,1)S(1)} %shard_map.95.refs_4_), channel_id=1, source_target_pairs={{0,32},{1,33},{2,34},{3,35},{4,36},{5,37},{6,38},{7,39},{8,40},{9,... | collective-permute-start | bytes 1572872 | tf_op jit(solution)/shard_map/ppermute | solution.py:25
  23.1 1.9 collective-permute-done.4.refs_2_
  25.0 1.4 collective-permute-done.5.refs_3_
  26.4 1.7 collective-permute-start.17
  28.0 10.3 %collective-permute-start.9 = (bf16[4,88,256]{2,1,0:T(8,128)(2,1)S(1)}, bf16[4,88,256]{2,1,0:T(8,128)(2,1)S(1)}, u32[]{:S(2)}, u32[]{:S(2)}) collective-permute-start(bf16[4,88,256]{2,1,0:T(8,128)(2,1)S(1)} %collective-permute-done.6.refs_0_), channel_id=1, source_target_pairs={{0,12},{1,13},{2,14},{3,15},{4,0},{5,1},{6,2},{7,3},{8,4},{9,5},{1... | collective-permute-start | bytes 540680 | tf_op jit(solution)/shard_map/ppermute | solution.py:25
  38.5 1.4 collective-permute-start.7
  39.9 5.9 %collective-permute-done.9.refs_3_ = bf16[4,88,256]{2,1,0:T(8,128)(2,1)S(1)} collective-permute-done((bf16[4,88,256]{2,1,0:T(8,128)(2,1)S(1)}, bf16[4,88,256]{2,1,0:T(8,128)(2,1)S(1)}, u32[]{:S(2)}, u32[]{:S(2)}) %collective-permute-start.9) | collective-permute-done | bytes 180256 | tf_op jit(solution)/shard_map/ppermute | solution.py:25
  45.8 1.5 collective-permute-done.8.refs_2_
  47.3 1.9 collective-permute-done.7.refs_1_
  51.6 3.3 %collective-permute-start.23 = (bf16[384,256]{1,0:T(8,128)(2,1)S(1)}, bf16[384,256]{1,0:T(8,128)(2,1)S(1)}, u32[]{:S(2)}, u32[]{:S(2)}) collective-permute-start(bf16[384,256]{1,0:T(8,128)(2,1)S(1)} %get-tuple-element.116), channel_id=1, source_target_pairs={{0,2},{1,3},{2,0},{3,1},{4,6},{5,7},{6,4},{7,5},{8,10},{9,11},{10,... | collective-permute-start | bytes 589832 | tf_op jit(solution)/shard_map/ppermute | solution.py:25
  54.9 2.4 %shard_map.97 = (bf16[88,1024]{1,0:T(8,128)(2,1)S(1)}, bf16[88,1024]{1,0:T(8,128)(2,1)S(1)}, bf16[88,1024]{1,0:T(8,128)(2,1)S(1)}, bf16[88,1024]{1,0:T(8,128)(2,1)S(1)}) custom-call(bf16[4,88,256]{2,1,0:T(8,128)(2,1)S(1)} %collective-permute-done.6.refs_0_, bf16[4,88,256]{2,1,0:T(8,128)(2,1)S(1)} %collective-permute-done.7.refs_1_, ...), custom_call_target="tpu_custom_call" | custom-call | flops 738197504 | bytes 5636096 | tf_op jit(solution)/shard_map/pallas_call | solution.py:106
  57.3 3.0 %collective-permute-start.19 = (bf16[88,1024]{1,0:T(8,128)(2,1)S(1)}, bf16[88,1024]{1,0:T(8,128)(2,1)S(1)}, u32[]{:S(2)}, u32[]{:S(2)}) collective-permute-start(bf16[88,1024]{1,0:T(8,128)(2,1)S(1)} %get-tuple-element.109), channel_id=1, source_target_pairs={{0,64},{1,65},{2,66},{3,67},{4,68},{5,69},{6,70},{7,71},{8,72},{9,... | collective-permute-start | bytes 540680 | tf_op jit(solution)/shard_map/ppermute | solution.py:25
  60.3 2.6 %collective-permute-start.20 = (bf16[88,1024]{1,0:T(8,128)(2,1)S(1)}, bf16[88,1024]{1,0:T(8,128)(2,1)S(1)}, u32[]{:S(2)}, u32[]{:S(2)}) collective-permute-start(bf16[88,1024]{1,0:T(8,128)(2,1)S(1)} %get-tuple-element.110), channel_id=1, source_target_pairs={{0,128},{1,129},{2,130},{3,131},{4,132},{5,133},{6,134},{7,135},{8... | collective-permute-start | bytes 540680 | tf_op jit(solution)/shard_map/ppermute | solution.py:25
  62.9 3.1 %collective-permute-start.21 = (bf16[88,1024]{1,0:T(8,128)(2,1)S(1)}, bf16[88,1024]{1,0:T(8,128)(2,1)S(1)}, u32[]{:S(2)}, u32[]{:S(2)}) collective-permute-start(bf16[88,1024]{1,0:T(8,128)(2,1)S(1)} %get-tuple-element.111), channel_id=1, source_target_pairs={{0,192},{1,193},{2,194},{3,195},{4,196},{5,197},{6,198},{7,199},{8... | collective-permute-start | bytes 540680 | tf_op jit(solution)/shard_map/ppermute | solution.py:25
  66.8 7.1 %collective-permute-done.20.refs_2_ = bf16[88,1024]{1,0:T(8,128)(2,1)S(1)} collective-permute-done((bf16[88,1024]{1,0:T(8,128)(2,1)S(1)}, bf16[88,1024]{1,0:T(8,128)(2,1)S(1)}, u32[]{:S(2)}, u32[]{:S(2)}) %collective-permute-start.20) | collective-permute-done | bytes 180256 | tf_op jit(solution)/shard_map/ppermute | solution.py:25
  73.9 5.5 %collective-permute-done.21.refs_3_ = bf16[88,1024]{1,0:T(8,128)(2,1)S(1)} collective-permute-done((bf16[88,1024]{1,0:T(8,128)(2,1)S(1)}, bf16[88,1024]{1,0:T(8,128)(2,1)S(1)}, u32[]{:S(2)}, u32[]{:S(2)}) %collective-permute-start.21) | collective-permute-done | bytes 180256 | tf_op jit(solution)/shard_map/ppermute | solution.py:25
  79.5 19.6 %all_to_all.5.mine_ref = bf16[8,24,1024]{2,1,0:T(8,128)(2,1)S(1)} all-to-all(bf16[8,24,1024]{2,1,0:T(8,128)(2,1)S(1)} %get-tuple-element.123), channel_id=1, replica_groups={{0,32,64,96,128,160,192,224},{16,48,80,112,144,176,208,240},{1,33,65,97..., dimensions={0} | all-to-all | bytes 786432 | tf_op jit(solution)/shard_map/all_to_all | solution.py:55
  99.1 1.7 collective-permute-done.25.other_ref
  101.5 5.8 %collective-permute-start.28 = (bf16[448,128]{1,0:T(8,128)(2,1)S(1)}, bf16[448,128]{1,0:T(8,128)(2,1)S(1)}, u32[]{:S(2)}, u32[]{:S(2)}) collective-permute-start(bf16[448,128]{1,0:T(8,128)(2,1)S(1)} %get-tuple-element.128.refs_0_), channel_id=1, source_target_pairs={{0,12},{1,13},{2,14},{3,15},{4,0},{5,1},{6,2},{7,3},{8,4},{9,5},{1... | collective-permute-start | bytes 344072 | tf_op jit(solution)/shard_map/ppermute | solution.py:25
  108.3 4.2 %collective-permute-done.28.refs_3_ = bf16[448,128]{1,0:T(8,128)(2,1)S(1)} collective-permute-done((bf16[448,128]{1,0:T(8,128)(2,1)S(1)}, bf16[448,128]{1,0:T(8,128)(2,1)S(1)}, u32[]{:S(2)}, u32[]{:S(2)}) %collective-permute-start.28) | collective-permute-done | bytes 114720 | tf_op jit(solution)/shard_map/ppermute | solution.py:25
  112.5 2.4 %collective-permute-done.27.refs_2_ = bf16[448,128]{1,0:T(8,128)(2,1)S(1)} collective-permute-done((bf16[448,128]{1,0:T(8,128)(2,1)S(1)}, bf16[448,128]{1,0:T(8,128)(2,1)S(1)}, u32[]{:S(2)}, u32[]{:S(2)}) %collective-permute-start.27) | collective-permute-done | bytes 114720 | tf_op jit(solution)/shard_map/ppermute | solution.py:25
  119.2 2.4 %collective-permute-done.31.refs_3_ = bf16[448,128]{1,0:T(8,128)(2,1)S(1)} collective-permute-done((bf16[448,128]{1,0:T(8,128)(2,1)S(1)}, bf16[448,128]{1,0:T(8,128)(2,1)S(1)}, u32[]{:S(2)}, u32[]{:S(2)}) %collective-permute-start.31) | collective-permute-done | bytes 114720 | tf_op jit(solution)/shard_map/ppermute | solution.py:25
  121.6 1.8 collective-permute-done.30.refs_2_
  123.3 1.8 collective-permute-done.29.refs_1_
  126.8 12.7 %collective-permute-start.35 = (bf16[4,64,256]{2,1,0:T(8,128)(2,1)S(1)}, bf16[4,64,256]{2,1,0:T(8,128)(2,1)S(1)}, u32[]{:S(2)}, u32[]{:S(2)}) collective-permute-start(bf16[4,64,256]{2,1,0:T(8,128)(2,1)S(1)} %collective-permute-done.32.refs_0_), channel_id=1, source_target_pairs={{0,12},{1,13},{2,14},{3,15},{4,0},{5,1},{6,2},{7,3},{8,4},{9,5},{1... | collective-permute-start | bytes 393224 | tf_op jit(solution)/shard_map/ppermute | solution.py:25
  139.7 1.4 collective-permute-start.33
  141.2 2.2 %collective-permute-done.35.refs_3_ = bf16[4,64,256]{2,1,0:T(8,128)(2,1)S(1)} collective-permute-done((bf16[4,64,256]{2,1,0:T(8,128)(2,1)S(1)}, bf16[4,64,256]{2,1,0:T(8,128)(2,1)S(1)}, u32[]{:S(2)}, u32[]{:S(2)}) %collective-permute-start.35) | collective-permute-done | bytes 131104 | tf_op jit(solution)/shard_map/ppermute | solution.py:25
  143.4 2.7 %collective-permute-done.34.refs_2_ = bf16[4,64,256]{2,1,0:T(8,128)(2,1)S(1)} collective-permute-done((bf16[4,64,256]{2,1,0:T(8,128)(2,1)S(1)}, bf16[4,64,256]{2,1,0:T(8,128)(2,1)S(1)}, u32[]{:S(2)}, u32[]{:S(2)}) %collective-permute-start.34) | collective-permute-done | bytes 131104 | tf_op jit(solution)/shard_map/ppermute | solution.py:25
  147.3 1.5 shard_map.103
  149.2 5.9 %collective-permute-start.37 = (bf16[64,1024]{1,0:T(8,128)(2,1)S(1)}, bf16[64,1024]{1,0:T(8,128)(2,1)S(1)}, u32[]{:S(2)}, u32[]{:S(2)}) collective-permute-start(bf16[64,1024]{1,0:T(8,128)(2,1)S(1)} %get-tuple-element.132), channel_id=1, source_target_pairs={{0,128},{1,129},{2,130},{3,131},{4,132},{5,133},{6,134},{7,135},{8... | collective-permute-start | bytes 393224 | tf_op jit(solution)/shard_map/ppermute | solution.py:25
  155.1 2.4 %collective-permute-done.36.refs_1_ = bf16[64,1024]{1,0:T(8,128)(2,1)S(1)} collective-permute-done((bf16[64,1024]{1,0:T(8,128)(2,1)S(1)}, bf16[64,1024]{1,0:T(8,128)(2,1)S(1)}, u32[]{:S(2)}, u32[]{:S(2)}) %collective-permute-start.36) | collective-permute-done | bytes 131104 | tf_op jit(solution)/shard_map/ppermute | solution.py:25
  157.5 7.7 %collective-permute-done.37.refs_2_ = bf16[64,1024]{1,0:T(8,128)(2,1)S(1)} collective-permute-done((bf16[64,1024]{1,0:T(8,128)(2,1)S(1)}, bf16[64,1024]{1,0:T(8,128)(2,1)S(1)}, u32[]{:S(2)}, u32[]{:S(2)}) %collective-permute-start.37) | collective-permute-done | bytes 131104 | tf_op jit(solution)/shard_map/ppermute | solution.py:25
  166.3 1.4 collective-permute-start.39
  167.7 3.8 %collective-permute-done.41.refs_3_ = bf16[448,128]{1,0:T(8,128)(2,1)S(1)} collective-permute-done((bf16[448,128]{1,0:T(8,128)(2,1)S(1)}, bf16[448,128]{1,0:T(8,128)(2,1)S(1)}, u32[]{:S(2)}, u32[]{:S(2)}) %collective-permute-start.41) | collective-permute-done | bytes 114720 | tf_op jit(solution)/shard_map/ppermute | solution.py:25
  171.5 2.3 %collective-permute-done.40.refs_2_ = bf16[448,128]{1,0:T(8,128)(2,1)S(1)} collective-permute-done((bf16[448,128]{1,0:T(8,128)(2,1)S(1)}, bf16[448,128]{1,0:T(8,128)(2,1)S(1)}, u32[]{:S(2)}, u32[]{:S(2)}) %collective-permute-start.40) | collective-permute-done | bytes 114720 | tf_op jit(solution)/shard_map/ppermute | solution.py:25
  174.4 6.1 %collective-permute-start.44 = (bf16[448,128]{1,0:T(8,128)(2,1)S(1)}, bf16[448,128]{1,0:T(8,128)(2,1)S(1)}, u32[]{:S(2)}, u32[]{:S(2)}) collective-permute-start(bf16[448,128]{1,0:T(8,128)(2,1)S(1)} %shard_map.105.refs_0_), channel_id=1, source_target_pairs={{0,3},{1,0},{2,1},{3,2},{4,7},{5,4},{6,5},{7,6},{8,11},{9,8},{10,9... | collective-permute-start | bytes 344072 | tf_op jit(solution)/shard_map/ppermute | solution.py:25
  180.5 1.6 collective-permute-start.42
  182.1 2.0 collective-permute-done.44.refs_3_
  184.0 2.8 %collective-permute-done.43.refs_2_ = bf16[448,128]{1,0:T(8,128)(2,1)S(1)} collective-permute-done((bf16[448,128]{1,0:T(8,128)(2,1)S(1)}, bf16[448,128]{1,0:T(8,128)(2,1)S(1)}, u32[]{:S(2)}, u32[]{:S(2)}) %collective-permute-start.43) | collective-permute-done | bytes 114720 | tf_op jit(solution)/shard_map/ppermute | solution.py:25
  187.9 2.9 %collective-permute-start.45 = (bf16[64,256]{1,0:T(8,128)(2,1)S(1)}, bf16[64,256]{1,0:T(8,128)(2,1)S(1)}, u32[]{:S(2)}, u32[]{:S(2)}) collective-permute-start(bf16[64,256]{1,0:T(8,128)(2,1)S(1)} %get-tuple-element.138), channel_id=1, source_target_pairs={{0,3},{1,0},{2,1},{3,2},{4,7},{5,4},{6,5},{7,6},{8,11},{9,8},{10,9... | collective-permute-start | bytes 98312 | tf_op jit(solution)/shard_map/ppermute | solution.py:25
  190.8 2.5 %collective-permute-start.47 = (bf16[64,256]{1,0:T(8,128)(2,1)S(1)}, bf16[64,256]{1,0:T(8,128)(2,1)S(1)}, u32[]{:S(2)}, u32[]{:S(2)}) collective-permute-start(bf16[64,256]{1,0:T(8,128)(2,1)S(1)} %get-tuple-element.140), channel_id=1, source_target_pairs={{0,1},{1,2},{2,3},{3,0},{4,5},{5,6},{6,7},{7,4},{8,9},{9,10},{10,1... | collective-permute-start | bytes 98312 | tf_op jit(solution)/shard_map/ppermute | solution.py:25
  193.4 2.9 %collective-permute-done.46.refs_2_ = bf16[64,256]{1,0:T(8,128)(2,1)S(1)} collective-permute-done((bf16[64,256]{1,0:T(8,128)(2,1)S(1)}, bf16[64,256]{1,0:T(8,128)(2,1)S(1)}, u32[]{:S(2)}, u32[]{:S(2)}) %collective-permute-start.46) | collective-permute-done | bytes 32800 | tf_op jit(solution)/shard_map/ppermute | solution.py:25
  (84 shorter events, 23.1 us)
Async XLA Ops:
  3.6 14.1 %collective-permute-start.10 = (bf16[256,256]{1,0:T(8,128)(2,1)S(1)}, bf16[256,256]{1,0:T(8,128)(2,1)S(1)}, u32[]{:S(2)}, u32[]{:S(2)}) collective-permute-start(bf16[256,256]{1,0:T(8,128)(2,1)S(1)} %get-tuple-element.90), channel_id=1, source_target_pairs={{0,1},{1,2},{2,3},{3,0},{4,5},{5,6},{6,7},{7,4},{8,9},{9,10},{10,1... | collective-permute-start | bytes 393224 | tf_op jit(solution)/shard_map/ppermute | solution.py:25
  5.1 15.8 %collective-permute-start.11 = (bf16[256,256]{1,0:T(8,128)(2,1)S(1)}, bf16[256,256]{1,0:T(8,128)(2,1)S(1)}, u32[]{:S(2)}, u32[]{:S(2)}) collective-permute-start(bf16[256,256]{1,0:T(8,128)(2,1)S(1)} %get-tuple-element.91), channel_id=1, source_target_pairs={{0,2},{1,3},{2,0},{3,1},{4,6},{5,7},{6,4},{7,5},{8,10},{9,11},{10,... | collective-permute-start | bytes 393224 | tf_op jit(solution)/shard_map/ppermute | solution.py:25
  8.0 5.2 %collective-permute-start = (bf16[88,256]{1,0:T(8,128)(2,1)S(1)}, bf16[88,256]{1,0:T(8,128)(2,1)S(1)}, u32[]{:S(2)}, u32[]{:S(2)}) collective-permute-start(bf16[88,256]{1,0:T(8,128)(2,1)S(1)} %get-tuple-element.78), channel_id=1, source_target_pairs={{0,1},{1,2},{2,3},{3,0},{4,5},{5,6},{6,7},{7,4},{8,9},{9,10},{10,1... | collective-permute-start | bytes 135176 | tf_op jit(solution)/shard_map/ppermute | solution.py:25
  8.0 5.6 %collective-permute-start.1 = (bf16[88,256]{1,0:T(8,128)(2,1)S(1)}, bf16[88,256]{1,0:T(8,128)(2,1)S(1)}, u32[]{:S(2)}, u32[]{:S(2)}) collective-permute-start(bf16[88,256]{1,0:T(8,128)(2,1)S(1)} %get-tuple-element.79), channel_id=1, source_target_pairs={{0,2},{1,3},{2,0},{3,1},{4,6},{5,7},{6,4},{7,5},{8,10},{9,11},{10,... | collective-permute-start | bytes 135176 | tf_op jit(solution)/shard_map/ppermute | solution.py:25
  10.5 4.0 %collective-permute-start.2 = (bf16[88,256]{1,0:T(8,128)(2,1)S(1)}, bf16[88,256]{1,0:T(8,128)(2,1)S(1)}, u32[]{:S(2)}, u32[]{:S(2)}) collective-permute-start(bf16[88,256]{1,0:T(8,128)(2,1)S(1)} %get-tuple-element.80), channel_id=1, source_target_pairs={{0,3},{1,0},{2,1},{3,2},{4,7},{5,4},{6,5},{7,6},{8,11},{9,8},{10,9... | collective-permute-start | bytes 135176 | tf_op jit(solution)/shard_map/ppermute | solution.py:25
  14.6 11.8 %collective-permute-start.6 = (bf16[4,88,256]{2,1,0:T(8,128)(2,1)S(1)}, bf16[4,88,256]{2,1,0:T(8,128)(2,1)S(1)}, u32[]{:S(2)}, u32[]{:S(2)}) collective-permute-start(bf16[4,88,256]{2,1,0:T(8,128)(2,1)S(1)} %shard_map.92), channel_id=1, source_target_pairs={{0,0},{1,1},{2,2},{3,3},{4,64},{5,65},{6,66},{7,67},{8,128},{9,129... | collective-permute-start | bytes 540680 | tf_op jit(solution)/shard_map/ppermute | solution.py:25
  15.2 5.7 %collective-permute-start.12 = (bf16[256,256]{1,0:T(8,128)(2,1)S(1)}, bf16[256,256]{1,0:T(8,128)(2,1)S(1)}, u32[]{:S(2)}, u32[]{:S(2)}) collective-permute-start(bf16[256,256]{1,0:T(8,128)(2,1)S(1)} %get-tuple-element.92), channel_id=1, source_target_pairs={{0,3},{1,0},{2,1},{3,2},{4,7},{5,4},{6,5},{7,6},{8,11},{9,8},{10,9... | collective-permute-start | bytes 393224 | tf_op jit(solution)/shard_map/ppermute | solution.py:25
  17.6 5.5 %collective-permute-start.3 = (bf16[256,256]{1,0:T(8,128)(2,1)S(1)}, bf16[256,256]{1,0:T(8,128)(2,1)S(1)}, u32[]{:S(2)}, u32[]{:S(2)}) collective-permute-start(bf16[256,256]{1,0:T(8,128)(2,1)S(1)} %get-tuple-element.83), channel_id=1, source_target_pairs={{0,1},{1,2},{2,3},{3,0},{4,5},{5,6},{6,7},{7,4},{8,9},{9,10},{10,1... | collective-permute-start | bytes 393224 | tf_op jit(solution)/shard_map/ppermute | solution.py:25
  17.7 7.3 %collective-permute-start.4 = (bf16[256,256]{1,0:T(8,128)(2,1)S(1)}, bf16[256,256]{1,0:T(8,128)(2,1)S(1)}, u32[]{:S(2)}, u32[]{:S(2)}) collective-permute-start(bf16[256,256]{1,0:T(8,128)(2,1)S(1)} %get-tuple-element.84), channel_id=1, source_target_pairs={{0,2},{1,3},{2,0},{3,1},{4,6},{5,7},{6,4},{7,5},{8,10},{9,11},{10,... | collective-permute-start | bytes 393224 | tf_op jit(solution)/shard_map/ppermute | solution.py:25
  20.9 5.4 %collective-permute-start.5 = (bf16[256,256]{1,0:T(8,128)(2,1)S(1)}, bf16[256,256]{1,0:T(8,128)(2,1)S(1)}, u32[]{:S(2)}, u32[]{:S(2)}) collective-permute-start(bf16[256,256]{1,0:T(8,128)(2,1)S(1)} %get-tuple-element.85), channel_id=1, source_target_pairs={{0,3},{1,0},{2,1},{3,2},{4,7},{5,4},{6,5},{7,6},{8,11},{9,8},{10,9... | collective-permute-start | bytes 393224 | tf_op jit(solution)/shard_map/ppermute | solution.py:25
  21.0 28.2 %collective-permute-start.13 = (bf16[1024,256]{1,0:T(8,128)(2,1)S(1)}, bf16[1024,256]{1,0:T(8,128)(2,1)S(1)}, u32[]{:S(2)}, u32[]{:S(2)}) collective-permute-start(bf16[1024,256]{1,0:T(8,128)(2,1)S(1)} %shard_map.95.refs_4_), channel_id=1, source_target_pairs={{0,32},{1,33},{2,34},{3,35},{4,36},{5,37},{6,38},{7,39},{8,40},{9,... | collective-permute-start | bytes 1572872 | tf_op jit(solution)/shard_map/ppermute | solution.py:25
  26.4 23.4 %collective-permute-start.17 = (bf16[1024,256]{1,0:T(8,128)(2,1)S(1)}, bf16[1024,256]{1,0:T(8,128)(2,1)S(1)}, u32[]{:S(2)}, u32[]{:S(2)}) collective-permute-start(bf16[1024,256]{1,0:T(8,128)(2,1)S(1)} %shard_map.96.refs_8_.refs_4_), channel_id=1, source_target_pairs={{0,32},{1,33},{2,34},{3,35},{4,36},{5,37},{6,38},{7,39},{8,40},{9,... | collective-permute-start | bytes 1572872 | tf_op jit(solution)/shard_map/ppermute | solution.py:25
  28.0 17.8 %collective-permute-start.9 = (bf16[4,88,256]{2,1,0:T(8,128)(2,1)S(1)}, bf16[4,88,256]{2,1,0:T(8,128)(2,1)S(1)}, u32[]{:S(2)}, u32[]{:S(2)}) collective-permute-start(bf16[4,88,256]{2,1,0:T(8,128)(2,1)S(1)} %collective-permute-done.6.refs_0_), channel_id=1, source_target_pairs={{0,12},{1,13},{2,14},{3,15},{4,0},{5,1},{6,2},{7,3},{8,4},{9,5},{1... | collective-permute-start | bytes 540680 | tf_op jit(solution)/shard_map/ppermute | solution.py:25
  38.4 9.0 %collective-permute-start.8 = (bf16[4,88,256]{2,1,0:T(8,128)(2,1)S(1)}, bf16[4,88,256]{2,1,0:T(8,128)(2,1)S(1)}, u32[]{:S(2)}, u32[]{:S(2)}) collective-permute-start(bf16[4,88,256]{2,1,0:T(8,128)(2,1)S(1)} %collective-permute-done.6.refs_0_), channel_id=1, source_target_pairs={{0,8},{1,9},{2,10},{3,11},{4,12},{5,13},{6,14},{7,15},{8,0},{9,1},... | collective-permute-start | bytes 540680 | tf_op jit(solution)/shard_map/ppermute | solution.py:25
  38.5 10.7 %collective-permute-start.7 = (bf16[4,88,256]{2,1,0:T(8,128)(2,1)S(1)}, bf16[4,88,256]{2,1,0:T(8,128)(2,1)S(1)}, u32[]{:S(2)}, u32[]{:S(2)}) collective-permute-start(bf16[4,88,256]{2,1,0:T(8,128)(2,1)S(1)} %collective-permute-done.6.refs_0_), channel_id=1, source_target_pairs={{0,4},{1,5},{2,6},{3,7},{4,8},{5,9},{6,10},{7,11},{8,12},{9,13},{1... | collective-permute-start | bytes 540680 | tf_op jit(solution)/shard_map/ppermute | solution.py:25
  49.2 2.3 %collective-permute-start.14 = (bf16[1024,256]{1,0:T(8,128)(2,1)S(1)}, bf16[1024,256]{1,0:T(8,128)(2,1)S(1)}, u32[]{:S(2)}, u32[]{:S(2)}) collective-permute-start(bf16[1024,256]{1,0:T(8,128)(2,1)S(1)} %shard_map.95.refs_4_), channel_id=1, source_target_pairs={{0,16},{1,17},{2,18},{3,19},{4,20},{5,21},{6,22},{7,23},{8,24},{9,... | collective-permute-start | bytes 1572872 | tf_op jit(solution)/shard_map/ppermute | solution.py:25
  49.2 5.6 %collective-permute-start.15 = (bf16[1024,256]{1,0:T(8,128)(2,1)S(1)}, bf16[1024,256]{1,0:T(8,128)(2,1)S(1)}, u32[]{:S(2)}, u32[]{:S(2)}) collective-permute-start(bf16[1024,256]{1,0:T(8,128)(2,1)S(1)} %collective-permute-done.13.refs_6_), channel_id=1, source_target_pairs={{0,16},{1,17},{2,18},{3,19},{4,20},{5,21},{6,22},{7,23},{8,24},{9,... | collective-permute-start | bytes 1572872 | tf_op jit(solution)/shard_map/ppermute | solution.py:25
  49.8 5.1 %collective-permute-start.16 = (bf16[1024,256]{1,0:T(8,128)(2,1)S(1)}, bf16[1024,256]{1,0:T(8,128)(2,1)S(1)}, u32[]{:S(2)}, u32[]{:S(2)}) collective-permute-start(bf16[1024,256]{1,0:T(8,128)(2,1)S(1)} %shard_map.96.refs_8_.refs_4_), channel_id=1, source_target_pairs={{0,16},{1,17},{2,18},{3,19},{4,20},{5,21},{6,22},{7,23},{8,24},{9,... | collective-permute-start | bytes 1572872 | tf_op jit(solution)/shard_map/ppermute | solution.py:25
  49.8 5.1 %collective-permute-start.18 = (bf16[1024,256]{1,0:T(8,128)(2,1)S(1)}, bf16[1024,256]{1,0:T(8,128)(2,1)S(1)}, u32[]{:S(2)}, u32[]{:S(2)}) collective-permute-start(bf16[1024,256]{1,0:T(8,128)(2,1)S(1)} %collective-permute-done.17.refs_10_.refs_6_), channel_id=1, source_target_pairs={{0,16},{1,17},{2,18},{3,19},{4,20},{5,21},{6,22},{7,23},{8,24},{9,... | collective-permute-start | bytes 1572872 | tf_op jit(solution)/shard_map/ppermute | solution.py:25
  50.7 12.2 %collective-permute-start.22 = (bf16[384,256]{1,0:T(8,128)(2,1)S(1)}, bf16[384,256]{1,0:T(8,128)(2,1)S(1)}, u32[]{:S(2)}, u32[]{:S(2)}) collective-permute-start(bf16[384,256]{1,0:T(8,128)(2,1)S(1)} %get-tuple-element.115), channel_id=1, source_target_pairs={{0,1},{1,2},{2,3},{3,0},{4,5},{5,6},{6,7},{7,4},{8,9},{9,10},{10,1... | collective-permute-start | bytes 589832 | tf_op jit(solution)/shard_map/ppermute | solution.py:25
  51.6 14.4 %collective-permute-start.23 = (bf16[384,256]{1,0:T(8,128)(2,1)S(1)}, bf16[384,256]{1,0:T(8,128)(2,1)S(1)}, u32[]{:S(2)}, u32[]{:S(2)}) collective-permute-start(bf16[384,256]{1,0:T(8,128)(2,1)S(1)} %get-tuple-element.116), channel_id=1, source_target_pairs={{0,2},{1,3},{2,0},{3,1},{4,6},{5,7},{6,4},{7,5},{8,10},{9,11},{10,... | collective-permute-start | bytes 589832 | tf_op jit(solution)/shard_map/ppermute | solution.py:25
  54.8 11.1 %collective-permute-start.24 = (bf16[384,256]{1,0:T(8,128)(2,1)S(1)}, bf16[384,256]{1,0:T(8,128)(2,1)S(1)}, u32[]{:S(2)}, u32[]{:S(2)}) collective-permute-start(bf16[384,256]{1,0:T(8,128)(2,1)S(1)} %get-tuple-element.117), channel_id=1, source_target_pairs={{0,3},{1,0},{2,1},{3,2},{4,7},{5,4},{6,5},{7,6},{8,11},{9,8},{10,9... | collective-permute-start | bytes 589832 | tf_op jit(solution)/shard_map/ppermute | solution.py:25
  57.3 9.5 %collective-permute-start.19 = (bf16[88,1024]{1,0:T(8,128)(2,1)S(1)}, bf16[88,1024]{1,0:T(8,128)(2,1)S(1)}, u32[]{:S(2)}, u32[]{:S(2)}) collective-permute-start(bf16[88,1024]{1,0:T(8,128)(2,1)S(1)} %get-tuple-element.109), channel_id=1, source_target_pairs={{0,64},{1,65},{2,66},{3,67},{4,68},{5,69},{6,70},{7,71},{8,72},{9,... | collective-permute-start | bytes 540680 | tf_op jit(solution)/shard_map/ppermute | solution.py:25
  60.3 13.7 %collective-permute-start.20 = (bf16[88,1024]{1,0:T(8,128)(2,1)S(1)}, bf16[88,1024]{1,0:T(8,128)(2,1)S(1)}, u32[]{:S(2)}, u32[]{:S(2)}) collective-permute-start(bf16[88,1024]{1,0:T(8,128)(2,1)S(1)} %get-tuple-element.110), channel_id=1, source_target_pairs={{0,128},{1,129},{2,130},{3,131},{4,132},{5,133},{6,134},{7,135},{8... | collective-permute-start | bytes 540680 | tf_op jit(solution)/shard_map/ppermute | solution.py:25
  62.9 16.5 %collective-permute-start.21 = (bf16[88,1024]{1,0:T(8,128)(2,1)S(1)}, bf16[88,1024]{1,0:T(8,128)(2,1)S(1)}, u32[]{:S(2)}, u32[]{:S(2)}) collective-permute-start(bf16[88,1024]{1,0:T(8,128)(2,1)S(1)} %get-tuple-element.111), channel_id=1, source_target_pairs={{0,192},{1,193},{2,194},{3,195},{4,196},{5,197},{6,198},{7,199},{8... | collective-permute-start | bytes 540680 | tf_op jit(solution)/shard_map/ppermute | solution.py:25
  99.1 1.7 collective-permute-start.25
  101.5 11.0 %collective-permute-start.28 = (bf16[448,128]{1,0:T(8,128)(2,1)S(1)}, bf16[448,128]{1,0:T(8,128)(2,1)S(1)}, u32[]{:S(2)}, u32[]{:S(2)}) collective-permute-start(bf16[448,128]{1,0:T(8,128)(2,1)S(1)} %get-tuple-element.128.refs_0_), channel_id=1, source_target_pairs={{0,12},{1,13},{2,14},{3,15},{4,0},{5,1},{6,2},{7,3},{8,4},{9,5},{1... | collective-permute-start | bytes 344072 | tf_op jit(solution)/shard_map/ppermute | solution.py:25
  107.3 7.5 %collective-permute-start.27 = (bf16[448,128]{1,0:T(8,128)(2,1)S(1)}, bf16[448,128]{1,0:T(8,128)(2,1)S(1)}, u32[]{:S(2)}, u32[]{:S(2)}) collective-permute-start(bf16[448,128]{1,0:T(8,128)(2,1)S(1)} %get-tuple-element.128.refs_0_), channel_id=1, source_target_pairs={{0,8},{1,9},{2,10},{3,11},{4,12},{5,13},{6,14},{7,15},{8,0},{9,1},... | collective-permute-start | bytes 344072 | tf_op jit(solution)/shard_map/ppermute | solution.py:25
  107.4 8.6 %collective-permute-start.26 = (bf16[448,128]{1,0:T(8,128)(2,1)S(1)}, bf16[448,128]{1,0:T(8,128)(2,1)S(1)}, u32[]{:S(2)}, u32[]{:S(2)}) collective-permute-start(bf16[448,128]{1,0:T(8,128)(2,1)S(1)} %get-tuple-element.128.refs_0_), channel_id=1, source_target_pairs={{0,4},{1,5},{2,6},{3,7},{4,8},{5,9},{6,10},{7,11},{8,12},{9,13},{1... | collective-permute-start | bytes 344072 | tf_op jit(solution)/shard_map/ppermute | solution.py:25
  116.0 5.6 %collective-permute-start.31 = (bf16[448,128]{1,0:T(8,128)(2,1)S(1)}, bf16[448,128]{1,0:T(8,128)(2,1)S(1)}, u32[]{:S(2)}, u32[]{:S(2)}) collective-permute-start(bf16[448,128]{1,0:T(8,128)(2,1)S(1)} %shard_map.101.refs_0_), channel_id=1, source_target_pairs={{0,3},{1,0},{2,1},{3,2},{4,7},{5,4},{6,5},{7,6},{8,11},{9,8},{10,9... | collective-permute-start | bytes 344072 | tf_op jit(solution)/shard_map/ppermute | solution.py:25
  117.0 6.3 %collective-permute-start.30 = (bf16[448,128]{1,0:T(8,128)(2,1)S(1)}, bf16[448,128]{1,0:T(8,128)(2,1)S(1)}, u32[]{:S(2)}, u32[]{:S(2)}) collective-permute-start(bf16[448,128]{1,0:T(8,128)(2,1)S(1)} %shard_map.101.refs_0_), channel_id=1, source_target_pairs={{0,2},{1,3},{2,0},{3,1},{4,6},{5,7},{6,4},{7,5},{8,10},{9,11},{10,... | collective-permute-start | bytes 344072 | tf_op jit(solution)/shard_map/ppermute | solution.py:25
  118.1 7.1 %collective-permute-start.29 = (bf16[448,128]{1,0:T(8,128)(2,1)S(1)}, bf16[448,128]{1,0:T(8,128)(2,1)S(1)}, u32[]{:S(2)}, u32[]{:S(2)}) collective-permute-start(bf16[448,128]{1,0:T(8,128)(2,1)S(1)} %shard_map.101.refs_0_), channel_id=1, source_target_pairs={{0,1},{1,2},{2,3},{3,0},{4,5},{5,6},{6,7},{7,4},{8,9},{9,10},{10,1... | collective-permute-start | bytes 344072 | tf_op jit(solution)/shard_map/ppermute | solution.py:25
  126.2 0.7 collective-permute-start.32
  126.8 16.6 %collective-permute-start.35 = (bf16[4,64,256]{2,1,0:T(8,128)(2,1)S(1)}, bf16[4,64,256]{2,1,0:T(8,128)(2,1)S(1)}, u32[]{:S(2)}, u32[]{:S(2)}) collective-permute-start(bf16[4,64,256]{2,1,0:T(8,128)(2,1)S(1)} %collective-permute-done.32.refs_0_), channel_id=1, source_target_pairs={{0,12},{1,13},{2,14},{3,15},{4,0},{5,1},{6,2},{7,3},{8,4},{9,5},{1... | collective-permute-start | bytes 393224 | tf_op jit(solution)/shard_map/ppermute | solution.py:25
  139.5 6.6 %collective-permute-start.34 = (bf16[4,64,256]{2,1,0:T(8,128)(2,1)S(1)}, bf16[4,64,256]{2,1,0:T(8,128)(2,1)S(1)}, u32[]{:S(2)}, u32[]{:S(2)}) collective-permute-start(bf16[4,64,256]{2,1,0:T(8,128)(2,1)S(1)} %collective-permute-done.32.refs_0_), channel_id=1, source_target_pairs={{0,8},{1,9},{2,10},{3,11},{4,12},{5,13},{6,14},{7,15},{8,0},{9,1},... | collective-permute-start | bytes 393224 | tf_op jit(solution)/shard_map/ppermute | solution.py:25
  139.7 7.6 %collective-permute-start.33 = (bf16[4,64,256]{2,1,0:T(8,128)(2,1)S(1)}, bf16[4,64,256]{2,1,0:T(8,128)(2,1)S(1)}, u32[]{:S(2)}, u32[]{:S(2)}) collective-permute-start(bf16[4,64,256]{2,1,0:T(8,128)(2,1)S(1)} %collective-permute-done.32.refs_0_), channel_id=1, source_target_pairs={{0,4},{1,5},{2,6},{3,7},{4,8},{5,9},{6,10},{7,11},{8,12},{9,13},{1... | collective-permute-start | bytes 393224 | tf_op jit(solution)/shard_map/ppermute | solution.py:25
  148.9 8.7 %collective-permute-start.36 = (bf16[64,1024]{1,0:T(8,128)(2,1)S(1)}, bf16[64,1024]{1,0:T(8,128)(2,1)S(1)}, u32[]{:S(2)}, u32[]{:S(2)}) collective-permute-start(bf16[64,1024]{1,0:T(8,128)(2,1)S(1)} %get-tuple-element.131), channel_id=1, source_target_pairs={{0,64},{1,65},{2,66},{3,67},{4,68},{5,69},{6,70},{7,71},{8,72},{9,... | collective-permute-start | bytes 393224 | tf_op jit(solution)/shard_map/ppermute | solution.py:25
  149.2 16.0 %collective-permute-start.37 = (bf16[64,1024]{1,0:T(8,128)(2,1)S(1)}, bf16[64,1024]{1,0:T(8,128)(2,1)S(1)}, u32[]{:S(2)}, u32[]{:S(2)}) collective-permute-start(bf16[64,1024]{1,0:T(8,128)(2,1)S(1)} %get-tuple-element.132), channel_id=1, source_target_pairs={{0,128},{1,129},{2,130},{3,131},{4,132},{5,133},{6,134},{7,135},{8... | collective-permute-start | bytes 393224 | tf_op jit(solution)/shard_map/ppermute | solution.py:25
  155.1 10.1 %collective-permute-start.38 = (bf16[64,1024]{1,0:T(8,128)(2,1)S(1)}, bf16[64,1024]{1,0:T(8,128)(2,1)S(1)}, u32[]{:S(2)}, u32[]{:S(2)}) collective-permute-start(bf16[64,1024]{1,0:T(8,128)(2,1)S(1)} %get-tuple-element.133), channel_id=1, source_target_pairs={{0,192},{1,193},{2,194},{3,195},{4,196},{5,197},{6,198},{7,199},{8... | collective-permute-start | bytes 393224 | tf_op jit(solution)/shard_map/ppermute | solution.py:25
  165.6 5.9 %collective-permute-start.41 = (bf16[448,128]{1,0:T(8,128)(2,1)S(1)}, bf16[448,128]{1,0:T(8,128)(2,1)S(1)}, u32[]{:S(2)}, u32[]{:S(2)}) collective-permute-start(bf16[448,128]{1,0:T(8,128)(2,1)S(1)} %get-tuple-element.135.refs_0_), channel_id=1, source_target_pairs={{0,12},{1,13},{2,14},{3,15},{4,0},{5,1},{6,2},{7,3},{8,4},{9,5},{1... | collective-permute-start | bytes 344072 | tf_op jit(solution)/shard_map/ppermute | solution.py:25
  166.3 7.5 %collective-permute-start.40 = (bf16[448,128]{1,0:T(8,128)(2,1)S(1)}, bf16[448,128]{1,0:T(8,128)(2,1)S(1)}, u32[]{:S(2)}, u32[]{:S(2)}) collective-permute-start(bf16[448,128]{1,0:T(8,128)(2,1)S(1)} %get-tuple-element.135.refs_0_), channel_id=1, source_target_pairs={{0,8},{1,9},{2,10},{3,11},{4,12},{5,13},{6,14},{7,15},{8,0},{9,1},... | collective-permute-start | bytes 344072 | tf_op jit(solution)/shard_map/ppermute | solution.py:25
  166.3 8.0 %collective-permute-start.39 = (bf16[448,128]{1,0:T(8,128)(2,1)S(1)}, bf16[448,128]{1,0:T(8,128)(2,1)S(1)}, u32[]{:S(2)}, u32[]{:S(2)}) collective-permute-start(bf16[448,128]{1,0:T(8,128)(2,1)S(1)} %get-tuple-element.135.refs_0_), channel_id=1, source_target_pairs={{0,4},{1,5},{2,6},{3,7},{4,8},{5,9},{6,10},{7,11},{8,12},{9,13},{1... | collective-permute-start | bytes 344072 | tf_op jit(solution)/shard_map/ppermute | solution.py:25
  174.4 9.7 %collective-permute-start.44 = (bf16[448,128]{1,0:T(8,128)(2,1)S(1)}, bf16[448,128]{1,0:T(8,128)(2,1)S(1)}, u32[]{:S(2)}, u32[]{:S(2)}) collective-permute-start(bf16[448,128]{1,0:T(8,128)(2,1)S(1)} %shard_map.105.refs_0_), channel_id=1, source_target_pairs={{0,3},{1,0},{2,1},{3,2},{4,7},{5,4},{6,5},{7,6},{8,11},{9,8},{10,9... | collective-permute-start | bytes 344072 | tf_op jit(solution)/shard_map/ppermute | solution.py:25
  180.5 6.3 %collective-permute-start.43 = (bf16[448,128]{1,0:T(8,128)(2,1)S(1)}, bf16[448,128]{1,0:T(8,128)(2,1)S(1)}, u32[]{:S(2)}, u32[]{:S(2)}) collective-permute-start(bf16[448,128]{1,0:T(8,128)(2,1)S(1)} %shard_map.105.refs_0_), channel_id=1, source_target_pairs={{0,2},{1,3},{2,0},{3,1},{4,6},{5,7},{6,4},{7,5},{8,10},{9,11},{10,... | collective-permute-start | bytes 344072 | tf_op jit(solution)/shard_map/ppermute | solution.py:25
  180.5 6.3 %collective-permute-start.42 = (bf16[448,128]{1,0:T(8,128)(2,1)S(1)}, bf16[448,128]{1,0:T(8,128)(2,1)S(1)}, u32[]{:S(2)}, u32[]{:S(2)}) collective-permute-start(bf16[448,128]{1,0:T(8,128)(2,1)S(1)} %shard_map.105.refs_0_), channel_id=1, source_target_pairs={{0,1},{1,2},{2,3},{3,0},{4,5},{5,6},{6,7},{7,4},{8,9},{9,10},{10,1... | collective-permute-start | bytes 344072 | tf_op jit(solution)/shard_map/ppermute | solution.py:25
  187.9 5.4 %collective-permute-start.45 = (bf16[64,256]{1,0:T(8,128)(2,1)S(1)}, bf16[64,256]{1,0:T(8,128)(2,1)S(1)}, u32[]{:S(2)}, u32[]{:S(2)}) collective-permute-start(bf16[64,256]{1,0:T(8,128)(2,1)S(1)} %get-tuple-element.138), channel_id=1, source_target_pairs={{0,3},{1,0},{2,1},{3,2},{4,7},{5,4},{6,5},{7,6},{8,11},{9,8},{10,9... | collective-permute-start | bytes 98312 | tf_op jit(solution)/shard_map/ppermute | solution.py:25
  190.8 5.4 %collective-permute-start.46 = (bf16[64,256]{1,0:T(8,128)(2,1)S(1)}, bf16[64,256]{1,0:T(8,128)(2,1)S(1)}, u32[]{:S(2)}, u32[]{:S(2)}) collective-permute-start(bf16[64,256]{1,0:T(8,128)(2,1)S(1)} %get-tuple-element.139), channel_id=1, source_target_pairs={{0,2},{1,3},{2,0},{3,1},{4,6},{5,7},{6,4},{7,5},{8,10},{9,11},{10,... | collective-permute-start | bytes 98312 | tf_op jit(solution)/shard_map/ppermute | solution.py:25
  190.8 5.4 %collective-permute-start.47 = (bf16[64,256]{1,0:T(8,128)(2,1)S(1)}, bf16[64,256]{1,0:T(8,128)(2,1)S(1)}, u32[]{:S(2)}, u32[]{:S(2)}) collective-permute-start(bf16[64,256]{1,0:T(8,128)(2,1)S(1)} %get-tuple-element.140), channel_id=1, source_target_pairs={{0,1},{1,2},{2,3},{3,0},{4,5},{5,6},{6,7},{7,4},{8,9},{9,10},{10,1... | collective-permute-start | bytes 98312 | tf_op jit(solution)/shard_map/ppermute | solution.py:25
  (9 other events, 90.0 us)

commit v8 on v7

--- a/solution.py
+++ b/solution.py
@@ -108,7 +108,7 @@
             out_shape=out_shape,
             in_specs=specs,
             scratch_shapes=list(scratch),
-            compiler_params=pltpu.CompilerParams(vmem_limit_bytes=30 * 2**20),
+            compiler_params=pltpu.CompilerParams(vmem_limit_bytes=14 * 2**20),
             cost_estimate=pl.CostEstimate(
                 flops=flops, bytes_accessed=moved, transcendentals=0
             ),

time: 197 us -> 197 us (level)
  no operation moved by 1% of the time
where the time goes in v8:
time: 197 us
  starting transfers between devices  89.9 us (46%)
  waiting for transfers between devices  75 us (38%)
  blocking collectives  19.6 us (10%)
  Pallas kernels  9.19 us (5%)
  local copies, waits for them, and re-layouts  3.03 us (2%)
    ppermute x48, starting transfers between devices, permuted(): return lax.ppermute(value, ('row', 'col'), routes(to))  89.9 us
    ppermute x48, waiting for transfers between devices, permuted(): return lax.ppermute(value, ('row', 'col'), routes(to))  75 us
    all_to_all x1, blocking collectives, from_every_z(): lax.all_to_all(value, 'row', 0, 0, tiled=True, axis_index_groups=Z_GROUPS)  19.6 us
    pallas_call x17, Pallas kernels, run(): pl.pallas_call(body, out_shape=out_shape, in_specs=specs, scratch_shapes=...  9.19 us
  transfers between devices with their start and end apart: 48, of which 29 were waited for; matrix products, arithmetic and copies ran while one was open for 0% of the time, Pallas kernels for 2%

profile of v8, /device:TPU:2, one launch (start us, length us, event | category | flops | bytes accessed | tf_op | source)
XLA Modules:
  0.0 197.0 jit_solution(7483779392767135259)
XLA Ops:
  3.6 1.6 collective-permute-start.10
  5.1 2.8 %collective-permute-start.11 = (bf16[256,256]{1,0:T(8,128)(2,1)S(1)}, bf16[256,256]{1,0:T(8,128)(2,1)S(1)}, u32[]{:S(2)}, u32[]{:S(2)}) collective-permute-start(bf16[256,256]{1,0:T(8,128)(2,1)S(1)} %get-tuple-element.91), channel_id=1, source_target_pairs={{0,2},{1,3},{2,0},{3,1},{4,6},{5,7},{6,4},{7,5},{8,10},{9,11},{10,... | collective-permute-start | bytes 393224 | tf_op jit(solution)/shard_map/ppermute | solution.py:25
  8.0 2.5 %collective-permute-start.1 = (bf16[88,256]{1,0:T(8,128)(2,1)S(1)}, bf16[88,256]{1,0:T(8,128)(2,1)S(1)}, u32[]{:S(2)}, u32[]{:S(2)}) collective-permute-start(bf16[88,256]{1,0:T(8,128)(2,1)S(1)} %get-tuple-element.79), channel_id=1, source_target_pairs={{0,2},{1,3},{2,0},{3,1},{4,6},{5,7},{6,4},{7,5},{8,10},{9,11},{10,... | collective-permute-start | bytes 135176 | tf_op jit(solution)/shard_map/ppermute | solution.py:25
  11.3 1.9 collective-permute-done.refs_1_
  15.2 2.3 %collective-permute-start.12 = (bf16[256,256]{1,0:T(8,128)(2,1)S(1)}, bf16[256,256]{1,0:T(8,128)(2,1)S(1)}, u32[]{:S(2)}, u32[]{:S(2)}) collective-permute-start(bf16[256,256]{1,0:T(8,128)(2,1)S(1)} %get-tuple-element.92), channel_id=1, source_target_pairs={{0,3},{1,0},{2,1},{3,2},{4,7},{5,4},{6,5},{7,6},{8,11},{9,8},{10,9... | collective-permute-start | bytes 393224 | tf_op jit(solution)/shard_map/ppermute | solution.py:25
  17.7 3.3 %collective-permute-start.4 = (bf16[256,256]{1,0:T(8,128)(2,1)S(1)}, bf16[256,256]{1,0:T(8,128)(2,1)S(1)}, u32[]{:S(2)}, u32[]{:S(2)}) collective-permute-start(bf16[256,256]{1,0:T(8,128)(2,1)S(1)} %get-tuple-element.84), channel_id=1, source_target_pairs={{0,2},{1,3},{2,0},{3,1},{4,6},{5,7},{6,4},{7,5},{8,10},{9,11},{10,... | collective-permute-start | bytes 393224 | tf_op jit(solution)/shard_map/ppermute | solution.py:25
  21.0 2.1 %collective-permute-start.13 = (bf16[1024,256]{1,0:T(8,128)(2,1)S(1)}, bf16[1024,256]{1,0:T(8,128)(2,1)S(1)}, u32[]{:S(2)}, u32[]{:S(2)}) collective-permute-start(bf16[1024,256]{1,0:T(8,128)(2,1)S(1)} %shard_map.95.refs_4_), channel_id=1, source_target_pairs={{0,32},{1,33},{2,34},{3,35},{4,36},{5,37},{6,38},{7,39},{8,40},{9,... | collective-permute-start | bytes 1572872 | tf_op jit(solution)/shard_map/ppermute | solution.py:25
  23.1 1.9 collective-permute-done.4.refs_2_
  25.0 1.4 collective-permute-done.5.refs_3_
  26.4 1.7 collective-permute-start.17
  28.0 10.3 %collective-permute-start.9 = (bf16[4,88,256]{2,1,0:T(8,128)(2,1)S(1)}, bf16[4,88,256]{2,1,0:T(8,128)(2,1)S(1)}, u32[]{:S(2)}, u32[]{:S(2)}) collective-permute-start(bf16[4,88,256]{2,1,0:T(8,128)(2,1)S(1)} %collective-permute-done.6.refs_0_), channel_id=1, source_target_pairs={{0,12},{1,13},{2,14},{3,15},{4,0},{5,1},{6,2},{7,3},{8,4},{9,5},{1... | collective-permute-start | bytes 540680 | tf_op jit(solution)/shard_map/ppermute | solution.py:25
  38.5 1.4 collective-permute-start.7
  39.9 5.9 %collective-permute-done.9.refs_3_ = bf16[4,88,256]{2,1,0:T(8,128)(2,1)S(1)} collective-permute-done((bf16[4,88,256]{2,1,0:T(8,128)(2,1)S(1)}, bf16[4,88,256]{2,1,0:T(8,128)(2,1)S(1)}, u32[]{:S(2)}, u32[]{:S(2)}) %collective-permute-start.9) | collective-permute-done | bytes 180256 | tf_op jit(solution)/shard_map/ppermute | solution.py:25
  45.8 1.5 collective-permute-done.8.refs_2_
  47.3 1.9 collective-permute-done.7.refs_1_
  51.6 3.3 %collective-permute-start.23 = (bf16[384,256]{1,0:T(8,128)(2,1)S(1)}, bf16[384,256]{1,0:T(8,128)(2,1)S(1)}, u32[]{:S(2)}, u32[]{:S(2)}) collective-permute-start(bf16[384,256]{1,0:T(8,128)(2,1)S(1)} %get-tuple-element.116), channel_id=1, source_target_pairs={{0,2},{1,3},{2,0},{3,1},{4,6},{5,7},{6,4},{7,5},{8,10},{9,11},{10,... | collective-permute-start | bytes 589832 | tf_op jit(solution)/shard_map/ppermute | solution.py:25
  54.9 2.4 %shard_map.97 = (bf16[88,1024]{1,0:T(8,128)(2,1)S(1)}, bf16[88,1024]{1,0:T(8,128)(2,1)S(1)}, bf16[88,1024]{1,0:T(8,128)(2,1)S(1)}, bf16[88,1024]{1,0:T(8,128)(2,1)S(1)}) custom-call(bf16[4,88,256]{2,1,0:T(8,128)(2,1)S(1)} %collective-permute-done.6.refs_0_, bf16[4,88,256]{2,1,0:T(8,128)(2,1)S(1)} %collective-permute-done.7.refs_1_, ...), custom_call_target="tpu_custom_call" | custom-call | flops 738197504 | bytes 5636096 | tf_op jit(solution)/shard_map/pallas_call | solution.py:106
  57.3 3.0 %collective-permute-start.19 = (bf16[88,1024]{1,0:T(8,128)(2,1)S(1)}, bf16[88,1024]{1,0:T(8,128)(2,1)S(1)}, u32[]{:S(2)}, u32[]{:S(2)}) collective-permute-start(bf16[88,1024]{1,0:T(8,128)(2,1)S(1)} %get-tuple-element.109), channel_id=1, source_target_pairs={{0,64},{1,65},{2,66},{3,67},{4,68},{5,69},{6,70},{7,71},{8,72},{9,... | collective-permute-start | bytes 540680 | tf_op jit(solution)/shard_map/ppermute | solution.py:25
  60.3 2.6 %collective-permute-start.20 = (bf16[88,1024]{1,0:T(8,128)(2,1)S(1)}, bf16[88,1024]{1,0:T(8,128)(2,1)S(1)}, u32[]{:S(2)}, u32[]{:S(2)}) collective-permute-start(bf16[88,1024]{1,0:T(8,128)(2,1)S(1)} %get-tuple-element.110), channel_id=1, source_target_pairs={{0,128},{1,129},{2,130},{3,131},{4,132},{5,133},{6,134},{7,135},{8... | collective-permute-start | bytes 540680 | tf_op jit(solution)/shard_map/ppermute | solution.py:25
  62.9 3.1 %collective-permute-start.21 = (bf16[88,1024]{1,0:T(8,128)(2,1)S(1)}, bf16[88,1024]{1,0:T(8,128)(2,1)S(1)}, u32[]{:S(2)}, u32[]{:S(2)}) collective-permute-start(bf16[88,1024]{1,0:T(8,128)(2,1)S(1)} %get-tuple-element.111), channel_id=1, source_target_pairs={{0,192},{1,193},{2,194},{3,195},{4,196},{5,197},{6,198},{7,199},{8... | collective-permute-start | bytes 540680 | tf_op jit(solution)/shard_map/ppermute | solution.py:25
  66.8 7.1 %collective-permute-done.20.refs_2_ = bf16[88,1024]{1,0:T(8,128)(2,1)S(1)} collective-permute-done((bf16[88,1024]{1,0:T(8,128)(2,1)S(1)}, bf16[88,1024]{1,0:T(8,128)(2,1)S(1)}, u32[]{:S(2)}, u32[]{:S(2)}) %collective-permute-start.20) | collective-permute-done | bytes 180256 | tf_op jit(solution)/shard_map/ppermute | solution.py:25
  73.9 5.5 %collective-permute-done.21.refs_3_ = bf16[88,1024]{1,0:T(8,128)(2,1)S(1)} collective-permute-done((bf16[88,1024]{1,0:T(8,128)(2,1)S(1)}, bf16[88,1024]{1,0:T(8,128)(2,1)S(1)}, u32[]{:S(2)}, u32[]{:S(2)}) %collective-permute-start.21) | collective-permute-done | bytes 180256 | tf_op jit(solution)/shard_map/ppermute | solution.py:25
  79.5 19.6 %all_to_all.5.mine_ref = bf16[8,24,1024]{2,1,0:T(8,128)(2,1)S(1)} all-to-all(bf16[8,24,1024]{2,1,0:T(8,128)(2,1)S(1)} %get-tuple-element.123), channel_id=1, replica_groups={{0,32,64,96,128,160,192,224},{16,48,80,112,144,176,208,240},{1,33,65,97..., dimensions={0} | all-to-all | bytes 786432 | tf_op jit(solution)/shard_map/all_to_all | solution.py:55
  99.1 1.7 collective-permute-done.25.other_ref
  101.5 5.8 %collective-permute-start.28 = (bf16[448,128]{1,0:T(8,128)(2,1)S(1)}, bf16[448,128]{1,0:T(8,128)(2,1)S(1)}, u32[]{:S(2)}, u32[]{:S(2)}) collective-permute-start(bf16[448,128]{1,0:T(8,128)(2,1)S(1)} %get-tuple-element.128.refs_0_), channel_id=1, source_target_pairs={{0,12},{1,13},{2,14},{3,15},{4,0},{5,1},{6,2},{7,3},{8,4},{9,5},{1... | collective-permute-start | bytes 344072 | tf_op jit(solution)/shard_map/ppermute | solution.py:25
  108.3 4.2 %collective-permute-done.28.refs_3_ = bf16[448,128]{1,0:T(8,128)(2,1)S(1)} collective-permute-done((bf16[448,128]{1,0:T(8,128)(2,1)S(1)}, bf16[448,128]{1,0:T(8,128)(2,1)S(1)}, u32[]{:S(2)}, u32[]{:S(2)}) %collective-permute-start.28) | collective-permute-done | bytes 114720 | tf_op jit(solution)/shard_map/ppermute | solution.py:25
  112.5 2.4 %collective-permute-done.27.refs_2_ = bf16[448,128]{1,0:T(8,128)(2,1)S(1)} collective-permute-done((bf16[448,128]{1,0:T(8,128)(2,1)S(1)}, bf16[448,128]{1,0:T(8,128)(2,1)S(1)}, u32[]{:S(2)}, u32[]{:S(2)}) %collective-permute-start.27) | collective-permute-done | bytes 114720 | tf_op jit(solution)/shard_map/ppermute | solution.py:25
  119.2 2.4 %collective-permute-done.31.refs_3_ = bf16[448,128]{1,0:T(8,128)(2,1)S(1)} collective-permute-done((bf16[448,128]{1,0:T(8,128)(2,1)S(1)}, bf16[448,128]{1,0:T(8,128)(2,1)S(1)}, u32[]{:S(2)}, u32[]{:S(2)}) %collective-permute-start.31) | collective-permute-done | bytes 114720 | tf_op jit(solution)/shard_map/ppermute | solution.py:25
  121.6 1.8 collective-permute-done.30.refs_2_
  123.3 1.8 collective-permute-done.29.refs_1_
  126.8 12.7 %collective-permute-start.35 = (bf16[4,64,256]{2,1,0:T(8,128)(2,1)S(1)}, bf16[4,64,256]{2,1,0:T(8,128)(2,1)S(1)}, u32[]{:S(2)}, u32[]{:S(2)}) collective-permute-start(bf16[4,64,256]{2,1,0:T(8,128)(2,1)S(1)} %collective-permute-done.32.refs_0_), channel_id=1, source_target_pairs={{0,12},{1,13},{2,14},{3,15},{4,0},{5,1},{6,2},{7,3},{8,4},{9,5},{1... | collective-permute-start | bytes 393224 | tf_op jit(solution)/shard_map/ppermute | solution.py:25
  139.7 1.4 collective-permute-start.33
  141.2 2.2 %collective-permute-done.35.refs_3_ = bf16[4,64,256]{2,1,0:T(8,128)(2,1)S(1)} collective-permute-done((bf16[4,64,256]{2,1,0:T(8,128)(2,1)S(1)}, bf16[4,64,256]{2,1,0:T(8,128)(2,1)S(1)}, u32[]{:S(2)}, u32[]{:S(2)}) %collective-permute-start.35) | collective-permute-done | bytes 131104 | tf_op jit(solution)/shard_map/ppermute | solution.py:25
  143.4 2.7 %collective-permute-done.34.refs_2_ = bf16[4,64,256]{2,1,0:T(8,128)(2,1)S(1)} collective-permute-done((bf16[4,64,256]{2,1,0:T(8,128)(2,1)S(1)}, bf16[4,64,256]{2,1,0:T(8,128)(2,1)S(1)}, u32[]{:S(2)}, u32[]{:S(2)}) %collective-permute-start.34) | collective-permute-done | bytes 131104 | tf_op jit(solution)/shard_map/ppermute | solution.py:25
  147.3 1.5 shard_map.103
  149.2 5.9 %collective-permute-start.37 = (bf16[64,1024]{1,0:T(8,128)(2,1)S(1)}, bf16[64,1024]{1,0:T(8,128)(2,1)S(1)}, u32[]{:S(2)}, u32[]{:S(2)}) collective-permute-start(bf16[64,1024]{1,0:T(8,128)(2,1)S(1)} %get-tuple-element.132), channel_id=1, source_target_pairs={{0,128},{1,129},{2,130},{3,131},{4,132},{5,133},{6,134},{7,135},{8... | collective-permute-start | bytes 393224 | tf_op jit(solution)/shard_map/ppermute | solution.py:25
  155.1 2.4 %collective-permute-done.36.refs_1_ = bf16[64,1024]{1,0:T(8,128)(2,1)S(1)} collective-permute-done((bf16[64,1024]{1,0:T(8,128)(2,1)S(1)}, bf16[64,1024]{1,0:T(8,128)(2,1)S(1)}, u32[]{:S(2)}, u32[]{:S(2)}) %collective-permute-start.36) | collective-permute-done | bytes 131104 | tf_op jit(solution)/shard_map/ppermute | solution.py:25
  157.5 7.7 %collective-permute-done.37.refs_2_ = bf16[64,1024]{1,0:T(8,128)(2,1)S(1)} collective-permute-done((bf16[64,1024]{1,0:T(8,128)(2,1)S(1)}, bf16[64,1024]{1,0:T(8,128)(2,1)S(1)}, u32[]{:S(2)}, u32[]{:S(2)}) %collective-permute-start.37) | collective-permute-done | bytes 131104 | tf_op jit(solution)/shard_map/ppermute | solution.py:25
  166.3 1.4 collective-permute-start.39
  167.7 3.8 %collective-permute-done.41.refs_3_ = bf16[448,128]{1,0:T(8,128)(2,1)S(1)} collective-permute-done((bf16[448,128]{1,0:T(8,128)(2,1)S(1)}, bf16[448,128]{1,0:T(8,128)(2,1)S(1)}, u32[]{:S(2)}, u32[]{:S(2)}) %collective-permute-start.41) | collective-permute-done | bytes 114720 | tf_op jit(solution)/shard_map/ppermute | solution.py:25
  171.5 2.3 %collective-permute-done.40.refs_2_ = bf16[448,128]{1,0:T(8,128)(2,1)S(1)} collective-permute-done((bf16[448,128]{1,0:T(8,128)(2,1)S(1)}, bf16[448,128]{1,0:T(8,128)(2,1)S(1)}, u32[]{:S(2)}, u32[]{:S(2)}) %collective-permute-start.40) | collective-permute-done | bytes 114720 | tf_op jit(solution)/shard_map/ppermute | solution.py:25
  174.4 6.1 %collective-permute-start.44 = (bf16[448,128]{1,0:T(8,128)(2,1)S(1)}, bf16[448,128]{1,0:T(8,128)(2,1)S(1)}, u32[]{:S(2)}, u32[]{:S(2)}) collective-permute-start(bf16[448,128]{1,0:T(8,128)(2,1)S(1)} %shard_map.105.refs_0_), channel_id=1, source_target_pairs={{0,3},{1,0},{2,1},{3,2},{4,7},{5,4},{6,5},{7,6},{8,11},{9,8},{10,9... | collective-permute-start | bytes 344072 | tf_op jit(solution)/shard_map/ppermute | solution.py:25
  180.5 1.6 collective-permute-start.42
  182.1 2.0 collective-permute-done.44.refs_3_
  184.0 2.8 %collective-permute-done.43.refs_2_ = bf16[448,128]{1,0:T(8,128)(2,1)S(1)} collective-permute-done((bf16[448,128]{1,0:T(8,128)(2,1)S(1)}, bf16[448,128]{1,0:T(8,128)(2,1)S(1)}, u32[]{:S(2)}, u32[]{:S(2)}) %collective-permute-start.43) | collective-permute-done | bytes 114720 | tf_op jit(solution)/shard_map/ppermute | solution.py:25
  187.9 2.9 %collective-permute-start.45 = (bf16[64,256]{1,0:T(8,128)(2,1)S(1)}, bf16[64,256]{1,0:T(8,128)(2,1)S(1)}, u32[]{:S(2)}, u32[]{:S(2)}) collective-permute-start(bf16[64,256]{1,0:T(8,128)(2,1)S(1)} %get-tuple-element.138), channel_id=1, source_target_pairs={{0,3},{1,0},{2,1},{3,2},{4,7},{5,4},{6,5},{7,6},{8,11},{9,8},{10,9... | collective-permute-start | bytes 98312 | tf_op jit(solution)/shard_map/ppermute | solution.py:25
  190.8 2.5 %collective-permute-start.47 = (bf16[64,256]{1,0:T(8,128)(2,1)S(1)}, bf16[64,256]{1,0:T(8,128)(2,1)S(1)}, u32[]{:S(2)}, u32[]{:S(2)}) collective-permute-start(bf16[64,256]{1,0:T(8,128)(2,1)S(1)} %get-tuple-element.140), channel_id=1, source_target_pairs={{0,1},{1,2},{2,3},{3,0},{4,5},{5,6},{6,7},{7,4},{8,9},{9,10},{10,1... | collective-permute-start | bytes 98312 | tf_op jit(solution)/shard_map/ppermute | solution.py:25
  193.4 2.9 %collective-permute-done.46.refs_2_ = bf16[64,256]{1,0:T(8,128)(2,1)S(1)} collective-permute-done((bf16[64,256]{1,0:T(8,128)(2,1)S(1)}, bf16[64,256]{1,0:T(8,128)(2,1)S(1)}, u32[]{:S(2)}, u32[]{:S(2)}) %collective-permute-start.46) | collective-permute-done | bytes 32800 | tf_op jit(solution)/shard_map/ppermute | solution.py:25
  (84 shorter events, 23.1 us)
Async XLA Ops:
  3.6 14.1 %collective-permute-start.10 = (bf16[256,256]{1,0:T(8,128)(2,1)S(1)}, bf16[256,256]{1,0:T(8,128)(2,1)S(1)}, u32[]{:S(2)}, u32[]{:S(2)}) collective-permute-start(bf16[256,256]{1,0:T(8,128)(2,1)S(1)} %get-tuple-element.90), channel_id=1, source_target_pairs={{0,1},{1,2},{2,3},{3,0},{4,5},{5,6},{6,7},{7,4},{8,9},{9,10},{10,1... | collective-permute-start | bytes 393224 | tf_op jit(solution)/shard_map/ppermute | solution.py:25
  5.1 15.8 %collective-permute-start.11 = (bf16[256,256]{1,0:T(8,128)(2,1)S(1)}, bf16[256,256]{1,0:T(8,128)(2,1)S(1)}, u32[]{:S(2)}, u32[]{:S(2)}) collective-permute-start(bf16[256,256]{1,0:T(8,128)(2,1)S(1)} %get-tuple-element.91), channel_id=1, source_target_pairs={{0,2},{1,3},{2,0},{3,1},{4,6},{5,7},{6,4},{7,5},{8,10},{9,11},{10,... | collective-permute-start | bytes 393224 | tf_op jit(solution)/shard_map/ppermute | solution.py:25
  8.0 5.2 %collective-permute-start = (bf16[88,256]{1,0:T(8,128)(2,1)S(1)}, bf16[88,256]{1,0:T(8,128)(2,1)S(1)}, u32[]{:S(2)}, u32[]{:S(2)}) collective-permute-start(bf16[88,256]{1,0:T(8,128)(2,1)S(1)} %get-tuple-element.78), channel_id=1, source_target_pairs={{0,1},{1,2},{2,3},{3,0},{4,5},{5,6},{6,7},{7,4},{8,9},{9,10},{10,1... | collective-permute-start | bytes 135176 | tf_op jit(solution)/shard_map/ppermute | solution.py:25
  8.0 5.6 %collective-permute-start.1 = (bf16[88,256]{1,0:T(8,128)(2,1)S(1)}, bf16[88,256]{1,0:T(8,128)(2,1)S(1)}, u32[]{:S(2)}, u32[]{:S(2)}) collective-permute-start(bf16[88,256]{1,0:T(8,128)(2,1)S(1)} %get-tuple-element.79), channel_id=1, source_target_pairs={{0,2},{1,3},{2,0},{3,1},{4,6},{5,7},{6,4},{7,5},{8,10},{9,11},{10,... | collective-permute-start | bytes 135176 | tf_op jit(solution)/shard_map/ppermute | solution.py:25
  10.5 4.0 %collective-permute-start.2 = (bf16[88,256]{1,0:T(8,128)(2,1)S(1)}, bf16[88,256]{1,0:T(8,128)(2,1)S(1)}, u32[]{:S(2)}, u32[]{:S(2)}) collective-permute-start(bf16[88,256]{1,0:T(8,128)(2,1)S(1)} %get-tuple-element.80), channel_id=1, source_target_pairs={{0,3},{1,0},{2,1},{3,2},{4,7},{5,4},{6,5},{7,6},{8,11},{9,8},{10,9... | collective-permute-start | bytes 135176 | tf_op jit(solution)/shard_map/ppermute | solution.py:25
  14.6 11.8 %collective-permute-start.6 = (bf16[4,88,256]{2,1,0:T(8,128)(2,1)S(1)}, bf16[4,88,256]{2,1,0:T(8,128)(2,1)S(1)}, u32[]{:S(2)}, u32[]{:S(2)}) collective-permute-start(bf16[4,88,256]{2,1,0:T(8,128)(2,1)S(1)} %shard_map.92), channel_id=1, source_target_pairs={{0,0},{1,1},{2,2},{3,3},{4,64},{5,65},{6,66},{7,67},{8,128},{9,129... | collective-permute-start | bytes 540680 | tf_op jit(solution)/shard_map/ppermute | solution.py:25
  15.2 5.7 %collective-permute-start.12 = (bf16[256,256]{1,0:T(8,128)(2,1)S(1)}, bf16[256,256]{1,0:T(8,128)(2,1)S(1)}, u32[]{:S(2)}, u32[]{:S(2)}) collective-permute-start(bf16[256,256]{1,0:T(8,128)(2,1)S(1)} %get-tuple-element.92), channel_id=1, source_target_pairs={{0,3},{1,0},{2,1},{3,2},{4,7},{5,4},{6,5},{7,6},{8,11},{9,8},{10,9... | collective-permute-start | bytes 393224 | tf_op jit(solution)/shard_map/ppermute | solution.py:25
  17.6 5.5 %collective-permute-start.3 = (bf16[256,256]{1,0:T(8,128)(2,1)S(1)}, bf16[256,256]{1,0:T(8,128)(2,1)S(1)}, u32[]{:S(2)}, u32[]{:S(2)}) collective-permute-start(bf16[256,256]{1,0:T(8,128)(2,1)S(1)} %get-tuple-element.83), channel_id=1, source_target_pairs={{0,1},{1,2},{2,3},{3,0},{4,5},{5,6},{6,7},{7,4},{8,9},{9,10},{10,1... | collective-permute-start | bytes 393224 | tf_op jit(solution)/shard_map/ppermute | solution.py:25
  17.7 7.3 %collective-permute-start.4 = (bf16[256,256]{1,0:T(8,128)(2,1)S(1)}, bf16[256,256]{1,0:T(8,128)(2,1)S(1)}, u32[]{:S(2)}, u32[]{:S(2)}) collective-permute-start(bf16[256,256]{1,0:T(8,128)(2,1)S(1)} %get-tuple-element.84), channel_id=1, source_target_pairs={{0,2},{1,3},{2,0},{3,1},{4,6},{5,7},{6,4},{7,5},{8,10},{9,11},{10,... | collective-permute-start | bytes 393224 | tf_op jit(solution)/shard_map/ppermute | solution.py:25
  20.9 5.4 %collective-permute-start.5 = (bf16[256,256]{1,0:T(8,128)(2,1)S(1)}, bf16[256,256]{1,0:T(8,128)(2,1)S(1)}, u32[]{:S(2)}, u32[]{:S(2)}) collective-permute-start(bf16[256,256]{1,0:T(8,128)(2,1)S(1)} %get-tuple-element.85), channel_id=1, source_target_pairs={{0,3},{1,0},{2,1},{3,2},{4,7},{5,4},{6,5},{7,6},{8,11},{9,8},{10,9... | collective-permute-start | bytes 393224 | tf_op jit(solution)/shard_map/ppermute | solution.py:25
  21.0 28.2 %collective-permute-start.13 = (bf16[1024,256]{1,0:T(8,128)(2,1)S(1)}, bf16[1024,256]{1,0:T(8,128)(2,1)S(1)}, u32[]{:S(2)}, u32[]{:S(2)}) collective-permute-start(bf16[1024,256]{1,0:T(8,128)(2,1)S(1)} %shard_map.95.refs_4_), channel_id=1, source_target_pairs={{0,32},{1,33},{2,34},{3,35},{4,36},{5,37},{6,38},{7,39},{8,40},{9,... | collective-permute-start | bytes 1572872 | tf_op jit(solution)/shard_map/ppermute | solution.py:25
  26.4 23.4 %collective-permute-start.17 = (bf16[1024,256]{1,0:T(8,128)(2,1)S(1)}, bf16[1024,256]{1,0:T(8,128)(2,1)S(1)}, u32[]{:S(2)}, u32[]{:S(2)}) collective-permute-start(bf16[1024,256]{1,0:T(8,128)(2,1)S(1)} %shard_map.96.refs_8_.refs_4_), channel_id=1, source_target_pairs={{0,32},{1,33},{2,34},{3,35},{4,36},{5,37},{6,38},{7,39},{8,40},{9,... | collective-permute-start | bytes 1572872 | tf_op jit(solution)/shard_map/ppermute | solution.py:25
  28.0 17.8 %collective-permute-start.9 = (bf16[4,88,256]{2,1,0:T(8,128)(2,1)S(1)}, bf16[4,88,256]{2,1,0:T(8,128)(2,1)S(1)}, u32[]{:S(2)}, u32[]{:S(2)}) collective-permute-start(bf16[4,88,256]{2,1,0:T(8,128)(2,1)S(1)} %collective-permute-done.6.refs_0_), channel_id=1, source_target_pairs={{0,12},{1,13},{2,14},{3,15},{4,0},{5,1},{6,2},{7,3},{8,4},{9,5},{1... | collective-permute-start | bytes 540680 | tf_op jit(solution)/shard_map/ppermute | solution.py:25
  38.4 9.0 %collective-permute-start.8 = (bf16[4,88,256]{2,1,0:T(8,128)(2,1)S(1)}, bf16[4,88,256]{2,1,0:T(8,128)(2,1)S(1)}, u32[]{:S(2)}, u32[]{:S(2)}) collective-permute-start(bf16[4,88,256]{2,1,0:T(8,128)(2,1)S(1)} %collective-permute-done.6.refs_0_), channel_id=1, source_target_pairs={{0,8},{1,9},{2,10},{3,11},{4,12},{5,13},{6,14},{7,15},{8,0},{9,1},... | collective-permute-start | bytes 540680 | tf_op jit(solution)/shard_map/ppermute | solution.py:25
  38.5 10.7 %collective-permute-start.7 = (bf16[4,88,256]{2,1,0:T(8,128)(2,1)S(1)}, bf16[4,88,256]{2,1,0:T(8,128)(2,1)S(1)}, u32[]{:S(2)}, u32[]{:S(2)}) collective-permute-start(bf16[4,88,256]{2,1,0:T(8,128)(2,1)S(1)} %collective-permute-done.6.refs_0_), channel_id=1, source_target_pairs={{0,4},{1,5},{2,6},{3,7},{4,8},{5,9},{6,10},{7,11},{8,12},{9,13},{1... | collective-permute-start | bytes 540680 | tf_op jit(solution)/shard_map/ppermute | solution.py:25
  49.2 2.3 %collective-permute-start.14 = (bf16[1024,256]{1,0:T(8,128)(2,1)S(1)}, bf16[1024,256]{1,0:T(8,128)(2,1)S(1)}, u32[]{:S(2)}, u32[]{:S(2)}) collective-permute-start(bf16[1024,256]{1,0:T(8,128)(2,1)S(1)} %shard_map.95.refs_4_), channel_id=1, source_target_pairs={{0,16},{1,17},{2,18},{3,19},{4,20},{5,21},{6,22},{7,23},{8,24},{9,... | collective-permute-start | bytes 1572872 | tf_op jit(solution)/shard_map/ppermute | solution.py:25
  49.2 5.6 %collective-permute-start.15 = (bf16[1024,256]{1,0:T(8,128)(2,1)S(1)}, bf16[1024,256]{1,0:T(8,128)(2,1)S(1)}, u32[]{:S(2)}, u32[]{:S(2)}) collective-permute-start(bf16[1024,256]{1,0:T(8,128)(2,1)S(1)} %collective-permute-done.13.refs_6_), channel_id=1, source_target_pairs={{0,16},{1,17},{2,18},{3,19},{4,20},{5,21},{6,22},{7,23},{8,24},{9,... | collective-permute-start | bytes 1572872 | tf_op jit(solution)/shard_map/ppermute | solution.py:25
  49.8 5.1 %collective-permute-start.16 = (bf16[1024,256]{1,0:T(8,128)(2,1)S(1)}, bf16[1024,256]{1,0:T(8,128)(2,1)S(1)}, u32[]{:S(2)}, u32[]{:S(2)}) collective-permute-start(bf16[1024,256]{1,0:T(8,128)(2,1)S(1)} %shard_map.96.refs_8_.refs_4_), channel_id=1, source_target_pairs={{0,16},{1,17},{2,18},{3,19},{4,20},{5,21},{6,22},{7,23},{8,24},{9,... | collective-permute-start | bytes 1572872 | tf_op jit(solution)/shard_map/ppermute | solution.py:25
  49.8 5.1 %collective-permute-start.18 = (bf16[1024,256]{1,0:T(8,128)(2,1)S(1)}, bf16[1024,256]{1,0:T(8,128)(2,1)S(1)}, u32[]{:S(2)}, u32[]{:S(2)}) collective-permute-start(bf16[1024,256]{1,0:T(8,128)(2,1)S(1)} %collective-permute-done.17.refs_10_.refs_6_), channel_id=1, source_target_pairs={{0,16},{1,17},{2,18},{3,19},{4,20},{5,21},{6,22},{7,23},{8,24},{9,... | collective-permute-start | bytes 1572872 | tf_op jit(solution)/shard_map/ppermute | solution.py:25
  50.7 12.2 %collective-permute-start.22 = (bf16[384,256]{1,0:T(8,128)(2,1)S(1)}, bf16[384,256]{1,0:T(8,128)(2,1)S(1)}, u32[]{:S(2)}, u32[]{:S(2)}) collective-permute-start(bf16[384,256]{1,0:T(8,128)(2,1)S(1)} %get-tuple-element.115), channel_id=1, source_target_pairs={{0,1},{1,2},{2,3},{3,0},{4,5},{5,6},{6,7},{7,4},{8,9},{9,10},{10,1... | collective-permute-start | bytes 589832 | tf_op jit(solution)/shard_map/ppermute | solution.py:25
  51.6 14.4 %collective-permute-start.23 = (bf16[384,256]{1,0:T(8,128)(2,1)S(1)}, bf16[384,256]{1,0:T(8,128)(2,1)S(1)}, u32[]{:S(2)}, u32[]{:S(2)}) collective-permute-start(bf16[384,256]{1,0:T(8,128)(2,1)S(1)} %get-tuple-element.116), channel_id=1, source_target_pairs={{0,2},{1,3},{2,0},{3,1},{4,6},{5,7},{6,4},{7,5},{8,10},{9,11},{10,... | collective-permute-start | bytes 589832 | tf_op jit(solution)/shard_map/ppermute | solution.py:25
  54.8 11.1 %collective-permute-start.24 = (bf16[384,256]{1,0:T(8,128)(2,1)S(1)}, bf16[384,256]{1,0:T(8,128)(2,1)S(1)}, u32[]{:S(2)}, u32[]{:S(2)}) collective-permute-start(bf16[384,256]{1,0:T(8,128)(2,1)S(1)} %get-tuple-element.117), channel_id=1, source_target_pairs={{0,3},{1,0},{2,1},{3,2},{4,7},{5,4},{6,5},{7,6},{8,11},{9,8},{10,9... | collective-permute-start | bytes 589832 | tf_op jit(solution)/shard_map/ppermute | solution.py:25
  57.3 9.5 %collective-permute-start.19 = (bf16[88,1024]{1,0:T(8,128)(2,1)S(1)}, bf16[88,1024]{1,0:T(8,128)(2,1)S(1)}, u32[]{:S(2)}, u32[]{:S(2)}) collective-permute-start(bf16[88,1024]{1,0:T(8,128)(2,1)S(1)} %get-tuple-element.109), channel_id=1, source_target_pairs={{0,64},{1,65},{2,66},{3,67},{4,68},{5,69},{6,70},{7,71},{8,72},{9,... | collective-permute-start | bytes 540680 | tf_op jit(solution)/shard_map/ppermute | solution.py:25
  60.3 13.7 %collective-permute-start.20 = (bf16[88,1024]{1,0:T(8,128)(2,1)S(1)}, bf16[88,1024]{1,0:T(8,128)(2,1)S(1)}, u32[]{:S(2)}, u32[]{:S(2)}) collective-permute-start(bf16[88,1024]{1,0:T(8,128)(2,1)S(1)} %get-tuple-element.110), channel_id=1, source_target_pairs={{0,128},{1,129},{2,130},{3,131},{4,132},{5,133},{6,134},{7,135},{8... | collective-permute-start | bytes 540680 | tf_op jit(solution)/shard_map/ppermute | solution.py:25
  62.9 16.5 %collective-permute-start.21 = (bf16[88,1024]{1,0:T(8,128)(2,1)S(1)}, bf16[88,1024]{1,0:T(8,128)(2,1)S(1)}, u32[]{:S(2)}, u32[]{:S(2)}) collective-permute-start(bf16[88,1024]{1,0:T(8,128)(2,1)S(1)} %get-tuple-element.111), channel_id=1, source_target_pairs={{0,192},{1,193},{2,194},{3,195},{4,196},{5,197},{6,198},{7,199},{8... | collective-permute-start | bytes 540680 | tf_op jit(solution)/shard_map/ppermute | solution.py:25
  99.1 1.7 collective-permute-start.25
  101.5 11.0 %collective-permute-start.28 = (bf16[448,128]{1,0:T(8,128)(2,1)S(1)}, bf16[448,128]{1,0:T(8,128)(2,1)S(1)}, u32[]{:S(2)}, u32[]{:S(2)}) collective-permute-start(bf16[448,128]{1,0:T(8,128)(2,1)S(1)} %get-tuple-element.128.refs_0_), channel_id=1, source_target_pairs={{0,12},{1,13},{2,14},{3,15},{4,0},{5,1},{6,2},{7,3},{8,4},{9,5},{1... | collective-permute-start | bytes 344072 | tf_op jit(solution)/shard_map/ppermute | solution.py:25
  107.3 7.5 %collective-permute-start.27 = (bf16[448,128]{1,0:T(8,128)(2,1)S(1)}, bf16[448,128]{1,0:T(8,128)(2,1)S(1)}, u32[]{:S(2)}, u32[]{:S(2)}) collective-permute-start(bf16[448,128]{1,0:T(8,128)(2,1)S(1)} %get-tuple-element.128.refs_0_), channel_id=1, source_target_pairs={{0,8},{1,9},{2,10},{3,11},{4,12},{5,13},{6,14},{7,15},{8,0},{9,1},... | collective-permute-start | bytes 344072 | tf_op jit(solution)/shard_map/ppermute | solution.py:25
  107.4 8.6 %collective-permute-start.26 = (bf16[448,128]{1,0:T(8,128)(2,1)S(1)}, bf16[448,128]{1,0:T(8,128)(2,1)S(1)}, u32[]{:S(2)}, u32[]{:S(2)}) collective-permute-start(bf16[448,128]{1,0:T(8,128)(2,1)S(1)} %get-tuple-element.128.refs_0_), channel_id=1, source_target_pairs={{0,4},{1,5},{2,6},{3,7},{4,8},{5,9},{6,10},{7,11},{8,12},{9,13},{1... | collective-permute-start | bytes 344072 | tf_op jit(solution)/shard_map/ppermute | solution.py:25
  116.0 5.6 %collective-permute-start.31 = (bf16[448,128]{1,0:T(8,128)(2,1)S(1)}, bf16[448,128]{1,0:T(8,128)(2,1)S(1)}, u32[]{:S(2)}, u32[]{:S(2)}) collective-permute-start(bf16[448,128]{1,0:T(8,128)(2,1)S(1)} %shard_map.101.refs_0_), channel_id=1, source_target_pairs={{0,3},{1,0},{2,1},{3,2},{4,7},{5,4},{6,5},{7,6},{8,11},{9,8},{10,9... | collective-permute-start | bytes 344072 | tf_op jit(solution)/shard_map/ppermute | solution.py:25
  117.0 6.3 %collective-permute-start.30 = (bf16[448,128]{1,0:T(8,128)(2,1)S(1)}, bf16[448,128]{1,0:T(8,128)(2,1)S(1)}, u32[]{:S(2)}, u32[]{:S(2)}) collective-permute-start(bf16[448,128]{1,0:T(8,128)(2,1)S(1)} %shard_map.101.refs_0_), channel_id=1, source_target_pairs={{0,2},{1,3},{2,0},{3,1},{4,6},{5,7},{6,4},{7,5},{8,10},{9,11},{10,... | collective-permute-start | bytes 344072 | tf_op jit(solution)/shard_map/ppermute | solution.py:25
  118.1 7.1 %collective-permute-start.29 = (bf16[448,128]{1,0:T(8,128)(2,1)S(1)}, bf16[448,128]{1,0:T(8,128)(2,1)S(1)}, u32[]{:S(2)}, u32[]{:S(2)}) collective-permute-start(bf16[448,128]{1,0:T(8,128)(2,1)S(1)} %shard_map.101.refs_0_), channel_id=1, source_target_pairs={{0,1},{1,2},{2,3},{3,0},{4,5},{5,6},{6,7},{7,4},{8,9},{9,10},{10,1... | collective-permute-start | bytes 344072 | tf_op jit(solution)/shard_map/ppermute | solution.py:25
  126.2 0.7 collective-permute-start.32
  126.8 16.6 %collective-permute-start.35 = (bf16[4,64,256]{2,1,0:T(8,128)(2,1)S(1)}, bf16[4,64,256]{2,1,0:T(8,128)(2,1)S(1)}, u32[]{:S(2)}, u32[]{:S(2)}) collective-permute-start(bf16[4,64,256]{2,1,0:T(8,128)(2,1)S(1)} %collective-permute-done.32.refs_0_), channel_id=1, source_target_pairs={{0,12},{1,13},{2,14},{3,15},{4,0},{5,1},{6,2},{7,3},{8,4},{9,5},{1... | collective-permute-start | bytes 393224 | tf_op jit(solution)/shard_map/ppermute | solution.py:25
  139.5 6.6 %collective-permute-start.34 = (bf16[4,64,256]{2,1,0:T(8,128)(2,1)S(1)}, bf16[4,64,256]{2,1,0:T(8,128)(2,1)S(1)}, u32[]{:S(2)}, u32[]{:S(2)}) collective-permute-start(bf16[4,64,256]{2,1,0:T(8,128)(2,1)S(1)} %collective-permute-done.32.refs_0_), channel_id=1, source_target_pairs={{0,8},{1,9},{2,10},{3,11},{4,12},{5,13},{6,14},{7,15},{8,0},{9,1},... | collective-permute-start | bytes 393224 | tf_op jit(solution)/shard_map/ppermute | solution.py:25
  139.7 7.6 %collective-permute-start.33 = (bf16[4,64,256]{2,1,0:T(8,128)(2,1)S(1)}, bf16[4,64,256]{2,1,0:T(8,128)(2,1)S(1)}, u32[]{:S(2)}, u32[]{:S(2)}) collective-permute-start(bf16[4,64,256]{2,1,0:T(8,128)(2,1)S(1)} %collective-permute-done.32.refs_0_), channel_id=1, source_target_pairs={{0,4},{1,5},{2,6},{3,7},{4,8},{5,9},{6,10},{7,11},{8,12},{9,13},{1... | collective-permute-start | bytes 393224 | tf_op jit(solution)/shard_map/ppermute | solution.py:25
  148.9 8.7 %collective-permute-start.36 = (bf16[64,1024]{1,0:T(8,128)(2,1)S(1)}, bf16[64,1024]{1,0:T(8,128)(2,1)S(1)}, u32[]{:S(2)}, u32[]{:S(2)}) collective-permute-start(bf16[64,1024]{1,0:T(8,128)(2,1)S(1)} %get-tuple-element.131), channel_id=1, source_target_pairs={{0,64},{1,65},{2,66},{3,67},{4,68},{5,69},{6,70},{7,71},{8,72},{9,... | collective-permute-start | bytes 393224 | tf_op jit(solution)/shard_map/ppermute | solution.py:25
  149.2 16.0 %collective-permute-start.37 = (bf16[64,1024]{1,0:T(8,128)(2,1)S(1)}, bf16[64,1024]{1,0:T(8,128)(2,1)S(1)}, u32[]{:S(2)}, u32[]{:S(2)}) collective-permute-start(bf16[64,1024]{1,0:T(8,128)(2,1)S(1)} %get-tuple-element.132), channel_id=1, source_target_pairs={{0,128},{1,129},{2,130},{3,131},{4,132},{5,133},{6,134},{7,135},{8... | collective-permute-start | bytes 393224 | tf_op jit(solution)/shard_map/ppermute | solution.py:25
  155.1 10.1 %collective-permute-start.38 = (bf16[64,1024]{1,0:T(8,128)(2,1)S(1)}, bf16[64,1024]{1,0:T(8,128)(2,1)S(1)}, u32[]{:S(2)}, u32[]{:S(2)}) collective-permute-start(bf16[64,1024]{1,0:T(8,128)(2,1)S(1)} %get-tuple-element.133), channel_id=1, source_target_pairs={{0,192},{1,193},{2,194},{3,195},{4,196},{5,197},{6,198},{7,199},{8... | collective-permute-start | bytes 393224 | tf_op jit(solution)/shard_map/ppermute | solution.py:25
  165.6 5.9 %collective-permute-start.41 = (bf16[448,128]{1,0:T(8,128)(2,1)S(1)}, bf16[448,128]{1,0:T(8,128)(2,1)S(1)}, u32[]{:S(2)}, u32[]{:S(2)}) collective-permute-start(bf16[448,128]{1,0:T(8,128)(2,1)S(1)} %get-tuple-element.135.refs_0_), channel_id=1, source_target_pairs={{0,12},{1,13},{2,14},{3,15},{4,0},{5,1},{6,2},{7,3},{8,4},{9,5},{1... | collective-permute-start | bytes 344072 | tf_op jit(solution)/shard_map/ppermute | solution.py:25
  166.3 7.5 %collective-permute-start.40 = (bf16[448,128]{1,0:T(8,128)(2,1)S(1)}, bf16[448,128]{1,0:T(8,128)(2,1)S(1)}, u32[]{:S(2)}, u32[]{:S(2)}) collective-permute-start(bf16[448,128]{1,0:T(8,128)(2,1)S(1)} %get-tuple-element.135.refs_0_), channel_id=1, source_target_pairs={{0,8},{1,9},{2,10},{3,11},{4,12},{5,13},{6,14},{7,15},{8,0},{9,1},... | collective-permute-start | bytes 344072 | tf_op jit(solution)/shard_map/ppermute | solution.py:25
  166.3 8.0 %collective-permute-start.39 = (bf16[448,128]{1,0:T(8,128)(2,1)S(1)}, bf16[448,128]{1,0:T(8,128)(2,1)S(1)}, u32[]{:S(2)}, u32[]{:S(2)}) collective-permute-start(bf16[448,128]{1,0:T(8,128)(2,1)S(1)} %get-tuple-element.135.refs_0_), channel_id=1, source_target_pairs={{0,4},{1,5},{2,6},{3,7},{4,8},{5,9},{6,10},{7,11},{8,12},{9,13},{1... | collective-permute-start | bytes 344072 | tf_op jit(solution)/shard_map/ppermute | solution.py:25
  174.4 9.7 %collective-permute-start.44 = (bf16[448,128]{1,0:T(8,128)(2,1)S(1)}, bf16[448,128]{1,0:T(8,128)(2,1)S(1)}, u32[]{:S(2)}, u32[]{:S(2)}) collective-permute-start(bf16[448,128]{1,0:T(8,128)(2,1)S(1)} %shard_map.105.refs_0_), channel_id=1, source_target_pairs={{0,3},{1,0},{2,1},{3,2},{4,7},{5,4},{6,5},{7,6},{8,11},{9,8},{10,9... | collective-permute-start | bytes 344072 | tf_op jit(solution)/shard_map/ppermute | solution.py:25
  180.5 6.3 %collective-permute-start.43 = (bf16[448,128]{1,0:T(8,128)(2,1)S(1)}, bf16[448,128]{1,0:T(8,128)(2,1)S(1)}, u32[]{:S(2)}, u32[]{:S(2)}) collective-permute-start(bf16[448,128]{1,0:T(8,128)(2,1)S(1)} %shard_map.105.refs_0_), channel_id=1, source_target_pairs={{0,2},{1,3},{2,0},{3,1},{4,6},{5,7},{6,4},{7,5},{8,10},{9,11},{10,... | collective-permute-start | bytes 344072 | tf_op jit(solution)/shard_map/ppermute | solution.py:25
  180.5 6.3 %collective-permute-start.42 = (bf16[448,128]{1,0:T(8,128)(2,1)S(1)}, bf16[448,128]{1,0:T(8,128)(2,1)S(1)}, u32[]{:S(2)}, u32[]{:S(2)}) collective-permute-start(bf16[448,128]{1,0:T(8,128)(2,1)S(1)} %shard_map.105.refs_0_), channel_id=1, source_target_pairs={{0,1},{1,2},{2,3},{3,0},{4,5},{5,6},{6,7},{7,4},{8,9},{9,10},{10,1... | collective-permute-start | bytes 344072 | tf_op jit(solution)/shard_map/ppermute | solution.py:25
  187.9 5.4 %collective-permute-start.45 = (bf16[64,256]{1,0:T(8,128)(2,1)S(1)}, bf16[64,256]{1,0:T(8,128)(2,1)S(1)}, u32[]{:S(2)}, u32[]{:S(2)}) collective-permute-start(bf16[64,256]{1,0:T(8,128)(2,1)S(1)} %get-tuple-element.138), channel_id=1, source_target_pairs={{0,3},{1,0},{2,1},{3,2},{4,7},{5,4},{6,5},{7,6},{8,11},{9,8},{10,9... | collective-permute-start | bytes 98312 | tf_op jit(solution)/shard_map/ppermute | solution.py:25
  190.8 5.4 %collective-permute-start.46 = (bf16[64,256]{1,0:T(8,128)(2,1)S(1)}, bf16[64,256]{1,0:T(8,128)(2,1)S(1)}, u32[]{:S(2)}, u32[]{:S(2)}) collective-permute-start(bf16[64,256]{1,0:T(8,128)(2,1)S(1)} %get-tuple-element.139), channel_id=1, source_target_pairs={{0,2},{1,3},{2,0},{3,1},{4,6},{5,7},{6,4},{7,5},{8,10},{9,11},{10,... | collective-permute-start | bytes 98312 | tf_op jit(solution)/shard_map/ppermute | solution.py:25
  190.8 5.4 %collective-permute-start.47 = (bf16[64,256]{1,0:T(8,128)(2,1)S(1)}, bf16[64,256]{1,0:T(8,128)(2,1)S(1)}, u32[]{:S(2)}, u32[]{:S(2)}) collective-permute-start(bf16[64,256]{1,0:T(8,128)(2,1)S(1)} %get-tuple-element.140), channel_id=1, source_target_pairs={{0,1},{1,2},{2,3},{3,0},{4,5},{5,6},{6,7},{7,4},{8,9},{9,10},{10,1... | collective-permute-start | bytes 98312 | tf_op jit(solution)/shard_map/ppermute | solution.py:25
  (9 other events, 90.0 us)
